TPU v7x, 512 devices: a whole 4x8x8 slice. The times are simulated.
512 devices in a mesh: ctx: 64 (over y_hi, x, z), exp: 8 (over y_lo, core).
Axes of the slice: x: 4, y: 8 (y_hi: 2, y_lo: 4; y = y_hi * 4 + y_lo), z: 8, core: 2. Of those that a mesh axis runs over, the one named last changes fastest.
Arguments:
- queries: bfloat16 [4096, 6144], P('ctx', 'exp'), may hold values from -5 to 5
- keys: bfloat16 [4096, 1024], P('ctx', 'exp'), may hold values from -5 to 5
- values: bfloat16 [4096, 1024], P('ctx', 'exp'), may hold values from -16 to 16
- residual: bfloat16 [4096, 6144], P('ctx', 'exp'), may hold values from -25 to 25
- norm_gain: float32 [6144], P('exp'), may hold values from 0.5 to 1.5
- routes: int32 [4096, 1], P('ctx'), may hold values from 0 to 3; in each aligned block of 64 rows (0 to 63, 64 to 127, ...) at most 24 rows name the same one
- route_weight: float32 [4096], P('ctx'), may hold values from 0.25 to 1
- w_gate: bfloat16 [65536, 6144], P('ctx', 'exp'), may hold values from -0.078125 to 0.078125
- w_up: bfloat16 [65536, 6144], P('ctx', 'exp'), may hold values from -0.078125 to 0.078125
- w_down: bfloat16 [65536, 6144], P('ctx', 'exp'), may hold values from -0.046875 to 0.046875
Outputs:
- moe_out: bfloat16 [4096, 6144], P('ctx', 'exp')
Inputs may be any that keep to these rules, and one draw needn't show every extreme that they name: `routes`: within the 64 rows of one device, at most 24 tokens have the same route.
All inputs are finite; a program needn't handle non-finite values.
Results may differ from a plain program's by a relative error of at most 0.029.
Values may be sent and summed in bfloat16 or wider, within the bound.
No kernel may reach another device: no remote copies, remote signals or barrier semaphores. Data moves between devices by JAX's collectives and lax.ppermute only.
A program may use at most 64 MiB of HBM per device.

v0:
```python
import math

import jax
import jax.numpy as jnp
from jax import lax
from jax.sharding import PartitionSpec as P

D = 6144
HD = 128
EXPERTS = 4
CAP = 24


def body(queries, keys, values, residual, norm_gain, routes, route_weight, w_gate, w_up, w_down):
    tok_rows = queries.shape[0]
    heads_kv = keys.shape[1] // HD
    heads_query = queries.shape[1] // HD
    group_size = heads_query // heads_kv
    first_pos = lax.axis_index("ctx") * tok_rows
    last_pos = first_pos + tok_rows - 1
    score_scale = 1.0 / math.sqrt(HD)
    query_block = (
        queries.reshape(tok_rows, heads_kv, group_size, HD)
        .transpose(1, 2, 0, 3)
        .reshape(heads_kv, group_size * tok_rows, HD)
    )
    query_pos = first_pos + jnp.tile(jnp.arange(tok_rows, dtype=jnp.int32), group_size)
    initial = (
        jnp.full((heads_kv, group_size * tok_rows), -1e30, jnp.float32),
        jnp.zeros((heads_kv, group_size * tok_rows), jnp.float32),
        jnp.zeros((heads_kv, group_size * tok_rows, HD), jnp.float32),
    )
    key_shard = lax.all_gather(keys, "ctx", axis=0, tiled=True)
    value_shard = lax.all_gather(values, "ctx", axis=0, tiled=True)
    key_count = key_shard.shape[0]

    def compute(status):
        running_max, running_sum, running_acc = status
        key_block = key_shard.reshape(key_count, heads_kv, HD).transpose(1, 0, 2)
        value_block = value_shard.reshape(key_count, heads_kv, HD).transpose(1, 0, 2)
        scores = (
            jnp.einsum("gqd,gkd->gqk", query_block, key_block, preferred_element_type=jnp.float32)
            * score_scale
        )
        key_pos = jnp.arange(key_count, dtype=jnp.int32)
        allowed = (key_pos[None, :] <= query_pos[:, None])[None, :, :]
        masked = jnp.where(allowed, scores, -1e30)
        fresh_max = jnp.maximum(running_max, jnp.max(masked, axis=2))
        weights = jnp.where(allowed, jnp.exp(masked - fresh_max[:, :, None]), 0.0)
        new_sum = jnp.sum(weights, axis=2)
        products = jnp.einsum(
            "gqk,gkd->gqd",
            weights.astype(jnp.bfloat16),
            value_block,
            preferred_element_type=jnp.float32,
        )
        return (fresh_max, new_sum, products)

    def unchanged(status):
        return status

    final_max, final_sum, final_acc = lax.cond(
        jnp.int32(0) <= last_pos, compute, unchanged, initial
    )
    attn_heads = final_acc / final_sum[:, :, None]
    attn = (
        attn_heads.reshape(heads_kv, group_size, tok_rows, HD)
        .transpose(2, 0, 1, 3)
        .reshape(tok_rows, heads_query * HD)
        .astype(jnp.bfloat16)
    )
    mixed = residual.astype(jnp.float32) + attn.astype(jnp.float32)
    local_squares = jnp.sum(mixed * mixed, axis=1)
    total_squares = lax.psum(local_squares, "exp")
    normed = (mixed * lax.rsqrt(total_squares / D + 1e-05)[:, None] * norm_gain[None, :]).astype(
        jnp.bfloat16
    )
    feat_local = normed.shape[1]
    chosen = routes[:, 0]
    expert_ids = jnp.arange(EXPERTS, dtype=jnp.int32)
    onehot = (chosen[:, None] == expert_ids[None, :]).astype(jnp.int32)
    slot_index = jnp.sum((jnp.cumsum(onehot, axis=0) - 1) * onehot, axis=1)
    slot_ids = jnp.arange(CAP, dtype=jnp.int32)
    select = (
        (chosen[None, None, :] == expert_ids[:, None, None])
        & (slot_index[None, None, :] == slot_ids[None, :, None])
    ).astype(jnp.float32)
    packed = jnp.einsum(
        "ect,td->ecd", select.astype(jnp.bfloat16), normed, preferred_element_type=jnp.float32
    ).astype(jnp.bfloat16)
    ctx_count = lax.axis_size("ctx")
    members = ctx_count // EXPERTS
    outgoing = jnp.broadcast_to(packed[:, None], (EXPERTS, members, CAP, feat_local)).reshape(
        ctx_count, CAP, feat_local
    )
    incoming = lax.all_to_all(outgoing, "ctx", split_axis=0, concat_axis=0, tiled=True)
    slot_count = incoming.shape[1]
    flat_rows = incoming.reshape(ctx_count * slot_count, feat_local)
    gate_part = jnp.einsum("rd,fd->rf", flat_rows, w_gate, preferred_element_type=jnp.float32)
    up_part = jnp.einsum("rd,fd->rf", flat_rows, w_up, preferred_element_type=jnp.float32)
    gate_full = lax.psum(gate_part.astype(jnp.bfloat16), "exp").astype(jnp.float32)
    up_full = lax.psum(up_part.astype(jnp.bfloat16), "exp").astype(jnp.float32)
    hidden = (jax.nn.silu(gate_full) * up_full).astype(jnp.bfloat16)
    down_part = jnp.dot(hidden, w_down, preferred_element_type=jnp.float32).reshape(
        ctx_count, slot_count, feat_local
    )
    returned = lax.all_to_all(
        down_part.astype(jnp.bfloat16), "ctx", split_axis=0, concat_axis=0, tiled=True
    ).astype(down_part.dtype)
    combined = returned.reshape(EXPERTS, members, CAP, feat_local).sum(axis=1)
    moe_rows = jnp.einsum(
        "ect,ecd->td",
        select,
        combined,
        precision=lax.Precision.HIGHEST,
        preferred_element_type=jnp.float32,
    )
    return (route_weight[:, None] * moe_rows).astype(jnp.bfloat16)


def solution(mesh):
    in_specs = (
        P("ctx", "exp"),
        P("ctx", "exp"),
        P("ctx", "exp"),
        P("ctx", "exp"),
        P("exp"),
        P("ctx", None),
        P("ctx"),
        P("ctx", "exp"),
        P("ctx", "exp"),
        P("ctx", "exp"),
    )
    out_specs = P("ctx", "exp")
    return jax.shard_map(body, mesh=mesh, in_specs=in_specs, out_specs=out_specs, check_vma=False)
```

profile of v0, /device:TPU:40, one launch (start us, length us, event | category | flops | bytes accessed | tf_op | source)
XLA Modules:
  0.0 611.7 jit_solution(5762565364103222619)
XLA Ops:
  6.5 0.7 all-gather.3.cloned.1.call-update
  7.3 0.7 all-gather.5.cloned.1.call-update
  8.1 0.7 fusion.22
  8.9 1.0 reshape.116
  9.9 0.8 select_reduce_fusion
  10.8 0.7 iota_compare_fusion.3
  11.4 128.2 %all-gather.3.cloned.1.call-done = bf16[4096,128]{1,0:T(8,128)(2,1)} async-done(((bf16[64,128]{1,0:T(8,128)(2,1)}), bf16[4096,128]{1,0:T(8,128)(2,1)}) %all-gather.3.cloned.1.call-update) | async-done | bytes 1048592 | tf_op jit(solution)/shard_map/all_gather | solution.py:33
  139.6 125.6 %all-gather.5.cloned.1.call-done = bf16[4096,128]{1,0:T(8,128)(2,1)} async-done(((bf16[64,128]{1,0:T(8,128)(2,1)}), bf16[4096,128]{1,0:T(8,128)(2,1)}) %all-gather.5.cloned.1.call-update) | async-done | bytes 1048592 | tf_op jit(solution)/shard_map/all_gather | solution.py:34
  265.2 6.3 %conditional.1 = (f32[1,384]{1,0:T(1,128)S(1)}, f32[1,384,128]{2,1,0:T(8,128)S(1)}) conditional(s32[]{:T(128)} %convert_element_type.72, () %tuple.13, (s32[]{:T(128)}, s32[6,64]{1,0:T(8,128)S(1)}, bf16[1,6,64,128]{3,1,2,0:T(8,128)(2,1)S(1)}, bf16[4096,128]{1,0:T(8,128)(2,1)}, bf16[4096,128]{1,0:T(8,128)(2,1)}) %tuple.26), branch_computations={%region_2.0_spmd, %region_3.6_spmd} | conditional | flops 824180736 | bytes 25680432 | solution.py:62
  265.3 2.6 fusion.29
  268.0 1.9 fusion.4
  269.9 1.6 fusion.1
  271.7 0.1 multiply_reduce_fusion
  271.9 10.3 %psum.21 = f32[64]{0:T(128)S(1)} all-reduce(f32[64]{0:T(128)S(1)} %multiply_reduce_fusion), channel_id=1, replica_groups=mesh['ctx'=64,'exp'=8] {'exp'}, use_global_device_ids=true, to_apply=%region_7.8 | all-reduce | flops 64 | bytes 512 | tf_op jit(solution)/shard_map/psum | solution.py:74
  282.2 0.2 convolution_convert_fusion.3
  282.4 0.2 broadcast_in_dim.22
  282.6 69.9 %all_to_all.10 = bf16[64,24,768]{2,1,0:T(8,128)(2,1)S(1)} all-to-all(bf16[64,24,768]{2,1,0:T(8,128)(2,1)S(1)} %bitcast.42), channel_id=1, replica_groups=mesh['ctx'=64,'exp'=8] {'ctx'}, dimensions={0} | all-to-all | bytes 4718592 | tf_op jit(solution)/shard_map/all_to_all | solution.py:96
  352.5 4.2 convolution_convert_fusion
  356.7 4.2 convolution_convert_fusion.1
  360.9 154.0 %all-reduce.3.cloned.1.call-done = (bf16[1536,1024]{1,0:T(8,128)(2,1)}, bf16[1536,1024]{1,0:T(8,128)(2,1)}) async-done(((bf16[1536,1024]{1,0:T(8,128)(2,1)}, bf16[1536,1024]{1,0:T(8,128)(2,1)}), (bf16[1536,1024]{1,0:T(8,128)(2,1)}, bf16[1536,1024]{1,0:T(8,128)(2,1)})) %all-reduce.3.cloned.1.call-update) | async-done | bytes 6291472 | tf_op jit(solution)/shard_map/psum | solution.py:102
  514.9 6.7 %convolution_convert_fusion.2 = bf16[1536,768]{1,0:T(8,128)(2,1)S(1)} fusion(bf16[1024,768]{1,0:T(8,128)(2,1)S(1)} %copy-done.5, bf16[1536,1024]{1,0:T(8,128)(2,1)} %get-tuple-element.33, bf16[1536,1024]{1,0:T(8,128)(2,1)} %get-tuple-element.34), kind=kOutput, calls=%fused_computation.20 | convolution fusion | flops 2429681664 | bytes 10223616 | tf_op jit(solution)/shard_map/dot_general | solution.py:104
  521.6 82.3 %all_to_all.11 = bf16[64,24,768]{2,1,0:T(8,128)(2,1)S(1)} all-to-all(bf16[64,24,768]{2,1,0:T(8,128)(2,1)S(1)} %bitcast.45), channel_id=1, replica_groups=mesh['ctx'=64,'exp'=8] {'ctx'}, dimensions={0} | all-to-all | bytes 4718592 | tf_op jit(solution)/shard_map/all_to_all | solution.py:107
  603.9 0.3 convert_reduce_fusion
  604.2 0.9 fusion.15
  (30 shorter events, 0.6 us)
Async XLA Ops:
  6.5 345.9 %copy-start = (bf16[1024,768]{1,0:T(8,128)(2,1)S(1)}, bf16[1024,768]{1,0:T(8,128)(2,1)}, u32[]{:S(2)}) copy-start(bf16[1024,768]{1,0:T(8,128)(2,1)} %param.20) | copy-start | bytes 4718596
  6.5 133.1 %all-gather.3.cloned.1.call-start = ((), (), s32[]{:S(2)}) async-start(), calls=%async_computation.2 | async-start | bytes 1064960 | tf_op jit(solution)/shard_map/all_gather | solution.py:33
  7.3 257.9 %all-gather.5.cloned.1.call-start = ((), (), s32[]{:S(2)}) async-start(), calls=%async_computation.3 | async-start | bytes 1064960 | tf_op jit(solution)/shard_map/all_gather | solution.py:34
  8.0 506.9 %all-reduce.3.cloned.1.call-start = ((), (), s32[]{:S(2)}) async-start(), calls=%async_computation.4 | async-start | bytes 12582912 | tf_op jit(solution)/shard_map/psum | solution.py:102
  265.2 6.5 %copy-start.1 = (bf16[64,768]{1,0:T(8,128)(2,1)S(1)}, bf16[64,768]{1,0:T(8,128)(2,1)}, u32[]{:S(2)}) copy-start(bf16[64,768]{1,0:T(8,128)(2,1)} %param.15) | copy-start | bytes 294916
  265.2 17.0 %copy-start.2 = (f32[768]{0:T(1024)S(1)}, f32[768]{0:T(1024)}, u32[]{:S(2)}) copy-start(f32[768]{0:T(1024)} %param.16) | copy-start | bytes 9220
  265.3 2.7 copy-start.6
  352.5 4.2 copy-start.4
  360.8 154.0 %copy-start.5 = (bf16[1024,768]{1,0:T(8,128)(2,1)S(1)}, bf16[1024,768]{1,0:T(8,128)(2,1)}, u32[]{:S(2)}) copy-start(bf16[1024,768]{1,0:T(8,128)(2,1)} %param.21) | copy-start | bytes 4718596
  521.6 82.6 %copy-start.3 = (f32[64]{0:T(128)S(1)}, f32[64]{0:T(128)}, u32[]{:S(2)}) copy-start(f32[64]{0:T(128)} %param.18) | copy-start | bytes 772
Sparse Core Ops, SparseCore 0:
  11.7 127.8 all-gather.2
  144.0 121.1 all-gather.4
  361.0 153.8 all-reduce.2
where the time goes:
time: 612 us
  waiting for transfers between devices  409 us (67%)
  blocking collectives  162 us (26%)
  matrix products  20.8 us (3%)
  between operations  13.2 us (2%)
    psum x1, waiting for transfers between devices, body(): up_full = lax.psum(up_part.astype(jnp.bfloat16), 'exp').astype(jnp.float32)  154 us
    all_gather x1, waiting for transfers between devices, body(): key_shard = lax.all_gather(keys, 'ctx', axis=0, tiled=True)  128 us
    all_gather x1, waiting for transfers between devices, body(): value_shard = lax.all_gather(values, 'ctx', axis=0, tiled=True)  126 us
    all_to_all x1, blocking collectives, body(): lax.all_to_all(down_part.astype(jnp.bfloat16), 'ctx', split_axis=0, conca...  82.3 us
    all_to_all x1, blocking collectives, body(): lax.all_to_all(outgoing, 'ctx', split_axis=0, concat_axis=0, tiled=True)  69.9 us
  transfers between devices with their start and end apart: 3, of which 3 were waited for; matrix products, arithmetic and copies ran while one was open for 1% of the time, Pallas kernels for 0%

commit v1 on v0

v1 whole, which is shorter than its diff:
```python
import math

import jax
import jax.numpy as jnp
from jax import lax
from jax.sharding import Mesh, PartitionSpec as P

D = 6144
HD = 128
EXPERTS = 4
CAP = 24
CHUNKS = 2
F32 = jnp.float32
BF16 = jnp.bfloat16

CTX = ("yh", "xh", "xl", "z")
EXP = ("yl", "c")
HALF = ("xh", "xl", "z")
SWAP = [(0, 1), (1, 0)]
Y_XOR = [[(i, i ^ k) for i in range(4)] for k in range(4)]


def swap(x, axis):
    return lax.ppermute(x, axis, SWAP)


def split3(v):
    hi = lax.reduce_precision(v, 8, 7)
    mid = lax.reduce_precision(v - hi, 8, 7)
    lo = (v - hi) - mid
    return [p.astype(BF16) for p in (hi, mid, lo)]


def attend(queries, keys, values):
    rows = queries.shape[0]
    heads = queries.shape[1] // HD
    yh = lax.axis_index("yh")
    scale = 1.0 / math.sqrt(HD)

    foreign = lax.ppermute(queries, "yh", [(1, 0)])
    kv = jnp.concatenate([keys, values], axis=1)
    members = lax.axis_size(HALF)
    kv = lax.all_to_all(
        jnp.broadcast_to(kv[None], (members,) + kv.shape), HALF, split_axis=0, concat_axis=0, tiled=True
    ).reshape(members * rows, 2 * HD)
    k_all, v_all = kv[:, :HD], kv[:, HD:]
    count = members * rows

    def stacked(q):
        return q.reshape(rows, heads, HD).transpose(1, 0, 2).reshape(heads * rows, HD)

    q_all = jnp.concatenate([stacked(queries), stacked(foreign)], axis=0)
    own_pos = lax.axis_index(HALF) * rows + jnp.tile(jnp.arange(rows, dtype=jnp.int32), heads)
    limit = jnp.concatenate([own_pos, jnp.full_like(own_pos, count)])
    scores = jnp.einsum("qd,kd->qk", q_all, k_all, preferred_element_type=F32) * scale
    allowed = jnp.arange(count, dtype=jnp.int32)[None, :] <= limit[:, None]
    scores = jnp.where(allowed, scores, -1e30)
    top = jnp.max(scores, axis=1)
    weights = jnp.exp(scores - top[:, None])
    total = jnp.sum(weights, axis=1)
    acc = jnp.einsum("qk,kd->qd", weights.astype(BF16), v_all, preferred_element_type=F32)
    out = acc / total[:, None]
    lse = top + jnp.log(total)

    n = heads * rows

    def unstacked(o):
        return o.reshape(heads, rows, HD).transpose(1, 0, 2).reshape(rows, heads * HD)

    out_own, out_far = unstacked(out[:n]), unstacked(out[n:])
    lse_own, lse_far = lse[:n].reshape(heads, rows).T, lse[n:].reshape(heads, rows).T
    tail = jnp.concatenate(split3(lse_far), axis=1)
    tail = jnp.pad(tail, ((0, 0), (0, HD - tail.shape[1])))
    message = jnp.concatenate([out_far.astype(BF16), tail], axis=1)
    got = lax.ppermute(message, "yh", [(0, 1)])
    got_out = got[:, : heads * HD].astype(F32)
    parts = got[:, heads * HD : heads * HD + 3 * heads].astype(F32)
    got_lse = parts[:, :heads] + parts[:, heads : 2 * heads] + parts[:, 2 * heads :]
    share = jnp.where(yh == 1, jax.nn.sigmoid(got_lse - lse_own), 0.0)
    share = jnp.repeat(share, HD, axis=1)
    return (out_own * (1.0 - share) + got_out * share).astype(BF16)


def body(queries, keys, values, residual, norm_gain, routes, route_weight, w_gate, w_up, w_down):
    rows = queries.shape[0]
    feat = residual.shape[1]
    hidden_local = w_gate.shape[0]
    half = hidden_local // 2
    core = lax.axis_index("c")

    def halves(w, which):
        return lax.dynamic_slice_in_dim(w, which * half, half, axis=0)

    w_in = jnp.concatenate([halves(w_gate, core), halves(w_up, core)], axis=0)
    w_in_other = swap(jnp.concatenate([halves(w_gate, 1 - core), halves(w_up, 1 - core)], axis=0), "c")
    w_out = halves(w_down, core)
    w_out_other = halves(w_down, 1 - core)

    attn = attend(queries, keys, values)
    mixed = residual.astype(F32) + attn.astype(F32)
    total_squares = lax.psum(jnp.sum(mixed * mixed, axis=1), EXP)
    normed = (mixed * lax.rsqrt(total_squares / D + 1e-05)[:, None] * norm_gain[None, :]).astype(BF16)

    chosen = routes[:, 0]
    expert_ids = jnp.arange(EXPERTS, dtype=jnp.int32)
    onehot = (chosen[:, None] == expert_ids[None, :]).astype(jnp.int32)
    slot_index = jnp.sum((jnp.cumsum(onehot, axis=0) - 1) * onehot, axis=1)
    slot_ids = jnp.arange(CAP, dtype=jnp.int32)
    select = (
        (chosen[None, None, :] == expert_ids[:, None, None])
        & (slot_index[None, None, :] == slot_ids[None, :, None])
    ).astype(BF16)
    packed = jnp.einsum("ect,td->ecd", select, normed, preferred_element_type=F32).astype(BF16)
    incoming = lax.all_to_all(packed, ("yh", "xh"), split_axis=0, concat_axis=0, tiled=True)

    nz = lax.axis_size("z")
    ny = lax.axis_size("yl")
    slots = CAP // CHUNKS
    block = EXPERTS * slots
    outs = []
    for k in range(CHUNKS):
        part = incoming[:, k * slots : (k + 1) * slots].reshape(block, feat)
        near = lax.all_to_all(
            jnp.broadcast_to(part[None], (nz, block, feat)), "z", split_axis=0, concat_axis=0, tiled=True
        ).reshape(nz * block, feat)
        x = jnp.concatenate([near, swap(near, "xl")], axis=0)
        x_other = swap(x, "c")
        gate_up = (
            jnp.einsum("rd,fd->rf", x, w_in, preferred_element_type=F32)
            + jnp.einsum("rd,fd->rf", x_other, w_in_other, preferred_element_type=F32)
        )
        n_rows = gate_up.shape[0]
        share = n_rows // ny
        gate_up = gate_up.astype(BF16).reshape(ny, share, 2 * half)
        me = lax.axis_index("yl")

        def piece(i):
            return lax.dynamic_index_in_dim(gate_up, me ^ i, 0, keepdims=False)

        full = piece(0).astype(F32)
        for i in range(1, ny):
            full = full + lax.ppermute(piece(i), "yl", Y_XOR[i]).astype(F32)
        hidden = (jax.nn.silu(full[:, :half]) * full[:, half:]).astype(BF16)
        hid = jnp.zeros((ny, share, half), BF16)
        hid = lax.dynamic_update_index_in_dim(hid, hidden, me, 0)
        for i in range(1, ny):
            hid = lax.dynamic_update_index_in_dim(hid, lax.ppermute(hidden, "yl", Y_XOR[i]), me ^ i, 0)
        hid = hid.reshape(n_rows, half)
        hid_other = swap(hid, "c")
        down = (
            jnp.dot(hid, w_out, preferred_element_type=F32)
            + jnp.dot(hid_other, w_out_other, preferred_element_type=F32)
        )
        stay, leave = down[: n_rows // 2], down[n_rows // 2 :]
        summed = (stay + swap(leave.astype(BF16), "xl").astype(F32)).astype(BF16)
        back = lax.all_to_all(summed.reshape(nz, block, feat), "z", split_axis=0, concat_axis=0, tiled=True)
        outs.append(jnp.sum(back.astype(F32), axis=0).astype(BF16).reshape(EXPERTS, slots, feat))
    out = jnp.concatenate(outs, axis=1)
    returned = lax.all_to_all(out, ("yh", "xh"), split_axis=0, concat_axis=0, tiled=True)
    moe_rows = jnp.einsum("ect,ecd->td", select, returned, preferred_element_type=F32)
    return (route_weight[:, None] * moe_rows).astype(BF16)


def solution(mesh):
    fine = Mesh(mesh.devices.reshape(2, 2, 2, 8, 4, 2), CTX + EXP)
    wide = P(CTX, EXP)
    in_specs = (wide, wide, wide, wide, P(EXP), P(CTX, None), P(CTX), wide, wide, wide)
    return jax.shard_map(body, mesh=fine, in_specs=in_specs, out_specs=wide, check_vma=False)
```

time: 612 us -> 369 us (0.60)
  the two profiles are of different devices: /device:TPU:40 before, /device:TPU:8 now
where the time goes in v1:
time: 369 us; the launch traced here: 368 us
  waiting for transfers between devices  187 us (51%)
  starting transfers between devices  97 us (26%)
  blocking collectives  44.6 us (12%)
  matrix products  19.7 us (5%)
  other arithmetic  10.2 us (3%)
  local copies, waits for them, and re-layouts  8.49 us (2%)
    ppermute x6, waiting for transfers between devices, body(): full = full + lax.ppermute(piece(i), 'yl', Y_XOR[i]).astype(F32)  51 us
    ppermute x9, waiting for transfers between devices, swap(): return lax.ppermute(x, axis, SWAP)  49.9 us
    ppermute x6, waiting for transfers between devices, body(): lax.ppermute(hidden, 'yl', Y_XOR[i])  21.5 us
    all_to_all x1, blocking collectives, body(): lax.all_to_all(packed, ('yh', 'xh'), split_axis=0, concat_axis=0, tiled=T...  20.1 us
    ppermute x6, starting transfers between devices, body(): full = full + lax.ppermute(piece(i), 'yl', Y_XOR[i]).astype(F32)  19.3 us
    ppermute x9, starting transfers between devices, swap(): return lax.ppermute(x, axis, SWAP)  18.1 us
    all_to_all x2, waiting for transfers between devices, body(): lax.all_to_all(jnp.broadcast_to(part[None], (nz, block, feat)), 'z', spli...  17.9 us
    all_to_all x2, waiting for transfers between devices, body(): lax.all_to_all(summed.reshape(nz, block, feat), 'z', split_axis=0, concat...  17.2 us
  transfers between devices with their start and end apart: 28, of which 16 were waited for; matrix products, arithmetic and copies ran while one was open for 7% of the time, Pallas kernels for 0%

profile of v1, /device:TPU:8, one launch (start us, length us, event | category | flops | bytes accessed | tf_op | source)
XLA Modules:
  0.0 368.0 jit_solution(5424616710159542530)
XLA Ops:
  2.0 13.2 %all-to-all-start = ((bf16[32,64,256]{2,1,0:T(8,128)(2,1)}), bf16[32,64,256]{2,1,0:T(8,128)(2,1)S(1)}, u32[]{:S(2)}, u32[]{:S(2)}) async-start(bf16[32,64,256]{2,1,0:T(8,128)(2,1)} %broadcast_in_dim.68), calls=%async_computation | async-start | bytes 2097152 | tf_op jit(solution)/shard_map/all_to_all | solution.py:43
  17.1 10.6 %collective-permute-done = bf16[64,768]{1,0:T(8,128)(2,1)S(1)} collective-permute-done((bf16[64,768]{1,0:T(8,128)(2,1)S(1)}, bf16[64,768]{1,0:T(8,128)(2,1)S(1)}, u32[]{:S(2)}, u32[]{:S(2)}) %collective-permute-start) | collective-permute-done | bytes 98336 | tf_op jit(solution)/shard_map/ppermute | solution.py:40
  27.8 15.9 %all-to-all-done = bf16[32,64,256]{2,1,0:T(8,128)(2,1)S(1)} async-done(((bf16[32,64,256]{2,1,0:T(8,128)(2,1)}), bf16[32,64,256]{2,1,0:T(8,128)(2,1)S(1)}, u32[]{:S(2)}, u32[]{:S(2)}) %all-to-all-start) | async-done | bytes 1048608 | tf_op jit(solution)/shard_map/all_to_all | solution.py:43
  49.4 6.8 %collective-permute-start.1 = (bf16[64,896]{1,0:T(8,128)(2,1)S(1)}, bf16[64,896]{1,0:T(8,128)(2,1)S(1)}, u32[]{:S(2)}, u32[]{:S(2)}) collective-permute-start(bf16[64,896]{1,0:T(8,128)(2,1)S(1)} %fusion.34), channel_id=1, source_target_pairs={{0,256},{1,257},{2,258},{3,259},{4,260},{5,261},{6,262},{7,263},{8... | collective-permute-start | bytes 344072 | tf_op jit(solution)/shard_map/ppermute | solution.py:75
  60.2 10.0 %psum.7 = f32[64]{0:T(128)S(1)} all-reduce(f32[64]{0:T(128)S(1)} %get-tuple-element.9), channel_id=1, replica_groups=mesh['yh'=2,'xh'=2,'xl'=2,'z'=8,'yl'=4,'c'=2] {'yl','c'}, use_global_device_ids=true, to_apply=%region_5.6 | all-reduce | flops 64 | bytes 512 | tf_op jit(solution)/shard_map/psum | solution.py:101
  70.5 20.1 %all_to_all.35 = bf16[4,24,768]{2,1,0:T(8,128)(2,1)S(1)} all-to-all(bf16[4,24,768]{2,1,0:T(8,128)(2,1)S(1)} %convolution_convert_fusion), channel_id=1, replica_groups=mesh['yh'=2,'xh'=2,'xl'=2,'z'=8,'yl'=4,'c'=2] {'yh','xh'}, dimensions={0} | all-to-all | bytes 294912 | tf_op jit(solution)/shard_map/all_to_all | solution.py:114
  91.5 4.8 %all-to-all-start.2 = ((bf16[8,48,768]{2,1,0:T(8,128)(2,1)}), bf16[8,48,768]{2,1,0:T(8,128)(2,1)S(1)}, u32[]{:S(2)}, u32[]{:S(2)}) async-start(bf16[8,48,768]{2,1,0:T(8,128)(2,1)} %broadcast_in_dim.73), calls=%async_computation.2 | async-start | bytes 1179648 | tf_op jit(solution)/shard_map/all_to_all | solution.py:123
  96.3 17.9 %all-to-all-done.2 = bf16[8,48,768]{2,1,0:T(8,128)(2,1)S(1)} async-done(((bf16[8,48,768]{2,1,0:T(8,128)(2,1)}), bf16[8,48,768]{2,1,0:T(8,128)(2,1)S(1)}, u32[]{:S(2)}, u32[]{:S(2)}) %all-to-all-start.2) | async-done | bytes 589856 | tf_op jit(solution)/shard_map/all_to_all | solution.py:123
  126.7 6.9 %collective-permute-done.2 = bf16[384,768]{1,0:T(8,128)(2,1)S(1)} collective-permute-done((bf16[384,768]{1,0:T(8,128)(2,1)S(1)}, bf16[384,768]{1,0:T(8,128)(2,1)S(1)}, u32[]{:S(2)}, u32[]{:S(2)}) %collective-permute-start.2) | collective-permute-done | bytes 589856 | tf_op jit(solution)/shard_map/ppermute | solution.py:24
  139.0 15.4 %collective-permute-done.13 = bf16[384,768]{1,0:T(8,128)(2,1)S(1)} collective-permute-done((bf16[384,768]{1,0:T(8,128)(2,1)S(1)}, bf16[384,768]{1,0:T(8,128)(2,1)S(1)}, u32[]{:S(2)}, u32[]{:S(2)}) %collective-permute-start.13) | collective-permute-done | bytes 589856 | tf_op jit(solution)/shard_map/ppermute | solution.py:24
  177.5 3.9 %collective-permute-start.15 = (bf16[192,1024]{1,0:T(8,128)(2,1)S(1)}, bf16[192,1024]{1,0:T(8,128)(2,1)S(1)}, u32[]{:S(2)}, u32[]{:S(2)}) collective-permute-start(bf16[192,1024]{1,0:T(8,128)(2,1)S(1)} %get-tuple-element.14), channel_id=1, source_target_pairs={{0,2},{2,0},{4,6},{6,4},{1,3},{3,1},{5,7},{7,5},{8,10},{10,8},{12,... | collective-permute-start | bytes 1179656 | tf_op jit(solution)/shard_map/ppermute | solution.py:142
  187.3 8.7 %collective-permute-done.6 = bf16[192,1024]{1,0:T(8,128)(2,1)S(1)} collective-permute-done((bf16[192,1024]{1,0:T(8,128)(2,1)S(1)}, bf16[192,1024]{1,0:T(8,128)(2,1)S(1)}, u32[]{:S(2)}, u32[]{:S(2)}) %collective-permute-start.6) | collective-permute-done | bytes 393248 | tf_op jit(solution)/shard_map/ppermute | solution.py:142
  196.0 26.7 %collective-permute-done.7 = bf16[192,1024]{1,0:T(8,128)(2,1)S(1)} collective-permute-done((bf16[192,1024]{1,0:T(8,128)(2,1)S(1)}, bf16[192,1024]{1,0:T(8,128)(2,1)S(1)}, u32[]{:S(2)}, u32[]{:S(2)}) %collective-permute-start.7) | collective-permute-done | bytes 393248 | tf_op jit(solution)/shard_map/ppermute | solution.py:142
  225.1 4.4 %collective-permute-start.9 = (bf16[192,512]{1,0:T(8,128)(2,1)S(1)}, bf16[192,512]{1,0:T(8,128)(2,1)S(1)}, u32[]{:S(2)}, u32[]{:S(2)}) collective-permute-start(bf16[192,512]{1,0:T(8,128)(2,1)S(1)} %get-tuple-element.6), channel_id=1, source_target_pairs={{0,4},{2,6},{4,0},{6,2},{1,5},{3,7},{5,1},{7,3},{8,12},{10,14},{12... | collective-permute-start | bytes 589832 | tf_op jit(solution)/shard_map/ppermute | solution.py:147
  232.4 15.6 %collective-permute-done.17 = bf16[192,1024]{1,0:T(8,128)(2,1)S(1)} collective-permute-done((bf16[192,1024]{1,0:T(8,128)(2,1)S(1)}, bf16[192,1024]{1,0:T(8,128)(2,1)S(1)}, u32[]{:S(2)}, u32[]{:S(2)}) %collective-permute-start.17) | collective-permute-done | bytes 393248 | tf_op jit(solution)/shard_map/ppermute | solution.py:142
  250.8 4.9 %collective-permute-done.10 = bf16[192,512]{1,0:T(8,128)(2,1)S(1)} collective-permute-done((bf16[192,512]{1,0:T(8,128)(2,1)S(1)}, bf16[192,512]{1,0:T(8,128)(2,1)S(1)}, u32[]{:S(2)}, u32[]{:S(2)}) %collective-permute-start.10) | collective-permute-done | bytes 196640 | tf_op jit(solution)/shard_map/ppermute | solution.py:147
  262.9 10.4 %collective-permute-done.19 = bf16[192,512]{1,0:T(8,128)(2,1)S(1)} collective-permute-done((bf16[192,512]{1,0:T(8,128)(2,1)S(1)}, bf16[192,512]{1,0:T(8,128)(2,1)S(1)}, u32[]{:S(2)}, u32[]{:S(2)}) %collective-permute-start.19) | collective-permute-done | bytes 196640 | tf_op jit(solution)/shard_map/ppermute | solution.py:147
  273.3 5.8 %collective-permute-done.20 = bf16[192,512]{1,0:T(8,128)(2,1)S(1)} collective-permute-done((bf16[192,512]{1,0:T(8,128)(2,1)S(1)}, bf16[192,512]{1,0:T(8,128)(2,1)S(1)}, u32[]{:S(2)}, u32[]{:S(2)}) %collective-permute-start.20) | collective-permute-done | bytes 196640 | tf_op jit(solution)/shard_map/ppermute | solution.py:147
  287.2 13.2 %collective-permute-done.12 = bf16[384,768]{1,0:T(8,128)(2,1)S(1)} collective-permute-done((bf16[384,768]{1,0:T(8,128)(2,1)S(1)}, bf16[384,768]{1,0:T(8,128)(2,1)S(1)}, u32[]{:S(2)}, u32[]{:S(2)}) %collective-permute-start.12) | collective-permute-done | bytes 589856 | tf_op jit(solution)/shard_map/ppermute | solution.py:24
  301.3 6.8 %all-to-all-start.3 = ((bf16[8,48,768]{2,1,0:T(8,128)(2,1)}), bf16[8,48,768]{2,1,0:T(8,128)(2,1)S(1)}, u32[]{:S(2)}, u32[]{:S(2)}) async-start(bf16[8,48,768]{2,1,0:T(8,128)(2,1)} %bitcast.24), calls=%async_computation.3 | async-start | bytes 1179648 | tf_op jit(solution)/shard_map/all_to_all | solution.py:156
  312.9 14.4 %collective-permute-done.22 = bf16[384,768]{1,0:T(8,128)(2,1)S(1)} collective-permute-done((bf16[384,768]{1,0:T(8,128)(2,1)S(1)}, bf16[384,768]{1,0:T(8,128)(2,1)S(1)}, u32[]{:S(2)}, u32[]{:S(2)}) %collective-permute-start.22) | collective-permute-done | bytes 589856 | tf_op jit(solution)/shard_map/ppermute | solution.py:24
  328.2 6.9 %all-to-all-start.5 = ((bf16[8,48,768]{2,1,0:T(8,128)(2,1)}), bf16[8,48,768]{2,1,0:T(8,128)(2,1)S(1)}, u32[]{:S(2)}, u32[]{:S(2)}) async-start(bf16[8,48,768]{2,1,0:T(8,128)(2,1)} %bitcast.36), calls=%async_computation.5 | async-start | bytes 1179648 | tf_op jit(solution)/shard_map/all_to_all | solution.py:156
  335.3 17.2 %all-to-all-done.5 = bf16[8,48,768]{2,1,0:T(8,128)(2,1)S(1)} async-done(((bf16[8,48,768]{2,1,0:T(8,128)(2,1)}), bf16[8,48,768]{2,1,0:T(8,128)(2,1)S(1)}, u32[]{:S(2)}, u32[]{:S(2)}) %all-to-all-start.5) | async-done | bytes 589856 | tf_op jit(solution)/shard_map/all_to_all | solution.py:156
  352.6 14.5 %all_to_all.36 = bf16[4,24,768]{2,1,0:T(8,128)(2,1)S(1)} all-to-all(bf16[4,24,768]{2,1,0:T(8,128)(2,1)S(1)} %pad_maximum_fusion.6), channel_id=1, replica_groups=mesh['yh'=2,'xh'=2,'xl'=2,'z'=8,'yl'=4,'c'=2] {'yh','xh'}, dimensions={0} | all-to-all | bytes 294912 | tf_op jit(solution)/shard_map/all_to_all | solution.py:159
  (135 shorter events, 92.1 us)
Async XLA Ops:
  2.0 41.8 %all-to-all-start = ((bf16[32,64,256]{2,1,0:T(8,128)(2,1)}), bf16[32,64,256]{2,1,0:T(8,128)(2,1)S(1)}, u32[]{:S(2)}, u32[]{:S(2)}) async-start(bf16[32,64,256]{2,1,0:T(8,128)(2,1)} %broadcast_in_dim.68), calls=%async_computation | async-start | bytes 2097152 | tf_op jit(solution)/shard_map/all_to_all | solution.py:43
  91.5 22.7 %all-to-all-start.2 = ((bf16[8,48,768]{2,1,0:T(8,128)(2,1)}), bf16[8,48,768]{2,1,0:T(8,128)(2,1)S(1)}, u32[]{:S(2)}, u32[]{:S(2)}) async-start(bf16[8,48,768]{2,1,0:T(8,128)(2,1)} %broadcast_in_dim.73), calls=%async_computation.2 | async-start | bytes 1179648 | tf_op jit(solution)/shard_map/all_to_all | solution.py:123
  115.1 21.7 %all-to-all-start.4 = ((bf16[8,48,768]{2,1,0:T(8,128)(2,1)}), bf16[8,48,768]{2,1,0:T(8,128)(2,1)S(1)}, u32[]{:S(2)}, u32[]{:S(2)}) async-start(bf16[8,48,768]{2,1,0:T(8,128)(2,1)} %broadcast_in_dim.79), calls=%async_computation.4 | async-start | bytes 1179648 | tf_op jit(solution)/shard_map/all_to_all | solution.py:123
  118.6 15.0 %collective-permute-start.2 = (bf16[384,768]{1,0:T(8,128)(2,1)S(1)}, bf16[384,768]{1,0:T(8,128)(2,1)S(1)}, u32[]{:S(2)}, u32[]{:S(2)}) collective-permute-start(bf16[384,768]{1,0:T(8,128)(2,1)S(1)} %bitcast.107), channel_id=1, source_target_pairs={{0,64},{64,0},{1,65},{65,1},{2,66},{66,2},{3,67},{67,3},{4,68},{68... | collective-permute-start | bytes 1769480 | tf_op jit(solution)/shard_map/ppermute | solution.py:24
  124.8 33.6 %collective-permute-start.4 = (bf16[1024,768]{1,0:T(8,128)(2,1)}, bf16[1024,768]{1,0:T(8,128)(2,1)}, u32[]{:S(2)}, u32[]{:S(2)}) collective-permute-start(bf16[1024,768]{1,0:T(8,128)(2,1)} %pad_maximum_fusion.1), channel_id=1, source_target_pairs={{0,1},{1,0},{2,3},{3,2},{4,5},{5,4},{6,7},{7,6},{8,9},{9,8},{10,11... | collective-permute-start | bytes 4718600 | tf_op jit(solution)/shard_map/ppermute | solution.py:24
  134.9 23.5 %collective-permute-start.3 = (bf16[768,768]{1,0:T(8,128)(2,1)}, bf16[768,768]{1,0:T(8,128)(2,1)}, u32[]{:S(2)}, u32[]{:S(2)}) collective-permute-start(bf16[768,768]{1,0:T(8,128)(2,1)} %pad_maximum_fusion.2), channel_id=1, source_target_pairs={{0,1},{1,0},{2,3},{3,2},{4,5},{5,4},{6,7},{7,6},{8,9},{9,8},{10,11... | collective-permute-start | bytes 3538952 | tf_op jit(solution)/shard_map/ppermute | solution.py:24
  136.8 17.6 %collective-permute-start.13 = (bf16[384,768]{1,0:T(8,128)(2,1)S(1)}, bf16[384,768]{1,0:T(8,128)(2,1)S(1)}, u32[]{:S(2)}, u32[]{:S(2)}) collective-permute-start(bf16[384,768]{1,0:T(8,128)(2,1)S(1)} %bitcast.104), channel_id=1, source_target_pairs={{0,64},{64,0},{1,65},{65,1},{2,66},{66,2},{3,67},{67,3},{4,68},{68... | collective-permute-start | bytes 1769480 | tf_op jit(solution)/shard_map/ppermute | solution.py:24
  156.4 16.4 %collective-permute-start.14 = (bf16[768,768]{1,0:T(8,128)(2,1)}, bf16[768,768]{1,0:T(8,128)(2,1)}, u32[]{:S(2)}, u32[]{:S(2)}) collective-permute-start(bf16[768,768]{1,0:T(8,128)(2,1)} %pad_maximum_fusion.3), channel_id=1, source_target_pairs={{0,1},{1,0},{2,3},{3,2},{4,5},{5,4},{6,7},{7,6},{8,9},{9,8},{10,11... | collective-permute-start | bytes 3538952 | tf_op jit(solution)/shard_map/ppermute | solution.py:24
  163.2 21.6 %collective-permute-start.5 = (bf16[192,1024]{1,0:T(8,128)(2,1)S(1)}, bf16[192,1024]{1,0:T(8,128)(2,1)S(1)}, u32[]{:S(2)}, u32[]{:S(2)}) collective-permute-start(bf16[192,1024]{1,0:T(8,128)(2,1)S(1)} %get-tuple-element.11), channel_id=1, source_target_pairs={{0,2},{2,0},{4,6},{6,4},{1,3},{3,1},{5,7},{7,5},{8,10},{10,8},{12,... | collective-permute-start | bytes 1179656 | tf_op jit(solution)/shard_map/ppermute | solution.py:142
  166.2 29.7 %collective-permute-start.6 = (bf16[192,1024]{1,0:T(8,128)(2,1)S(1)}, bf16[192,1024]{1,0:T(8,128)(2,1)S(1)}, u32[]{:S(2)}, u32[]{:S(2)}) collective-permute-start(bf16[192,1024]{1,0:T(8,128)(2,1)S(1)} %get-tuple-element.13), channel_id=1, source_target_pairs={{0,4},{2,6},{4,0},{6,2},{1,5},{3,7},{5,1},{7,3},{8,12},{10,14},{12... | collective-permute-start | bytes 1179656 | tf_op jit(solution)/shard_map/ppermute | solution.py:142
  169.6 53.1 %collective-permute-start.7 = (bf16[192,1024]{1,0:T(8,128)(2,1)S(1)}, bf16[192,1024]{1,0:T(8,128)(2,1)S(1)}, u32[]{:S(2)}, u32[]{:S(2)}) collective-permute-start(bf16[192,1024]{1,0:T(8,128)(2,1)S(1)} %get-tuple-element.12), channel_id=1, source_target_pairs={{0,6},{2,4},{4,2},{6,0},{1,7},{3,5},{5,3},{7,1},{8,14},{10,12},{12... | collective-permute-start | bytes 1179656 | tf_op jit(solution)/shard_map/ppermute | solution.py:142
  177.5 51.9 %collective-permute-start.15 = (bf16[192,1024]{1,0:T(8,128)(2,1)S(1)}, bf16[192,1024]{1,0:T(8,128)(2,1)S(1)}, u32[]{:S(2)}, u32[]{:S(2)}) collective-permute-start(bf16[192,1024]{1,0:T(8,128)(2,1)S(1)} %get-tuple-element.14), channel_id=1, source_target_pairs={{0,2},{2,0},{4,6},{6,4},{1,3},{3,1},{5,7},{7,5},{8,10},{10,8},{12,... | collective-permute-start | bytes 1179656 | tf_op jit(solution)/shard_map/ppermute | solution.py:142
  181.4 50.9 %collective-permute-start.16 = (bf16[192,1024]{1,0:T(8,128)(2,1)S(1)}, bf16[192,1024]{1,0:T(8,128)(2,1)S(1)}, u32[]{:S(2)}, u32[]{:S(2)}) collective-permute-start(bf16[192,1024]{1,0:T(8,128)(2,1)S(1)} %get-tuple-element.16), channel_id=1, source_target_pairs={{0,4},{2,6},{4,0},{6,2},{1,5},{3,7},{5,1},{7,3},{8,12},{10,14},{12... | collective-permute-start | bytes 1179656 | tf_op jit(solution)/shard_map/ppermute | solution.py:142
  184.8 63.2 %collective-permute-start.17 = (bf16[192,1024]{1,0:T(8,128)(2,1)S(1)}, bf16[192,1024]{1,0:T(8,128)(2,1)S(1)}, u32[]{:S(2)}, u32[]{:S(2)}) collective-permute-start(bf16[192,1024]{1,0:T(8,128)(2,1)S(1)} %get-tuple-element.15), channel_id=1, source_target_pairs={{0,6},{2,4},{4,2},{6,0},{1,7},{3,5},{5,3},{7,1},{8,14},{10,12},{12... | collective-permute-start | bytes 1179656 | tf_op jit(solution)/shard_map/ppermute | solution.py:142
  223.1 27.3 %collective-permute-start.8 = (bf16[192,512]{1,0:T(8,128)(2,1)S(1)}, bf16[192,512]{1,0:T(8,128)(2,1)S(1)}, u32[]{:S(2)}, u32[]{:S(2)}) collective-permute-start(bf16[192,512]{1,0:T(8,128)(2,1)S(1)} %get-tuple-element.6), channel_id=1, source_target_pairs={{0,2},{2,0},{4,6},{6,4},{1,3},{3,1},{5,7},{7,5},{8,10},{10,8},{12,... | collective-permute-start | bytes 589832 | tf_op jit(solution)/shard_map/ppermute | solution.py:147
  225.1 25.7 %collective-permute-start.9 = (bf16[192,512]{1,0:T(8,128)(2,1)S(1)}, bf16[192,512]{1,0:T(8,128)(2,1)S(1)}, u32[]{:S(2)}, u32[]{:S(2)}) collective-permute-start(bf16[192,512]{1,0:T(8,128)(2,1)S(1)} %get-tuple-element.6), channel_id=1, source_target_pairs={{0,4},{2,6},{4,0},{6,2},{1,5},{3,7},{5,1},{7,3},{8,12},{10,14},{12... | collective-permute-start | bytes 589832 | tf_op jit(solution)/shard_map/ppermute | solution.py:147
  229.5 26.2 %collective-permute-start.10 = (bf16[192,512]{1,0:T(8,128)(2,1)S(1)}, bf16[192,512]{1,0:T(8,128)(2,1)S(1)}, u32[]{:S(2)}, u32[]{:S(2)}) collective-permute-start(bf16[192,512]{1,0:T(8,128)(2,1)S(1)} %get-tuple-element.6), channel_id=1, source_target_pairs={{0,6},{2,4},{4,2},{6,0},{1,7},{3,5},{5,3},{7,1},{8,14},{10,12},{12... | collective-permute-start | bytes 589832 | tf_op jit(solution)/shard_map/ppermute | solution.py:147
  255.7 25.3 %collective-permute-start.11 = (bf16[768,512]{1,0:T(8,128)(2,1)S(1)}, bf16[768,512]{1,0:T(8,128)(2,1)S(1)}, u32[]{:S(2)}, u32[]{:S(2)}) collective-permute-start(bf16[768,512]{1,0:T(8,128)(2,1)S(1)} %bitcast.102), channel_id=1, source_target_pairs={{0,1},{1,0},{2,3},{3,2},{4,5},{5,4},{6,7},{7,6},{8,9},{9,8},{10,11... | collective-permute-start | bytes 2359304 | tf_op jit(solution)/shard_map/ppermute | solution.py:24
  257.7 15.6 %collective-permute-start.19 = (bf16[192,512]{1,0:T(8,128)(2,1)S(1)}, bf16[192,512]{1,0:T(8,128)(2,1)S(1)}, u32[]{:S(2)}, u32[]{:S(2)}) collective-permute-start(bf16[192,512]{1,0:T(8,128)(2,1)S(1)} %get-tuple-element.8), channel_id=1, source_target_pairs={{0,4},{2,6},{4,0},{6,2},{1,5},{3,7},{5,1},{7,3},{8,12},{10,14},{12... | collective-permute-start | bytes 589832 | tf_op jit(solution)/shard_map/ppermute | solution.py:147
  259.6 19.5 %collective-permute-start.20 = (bf16[192,512]{1,0:T(8,128)(2,1)S(1)}, bf16[192,512]{1,0:T(8,128)(2,1)S(1)}, u32[]{:S(2)}, u32[]{:S(2)}) collective-permute-start(bf16[192,512]{1,0:T(8,128)(2,1)S(1)} %get-tuple-element.8), channel_id=1, source_target_pairs={{0,6},{2,4},{4,2},{6,0},{1,7},{3,5},{5,3},{7,1},{8,14},{10,12},{12... | collective-permute-start | bytes 589832 | tf_op jit(solution)/shard_map/ppermute | solution.py:147
  282.7 17.6 %collective-permute-start.12 = (bf16[384,768]{1,0:T(8,128)(2,1)S(1)}, bf16[384,768]{1,0:T(8,128)(2,1)S(1)}, u32[]{:S(2)}, u32[]{:S(2)}) collective-permute-start(bf16[384,768]{1,0:T(8,128)(2,1)S(1)} %slice.157), channel_id=1, source_target_pairs={{0,64},{64,0},{1,65},{65,1},{2,66},{66,2},{3,67},{67,3},{4,68},{68... | collective-permute-start | bytes 1769480 | tf_op jit(solution)/shard_map/ppermute | solution.py:24
  301.3 26.9 %all-to-all-start.3 = ((bf16[8,48,768]{2,1,0:T(8,128)(2,1)}), bf16[8,48,768]{2,1,0:T(8,128)(2,1)S(1)}, u32[]{:S(2)}, u32[]{:S(2)}) async-start(bf16[8,48,768]{2,1,0:T(8,128)(2,1)} %bitcast.24), calls=%async_computation.3 | async-start | bytes 1179648 | tf_op jit(solution)/shard_map/all_to_all | solution.py:156
  310.7 16.6 %collective-permute-start.22 = (bf16[384,768]{1,0:T(8,128)(2,1)S(1)}, bf16[384,768]{1,0:T(8,128)(2,1)S(1)}, u32[]{:S(2)}, u32[]{:S(2)}) collective-permute-start(bf16[384,768]{1,0:T(8,128)(2,1)S(1)} %slice.156), channel_id=1, source_target_pairs={{0,64},{64,0},{1,65},{65,1},{2,66},{66,2},{3,67},{67,3},{4,68},{68... | collective-permute-start | bytes 1769480 | tf_op jit(solution)/shard_map/ppermute | solution.py:24
  328.2 24.2 %all-to-all-start.5 = ((bf16[8,48,768]{2,1,0:T(8,128)(2,1)}), bf16[8,48,768]{2,1,0:T(8,128)(2,1)S(1)}, u32[]{:S(2)}, u32[]{:S(2)}) async-start(bf16[8,48,768]{2,1,0:T(8,128)(2,1)} %bitcast.36), calls=%async_computation.5 | async-start | bytes 1179648 | tf_op jit(solution)/shard_map/all_to_all | solution.py:156
  (15 other events, 459.6 us)

commit v2 on v1

v2 whole, which is shorter than its diff:
```python
import math
from functools import partial

import jax
import jax.numpy as jnp
from jax import lax
from jax.experimental import pallas as pl
from jax.experimental.pallas import tpu as pltpu
from jax.sharding import Mesh, PartitionSpec as P

D = 6144
HD = 128
EXPERTS = 4
CAP = 24
SLOTS = (8, 8, 8)
F32 = jnp.float32
BF16 = jnp.bfloat16

CTX = ("yh", "xh", "xl", "z")
EXP = ("yl", "c")
HALF = ("xh", "xl", "z")
ROUTE = ("yh", "xh", "z")
SWAP = [(0, 1), (1, 0)]
Y_XOR = [[(i, i ^ k) for i in range(4)] for k in range(4)]
RELATIVE = (0, 2, 1, 3)


def swap(x, axis):
    return lax.ppermute(x, axis, SWAP)


def split3(v):
    hi = lax.reduce_precision(v, 8, 7)
    mid = lax.reduce_precision(v - hi, 8, 7)
    lo = (v - hi) - mid
    return [p.astype(BF16) for p in (hi, mid, lo)]


def attend(queries, keys, values, early, late):
    rows = queries.shape[0]
    heads = queries.shape[1] // HD
    yh = lax.axis_index("yh")
    scale = 1.0 / math.sqrt(HD)

    foreign = lax.ppermute(queries, "yh", [(1, 0)])
    kv = jnp.concatenate([keys, values], axis=1)
    members = lax.axis_size(HALF)
    kv = lax.all_to_all(
        jnp.broadcast_to(kv[None], (members,) + kv.shape), HALF, split_axis=0, concat_axis=0, tiled=True
    ).reshape(members * rows, 2 * HD)
    kv, *early = lax.optimization_barrier((kv,) + early)
    k_all, v_all = kv[:, :HD], kv[:, HD:]
    count = members * rows

    def stacked(q):
        return q.reshape(rows, heads, HD).transpose(1, 0, 2).reshape(heads * rows, HD)

    q_all = jnp.concatenate([stacked(queries), stacked(foreign)], axis=0)
    own_pos = lax.axis_index(HALF) * rows + jnp.tile(jnp.arange(rows, dtype=jnp.int32), heads)
    limit = jnp.concatenate([own_pos, jnp.full_like(own_pos, count)])
    scores = jnp.einsum("qd,kd->qk", q_all, k_all, preferred_element_type=F32) * scale
    allowed = jnp.arange(count, dtype=jnp.int32)[None, :] <= limit[:, None]
    scores = jnp.where(allowed, scores, -1e30)
    top = jnp.max(scores, axis=1)
    weights = jnp.exp(scores - top[:, None])
    total = jnp.sum(weights, axis=1)
    acc = jnp.einsum("qk,kd->qd", weights.astype(BF16), v_all, preferred_element_type=F32)
    out = acc / total[:, None]
    lse = top + jnp.log(total)

    n = heads * rows

    def unstacked(o):
        return o.reshape(heads, rows, HD).transpose(1, 0, 2).reshape(rows, heads * HD)

    out_own, out_far = unstacked(out[:n]), unstacked(out[n:])
    lse_own, lse_far = lse[:n].reshape(heads, rows).T, lse[n:].reshape(heads, rows).T
    tail = jnp.concatenate(split3(lse_far), axis=1)
    tail = jnp.pad(tail, ((0, 0), (0, HD - tail.shape[1])))
    message = jnp.concatenate([out_far.astype(BF16), tail], axis=1)
    message, *late = lax.optimization_barrier((message,) + late)
    got = lax.ppermute(message, "yh", [(0, 1)])
    got_out = got[:, : heads * HD].astype(F32)
    parts = got[:, heads * HD : heads * HD + 3 * heads].astype(F32)
    got_lse = parts[:, :heads] + parts[:, heads : 2 * heads] + parts[:, 2 * heads :]
    share = jnp.where(yh == 1, jax.nn.sigmoid(got_lse - lse_own), 0.0)
    share = jnp.repeat(share, HD, axis=1)
    return (out_own * (1.0 - share) + got_out * share).astype(BF16), early, late


def expand(order_ref, x_ref, xo_ref, wn_ref, won_ref, wf_ref, wof_ref, keep_ref, send_ref, acc_ref):
    step = pl.program_id(0)
    contract = (((1,), (1,)), ((), ()))

    def terms(a, b):
        return lax.dot_general(x_ref[...], a[...], contract, preferred_element_type=F32) + lax.dot_general(
            xo_ref[...], b[...], contract, preferred_element_type=F32
        )

    @pl.when(step < 2)
    def _():
        acc_ref[...] = terms(wn_ref, won_ref)

    @pl.when(step >= 2)
    def _():
        acc_ref[...] = terms(wf_ref, wof_ref)

    share = keep_ref.shape[1]
    for p in range(2):
        for ref, i in ((keep_ref, 2 * p), (send_ref, 2 * p + 1)):
            at = pl.multiple_of((order_ref[0] ^ i) * share, share)
            ref[p] = acc_ref[pl.ds(at, share), :].astype(BF16)


def gate_up_terms(order, x, xo, w, wo, wf, wof):
    rows, feat = x.shape
    cols = w.shape[0] // 2
    share = rows // 4
    full = pl.BlockSpec((rows, feat), lambda n, o: (0, 0))
    near = pl.BlockSpec((cols, feat), lambda n, o: (jnp.minimum(n, 1), 0))
    far = pl.BlockSpec((cols, feat), lambda n, o: (jnp.maximum(n - 2, 0), 0))
    out = pl.BlockSpec((2, share, cols), lambda n, o: (0, 0, n))
    shape = jax.ShapeDtypeStruct((2, share, 4 * cols), BF16)
    return pl.pallas_call(
        expand,
        grid_spec=pltpu.PrefetchScalarGridSpec(
            num_scalar_prefetch=1,
            grid=(4,),
            in_specs=[full, full, near, near, far, far],
            out_specs=[out, out],
            scratch_shapes=[pltpu.VMEM((rows, cols), F32)],
        ),
        out_shape=[shape, shape],
        cost_estimate=pl.CostEstimate(
            flops=16 * rows * cols * feat, transcendentals=0, bytes_accessed=16 * cols * feat + 20 * rows * cols
        ),
        compiler_params=pltpu.CompilerParams(vmem_limit_bytes=40 << 20),
        name="gate_up_terms",
    )(order, x, xo, w, wo, wf, wof)


def contract_hidden(order_ref, h_ref, ho_ref, w_ref, wf_ref, out_ref):
    core = order_ref[1]
    half = w_ref.shape[0] // 2
    own = pl.multiple_of(core * half, half)
    other = pl.multiple_of((1 - core) * half, half)
    acc = jnp.dot(h_ref[:, :half], w_ref[pl.ds(own, half), :], preferred_element_type=F32)
    acc += jnp.dot(ho_ref[:, :half], w_ref[pl.ds(other, half), :], preferred_element_type=F32)
    acc += jnp.dot(h_ref[:, half:], wf_ref[pl.ds(own, half), :], preferred_element_type=F32)
    acc += jnp.dot(ho_ref[:, half:], wf_ref[pl.ds(other, half), :], preferred_element_type=F32)
    share = out_ref.shape[0] // 4
    for p, i in enumerate(RELATIVE):
        at = pl.multiple_of((order_ref[0] ^ i) * share, share)
        out_ref[pl.ds(at, share), :] = acc[p * share : (p + 1) * share].astype(BF16)


def down_terms(order, h, ho, w, wf):
    rows = h.shape[0]
    hidden, feat = w.shape
    whole = pl.BlockSpec(memory_space=pltpu.VMEM)
    return pl.pallas_call(
        contract_hidden,
        in_specs=[pl.BlockSpec(memory_space=pltpu.SMEM), whole, whole, whole, whole],
        out_specs=whole,
        out_shape=jax.ShapeDtypeStruct((rows, feat), BF16),
        cost_estimate=pl.CostEstimate(
            flops=4 * rows * hidden * feat, transcendentals=0, bytes_accessed=4 * hidden * feat + 6 * rows * hidden
        ),
        compiler_params=pltpu.CompilerParams(vmem_limit_bytes=40 << 20),
        name="down_terms",
    )(order, h, ho, w, wf)


def after(value, *others):
    return lax.optimization_barrier((value,) + others)[0]


def body(queries, keys, values, residual, norm_gain, routes, route_weight, w_gate, w_up, w_down):
    feat = residual.shape[1]
    half = w_gate.shape[0] // 2
    core = lax.axis_index("c")
    me = lax.axis_index("yl")
    order = jnp.stack([me, core]).astype(jnp.int32)

    def halves(which):
        cut = partial(lax.dynamic_slice_in_dim, start_index=which * half, slice_size=half, axis=0)
        return jnp.concatenate([cut(w_gate), cut(w_up)], axis=0)

    w_in, w_give = halves(core), halves(1 - core)
    w_in_other = swap(w_give, "c")
    w_in_far = swap(w_in, "xl")
    w_in_other_far = lax.ppermute(w_give, ("xl", "c"), [(i, 3 - i) for i in range(4)])
    w_out_far = swap(w_down, "xl")

    attn, (w_in_other, w_in_far), (w_in_other_far,) = attend(
        queries, keys, values, (w_in_other, w_in_far), (w_in_other_far,)
    )
    mixed = residual.astype(F32) + attn.astype(F32)
    total_squares = lax.psum(jnp.sum(mixed * mixed, axis=1), EXP)
    total_squares, w_out_far = lax.optimization_barrier((total_squares, w_out_far))
    normed = (mixed * lax.rsqrt(total_squares / D + 1e-05)[:, None] * norm_gain[None, :]).astype(BF16)

    chosen = routes[:, 0]
    expert_ids = jnp.arange(EXPERTS, dtype=jnp.int32)
    onehot = (chosen[:, None] == expert_ids[None, :]).astype(jnp.int32)
    slot_index = jnp.sum((jnp.cumsum(onehot, axis=0) - 1) * onehot, axis=1)
    slot_ids = jnp.arange(CAP, dtype=jnp.int32)
    select = (
        (chosen[None, None, :] == expert_ids[:, None, None])
        & (slot_index[None, None, :] == slot_ids[None, :, None])
    ).astype(BF16)
    packed = jnp.einsum("ect,td->ecd", select, normed, preferred_element_type=F32).astype(BF16)

    nz = lax.axis_size("z")
    peers = EXPERTS * nz

    def dispatch(lo, n):
        part = packed[:, lo : lo + n]
        part = jnp.broadcast_to(part[:, None], (EXPERTS, nz, n, feat)).reshape(peers, n, feat)
        x = lax.all_to_all(part, ROUTE, split_axis=0, concat_axis=0, tiled=True)
        return x.reshape(peers * n, feat)

    def hidden_of(keep, send):
        got = lax.ppermute(send, "yl", Y_XOR[1])
        pair = (keep[1].astype(F32) + got[1].astype(F32)).astype(BF16)
        last = lax.ppermute(pair, "yl", Y_XOR[2])
        full = keep[0].astype(F32) + got[0].astype(F32) + last.astype(F32)
        near = jax.nn.silu(full[:, :half]) * full[:, half : 2 * half]
        far = jax.nn.silu(full[:, 2 * half : 3 * half]) * full[:, 3 * half :]
        return jnp.concatenate([near, far], axis=1).astype(BF16)

    def spread(hidden):
        two = jnp.concatenate([hidden, lax.ppermute(hidden, "yl", Y_XOR[2])], axis=0)
        return jnp.concatenate([two, lax.ppermute(two, "yl", Y_XOR[1])], axis=0)

    def give_back(down, n):
        back = lax.all_to_all(down.reshape(peers, n, feat), ROUTE, split_axis=0, concat_axis=0, tiled=True)
        return jnp.sum(back.reshape(EXPERTS, nz, n, feat).astype(F32), axis=1).astype(BF16)

    starts = [sum(SLOTS[:k]) for k in range(len(SLOTS))]
    terms = []
    for lo, n in zip(starts, SLOTS):
        x = dispatch(lo, n)
        if terms:
            x = after(x, *terms[-1])
        terms.append(gate_up_terms(order, x, swap(x, "c"), w_in, w_in_other, w_in_far, w_in_other_far))
    outs = []
    for (keep, send), n in zip(terms, SLOTS):
        hid = spread(hidden_of(keep, send))
        outs.append(give_back(down_terms(order, hid, swap(hid, "c"), w_down, w_out_far), n))
    returned = jnp.concatenate(outs, axis=1)
    moe_rows = jnp.einsum("ect,ecd->td", select, returned, preferred_element_type=F32)
    return (route_weight[:, None] * moe_rows).astype(BF16)


def solution(mesh):
    fine = Mesh(mesh.devices.reshape(2, 2, 2, 8, 4, 2), CTX + EXP)
    wide = P(CTX, EXP)
    in_specs = (wide, wide, wide, wide, P(EXP), P(CTX, None), P(CTX), wide, wide, wide)
    return jax.shard_map(body, mesh=fine, in_specs=in_specs, out_specs=wide, check_vma=False)
```

time: 369 us -> 389 us (1.054)
  waiting for transfers between devices: 187 us -> 156 us
  starting transfers between devices: 97 us -> 125 us
  Pallas kernels: 0 us -> 27.8 us
  matrix products: 19.7 us -> 6.37 us
  other arithmetic: 10.2 us -> 14.2 us
    pallas_call x0 -> x6, Pallas kernels: none -> 27.8 us  [the longest x3 16.9 us: gate_up_terms(): pl.pallas_call(expand, grid_spec=pltpu.PrefetchScalarGridSpec(num_scalar_...]
    all_to_all x1, waiting for transfers between devices: 15.9 us -> 0.01 us  [attend(): lax.all_to_all(jnp.broadcast_to(kv[None], (members,) + kv.shape), HALF, s...]
    dot_general x8 -> x0, matrix products: 15.5 us -> none  [the longest x2 6.45 us: body(): jnp.einsum('rd,fd->rf', x_other, w_in_other, preferred_element_type=F32)]
    all_to_all x4 -> x5, starting transfers between devices: 22.1 us -> 35.7 us  [the longest x3 27.8 us: give_back(): lax.all_to_all(down.reshape(peers, n, feat), ROUTE, split_axis=0, concat_...]
    all_to_all x4 -> x5, waiting for transfers between devices: 35.1 us -> 47.6 us  [the longest x3 32.5 us: give_back(): lax.all_to_all(down.reshape(peers, n, feat), ROUTE, split_axis=0, concat_...]
    ppermute x9, waiting for transfers between devices: 49.9 us -> 37.9 us  [swap(): return lax.ppermute(x, axis, SWAP)]
    ppermute x12 -> x13, starting transfers between devices: 35.6 us -> 46.6 us  [the longest x3 13.1 us: spread(): lax.ppermute(hidden, 'yl', Y_XOR[2])]
    ppermute x12 -> x13, waiting for transfers between devices: 72.5 us -> 62.1 us  [the longest x1 23.2 us: body(): lax.ppermute(w_give, ('xl', 'c'), [(i, 3 - i) for i in range(4)])]
  transfers between devices with their start and end apart: 28 -> 30, of which waited for: 16 -> 17; matrix products, arithmetic and copies ran while one was open for 7% -> 7% of each run, Pallas kernels for 0% -> 7%
where the time goes in v2:
time: 389 us; the launch traced here: 387 us
  waiting for transfers between devices  156 us (40%)
  starting transfers between devices  125 us (32%)
  blocking collectives  44.6 us (11%)
  Pallas kernels  27.8 us (7%)
  other arithmetic  14.2 us (4%)
  local copies, waits for them, and re-layouts  12.3 us (3%)
  matrix products  6.37 us (2%)
    ppermute x9, waiting for transfers between devices, swap(): return lax.ppermute(x, axis, SWAP)  37.9 us
    all_to_all x1, blocking collectives, dispatch(): x = lax.all_to_all(part, ROUTE, split_axis=0, concat_axis=0, tiled=True)  33.3 us
    all_to_all x3, waiting for transfers between devices, give_back(): lax.all_to_all(down.reshape(peers, n, feat), ROUTE, split_axis=0, concat_...  32.5 us
    all_to_all x3, starting transfers between devices, give_back(): lax.all_to_all(down.reshape(peers, n, feat), ROUTE, split_axis=0, concat_...  27.8 us
    ppermute x1, waiting for transfers between devices, body(): lax.ppermute(w_give, ('xl', 'c'), [(i, 3 - i) for i in range(4)])  23.2 us
    ppermute x9, starting transfers between devices, swap(): return lax.ppermute(x, axis, SWAP)  20.8 us
    ppermute x3, waiting for transfers between devices, spread(): lax.ppermute(hidden, 'yl', Y_XOR[2])  17.1 us
    pallas_call x3, Pallas kernels, gate_up_terms(): pl.pallas_call(expand, grid_spec=pltpu.PrefetchScalarGridSpec(num_scalar_...  16.9 us
  transfers between devices with their start and end apart: 30, of which 17 were waited for; matrix products, arithmetic and copies ran while one was open for 7% of the time, Pallas kernels for 7%

profile of v2, /device:TPU:8, one launch (start us, length us, event | category | flops | bytes accessed | tf_op | source)
XLA Modules:
  0.0 387.2 jit_solution(8958070581293626036)
XLA Ops:
  1.9 13.3 %all-to-all-start = ((bf16[32,64,256]{2,1,0:T(8,128)(2,1)}), bf16[32,64,256]{2,1,0:T(8,128)(2,1)}, u32[]{:S(2)}, u32[]{:S(2)}) async-start(bf16[32,64,256]{2,1,0:T(8,128)(2,1)} %broadcast_in_dim.18), calls=%async_computation | async-start | bytes 2097152 | tf_op jit(solution)/shard_map/all_to_all | solution.py:48
  32.9 4.4 %collective-permute-done = bf16[64,768]{1,0:T(8,128)(2,1)S(1)} collective-permute-done((bf16[64,768]{1,0:T(8,128)(2,1)S(1)}, bf16[64,768]{1,0:T(8,128)(2,1)S(1)}, u32[]{:S(2)}, u32[]{:S(2)}) %collective-permute-start) | collective-permute-done | bytes 98336 | tf_op jit(solution)/shard_map/ppermute | solution.py:45
  37.4 27.9 %collective-permute-done.2.wf_ref = bf16[1024,768]{1,0:T(8,128)(2,1)S(1)} collective-permute-done((bf16[1024,768]{1,0:T(8,128)(2,1)S(1)}, bf16[1024,768]{1,0:T(8,128)(2,1)S(1)}, u32[]{:S(2)}, u32[]{:S(2)}) %collective-permute-start.2) | collective-permute-done | bytes 1572896 | tf_op jit(solution)/shard_map/ppermute | solution.py:29
  74.4 23.2 %collective-permute-done.3.wof_ref = bf16[1024,768]{1,0:T(8,128)(2,1)} collective-permute-done((bf16[1024,768]{1,0:T(8,128)(2,1)}, bf16[1024,768]{1,0:T(8,128)(2,1)}, u32[]{:S(2)}, u32[]{:S(2)}) %collective-permute-start.3) | collective-permute-done | bytes 1572896 | tf_op jit(solution)/shard_map/ppermute | solution.py:192
  97.6 7.5 %collective-permute-start.4 = (bf16[64,896]{1,0:T(8,128)(2,1)}, bf16[64,896]{1,0:T(8,128)(2,1)}, u32[]{:S(2)}, u32[]{:S(2)}) collective-permute-start(bf16[64,896]{1,0:T(8,128)(2,1)} %fusion.34), channel_id=1, source_target_pairs={{0,256},{1,257},{2,258},{3,259},{4,260},{5,261},{6,262},{7,263},{8... | collective-permute-start | bytes 344072 | tf_op jit(solution)/shard_map/ppermute | solution.py:82
  112.5 11.2 %psum.7 = f32[64]{0:T(128)S(1)} all-reduce(f32[64]{0:T(128)S(1)} %get-tuple-element.35), channel_id=1, replica_groups=mesh['yh'=2,'xh'=2,'xl'=2,'z'=8,'yl'=4,'c'=2] {'yl','c'}, use_global_device_ids=true, to_apply=%region_5.6 | all-reduce | flops 64 | bytes 512 | tf_op jit(solution)/shard_map/psum | solution.py:199
  123.7 8.1 %collective-permute-done.5.wf_ref = bf16[1024,768]{1,0:T(8,128)(2,1)} collective-permute-done((bf16[1024,768]{1,0:T(8,128)(2,1)}, bf16[1024,768]{1,0:T(8,128)(2,1)}, u32[]{:S(2)}, u32[]{:S(2)}) %collective-permute-start.5) | collective-permute-done | bytes 1572896 | tf_op jit(solution)/shard_map/ppermute | solution.py:29
  132.8 33.3 %all_to_all.35 = bf16[32,8,768]{2,1,0:T(8,128)(2,1)} all-to-all(bf16[32,8,768]{2,1,0:T(8,128)(2,1)S(1)} %bitcast.84), channel_id=1, replica_groups=mesh['yh'=2,'xh'=2,'xl'=2,'z'=8,'yl'=4,'c'=2] {'yh','xh','z'}, dimensions={0} | all-to-all | bytes 786432 | tf_op jit(solution)/shard_map/all_to_all | solution.py:220
  172.8 6.0 %gate_up_terms.3 = (bf16[2,64,2048]{2,1,0:T(8,128)(2,1)S(1)}, bf16[2,64,2048]{2,1,0:T(8,128)(2,1)}) custom-call(s32[2]{0:T(128)S(1)} %pad_add_fusion.order_ref, bf16[256,768]{1,0:T(8,128)(2,1)} %bitcast.16.x_ref, bf16[256,768]{1,0:T(8,128)(2,1)} %collective-permute-done.6.xo_ref, bf16[1024,768]{1,0:T(8,128)(2,1)S(1)} %pad_maximum_fusion.1.wn_ref, ...), custom_call_target="tpu_custom_call" | custom-call | flops 1610612736 | bytes 8912896 | tf_op jit(solution)/shard_map/gate_up_terms/pallas_call | solution.py:124
  182.0 11.8 %all-to-all-done.3 = bf16[32,8,768]{2,1,0:T(8,128)(2,1)S(1)} async-done(((bf16[32,8,768]{2,1,0:T(8,128)(2,1)}), bf16[32,8,768]{2,1,0:T(8,128)(2,1)S(1)}, u32[]{:S(2)}, u32[]{:S(2)}) %all-to-all-start.3) | async-done | bytes 393248 | tf_op jit(solution)/shard_map/all_to_all | solution.py:220
  206.4 5.8 %gate_up_terms.4 = (bf16[2,64,2048]{2,1,0:T(8,128)(2,1)S(1)}, bf16[2,64,2048]{2,1,0:T(8,128)(2,1)}) custom-call(s32[2]{0:T(128)S(1)} %pad_add_fusion.order_ref, bf16[256,768]{1,0:T(8,128)(2,1)S(1)} %bitcast.81, bf16[256,768]{1,0:T(8,128)(2,1)S(1)} %collective-permute-done.12.xo_ref, bf16[1024,768]{1,0:T(8,128)(2,1)S(1)} %pad_maximum_fusion.1.wn_ref, ...), custom_call_target="tpu_custom_call" | custom-call | flops 1610612736 | bytes 8912896 | tf_op jit(solution)/shard_map/gate_up_terms/pallas_call | solution.py:124
  223.8 9.7 %collective-permute-done.13 = bf16[2,64,2048]{2,1,0:T(8,128)(2,1)} collective-permute-done((bf16[2,64,2048]{2,1,0:T(8,128)(2,1)}, bf16[2,64,2048]{2,1,0:T(8,128)(2,1)}, u32[]{:S(2)}, u32[]{:S(2)}) %collective-permute-start.13) | collective-permute-done | bytes 524320 | tf_op jit(solution)/shard_map/ppermute | solution.py:224
  241.6 5.1 %gate_up_terms.5 = (bf16[2,64,2048]{2,1,0:T(8,128)(2,1)S(1)}, bf16[2,64,2048]{2,1,0:T(8,128)(2,1)S(1)}) custom-call(s32[2]{0:T(128)S(1)} %pad_add_fusion.order_ref, bf16[256,768]{1,0:T(8,128)(2,1)S(1)} %bitcast.79, bf16[256,768]{1,0:T(8,128)(2,1)S(1)} %collective-permute-done.18.xo_ref, bf16[1024,768]{1,0:T(8,128)(2,1)S(1)} %pad_maximum_fusion.1.wn_ref, ...), custom_call_target="tpu_custom_call" | custom-call | flops 1610612736 | bytes 8912896 | tf_op jit(solution)/shard_map/gate_up_terms/pallas_call | solution.py:124
  253.8 5.3 %collective-permute-start.15 = (bf16[64,1024]{1,0:T(8,128)(2,1)S(1)}, bf16[64,1024]{1,0:T(8,128)(2,1)S(1)}, u32[]{:S(2)}, u32[]{:S(2)}) collective-permute-start(bf16[64,1024]{1,0:T(8,128)(2,1)S(1)} %pad_maximum_fusion.9), channel_id=1, source_target_pairs={{0,4},{2,6},{4,0},{6,2},{1,5},{3,7},{5,1},{7,3},{8,12},{10,14},{12... | collective-permute-start | bytes 393224 | tf_op jit(solution)/shard_map/ppermute | solution.py:233
  261.1 5.6 %collective-permute-done.15 = bf16[64,1024]{1,0:T(8,128)(2,1)S(1)} collective-permute-done((bf16[64,1024]{1,0:T(8,128)(2,1)S(1)}, bf16[64,1024]{1,0:T(8,128)(2,1)S(1)}, u32[]{:S(2)}, u32[]{:S(2)}) %collective-permute-start.15) | collective-permute-done | bytes 131104 | tf_op jit(solution)/shard_map/ppermute | solution.py:233
  269.6 5.1 %collective-permute-start.20 = (bf16[64,2048]{1,0:T(8,128)(2,1)S(1)}, bf16[64,2048]{1,0:T(8,128)(2,1)S(1)}, u32[]{:S(2)}, u32[]{:S(2)}) collective-permute-start(bf16[64,2048]{1,0:T(8,128)(2,1)S(1)} %fusion.15), channel_id=1, source_target_pairs={{0,4},{2,6},{4,0},{6,2},{1,5},{3,7},{5,1},{7,3},{8,12},{10,14},{12... | collective-permute-start | bytes 786440 | tf_op jit(solution)/shard_map/ppermute | solution.py:226
  277.1 9.2 %collective-permute-done.16 = bf16[128,1024]{1,0:T(8,128)(2,1)S(1)} collective-permute-done((bf16[128,1024]{1,0:T(8,128)(2,1)S(1)}, bf16[128,1024]{1,0:T(8,128)(2,1)S(1)}, u32[]{:S(2)}, u32[]{:S(2)}) %collective-permute-start.16) | collective-permute-done | bytes 262176 | tf_op jit(solution)/shard_map/ppermute | solution.py:234
  292.1 11.9 %all-to-all-start.2 = ((bf16[32,8,768]{2,1,0:T(8,128)(2,1)}), bf16[32,8,768]{2,1,0:T(8,128)(2,1)S(1)}, u32[]{:S(2)}, u32[]{:S(2)}) async-start(bf16[32,8,768]{2,1,0:T(8,128)(2,1)} %bitcast.19), calls=%async_computation.2 | async-start | bytes 786432 | tf_op jit(solution)/shard_map/all_to_all | solution.py:237
  304.1 4.9 %collective-permute-start.21 = (bf16[64,1024]{1,0:T(8,128)(2,1)S(1)}, bf16[64,1024]{1,0:T(8,128)(2,1)S(1)}, u32[]{:S(2)}, u32[]{:S(2)}) collective-permute-start(bf16[64,1024]{1,0:T(8,128)(2,1)S(1)} %pad_maximum_fusion.10), channel_id=1, source_target_pairs={{0,4},{2,6},{4,0},{6,2},{1,5},{3,7},{5,1},{7,3},{8,12},{10,14},{12... | collective-permute-start | bytes 393224 | tf_op jit(solution)/shard_map/ppermute | solution.py:233
  309.1 11.5 %collective-permute-done.21 = bf16[64,1024]{1,0:T(8,128)(2,1)S(1)} collective-permute-done((bf16[64,1024]{1,0:T(8,128)(2,1)S(1)}, bf16[64,1024]{1,0:T(8,128)(2,1)S(1)}, u32[]{:S(2)}, u32[]{:S(2)}) %collective-permute-start.21) | collective-permute-done | bytes 131104 | tf_op jit(solution)/shard_map/ppermute | solution.py:233
  320.6 5.0 %collective-permute-start.22 = (bf16[128,1024]{1,0:T(8,128)(2,1)S(1)}, bf16[128,1024]{1,0:T(8,128)(2,1)}, u32[]{:S(2)}, u32[]{:S(2)}) collective-permute-start(bf16[128,1024]{1,0:T(8,128)(2,1)S(1)} %pad_maximum_fusion.7), channel_id=1, source_target_pairs={{0,2},{2,0},{4,6},{6,4},{1,3},{3,1},{5,7},{7,5},{8,10},{10,8},{12,... | collective-permute-start | bytes 786440 | tf_op jit(solution)/shard_map/ppermute | solution.py:234
  329.3 12.0 %all-to-all-start.4 = ((bf16[32,8,768]{2,1,0:T(8,128)(2,1)}), bf16[32,8,768]{2,1,0:T(8,128)(2,1)S(1)}, u32[]{:S(2)}, u32[]{:S(2)}) async-start(bf16[32,8,768]{2,1,0:T(8,128)(2,1)} %bitcast.25), calls=%async_computation.4 | async-start | bytes 786432 | tf_op jit(solution)/shard_map/all_to_all | solution.py:237
  349.7 12.4 %all-to-all-done.4 = bf16[32,8,768]{2,1,0:T(8,128)(2,1)S(1)} async-done(((bf16[32,8,768]{2,1,0:T(8,128)(2,1)}), bf16[32,8,768]{2,1,0:T(8,128)(2,1)S(1)}, u32[]{:S(2)}, u32[]{:S(2)}) %all-to-all-start.4) | async-done | bytes 393248 | tf_op jit(solution)/shard_map/all_to_all | solution.py:237
  366.1 20.2 %all-to-all-done.6 = bf16[32,8,768]{2,1,0:T(8,128)(2,1)S(1)} async-done(((bf16[32,8,768]{2,1,0:T(8,128)(2,1)}), bf16[32,8,768]{2,1,0:T(8,128)(2,1)S(1)}, u32[]{:S(2)}, u32[]{:S(2)}) %all-to-all-start.6) | async-done | bytes 393248 | tf_op jit(solution)/shard_map/all_to_all | solution.py:237
  (133 shorter events, 116.0 us)
Async XLA Ops:
  1.9 63.4 %all-to-all-start = ((bf16[32,64,256]{2,1,0:T(8,128)(2,1)}), bf16[32,64,256]{2,1,0:T(8,128)(2,1)}, u32[]{:S(2)}, u32[]{:S(2)}) async-start(bf16[32,64,256]{2,1,0:T(8,128)(2,1)} %broadcast_in_dim.18), calls=%async_computation | async-start | bytes 2097152 | tf_op jit(solution)/shard_map/all_to_all | solution.py:48
  17.5 47.9 %collective-permute-start.2 = (bf16[1024,768]{1,0:T(8,128)(2,1)S(1)}, bf16[1024,768]{1,0:T(8,128)(2,1)S(1)}, u32[]{:S(2)}, u32[]{:S(2)}) collective-permute-start(bf16[1024,768]{1,0:T(8,128)(2,1)S(1)} %pad_maximum_fusion.1.wn_ref), channel_id=1, source_target_pairs={{0,64},{64,0},{1,65},{65,1},{2,66},{66,2},{3,67},{67,3},{4,68},{68... | collective-permute-start | bytes 4718600 | tf_op jit(solution)/shard_map/ppermute | solution.py:29
  22.4 42.9 %collective-permute-start.1 = (bf16[1024,768]{1,0:T(8,128)(2,1)}, bf16[1024,768]{1,0:T(8,128)(2,1)}, u32[]{:S(2)}, u32[]{:S(2)}) collective-permute-start(bf16[1024,768]{1,0:T(8,128)(2,1)} %pad_maximum_fusion), channel_id=1, source_target_pairs={{0,1},{1,0},{2,3},{3,2},{4,5},{5,4},{6,7},{7,6},{8,9},{9,8},{10,11... | collective-permute-start | bytes 4718600 | tf_op jit(solution)/shard_map/ppermute | solution.py:29
  24.3 73.3 %collective-permute-start.3 = (bf16[1024,768]{1,0:T(8,128)(2,1)}, bf16[1024,768]{1,0:T(8,128)(2,1)}, u32[]{:S(2)}, u32[]{:S(2)}) collective-permute-start(bf16[1024,768]{1,0:T(8,128)(2,1)} %pad_maximum_fusion), channel_id=1, source_target_pairs={{0,65},{1,64},{64,1},{65,0},{2,67},{3,66},{66,3},{67,2},{4,69},{5,... | collective-permute-start | bytes 4718600 | tf_op jit(solution)/shard_map/ppermute | solution.py:192
  28.0 103.9 %collective-permute-start.5 = (bf16[1024,768]{1,0:T(8,128)(2,1)}, bf16[1024,768]{1,0:T(8,128)(2,1)}, u32[]{:S(2)}, u32[]{:S(2)}) collective-permute-start(bf16[1024,768]{1,0:T(8,128)(2,1)} %w_ref.5), channel_id=1, source_target_pairs={{0,64},{64,0},{1,65},{65,1},{2,66},{66,2},{3,67},{67,3},{4,68},{68... | collective-permute-start | bytes 4718600 | tf_op jit(solution)/shard_map/ppermute | solution.py:29
  168.9 24.9 %all-to-all-start.3 = ((bf16[32,8,768]{2,1,0:T(8,128)(2,1)}), bf16[32,8,768]{2,1,0:T(8,128)(2,1)S(1)}, u32[]{:S(2)}, u32[]{:S(2)}) async-start(bf16[32,8,768]{2,1,0:T(8,128)(2,1)} %bitcast.83), calls=%async_computation.3 | async-start | bytes 786432 | tf_op jit(solution)/shard_map/all_to_all | solution.py:220
  179.6 21.7 %collective-permute-start.7 = (bf16[2,64,2048]{2,1,0:T(8,128)(2,1)}, bf16[2,64,2048]{2,1,0:T(8,128)(2,1)}, u32[]{:S(2)}, u32[]{:S(2)}) collective-permute-start(bf16[2,64,2048]{2,1,0:T(8,128)(2,1)} %get-tuple-element.27), channel_id=1, source_target_pairs={{0,2},{2,0},{4,6},{6,4},{1,3},{3,1},{5,7},{7,5},{8,10},{10,8},{12,... | collective-permute-start | bytes 1572872 | tf_op jit(solution)/shard_map/ppermute | solution.py:224
  195.4 25.1 %all-to-all-start.5 = ((bf16[32,8,768]{2,1,0:T(8,128)(2,1)}), bf16[32,8,768]{2,1,0:T(8,128)(2,1)S(1)}, u32[]{:S(2)}, u32[]{:S(2)}) async-start(bf16[32,8,768]{2,1,0:T(8,128)(2,1)} %bitcast.82), calls=%async_computation.5 | async-start | bytes 786432 | tf_op jit(solution)/shard_map/all_to_all | solution.py:220
  203.2 19.3 %collective-permute-start.8 = (bf16[64,2048]{1,0:T(8,128)(2,1)}, bf16[64,2048]{1,0:T(8,128)(2,1)}, u32[]{:S(2)}, u32[]{:S(2)}) collective-permute-start(bf16[64,2048]{1,0:T(8,128)(2,1)} %fusion.13), channel_id=1, source_target_pairs={{0,4},{2,6},{4,0},{6,2},{1,5},{3,7},{5,1},{7,3},{8,12},{10,14},{12... | collective-permute-start | bytes 786440 | tf_op jit(solution)/shard_map/ppermute | solution.py:226
  213.0 20.5 %collective-permute-start.13 = (bf16[2,64,2048]{2,1,0:T(8,128)(2,1)}, bf16[2,64,2048]{2,1,0:T(8,128)(2,1)}, u32[]{:S(2)}, u32[]{:S(2)}) collective-permute-start(bf16[2,64,2048]{2,1,0:T(8,128)(2,1)} %get-tuple-element.31), channel_id=1, source_target_pairs={{0,2},{2,0},{4,6},{6,4},{1,3},{3,1},{5,7},{7,5},{8,10},{10,8},{12,... | collective-permute-start | bytes 1572872 | tf_op jit(solution)/shard_map/ppermute | solution.py:224
  220.5 21.1 %collective-permute-start.18 = (bf16[256,768]{1,0:T(8,128)(2,1)S(1)}, bf16[256,768]{1,0:T(8,128)(2,1)S(1)}, u32[]{:S(2)}, u32[]{:S(2)}) collective-permute-start(bf16[256,768]{1,0:T(8,128)(2,1)S(1)} %bitcast.78), channel_id=1, source_target_pairs={{0,1},{1,0},{2,3},{3,2},{4,5},{5,4},{6,7},{7,6},{8,9},{9,8},{10,11... | collective-permute-start | bytes 1179656 | tf_op jit(solution)/shard_map/ppermute | solution.py:29
  234.6 18.0 %collective-permute-start.14 = (bf16[64,2048]{1,0:T(8,128)(2,1)S(1)}, bf16[64,2048]{1,0:T(8,128)(2,1)S(1)}, u32[]{:S(2)}, u32[]{:S(2)}) collective-permute-start(bf16[64,2048]{1,0:T(8,128)(2,1)S(1)} %fusion.14), channel_id=1, source_target_pairs={{0,4},{2,6},{4,0},{6,2},{1,5},{3,7},{5,1},{7,3},{8,12},{10,14},{12... | collective-permute-start | bytes 786440 | tf_op jit(solution)/shard_map/ppermute | solution.py:226
  238.8 20.3 %collective-permute-start.9 = (bf16[64,1024]{1,0:T(8,128)(2,1)S(1)}, bf16[64,1024]{1,0:T(8,128)(2,1)S(1)}, u32[]{:S(2)}, u32[]{:S(2)}) collective-permute-start(bf16[64,1024]{1,0:T(8,128)(2,1)S(1)} %pad_maximum_fusion.8), channel_id=1, source_target_pairs={{0,4},{2,6},{4,0},{6,2},{1,5},{3,7},{5,1},{7,3},{8,12},{10,14},{12... | collective-permute-start | bytes 393224 | tf_op jit(solution)/shard_map/ppermute | solution.py:233
  246.7 22.9 %collective-permute-start.19 = (bf16[2,64,2048]{2,1,0:T(8,128)(2,1)S(1)}, bf16[2,64,2048]{2,1,0:T(8,128)(2,1)S(1)}, u32[]{:S(2)}, u32[]{:S(2)}) collective-permute-start(bf16[2,64,2048]{2,1,0:T(8,128)(2,1)S(1)} %get-tuple-element.34), channel_id=1, source_target_pairs={{0,2},{2,0},{4,6},{6,4},{1,3},{3,1},{5,7},{7,5},{8,10},{10,8},{12,... | collective-permute-start | bytes 1572872 | tf_op jit(solution)/shard_map/ppermute | solution.py:224
  259.2 16.0 %collective-permute-start.10 = (bf16[128,1024]{1,0:T(8,128)(2,1)S(1)}, bf16[128,1024]{1,0:T(8,128)(2,1)S(1)}, u32[]{:S(2)}, u32[]{:S(2)}) collective-permute-start(bf16[128,1024]{1,0:T(8,128)(2,1)S(1)} %pad_maximum_fusion.5), channel_id=1, source_target_pairs={{0,2},{2,0},{4,6},{6,4},{1,3},{3,1},{5,7},{7,5},{8,10},{10,8},{12,... | collective-permute-start | bytes 786440 | tf_op jit(solution)/shard_map/ppermute | solution.py:234
  266.7 19.6 %collective-permute-start.16 = (bf16[128,1024]{1,0:T(8,128)(2,1)S(1)}, bf16[128,1024]{1,0:T(8,128)(2,1)S(1)}, u32[]{:S(2)}, u32[]{:S(2)}) collective-permute-start(bf16[128,1024]{1,0:T(8,128)(2,1)S(1)} %pad_maximum_fusion.6), channel_id=1, source_target_pairs={{0,2},{2,0},{4,6},{6,4},{1,3},{3,1},{5,7},{7,5},{8,10},{10,8},{12,... | collective-permute-start | bytes 786440 | tf_op jit(solution)/shard_map/ppermute | solution.py:234
  269.6 18.7 %collective-permute-start.20 = (bf16[64,2048]{1,0:T(8,128)(2,1)S(1)}, bf16[64,2048]{1,0:T(8,128)(2,1)S(1)}, u32[]{:S(2)}, u32[]{:S(2)}) collective-permute-start(bf16[64,2048]{1,0:T(8,128)(2,1)S(1)} %fusion.15), channel_id=1, source_target_pairs={{0,4},{2,6},{4,0},{6,2},{1,5},{3,7},{5,1},{7,3},{8,12},{10,14},{12... | collective-permute-start | bytes 786440 | tf_op jit(solution)/shard_map/ppermute | solution.py:226
  275.2 13.2 %collective-permute-start.11 = (bf16[256,1024]{1,0:T(8,128)(2,1)S(1)}, bf16[256,1024]{1,0:T(8,128)(2,1)S(1)}, u32[]{:S(2)}, u32[]{:S(2)}) collective-permute-start(bf16[256,1024]{1,0:T(8,128)(2,1)S(1)} %pad_maximum_fusion.2.h_ref), channel_id=1, source_target_pairs={{0,1},{1,0},{2,3},{3,2},{4,5},{5,4},{6,7},{7,6},{8,9},{9,8},{10,11... | collective-permute-start | bytes 1572872 | tf_op jit(solution)/shard_map/ppermute | solution.py:29
  286.4 39.2 %collective-permute-start.17 = (bf16[256,1024]{1,0:T(8,128)(2,1)S(1)}, bf16[256,1024]{1,0:T(8,128)(2,1)S(1)}, u32[]{:S(2)}, u32[]{:S(2)}) collective-permute-start(bf16[256,1024]{1,0:T(8,128)(2,1)S(1)} %pad_maximum_fusion.3.h_ref), channel_id=1, source_target_pairs={{0,1},{1,0},{2,3},{3,2},{4,5},{5,4},{6,7},{7,6},{8,9},{9,8},{10,11... | collective-permute-start | bytes 1572872 | tf_op jit(solution)/shard_map/ppermute | solution.py:29
  292.1 37.2 %all-to-all-start.2 = ((bf16[32,8,768]{2,1,0:T(8,128)(2,1)}), bf16[32,8,768]{2,1,0:T(8,128)(2,1)S(1)}, u32[]{:S(2)}, u32[]{:S(2)}) async-start(bf16[32,8,768]{2,1,0:T(8,128)(2,1)} %bitcast.19), calls=%async_computation.2 | async-start | bytes 786432 | tf_op jit(solution)/shard_map/all_to_all | solution.py:237
  304.1 16.4 %collective-permute-start.21 = (bf16[64,1024]{1,0:T(8,128)(2,1)S(1)}, bf16[64,1024]{1,0:T(8,128)(2,1)S(1)}, u32[]{:S(2)}, u32[]{:S(2)}) collective-permute-start(bf16[64,1024]{1,0:T(8,128)(2,1)S(1)} %pad_maximum_fusion.10), channel_id=1, source_target_pairs={{0,4},{2,6},{4,0},{6,2},{1,5},{3,7},{5,1},{7,3},{8,12},{10,14},{12... | collective-permute-start | bytes 393224 | tf_op jit(solution)/shard_map/ppermute | solution.py:233
  320.6 20.6 %collective-permute-start.22 = (bf16[128,1024]{1,0:T(8,128)(2,1)S(1)}, bf16[128,1024]{1,0:T(8,128)(2,1)}, u32[]{:S(2)}, u32[]{:S(2)}) collective-permute-start(bf16[128,1024]{1,0:T(8,128)(2,1)S(1)} %pad_maximum_fusion.7), channel_id=1, source_target_pairs={{0,2},{2,0},{4,6},{6,4},{1,3},{3,1},{5,7},{7,5},{8,10},{10,8},{12,... | collective-permute-start | bytes 786440 | tf_op jit(solution)/shard_map/ppermute | solution.py:234
  329.3 32.8 %all-to-all-start.4 = ((bf16[32,8,768]{2,1,0:T(8,128)(2,1)}), bf16[32,8,768]{2,1,0:T(8,128)(2,1)S(1)}, u32[]{:S(2)}, u32[]{:S(2)}) async-start(bf16[32,8,768]{2,1,0:T(8,128)(2,1)} %bitcast.25), calls=%async_computation.4 | async-start | bytes 786432 | tf_op jit(solution)/shard_map/all_to_all | solution.py:237
  362.0 24.2 %all-to-all-start.6 = ((bf16[32,8,768]{2,1,0:T(8,128)(2,1)}), bf16[32,8,768]{2,1,0:T(8,128)(2,1)S(1)}, u32[]{:S(2)}, u32[]{:S(2)}) async-start(bf16[32,8,768]{2,1,0:T(8,128)(2,1)} %bitcast.31), calls=%async_computation.6 | async-start | bytes 786432 | tf_op jit(solution)/shard_map/all_to_all | solution.py:237
  (17 other events, 287.0 us)

commit v3 on v1

v3 whole, which is shorter than its diff:
```python
import math
from functools import partial

import jax
import jax.numpy as jnp
from jax import lax
from jax.experimental import pallas as pl
from jax.experimental.pallas import tpu as pltpu
from jax.sharding import Mesh, PartitionSpec as P

D = 6144
HD = 128
EXPERTS = 4
CAP = 24
SLOT = 8
F32 = jnp.float32
BF16 = jnp.bfloat16

CTX = ("yh", "xh", "xl", "z")
EXP = ("yl", "c")
HALF = ("xh", "xl", "z")
GROUP = ("yh", "xh")
SWAP = [(0, 1), (1, 0)]
Y_XOR = [[(i, i ^ k) for i in range(4)] for k in range(4)]


def swap(x, axis):
    return lax.ppermute(x, axis, SWAP)


def split3(v):
    hi = lax.reduce_precision(v, 8, 7)
    mid = lax.reduce_precision(v - hi, 8, 7)
    lo = (v - hi) - mid
    return [p.astype(BF16) for p in (hi, mid, lo)]


def attend(queries, keys, values, early):
    rows = queries.shape[0]
    heads = queries.shape[1] // HD
    yh = lax.axis_index("yh")
    scale = 1.0 / math.sqrt(HD)

    foreign = lax.ppermute(queries, "yh", [(1, 0)])
    kv = jnp.concatenate([keys, values], axis=1)
    members = lax.axis_size(HALF)
    kv = lax.all_to_all(
        jnp.broadcast_to(kv[None], (members,) + kv.shape), HALF, split_axis=0, concat_axis=0, tiled=True
    ).reshape(members * rows, 2 * HD)
    kv, *early = lax.optimization_barrier((kv,) + early)
    k_all, v_all = kv[:, :HD], kv[:, HD:]
    count = members * rows

    def stacked(q):
        return q.reshape(rows, heads, HD).transpose(1, 0, 2).reshape(heads * rows, HD)

    q_all = jnp.concatenate([stacked(queries), stacked(foreign)], axis=0)
    own_pos = lax.axis_index(HALF) * rows + jnp.tile(jnp.arange(rows, dtype=jnp.int32), heads)
    limit = jnp.concatenate([own_pos, jnp.full_like(own_pos, count)])
    scores = jnp.einsum("qd,kd->qk", q_all, k_all, preferred_element_type=F32) * scale
    allowed = jnp.arange(count, dtype=jnp.int32)[None, :] <= limit[:, None]
    scores = jnp.where(allowed, scores, -1e30)
    top = jnp.max(scores, axis=1)
    weights = jnp.exp(scores - top[:, None])
    total = jnp.sum(weights, axis=1)
    acc = jnp.einsum("qk,kd->qd", weights.astype(BF16), v_all, preferred_element_type=F32)
    out = acc / total[:, None]
    lse = top + jnp.log(total)

    n = heads * rows

    def unstacked(o):
        return o.reshape(heads, rows, HD).transpose(1, 0, 2).reshape(rows, heads * HD)

    out_own, out_far = unstacked(out[:n]), unstacked(out[n:])
    lse_own, lse_far = lse[:n].reshape(heads, rows).T, lse[n:].reshape(heads, rows).T
    tail = jnp.concatenate(split3(lse_far), axis=1)
    tail = jnp.pad(tail, ((0, 0), (0, HD - tail.shape[1])))
    message = jnp.concatenate([out_far.astype(BF16), tail], axis=1)
    got = lax.ppermute(message, "yh", [(0, 1)])
    got_out = got[:, : heads * HD].astype(F32)
    parts = got[:, heads * HD : heads * HD + 3 * heads].astype(F32)
    got_lse = parts[:, :heads] + parts[:, heads : 2 * heads] + parts[:, 2 * heads :]
    share = jnp.where(yh == 1, jax.nn.sigmoid(got_lse - lse_own), 0.0)
    share = jnp.repeat(share, HD, axis=1)
    return (out_own * (1.0 - share) + got_out * share).astype(BF16), early


def expand(order_ref, xn_ref, xf_ref, on_ref, of_ref, w_ref, wo_ref, *rest):
    out_refs, acc_ref = rest[:4], rest[4]
    contract = (((1,), (1,)), ((), ()))
    rows = acc_ref.shape[0] // 2
    for p, (a, b) in enumerate(((xn_ref, on_ref), (xf_ref, of_ref))):
        a, b = (r[...].reshape(rows, r.shape[-1]) for r in (a, b))
        acc_ref[p * rows : (p + 1) * rows, :] = lax.dot_general(
            a, w_ref[...], contract, preferred_element_type=F32
        ) + lax.dot_general(b, wo_ref[...], contract, preferred_element_type=F32)
    share = out_refs[0].shape[0]
    for i, ref in enumerate(out_refs):
        at = pl.multiple_of((order_ref[0] ^ i) * share, share)
        ref[...] = acc_ref[pl.ds(at, share), :].astype(BF16)


def gate_up_terms(order, near, far, near_other, far_other, specs, w, wo, rows):
    hidden, feat = w.shape
    cols = hidden // 2
    share = rows // 4
    weight = pl.BlockSpec((cols, feat), lambda n, o: (n, 0))
    out = pl.BlockSpec((share, cols), lambda n, o: (0, n))
    shape = jax.ShapeDtypeStruct((share, hidden), BF16)
    return pl.pallas_call(
        expand,
        grid_spec=pltpu.PrefetchScalarGridSpec(
            num_scalar_prefetch=1,
            grid=(2,),
            in_specs=[specs[0], specs[1], specs[0], specs[1], weight, weight],
            out_specs=[out] * 4,
            scratch_shapes=[pltpu.VMEM((rows, cols), F32)],
        ),
        out_shape=[shape] * 4,
        cost_estimate=pl.CostEstimate(
            flops=4 * rows * hidden * feat, transcendentals=0, bytes_accessed=4 * hidden * feat + 2 * rows * hidden
        ),
        compiler_params=pltpu.CompilerParams(vmem_limit_bytes=40 << 20),
        name="gate_up_terms",
    )(order, near, far, near_other, far_other, w, wo)


def contract_hidden(order_ref, h_ref, ho_ref, w_ref, near_ref, far_ref):
    core = order_ref[1]
    half = w_ref.shape[0] // 2
    own = pl.multiple_of(core * half, half)
    other = pl.multiple_of((1 - core) * half, half)
    acc = jnp.dot(h_ref[...], w_ref[pl.ds(own, half), :], preferred_element_type=F32)
    acc += jnp.dot(ho_ref[...], w_ref[pl.ds(other, half), :], preferred_element_type=F32)
    share = h_ref.shape[0] // 4
    for i in range(4):
        block = order_ref[0] ^ i
        at = pl.multiple_of((block & 1) * share, share)
        part = acc[i * share : (i + 1) * share].astype(BF16)

        @pl.when(block < 2)
        def _():
            near_ref[pl.ds(at, share), :] = part

        @pl.when(block >= 2)
        def _():
            far_ref[pl.ds(at, share), :] = part


def down_terms(order, h, ho, w):
    rows = h.shape[0]
    hidden, feat = w.shape
    whole = pl.BlockSpec(memory_space=pltpu.VMEM)
    shape = jax.ShapeDtypeStruct((rows // 2, feat), BF16)
    return pl.pallas_call(
        contract_hidden,
        in_specs=[pl.BlockSpec(memory_space=pltpu.SMEM), whole, whole, whole],
        out_specs=[whole, whole],
        out_shape=[shape, shape],
        cost_estimate=pl.CostEstimate(
            flops=2 * rows * hidden * feat, transcendentals=0, bytes_accessed=2 * hidden * feat + 4 * rows * hidden
        ),
        compiler_params=pltpu.CompilerParams(vmem_limit_bytes=40 << 20),
        name="down_terms",
    )(order, h, ho, w)


def after(value, *others):
    return lax.optimization_barrier((value,) + others)[0]


def exchange(blocks, axes):
    me = lax.axis_index(axes)
    xor = [[(i, i ^ k) for i in range(4)] for k in range(4)]
    got = jnp.zeros_like(blocks)
    for k in range(4):
        block = lax.dynamic_index_in_dim(blocks, me ^ k, 0, keepdims=False)
        if k:
            block = lax.ppermute(block, axes, xor[k])
        got = lax.dynamic_update_index_in_dim(got, block, me ^ k, 0)
    return got


def body(queries, keys, values, residual, norm_gain, routes, route_weight, w_gate, w_up, w_down):
    feat = residual.shape[1]
    half = w_gate.shape[0] // 2
    core = lax.axis_index("c")
    me = lax.axis_index("yl")
    xl = lax.axis_index("xl")
    order = jnp.stack([me, core, xl]).astype(jnp.int32)

    def halves(which):
        cut = partial(lax.dynamic_slice_in_dim, start_index=which * half, slice_size=half, axis=0)
        return jnp.concatenate([cut(w_gate), cut(w_up)], axis=0)

    w_in = halves(core)
    w_in_other = swap(halves(1 - core), "c")

    attn, (w_in, w_in_other) = attend(queries, keys, values, (w_in, w_in_other))
    mixed = residual.astype(F32) + attn.astype(F32)
    total_squares = lax.psum(jnp.sum(mixed * mixed, axis=1), EXP)
    normed = (mixed * lax.rsqrt(total_squares / D + 1e-05)[:, None] * norm_gain[None, :]).astype(BF16)

    chosen = routes[:, 0]
    expert_ids = jnp.arange(EXPERTS, dtype=jnp.int32)
    onehot = (chosen[:, None] == expert_ids[None, :]).astype(jnp.int32)
    slot_index = jnp.sum((jnp.cumsum(onehot, axis=0) - 1) * onehot, axis=1)
    slot_ids = jnp.arange(CAP, dtype=jnp.int32)
    select = (
        (chosen[None, None, :] == expert_ids[:, None, None])
        & (slot_index[None, None, :] == slot_ids[None, :, None])
    ).astype(BF16)
    packed = jnp.einsum("ect,td->ecd", select, normed, preferred_element_type=F32).astype(BF16)

    nx = lax.axis_size("xl")
    nz = lax.axis_size("z")
    n = SLOT
    group = EXPERTS * n
    rows = nx * nz * group

    direct = jnp.broadcast_to(packed[:, None, :n], (EXPERTS, nx * nz, n, feat)).reshape(-1, n, feat)
    x_a = lax.all_to_all(direct, CTX, split_axis=0, concat_axis=0, tiled=True).reshape(EXPERTS, nx, nz * n, feat)
    rest = exchange(packed[:, n:], GROUP).reshape(EXPERTS, 2, n, feat).transpose(1, 0, 2, 3).reshape(2 * group, feat)
    rest = after(rest, x_a)
    near = lax.all_to_all(
        jnp.broadcast_to(rest[None], (nz, 2 * group, feat)), "z", split_axis=0, concat_axis=0, tiled=True
    ).reshape(nz, 2, group, feat)
    x_a_other = swap(x_a, "c")
    a_block = (EXPERTS, pl.Squeezed(), nz * n, feat)
    specs_a = (
        pl.BlockSpec(a_block, lambda k, o: (0, o[2], 0, 0)),
        pl.BlockSpec(a_block, lambda k, o: (0, 1 - o[2], 0, 0)),
    )
    terms = [gate_up_terms(order, x_a, x_a, x_a_other, x_a_other, specs_a, w_in, w_in_other, rows)]
    near = after(near, *terms[0])
    far = swap(near, "xl")
    near_other, far_other = swap(near, "c"), swap(far, "c")
    for chunk in range(2):
        spec = pl.BlockSpec((nz, pl.Squeezed(), group, feat), lambda k, o, chunk=chunk: (0, chunk, 0, 0))
        first = after(far_other, *terms[-1])
        terms.append(gate_up_terms(order, near, far, near_other, first, (spec, spec), w_in, w_in_other, rows))

    def hidden_of(parts):
        full = parts[0].astype(F32)
        for i in range(1, 4):
            full = full + lax.ppermute(parts[i], "yl", Y_XOR[i]).astype(F32)
        return (jax.nn.silu(full[:, :half]) * full[:, half:]).astype(BF16)

    def down_of(parts):
        hidden = hidden_of(parts)
        hid = jnp.concatenate([hidden] + [lax.ppermute(hidden, "yl", Y_XOR[i]) for i in range(1, 4)], axis=0)
        return down_terms(order, hid, swap(hid, "c"), w_down)

    def gather_z(down, dims):
        stay, leave = down
        summed = (stay.astype(F32) + swap(leave, "xl").astype(F32)).astype(BF16)
        if dims == "ez":
            summed = summed.reshape(EXPERTS, nz, group // EXPERTS, feat).transpose(1, 0, 2, 3)
        back = lax.all_to_all(summed.reshape(nz, group, feat), "z", split_axis=0, concat_axis=0, tiled=True)
        return jnp.sum(back.astype(F32), axis=0).astype(BF16).reshape(EXPERTS, n, feat)

    out_a = gather_z(down_of(terms[0]), "ez")
    out_b = gather_z(down_of(terms[1]), "ze")
    stay, leave = (d.reshape(nz, EXPERTS, n, feat).transpose(1, 0, 2, 3) for d in down_of(terms[2]))
    direct = jnp.where(xl == 0, jnp.stack([stay, leave], axis=1), jnp.stack([leave, stay], axis=1))
    out_c = lax.all_to_all(direct.reshape(-1, n, feat), CTX, split_axis=0, concat_axis=0, tiled=True)
    out_c = jnp.sum(out_c.reshape(EXPERTS, nx * nz, n, feat).astype(F32), axis=1).astype(BF16)
    out_ab = exchange(jnp.concatenate([out_a, out_b], axis=1), GROUP)
    returned = jnp.concatenate([out_ab, out_c], axis=1)
    moe_rows = jnp.einsum("ect,ecd->td", select, returned, preferred_element_type=F32)
    return (route_weight[:, None] * moe_rows).astype(BF16)


def solution(mesh):
    fine = Mesh(mesh.devices.reshape(2, 2, 2, 8, 4, 2), CTX + EXP)
    wide = P(CTX, EXP)
    in_specs = (wide, wide, wide, wide, P(EXP), P(CTX, None), P(CTX), wide, wide, wide)
    return jax.shard_map(body, mesh=fine, in_specs=in_specs, out_specs=wide, check_vma=False)
```

time: 369 us -> 360 us (0.976)
  starting transfers between devices: 97 us -> 160 us
  waiting for transfers between devices: 187 us -> 135 us
  blocking collectives: 44.6 us -> 10 us
  Pallas kernels: 0 us -> 17.5 us
  matrix products: 19.7 us -> 6.3 us
  local copies, waits for them, and re-layouts: 8.49 us -> 13.3 us
    ppermute x12 -> x24, starting transfers between devices: 35.6 us -> 84.8 us  [the longest x6 29.2 us: exchange(): block = lax.ppermute(block, axes, xor[k])]
    ppermute x9 -> x10, waiting for transfers between devices: 49.9 us -> 10.5 us  [swap(): return lax.ppermute(x, axis, SWAP)]
    all_to_all x2 -> x0, blocking collectives: 34.6 us -> none  [the longest x1 20.1 us: body(): lax.all_to_all(packed, ('yh', 'xh'), split_axis=0, concat_axis=0, tiled=T...]
    pallas_call x0 -> x6, Pallas kernels: none -> 17.5 us  [the longest x3 12.6 us: gate_up_terms(): pl.pallas_call(expand, grid_spec=pltpu.PrefetchScalarGridSpec(num_scalar_...]
    dot_general x8 -> x0, matrix products: 15.5 us -> none  [the longest x2 6.45 us: body(): jnp.einsum('rd,fd->rf', x_other, w_in_other, preferred_element_type=F32)]
    all_to_all x4 -> x5, starting transfers between devices: 22.1 us -> 29.3 us  [the longest x1 12.9 us: body(): lax.all_to_all(direct, CTX, split_axis=0, concat_axis=0, tiled=True)]
    all_to_all x4 -> x5, waiting for transfers between devices: 35.1 us -> 28.5 us  [the longest x2 12.8 us: gather_z(): lax.all_to_all(summed.reshape(nz, group, feat), 'z', split_axis=0, concat...]
    ppermute x9 -> x10, starting transfers between devices: 18.1 us -> 23.4 us  [swap(): return lax.ppermute(x, axis, SWAP)]
  transfers between devices with their start and end apart: 28 -> 42, of which waited for: 16 -> 23; matrix products, arithmetic and copies ran while one was open for 7% -> 4% of each run, Pallas kernels for 0% -> 5%
where the time goes in v3:
time: 360 us; the launch traced here: 357 us
  starting transfers between devices  160 us (44%)
  waiting for transfers between devices  135 us (38%)
  Pallas kernels  17.5 us (5%)
  other arithmetic  13.8 us (4%)
  local copies, waits for them, and re-layouts  13.3 us (4%)
  blocking collectives  10 us (3%)
  matrix products  6.3 us (2%)
    ppermute x9, waiting for transfers between devices, hidden_of(): full = full + lax.ppermute(parts[i], 'yl', Y_XOR[i]).astype(F32)  37.1 us
    ppermute x6, starting transfers between devices, exchange(): block = lax.ppermute(block, axes, xor[k])  29.2 us
    ppermute x9, starting transfers between devices, hidden_of(): full = full + lax.ppermute(parts[i], 'yl', Y_XOR[i]).astype(F32)  27.9 us
    ppermute x9, starting transfers between devices, down_of(): lax.ppermute(hidden, 'yl', Y_XOR[i])  27.6 us
    ppermute x10, starting transfers between devices, swap(): return lax.ppermute(x, axis, SWAP)  23.4 us
    ppermute x6, waiting for transfers between devices, exchange(): block = lax.ppermute(block, axes, xor[k])  22.7 us
    ppermute x9, waiting for transfers between devices, down_of(): lax.ppermute(hidden, 'yl', Y_XOR[i])  16 us
    all_to_all x1, starting transfers between devices, attend(): lax.all_to_all(jnp.broadcast_to(kv[None], (members,) + kv.shape), HALF, s...  13.4 us
  transfers between devices with their start and end apart: 42, of which 23 were waited for; matrix products, arithmetic and copies ran while one was open for 4% of the time, Pallas kernels for 5%

profile of v3, /device:TPU:8, one launch (start us, length us, event | category | flops | bytes accessed | tf_op | source)
XLA Modules:
  0.0 356.9 jit_solution(14094684518216933371)
XLA Ops:
  1.9 13.4 %all-to-all-start = ((bf16[32,64,256]{2,1,0:T(8,128)(2,1)}), bf16[32,64,256]{2,1,0:T(8,128)(2,1)}, u32[]{:S(2)}, u32[]{:S(2)}) async-start(bf16[32,64,256]{2,1,0:T(8,128)(2,1)} %broadcast_in_dim.62), calls=%async_computation | async-start | bytes 2097152 | tf_op jit(solution)/shard_map/all_to_all | solution.py:47
  25.2 7.6 %collective-permute-done = bf16[64,768]{1,0:T(8,128)(2,1)S(1)} collective-permute-done((bf16[64,768]{1,0:T(8,128)(2,1)S(1)}, bf16[64,768]{1,0:T(8,128)(2,1)S(1)}, u32[]{:S(2)}, u32[]{:S(2)}) %collective-permute-start) | collective-permute-done | bytes 98336 | tf_op jit(solution)/shard_map/ppermute | solution.py:44
  32.9 11.0 %all-to-all-done = bf16[32,64,256]{2,1,0:T(8,128)(2,1)} async-done(((bf16[32,64,256]{2,1,0:T(8,128)(2,1)}), bf16[32,64,256]{2,1,0:T(8,128)(2,1)}, u32[]{:S(2)}, u32[]{:S(2)}) %all-to-all-start) | async-done | bytes 1048608 | tf_op jit(solution)/shard_map/all_to_all | solution.py:47
  52.9 7.5 %collective-permute-start.2 = (bf16[64,896]{1,0:T(8,128)(2,1)}, bf16[64,896]{1,0:T(8,128)(2,1)}, u32[]{:S(2)}, u32[]{:S(2)}) collective-permute-start(bf16[64,896]{1,0:T(8,128)(2,1)} %fusion.26), channel_id=1, source_target_pairs={{0,256},{1,257},{2,258},{3,259},{4,260},{5,261},{6,262},{7,263},{8... | collective-permute-start | bytes 344072 | tf_op jit(solution)/shard_map/ppermute | solution.py:80
  65.6 10.0 %psum.7 = f32[64]{0:T(128)S(1)} all-reduce(f32[64]{0:T(128)S(1)} %get-tuple-element.55), channel_id=1, replica_groups=mesh['yh'=2,'xh'=2,'xl'=2,'z'=8,'yl'=4,'c'=2] {'yl','c'}, use_global_device_ids=true, to_apply=%region_5.6 | all-reduce | flops 64 | bytes 512 | tf_op jit(solution)/shard_map/psum | solution.py:202
  76.9 12.9 %all-to-all-start.1 = ((bf16[64,8,768]{2,1,0:T(8,128)(2,1)}), bf16[64,8,768]{2,1,0:T(8,128)(2,1)}, u32[]{:S(2)}, u32[]{:S(2)}) async-start(bf16[64,8,768]{2,1,0:T(8,128)(2,1)} %bitcast.109), calls=%async_computation.1 | async-start | bytes 1572864 | tf_op jit(solution)/shard_map/all_to_all | solution.py:223
  89.8 4.9 %collective-permute-start.12 = (bf16[16,768]{1,0:T(8,128)(2,1)S(1)}, bf16[16,768]{1,0:T(8,128)(2,1)S(1)}, u32[]{:S(2)}, u32[]{:S(2)}) collective-permute-start(bf16[16,768]{1,0:T(8,128)(2,1)S(1)} %get-tuple-element.67), channel_id=1, source_target_pairs={{0,128},{128,0},{256,384},{384,256},{1,129},{129,1},{257,385},{385... | collective-permute-start | bytes 73736 | tf_op jit(solution)/shard_map/ppermute | solution.py:180
  94.7 7.5 %collective-permute-start.13 = (bf16[16,768]{1,0:T(8,128)(2,1)S(1)}, bf16[16,768]{1,0:T(8,128)(2,1)S(1)}, u32[]{:S(2)}, u32[]{:S(2)}) collective-permute-start(bf16[16,768]{1,0:T(8,128)(2,1)S(1)} %get-tuple-element.66), channel_id=1, source_target_pairs={{0,256},{128,384},{256,0},{384,128},{1,257},{129,385},{257,1},{385... | collective-permute-start | bytes 73736 | tf_op jit(solution)/shard_map/ppermute | solution.py:180
  104.5 8.8 %collective-permute-done.13 = bf16[16,768]{1,0:T(8,128)(2,1)S(1)} collective-permute-done((bf16[16,768]{1,0:T(8,128)(2,1)S(1)}, bf16[16,768]{1,0:T(8,128)(2,1)S(1)}, u32[]{:S(2)}, u32[]{:S(2)}) %collective-permute-start.13) | collective-permute-done | bytes 24608 | tf_op jit(solution)/shard_map/ppermute | solution.py:180
  134.6 11.7 %all-to-all-done.3 = bf16[8,64,768]{2,1,0:T(8,128)(2,1)} async-done(((bf16[8,64,768]{2,1,0:T(8,128)(2,1)}), bf16[8,64,768]{2,1,0:T(8,128)(2,1)}, u32[]{:S(2)}, u32[]{:S(2)}) %all-to-all-start.3) | async-done | bytes 786464 | tf_op jit(solution)/shard_map/all_to_all | solution.py:226
  160.0 8.0 %collective-permute-done.15.xf_ref = bf16[8,2,32,768]{3,2,1,0:T(8,128)(2,1)S(1)} collective-permute-done((bf16[8,2,32,768]{3,2,1,0:T(8,128)(2,1)}, bf16[8,2,32,768]{3,2,1,0:T(8,128)(2,1)S(1)}, u32[]{:S(2)}, u32[]{:S(2)}) %collective-permute-start.15) | collective-permute-done | bytes 786464 | tf_op jit(solution)/shard_map/ppermute | solution.py:28
  171.8 6.7 %collective-permute-done.6 = bf16[128,1024]{1,0:T(8,128)(2,1)S(1)} collective-permute-done((bf16[128,1024]{1,0:T(8,128)(2,1)}, bf16[128,1024]{1,0:T(8,128)(2,1)S(1)}, u32[]{:S(2)}, u32[]{:S(2)}) %collective-permute-start.6) | collective-permute-done | bytes 262176 | tf_op jit(solution)/shard_map/ppermute | solution.py:247
  183.7 4.3 %collective-permute-start.9 = (bf16[128,512]{1,0:T(8,128)(2,1)S(1)}, bf16[128,512]{1,0:T(8,128)(2,1)S(1)}, u32[]{:S(2)}, u32[]{:S(2)}) collective-permute-start(bf16[128,512]{1,0:T(8,128)(2,1)S(1)} %fusion.15), channel_id=1, source_target_pairs={{0,6},{2,4},{4,2},{6,0},{1,7},{3,5},{5,3},{7,1},{8,14},{10,12},{12... | collective-permute-start | bytes 393224 | tf_op jit(solution)/shard_map/ppermute | solution.py:252
  191.9 4.6 %collective-permute-done.9 = bf16[128,512]{1,0:T(8,128)(2,1)S(1)} collective-permute-done((bf16[128,512]{1,0:T(8,128)(2,1)S(1)}, bf16[128,512]{1,0:T(8,128)(2,1)S(1)}, u32[]{:S(2)}, u32[]{:S(2)}) %collective-permute-start.9) | collective-permute-done | bytes 131104 | tf_op jit(solution)/shard_map/ppermute | solution.py:252
  217.2 8.3 %collective-permute-done.19 = bf16[128,1024]{1,0:T(8,128)(2,1)S(1)} collective-permute-done((bf16[128,1024]{1,0:T(8,128)(2,1)S(1)}, bf16[128,1024]{1,0:T(8,128)(2,1)S(1)}, u32[]{:S(2)}, u32[]{:S(2)}) %collective-permute-start.19) | collective-permute-done | bytes 262176 | tf_op jit(solution)/shard_map/ppermute | solution.py:247
  225.4 7.5 %collective-permute-done.20 = bf16[128,1024]{1,0:T(8,128)(2,1)S(1)} collective-permute-done((bf16[128,1024]{1,0:T(8,128)(2,1)S(1)}, bf16[128,1024]{1,0:T(8,128)(2,1)S(1)}, u32[]{:S(2)}, u32[]{:S(2)}) %collective-permute-start.20) | collective-permute-done | bytes 262176 | tf_op jit(solution)/shard_map/ppermute | solution.py:247
  242.4 4.5 %gate_up_terms.5 = (bf16[128,1024]{1,0:T(8,128)(2,1)S(1)}, bf16[128,1024]{1,0:T(8,128)(2,1)}, bf16[128,1024]{1,0:T(8,128)(2,1)}, bf16[128,1024]{1,0:T(8,128)(2,1)}) custom-call(s32[3]{0:T(128)S(1)} %pad_add_fusion.order_ref, bf16[8,2,32,768]{3,2,1,0:T(8,128)(2,1)} %bitcast.31.xn_ref, bf16[8,2,32,768]{3,2,1,0:T(8,128)(2,1)S(1)} %collective-permute-done.15.xf_ref, ...), custom_call_target="tpu_custom_call" | custom-call | flops 1610612736 | bytes 4194304 | tf_op jit(solution)/shard_map/gate_up_terms/pallas_call | solution.py:111
  263.3 6.8 %collective-permute-done.30 = bf16[128,1024]{1,0:T(8,128)(2,1)} collective-permute-done((bf16[128,1024]{1,0:T(8,128)(2,1)}, bf16[128,1024]{1,0:T(8,128)(2,1)}, u32[]{:S(2)}, u32[]{:S(2)}) %collective-permute-start.30) | collective-permute-done | bytes 262176 | tf_op jit(solution)/shard_map/ppermute | solution.py:247
  270.1 5.9 %collective-permute-done.31 = bf16[128,1024]{1,0:T(8,128)(2,1)} collective-permute-done((bf16[128,1024]{1,0:T(8,128)(2,1)}, bf16[128,1024]{1,0:T(8,128)(2,1)}, u32[]{:S(2)}, u32[]{:S(2)}) %collective-permute-start.31) | collective-permute-done | bytes 262176 | tf_op jit(solution)/shard_map/ppermute | solution.py:247
  310.0 12.8 %all-to-all-done.4 = bf16[8,32,768]{2,1,0:T(8,128)(2,1)S(1)} async-done(((bf16[8,32,768]{2,1,0:T(8,128)(2,1)}), bf16[8,32,768]{2,1,0:T(8,128)(2,1)S(1)}, u32[]{:S(2)}, u32[]{:S(2)}) %all-to-all-start.4) | async-done | bytes 393248 | tf_op jit(solution)/shard_map/all_to_all | solution.py:260
  322.8 4.6 %all-to-all-start.5 = ((bf16[64,8,768]{2,1,0:T(8,128)(2,1)}), bf16[64,8,768]{2,1,0:T(8,128)(2,1)S(1)}, u32[]{:S(2)}, u32[]{:S(2)}) async-start(bf16[64,8,768]{2,1,0:T(8,128)(2,1)} %bitcast.48), calls=%async_computation.5 | async-start | bytes 1572864 | tf_op jit(solution)/shard_map/all_to_all | solution.py:267
  328.6 5.0 %collective-permute-start.26 = (bf16[16,768]{1,0:T(8,128)(2,1)S(1)}, bf16[16,768]{1,0:T(8,128)(2,1)S(1)}, u32[]{:S(2)}, u32[]{:S(2)}) collective-permute-start(bf16[16,768]{1,0:T(8,128)(2,1)S(1)} %get-tuple-element.63), channel_id=1, source_target_pairs={{0,128},{128,0},{256,384},{384,256},{1,129},{129,1},{257,385},{385... | collective-permute-start | bytes 73736 | tf_op jit(solution)/shard_map/ppermute | solution.py:180
  333.6 7.5 %collective-permute-start.27 = (bf16[16,768]{1,0:T(8,128)(2,1)S(1)}, bf16[16,768]{1,0:T(8,128)(2,1)S(1)}, u32[]{:S(2)}, u32[]{:S(2)}) collective-permute-start(bf16[16,768]{1,0:T(8,128)(2,1)S(1)} %get-tuple-element.64), channel_id=1, source_target_pairs={{0,256},{128,384},{256,0},{384,128},{1,257},{129,385},{257,1},{385... | collective-permute-start | bytes 73736 | tf_op jit(solution)/shard_map/ppermute | solution.py:180
  343.3 7.5 %collective-permute-done.27 = bf16[16,768]{1,0:T(8,128)(2,1)S(1)} collective-permute-done((bf16[16,768]{1,0:T(8,128)(2,1)S(1)}, bf16[16,768]{1,0:T(8,128)(2,1)S(1)}, u32[]{:S(2)}, u32[]{:S(2)}) %collective-permute-start.27) | collective-permute-done | bytes 24608 | tf_op jit(solution)/shard_map/ppermute | solution.py:180
  (166 shorter events, 166.6 us)
Async XLA Ops:
  1.9 42.0 %all-to-all-start = ((bf16[32,64,256]{2,1,0:T(8,128)(2,1)}), bf16[32,64,256]{2,1,0:T(8,128)(2,1)}, u32[]{:S(2)}, u32[]{:S(2)}) async-start(bf16[32,64,256]{2,1,0:T(8,128)(2,1)} %broadcast_in_dim.62), calls=%async_computation | async-start | bytes 2097152 | tf_op jit(solution)/shard_map/all_to_all | solution.py:47
  76.9 41.7 %all-to-all-start.1 = ((bf16[64,8,768]{2,1,0:T(8,128)(2,1)}), bf16[64,8,768]{2,1,0:T(8,128)(2,1)}, u32[]{:S(2)}, u32[]{:S(2)}) async-start(bf16[64,8,768]{2,1,0:T(8,128)(2,1)} %bitcast.109), calls=%async_computation.1 | async-start | bytes 1572864 | tf_op jit(solution)/shard_map/all_to_all | solution.py:223
  94.7 18.6 %collective-permute-start.13 = (bf16[16,768]{1,0:T(8,128)(2,1)S(1)}, bf16[16,768]{1,0:T(8,128)(2,1)S(1)}, u32[]{:S(2)}, u32[]{:S(2)}) collective-permute-start(bf16[16,768]{1,0:T(8,128)(2,1)S(1)} %get-tuple-element.66), channel_id=1, source_target_pairs={{0,256},{128,384},{256,0},{384,128},{1,257},{129,385},{257,1},{385... | collective-permute-start | bytes 73736 | tf_op jit(solution)/shard_map/ppermute | solution.py:180
  119.5 26.8 %all-to-all-start.3 = ((bf16[8,64,768]{2,1,0:T(8,128)(2,1)}), bf16[8,64,768]{2,1,0:T(8,128)(2,1)}, u32[]{:S(2)}, u32[]{:S(2)}) async-start(bf16[8,64,768]{2,1,0:T(8,128)(2,1)} %broadcast_in_dim.70), calls=%async_computation.3 | async-start | bytes 1572864 | tf_op jit(solution)/shard_map/all_to_all | solution.py:226
  146.3 21.7 %collective-permute-start.15 = (bf16[8,2,32,768]{3,2,1,0:T(8,128)(2,1)}, bf16[8,2,32,768]{3,2,1,0:T(8,128)(2,1)S(1)}, u32[]{:S(2)}, u32[]{:S(2)}) collective-permute-start(bf16[8,2,32,768]{3,2,1,0:T(8,128)(2,1)} %bitcast.31.xn_ref), channel_id=1, source_target_pairs={{0,64},{64,0},{1,65},{65,1},{2,66},{66,2},{3,67},{67,3},{4,68},{68... | collective-permute-start | bytes 2359304 | tf_op jit(solution)/shard_map/ppermute | solution.py:28
  148.8 21.1 %collective-permute-start.4 = (bf16[128,1024]{1,0:T(8,128)(2,1)}, bf16[128,1024]{1,0:T(8,128)(2,1)S(1)}, u32[]{:S(2)}, u32[]{:S(2)}) collective-permute-start(bf16[128,1024]{1,0:T(8,128)(2,1)} %copy-done.5), channel_id=1, source_target_pairs={{0,2},{2,0},{4,6},{6,4},{1,3},{3,1},{5,7},{7,5},{8,10},{10,8},{12,... | collective-permute-start | bytes 786440 | tf_op jit(solution)/shard_map/ppermute | solution.py:247
  151.1 20.8 %collective-permute-start.5 = (bf16[128,1024]{1,0:T(8,128)(2,1)}, bf16[128,1024]{1,0:T(8,128)(2,1)S(1)}, u32[]{:S(2)}, u32[]{:S(2)}) collective-permute-start(bf16[128,1024]{1,0:T(8,128)(2,1)} %copy-done.4), channel_id=1, source_target_pairs={{0,4},{2,6},{4,0},{6,2},{1,5},{3,7},{5,1},{7,3},{8,12},{10,14},{12... | collective-permute-start | bytes 786440 | tf_op jit(solution)/shard_map/ppermute | solution.py:247
  154.6 23.9 %collective-permute-start.6 = (bf16[128,1024]{1,0:T(8,128)(2,1)}, bf16[128,1024]{1,0:T(8,128)(2,1)S(1)}, u32[]{:S(2)}, u32[]{:S(2)}) collective-permute-start(bf16[128,1024]{1,0:T(8,128)(2,1)} %copy-done.3), channel_id=1, source_target_pairs={{0,6},{2,4},{4,2},{6,0},{1,7},{3,5},{5,3},{7,1},{8,14},{10,12},{12... | collective-permute-start | bytes 786440 | tf_op jit(solution)/shard_map/ppermute | solution.py:247
  158.1 40.4 %collective-permute-start.16 = (bf16[8,2,32,768]{3,2,1,0:T(8,128)(2,1)}, bf16[8,2,32,768]{3,2,1,0:T(8,128)(2,1)S(1)}, u32[]{:S(2)}, u32[]{:S(2)}) collective-permute-start(bf16[8,2,32,768]{3,2,1,0:T(8,128)(2,1)} %bitcast.31.xn_ref), channel_id=1, source_target_pairs={{0,1},{1,0},{2,3},{3,2},{4,5},{5,4},{6,7},{7,6},{8,9},{9,8},{10,11... | collective-permute-start | bytes 2359304 | tf_op jit(solution)/shard_map/ppermute | solution.py:28
  168.0 30.5 %collective-permute-start.17 = (bf16[8,2,32,768]{3,2,1,0:T(8,128)(2,1)S(1)}, bf16[8,2,32,768]{3,2,1,0:T(8,128)(2,1)S(1)}, u32[]{:S(2)}, u32[]{:S(2)}) collective-permute-start(bf16[8,2,32,768]{3,2,1,0:T(8,128)(2,1)S(1)} %collective-permute-done.15.xf_ref), channel_id=1, source_target_pairs={{0,1},{1,0},{2,3},{3,2},{4,5},{5,4},{6,7},{7,6},{8,9},{9,8},{10,11... | collective-permute-start | bytes 2359304 | tf_op jit(solution)/shard_map/ppermute | solution.py:28
  204.2 21.2 %collective-permute-start.19 = (bf16[128,1024]{1,0:T(8,128)(2,1)S(1)}, bf16[128,1024]{1,0:T(8,128)(2,1)S(1)}, u32[]{:S(2)}, u32[]{:S(2)}) collective-permute-start(bf16[128,1024]{1,0:T(8,128)(2,1)S(1)} %get-tuple-element.44), channel_id=1, source_target_pairs={{0,4},{2,6},{4,0},{6,2},{1,5},{3,7},{5,1},{7,3},{8,12},{10,14},{12... | collective-permute-start | bytes 786440 | tf_op jit(solution)/shard_map/ppermute | solution.py:247
  207.5 25.4 %collective-permute-start.20 = (bf16[128,1024]{1,0:T(8,128)(2,1)S(1)}, bf16[128,1024]{1,0:T(8,128)(2,1)S(1)}, u32[]{:S(2)}, u32[]{:S(2)}) collective-permute-start(bf16[128,1024]{1,0:T(8,128)(2,1)S(1)} %get-tuple-element.45), channel_id=1, source_target_pairs={{0,6},{2,4},{4,2},{6,0},{1,7},{3,5},{5,3},{7,1},{8,14},{10,12},{12... | collective-permute-start | bytes 786440 | tf_op jit(solution)/shard_map/ppermute | solution.py:247
  213.4 44.9 %collective-permute-start.11 = (bf16[256,768]{1,0:T(8,128)(2,1)S(1)}, bf16[256,768]{1,0:T(8,128)(2,1)S(1)}, u32[]{:S(2)}, u32[]{:S(2)}) collective-permute-start(bf16[256,768]{1,0:T(8,128)(2,1)S(1)} %get-tuple-element.38), channel_id=1, source_target_pairs={{0,64},{64,0},{1,65},{65,1},{2,66},{66,2},{3,67},{67,3},{4,68},{68... | collective-permute-start | bytes 1179656 | tf_op jit(solution)/shard_map/ppermute | solution.py:28
  233.2 16.7 %collective-permute-start.21 = (bf16[128,512]{1,0:T(8,128)(2,1)S(1)}, bf16[128,512]{1,0:T(8,128)(2,1)S(1)}, u32[]{:S(2)}, u32[]{:S(2)}) collective-permute-start(bf16[128,512]{1,0:T(8,128)(2,1)S(1)} %fusion.14), channel_id=1, source_target_pairs={{0,2},{2,0},{4,6},{6,4},{1,3},{3,1},{5,7},{7,5},{8,10},{10,8},{12,... | collective-permute-start | bytes 393224 | tf_op jit(solution)/shard_map/ppermute | solution.py:252
  235.1 17.3 %collective-permute-start.22 = (bf16[128,512]{1,0:T(8,128)(2,1)S(1)}, bf16[128,512]{1,0:T(8,128)(2,1)S(1)}, u32[]{:S(2)}, u32[]{:S(2)}) collective-permute-start(bf16[128,512]{1,0:T(8,128)(2,1)S(1)} %fusion.14), channel_id=1, source_target_pairs={{0,4},{2,6},{4,0},{6,2},{1,5},{3,7},{5,1},{7,3},{8,12},{10,14},{12... | collective-permute-start | bytes 393224 | tf_op jit(solution)/shard_map/ppermute | solution.py:252
  238.4 18.0 %collective-permute-start.23 = (bf16[128,512]{1,0:T(8,128)(2,1)S(1)}, bf16[128,512]{1,0:T(8,128)(2,1)S(1)}, u32[]{:S(2)}, u32[]{:S(2)}) collective-permute-start(bf16[128,512]{1,0:T(8,128)(2,1)S(1)} %fusion.14), channel_id=1, source_target_pairs={{0,6},{2,4},{4,2},{6,0},{1,7},{3,5},{5,3},{7,1},{8,14},{10,12},{12... | collective-permute-start | bytes 393224 | tf_op jit(solution)/shard_map/ppermute | solution.py:252
  249.9 20.2 %collective-permute-start.30 = (bf16[128,1024]{1,0:T(8,128)(2,1)}, bf16[128,1024]{1,0:T(8,128)(2,1)}, u32[]{:S(2)}, u32[]{:S(2)}) collective-permute-start(bf16[128,1024]{1,0:T(8,128)(2,1)} %get-tuple-element.51), channel_id=1, source_target_pairs={{0,4},{2,6},{4,0},{6,2},{1,5},{3,7},{5,1},{7,3},{8,12},{10,14},{12... | collective-permute-start | bytes 786440 | tf_op jit(solution)/shard_map/ppermute | solution.py:247
  252.4 23.6 %collective-permute-start.31 = (bf16[128,1024]{1,0:T(8,128)(2,1)}, bf16[128,1024]{1,0:T(8,128)(2,1)}, u32[]{:S(2)}, u32[]{:S(2)}) collective-permute-start(bf16[128,1024]{1,0:T(8,128)(2,1)} %get-tuple-element.52), channel_id=1, source_target_pairs={{0,6},{2,4},{4,2},{6,0},{1,7},{3,5},{5,3},{7,1},{8,14},{10,12},{12... | collective-permute-start | bytes 786440 | tf_op jit(solution)/shard_map/ppermute | solution.py:247
  256.4 20.9 %collective-permute-start.24 = (bf16[512,512]{1,0:T(8,128)(2,1)S(1)}, bf16[512,512]{1,0:T(8,128)(2,1)S(1)}, u32[]{:S(2)}, u32[]{:S(2)}) collective-permute-start(bf16[512,512]{1,0:T(8,128)(2,1)S(1)} %pad_maximum_fusion.3.h_ref), channel_id=1, source_target_pairs={{0,1},{1,0},{2,3},{3,2},{4,5},{5,4},{6,7},{7,6},{8,9},{9,8},{10,11... | collective-permute-start | bytes 1572872 | tf_op jit(solution)/shard_map/ppermute | solution.py:28
  259.2 44.6 %all-to-all-start.2 = ((bf16[8,32,768]{2,1,0:T(8,128)(2,1)}), bf16[8,32,768]{2,1,0:T(8,128)(2,1)}, u32[]{:S(2)}, u32[]{:S(2)}) async-start(bf16[8,32,768]{2,1,0:T(8,128)(2,1)} %bitcast.105), calls=%async_computation.2 | async-start | bytes 786432 | tf_op jit(solution)/shard_map/all_to_all | solution.py:260
  280.3 22.6 %collective-permute-start.25 = (bf16[256,768]{1,0:T(8,128)(2,1)S(1)}, bf16[256,768]{1,0:T(8,128)(2,1)S(1)}, u32[]{:S(2)}, u32[]{:S(2)}) collective-permute-start(bf16[256,768]{1,0:T(8,128)(2,1)S(1)} %get-tuple-element.47), channel_id=1, source_target_pairs={{0,64},{64,0},{1,65},{65,1},{2,66},{66,2},{3,67},{67,3},{4,68},{68... | collective-permute-start | bytes 1179656 | tf_op jit(solution)/shard_map/ppermute | solution.py:28
  303.8 19.0 %all-to-all-start.4 = ((bf16[8,32,768]{2,1,0:T(8,128)(2,1)}), bf16[8,32,768]{2,1,0:T(8,128)(2,1)S(1)}, u32[]{:S(2)}, u32[]{:S(2)}) async-start(bf16[8,32,768]{2,1,0:T(8,128)(2,1)} %bitcast.110), calls=%async_computation.4 | async-start | bytes 786432 | tf_op jit(solution)/shard_map/all_to_all | solution.py:260
  322.8 33.1 %all-to-all-start.5 = ((bf16[64,8,768]{2,1,0:T(8,128)(2,1)}), bf16[64,8,768]{2,1,0:T(8,128)(2,1)S(1)}, u32[]{:S(2)}, u32[]{:S(2)}) async-start(bf16[64,8,768]{2,1,0:T(8,128)(2,1)} %bitcast.48), calls=%async_computation.5 | async-start | bytes 1572864 | tf_op jit(solution)/shard_map/all_to_all | solution.py:267
  333.6 17.2 %collective-permute-start.27 = (bf16[16,768]{1,0:T(8,128)(2,1)S(1)}, bf16[16,768]{1,0:T(8,128)(2,1)S(1)}, u32[]{:S(2)}, u32[]{:S(2)}) collective-permute-start(bf16[16,768]{1,0:T(8,128)(2,1)S(1)} %get-tuple-element.64), channel_id=1, source_target_pairs={{0,256},{128,384},{256,0},{384,128},{1,257},{129,385},{257,1},{385... | collective-permute-start | bytes 73736 | tf_op jit(solution)/shard_map/ppermute | solution.py:180
  (30 other events, 501.1 us)

commit v4 on v3

--- a/solution.py
+++ b/solution.py
@@ -12,7 +12,6 @@
 HD = 128
 EXPERTS = 4
 CAP = 24
-SLOT = 8
 F32 = jnp.float32
 BF16 = jnp.bfloat16
 
@@ -20,6 +19,7 @@
 EXP = ("yl", "c")
 HALF = ("xh", "xl", "z")
 GROUP = ("yh", "xh")
+ROUTE = ("yh", "xh", "z")
 SWAP = [(0, 1), (1, 0)]
 Y_XOR = [[(i, i ^ k) for i in range(4)] for k in range(4)]
 
@@ -101,10 +101,12 @@
         ref[...] = acc_ref[pl.ds(at, share), :].astype(BF16)
 
 
-def gate_up_terms(order, near, far, near_other, far_other, specs, w, wo, rows):
+def gate_up_terms(order, near, far, near_other, far_other, w, wo, block, chunk):
     hidden, feat = w.shape
     cols = hidden // 2
+    rows = 2 * near.shape[0] * block
     share = rows // 4
+    x = pl.BlockSpec((near.shape[0], block, feat), lambda n, o: (0, chunk, 0))
     weight = pl.BlockSpec((cols, feat), lambda n, o: (n, 0))
     out = pl.BlockSpec((share, cols), lambda n, o: (0, n))
     shape = jax.ShapeDtypeStruct((share, hidden), BF16)
@@ -113,7 +115,7 @@
         grid_spec=pltpu.PrefetchScalarGridSpec(
             num_scalar_prefetch=1,
             grid=(2,),
-            in_specs=[specs[0], specs[1], specs[0], specs[1], weight, weight],
+            in_specs=[x, x, x, x, weight, weight],
             out_specs=[out] * 4,
             scratch_shapes=[pltpu.VMEM((rows, cols), F32)],
         ),
@@ -170,16 +172,14 @@
     return lax.optimization_barrier((value,) + others)[0]
 
 
-def exchange(blocks, axes):
-    me = lax.axis_index(axes)
-    xor = [[(i, i ^ k) for i in range(4)] for k in range(4)]
-    got = jnp.zeros_like(blocks)
-    for k in range(4):
-        block = lax.dynamic_index_in_dim(blocks, me ^ k, 0, keepdims=False)
-        if k:
-            block = lax.ppermute(block, axes, xor[k])
-        got = lax.dynamic_update_index_in_dim(got, block, me ^ k, 0)
-    return got
+def as_rows(v, feat):
+    row = jnp.concatenate(split3(v), axis=-1)
+    return jnp.pad(row[..., None, :], [(0, 0)] * (v.ndim - 1) + [(0, 7), (0, feat - row.shape[-1])])
+
+
+def from_row(row, n):
+    hi, mid, lo = (row[..., k * n : (k + 1) * n].astype(F32) for k in range(3))
+    return hi + mid + lo
 
 
 def body(queries, keys, values, residual, norm_gain, routes, route_weight, w_gate, w_up, w_down):
@@ -187,8 +187,7 @@
     half = w_gate.shape[0] // 2
     core = lax.axis_index("c")
     me = lax.axis_index("yl")
-    xl = lax.axis_index("xl")
-    order = jnp.stack([me, core, xl]).astype(jnp.int32)
+    order = jnp.stack([me, core]).astype(jnp.int32)
 
     def halves(which):
         cut = partial(lax.dynamic_slice_in_dim, start_index=which * half, slice_size=half, axis=0)
@@ -196,78 +195,109 @@
 
     w_in = halves(core)
     w_in_other = swap(halves(1 - core), "c")
-
-    attn, (w_in, w_in_other) = attend(queries, keys, values, (w_in, w_in_other))
-    mixed = residual.astype(F32) + attn.astype(F32)
-    total_squares = lax.psum(jnp.sum(mixed * mixed, axis=1), EXP)
-    normed = (mixed * lax.rsqrt(total_squares / D + 1e-05)[:, None] * norm_gain[None, :]).astype(BF16)
 
     chosen = routes[:, 0]
     expert_ids = jnp.arange(EXPERTS, dtype=jnp.int32)
     onehot = (chosen[:, None] == expert_ids[None, :]).astype(jnp.int32)
     slot_index = jnp.sum((jnp.cumsum(onehot, axis=0) - 1) * onehot, axis=1)
     slot_ids = jnp.arange(CAP, dtype=jnp.int32)
-    select = (
-        (chosen[None, None, :] == expert_ids[:, None, None])
-        & (slot_index[None, None, :] == slot_ids[None, :, None])
+    taken = (chosen[None, None, :] == expert_ids[:, None, None]) & (
+        slot_index[None, None, :] == slot_ids[None, :, None]
+    )
+    select = taken.astype(BF16)
+
+    attn, (w_in, w_in_other) = attend(queries, keys, values, (w_in, w_in_other))
+    mixed = residual.astype(F32) + attn.astype(F32)
+    squares = jnp.sum(mixed * mixed, axis=1)
+    packed = jnp.einsum(
+        "ect,td->ecd", select, (mixed * norm_gain[None, :]).astype(BF16), preferred_element_type=F32
     ).astype(BF16)
-    packed = jnp.einsum("ect,td->ecd", select, normed, preferred_element_type=F32).astype(BF16)
-
-    nx = lax.axis_size("xl")
+
     nz = lax.axis_size("z")
-    n = SLOT
+    n = CAP // 3
     group = EXPERTS * n
-    rows = nx * nz * group
-
-    direct = jnp.broadcast_to(packed[:, None, :n], (EXPERTS, nx * nz, n, feat)).reshape(-1, n, feat)
-    x_a = lax.all_to_all(direct, CTX, split_axis=0, concat_axis=0, tiled=True).reshape(EXPERTS, nx, nz * n, feat)
-    rest = exchange(packed[:, n:], GROUP).reshape(EXPERTS, 2, n, feat).transpose(1, 0, 2, 3).reshape(2 * group, feat)
-    rest = after(rest, x_a)
-    near = lax.all_to_all(
-        jnp.broadcast_to(rest[None], (nz, 2 * group, feat)), "z", split_axis=0, concat_axis=0, tiled=True
-    ).reshape(nz, 2, group, feat)
-    x_a_other = swap(x_a, "c")
-    a_block = (EXPERTS, pl.Squeezed(), nz * n, feat)
-    specs_a = (
-        pl.BlockSpec(a_block, lambda k, o: (0, o[2], 0, 0)),
-        pl.BlockSpec(a_block, lambda k, o: (0, 1 - o[2], 0, 0)),
+    rows = nz * group
+
+    def all_to_all(x, axes):
+        return lax.all_to_all(x, axes, split_axis=0, concat_axis=0, tiled=True)
+
+    x_a = jnp.broadcast_to(packed[:, None, :n], (EXPERTS, nz, n, feat)).reshape(-1, n, feat)
+    x_a = all_to_all(x_a, ROUTE)
+    inverse = lax.rsqrt(lax.psum(squares, EXP) / D + 1e-05)
+    inverse = jnp.sum(jnp.where(taken, inverse[None, None, :], 0.0), axis=2)
+    x_a, inverse = lax.optimization_barrier((x_a, inverse))
+    x_a = x_a.reshape(EXPERTS, nz * n, feat)
+    far_a = swap(x_a, "xl")
+    rest = all_to_all(jnp.concatenate([packed[:, n:], as_rows(inverse, feat)], axis=1), GROUP)
+    terms_a = gate_up_terms(order, x_a, far_a, swap(x_a, "c"), swap(far_a, "c"), w_in, w_in_other, nz * n, 0)
+    rest = after(rest, *terms_a)
+    inverse = from_row(rest[:, 2 * n], CAP).reshape(EXPERTS, 3, n).transpose(1, 0, 2).reshape(3 * group)
+    near = jnp.concatenate(
+        [rest[:, :n].reshape(group, feat), rest[:, n : 2 * n].reshape(group, feat), as_rows(inverse, feat)], axis=0
     )
-    terms = [gate_up_terms(order, x_a, x_a, x_a_other, x_a_other, specs_a, w_in, w_in_other, rows)]
-    near = after(near, *terms[0])
+    near = all_to_all(jnp.broadcast_to(near[None], (nz,) + near.shape), "z").reshape((nz,) + near.shape)
+
+    def over_yl(parts):
+        return [parts[0]] + [lax.ppermute(parts[i], "yl", Y_XOR[i]) for i in range(1, 4)]
+
+    def hidden_of(parts, inverse):
+        full = sum(p.astype(F32) for p in parts) * inverse[:, None]
+        return (jax.nn.silu(full[:, :half]) * full[:, half:]).astype(BF16)
+
+    def to_xl(down):
+        return down[0], swap(down[1], "xl")
+
+    def total(stay, came):
+        return (stay.astype(F32) + came.astype(F32)).astype(BF16)
+
+    sums_a = over_yl(terms_a)
+    near = after(near, *sums_a[1:])
+    tail = near[:, 2 * group :, : 9 * group + 96]
+    tails = (tail, swap(tail, "xl"))
+    inverse = jnp.stack([from_row(t[:, 0], 3 * group).reshape(nz, 3, EXPERTS, n) for t in tails])
+    inverse_a = inverse[:, :, 0].transpose(0, 2, 1, 3).reshape(4, rows // 2)
+    inverse_bc = inverse[:, :, 1:].transpose(2, 0, 1, 3, 4).reshape(2, 4, rows // 2)
+
+    def own(v):
+        return lax.dynamic_index_in_dim(v, me, 0, keepdims=False)
+
     far = swap(near, "xl")
-    near_other, far_other = swap(near, "c"), swap(far, "c")
-    for chunk in range(2):
-        spec = pl.BlockSpec((nz, pl.Squeezed(), group, feat), lambda k, o, chunk=chunk: (0, chunk, 0, 0))
-        first = after(far_other, *terms[-1])
-        terms.append(gate_up_terms(order, near, far, near_other, first, (spec, spec), w_in, w_in_other, rows))
-
-    def hidden_of(parts):
-        full = parts[0].astype(F32)
-        for i in range(1, 4):
-            full = full + lax.ppermute(parts[i], "yl", Y_XOR[i]).astype(F32)
-        return (jax.nn.silu(full[:, :half]) * full[:, half:]).astype(BF16)
-
-    def down_of(parts):
-        hidden = hidden_of(parts)
-        hid = jnp.concatenate([hidden] + [lax.ppermute(hidden, "yl", Y_XOR[i]) for i in range(1, 4)], axis=0)
-        return down_terms(order, hid, swap(hid, "c"), w_down)
-
-    def gather_z(down, dims):
-        stay, leave = down
-        summed = (stay.astype(F32) + swap(leave, "xl").astype(F32)).astype(BF16)
-        if dims == "ez":
-            summed = summed.reshape(EXPERTS, nz, group // EXPERTS, feat).transpose(1, 0, 2, 3)
-        back = lax.all_to_all(summed.reshape(nz, group, feat), "z", split_axis=0, concat_axis=0, tiled=True)
-        return jnp.sum(back.astype(F32), axis=0).astype(BF16).reshape(EXPERTS, n, feat)
-
-    out_a = gather_z(down_of(terms[0]), "ez")
-    out_b = gather_z(down_of(terms[1]), "ze")
-    stay, leave = (d.reshape(nz, EXPERTS, n, feat).transpose(1, 0, 2, 3) for d in down_of(terms[2]))
-    direct = jnp.where(xl == 0, jnp.stack([stay, leave], axis=1), jnp.stack([leave, stay], axis=1))
-    out_c = lax.all_to_all(direct.reshape(-1, n, feat), CTX, split_axis=0, concat_axis=0, tiled=True)
-    out_c = jnp.sum(out_c.reshape(EXPERTS, nx * nz, n, feat).astype(F32), axis=1).astype(BF16)
-    out_ab = exchange(jnp.concatenate([out_a, out_b], axis=1), GROUP)
-    returned = jnp.concatenate([out_ab, out_c], axis=1)
+    near_other = swap(near, "c")
+    hidden_a = over_yl([hidden_of(sums_a, own(inverse_a))] * 4)
+    far = after(far, *hidden_a)
+    far_other = swap(far, "c")
+    terms_b = gate_up_terms(order, near, far, near_other, far_other, w_in, w_in_other, group, 0)
+    hid = jnp.concatenate(hidden_a, axis=0)
+    down_a = down_terms(order, hid, swap(hid, "c"), w_down)
+    stay_a, came_a = to_xl(down_a)
+    sums_b = over_yl(terms_b)
+    terms_c = gate_up_terms(
+        order, near, far, near_other, after(far_other, *terms_b), w_in, w_in_other, group, 1
+    )
+    sums_b[1] = after(sums_b[1], *down_a)
+    came_a = after(came_a, *sums_b[1:])
+    back_a = all_to_all(total(stay_a, came_a).reshape(-1, n, feat), ROUTE)
+    hidden_b = over_yl([hidden_of(sums_b, own(inverse_bc[0]))] * 4)
+    sums_c = over_yl(terms_c)
+    hid = jnp.concatenate(hidden_b, axis=0)
+    down_b = down_terms(order, hid, swap(hid, "c"), w_down)
+    stay_b, came_b = to_xl(down_b)
+    back_a = after(back_a, *sums_c[1:])
+    hidden_c = over_yl([hidden_of(sums_c, own(inverse_bc[1]))] * 4)
+    hid = jnp.concatenate(hidden_c, axis=0)
+    came_b = after(came_b, hid)
+    down_c = down_terms(order, hid, swap(hid, "c"), w_down)
+
+    def give_back(stay, came):
+        both = total(stay, came).reshape(nz, EXPERTS, n, feat).transpose(1, 0, 2, 3).reshape(-1, n, feat)
+        return all_to_all(both, ROUTE)
+
+    def over_z(back):
+        return jnp.sum(back.reshape(EXPERTS, nz, n, feat).astype(F32), axis=1).astype(BF16)
+
+    back_b = give_back(stay_b, came_b)
+    back_c = give_back(*to_xl(down_c))
+    returned = jnp.concatenate([over_z(back_a), over_z(after(back_b, down_c[0])), over_z(back_c)], axis=1)
     moe_rows = jnp.einsum("ect,ecd->td", select, returned, preferred_element_type=F32)
     return (route_weight[:, None] * moe_rows).astype(BF16)
 

time: 360 us -> 387 us (1.075)
  local copies, waits for them, and re-layouts: 13.3 us -> 22.1 us
  waiting for transfers between devices: 135 us -> 142 us
  starting transfers between devices: 160 us -> 166 us
  blocking collectives: 10 us -> 13.9 us
    ppermute x10 -> x14, waiting for transfers between devices: 10.5 us -> 39.1 us  [swap(): return lax.ppermute(x, axis, SWAP)]
    ppermute x24 -> x18, starting transfers between devices: 84.8 us -> 57.6 us  [over_yl(): lax.ppermute(parts[i], 'yl', Y_XOR[i])]
    all_to_all x5 -> x6, starting transfers between devices: 29.3 us -> 55.6 us  [all_to_all(): return lax.all_to_all(x, axes, split_axis=0, concat_axis=0, tiled=True)]
    ppermute x24 -> x18, waiting for transfers between devices: 75.8 us -> 51.3 us  [over_yl(): lax.ppermute(parts[i], 'yl', Y_XOR[i])]
    ppermute x10 -> x14, starting transfers between devices: 23.4 us -> 30.9 us  [swap(): return lax.ppermute(x, axis, SWAP)]
    unnamed x25 -> x45, local copies, waits for them, and re-layouts: 4.18 us -> 8.35 us
    psum x1, blocking collectives: 10 us -> 13.9 us  [body(): inverse = lax.rsqrt(lax.psum(squares, EXP) / D + 1e-05)]
    all_to_all x5 -> x6, waiting for transfers between devices: 28.5 us -> 31.5 us  [all_to_all(): return lax.all_to_all(x, axes, split_axis=0, concat_axis=0, tiled=True)]
  transfers between devices with their start and end apart: 42 -> 41, of which waited for: 23 -> 20; matrix products, arithmetic and copies ran while one was open for 4% -> 5% of each run, Pallas kernels for 5% -> 5%
where the time goes in v4:
time: 387 us; the launch traced here: 385 us
  starting transfers between devices  166 us (43%)
  waiting for transfers between devices  142 us (37%)
  local copies, waits for them, and re-layouts  22.1 us (6%)
  Pallas kernels  18.3 us (5%)
  other arithmetic  14.8 us (4%)
  blocking collectives  13.9 us (4%)
  matrix products  6.26 us (2%)
    ppermute x18, starting transfers between devices, over_yl(): lax.ppermute(parts[i], 'yl', Y_XOR[i])  57.6 us
    all_to_all x6, starting transfers between devices, all_to_all(): return lax.all_to_all(x, axes, split_axis=0, concat_axis=0, tiled=True)  55.6 us
    ppermute x18, waiting for transfers between devices, over_yl(): lax.ppermute(parts[i], 'yl', Y_XOR[i])  51.3 us
    ppermute x14, waiting for transfers between devices, swap(): return lax.ppermute(x, axis, SWAP)  39.1 us
    all_to_all x6, waiting for transfers between devices, all_to_all(): return lax.all_to_all(x, axes, split_axis=0, concat_axis=0, tiled=True)  31.5 us
    ppermute x14, starting transfers between devices, swap(): return lax.ppermute(x, axis, SWAP)  30.9 us
    psum x1, blocking collectives, body(): inverse = lax.rsqrt(lax.psum(squares, EXP) / D + 1e-05)  13.9 us
    all_to_all x1, starting transfers between devices, attend(): lax.all_to_all(jnp.broadcast_to(kv[None], (members,) + kv.shape), HALF, s...  13.4 us
  transfers between devices with their start and end apart: 41, of which 20 were waited for; matrix products, arithmetic and copies ran while one was open for 5% of the time, Pallas kernels for 5%

profile of v4, /device:TPU:8, one launch (start us, length us, event | category | flops | bytes accessed | tf_op | source)
XLA Modules:
  0.0 385.2 jit_solution(13224181828729199236)
XLA Ops:
  1.8 13.4 %all-to-all-start = ((bf16[32,64,256]{2,1,0:T(8,128)(2,1)}), bf16[32,64,256]{2,1,0:T(8,128)(2,1)}, u32[]{:S(2)}, u32[]{:S(2)}) async-start(bf16[32,64,256]{2,1,0:T(8,128)(2,1)} %broadcast_in_dim.32), calls=%async_computation | async-start | bytes 2097152 | tf_op jit(solution)/shard_map/all_to_all | solution.py:47
  25.1 7.6 %collective-permute-done = bf16[64,768]{1,0:T(8,128)(2,1)S(1)} collective-permute-done((bf16[64,768]{1,0:T(8,128)(2,1)S(1)}, bf16[64,768]{1,0:T(8,128)(2,1)S(1)}, u32[]{:S(2)}, u32[]{:S(2)}) %collective-permute-start) | collective-permute-done | bytes 98336 | tf_op jit(solution)/shard_map/ppermute | solution.py:44
  32.9 11.0 %all-to-all-done = bf16[32,64,256]{2,1,0:T(8,128)(2,1)} async-done(((bf16[32,64,256]{2,1,0:T(8,128)(2,1)}), bf16[32,64,256]{2,1,0:T(8,128)(2,1)}, u32[]{:S(2)}, u32[]{:S(2)}) %all-to-all-start) | async-done | bytes 1048608 | tf_op jit(solution)/shard_map/all_to_all | solution.py:47
  52.9 7.5 %collective-permute-start.2 = (bf16[64,896]{1,0:T(8,128)(2,1)}, bf16[64,896]{1,0:T(8,128)(2,1)}, u32[]{:S(2)}, u32[]{:S(2)}) collective-permute-start(bf16[64,896]{1,0:T(8,128)(2,1)} %fusion.32), channel_id=1, source_target_pairs={{0,256},{1,257},{2,258},{3,259},{4,260},{5,261},{6,262},{7,263},{8... | collective-permute-start | bytes 344072 | tf_op jit(solution)/shard_map/ppermute | solution.py:80
  67.3 11.7 %all-to-all-start.1 = ((bf16[32,8,768]{2,1,0:T(8,128)(2,1)}), bf16[32,8,768]{2,1,0:T(8,128)(2,1)S(1)}, u32[]{:S(2)}, u32[]{:S(2)}) async-start(bf16[32,8,768]{2,1,0:T(8,128)(2,1)} %bitcast.107), calls=%async_computation.1 | async-start | bytes 786432 | tf_op jit(solution)/shard_map/all_to_all | solution.py:222
  79.0 13.9 %psum.7 = f32[64]{0:T(128)S(1)} all-reduce(f32[64]{0:T(128)S(1)} %get-tuple-element.69), channel_id=1, replica_groups=mesh['yh'=2,'xh'=2,'xl'=2,'z'=8,'yl'=4,'c'=2] {'yl','c'}, use_global_device_ids=true, to_apply=%region_5.6 | all-reduce | flops 64 | bytes 512 | tf_op jit(solution)/shard_map/psum | solution.py:226
  93.0 4.6 %all-to-all-done.1 = bf16[32,8,768]{2,1,0:T(8,128)(2,1)S(1)} async-done(((bf16[32,8,768]{2,1,0:T(8,128)(2,1)}), bf16[32,8,768]{2,1,0:T(8,128)(2,1)S(1)}, u32[]{:S(2)}, u32[]{:S(2)}) %all-to-all-start.1) | async-done | bytes 393248 | tf_op jit(solution)/shard_map/all_to_all | solution.py:222
  102.8 7.5 %collective-permute-done.3.xf_ref = bf16[4,64,768]{2,1,0:T(8,128)(2,1)} collective-permute-done((bf16[4,64,768]{2,1,0:T(8,128)(2,1)S(1)}, bf16[4,64,768]{2,1,0:T(8,128)(2,1)}, u32[]{:S(2)}, u32[]{:S(2)}) %collective-permute-start.3) | collective-permute-done | bytes 393248 | tf_op jit(solution)/shard_map/ppermute | solution.py:28
  123.8 5.5 %all-to-all-done.2 = bf16[4,24,768]{2,1,0:T(8,128)(2,1)} async-done(((bf16[4,24,768]{2,1,0:T(8,128)(2,1)}), bf16[4,24,768]{2,1,0:T(8,128)(2,1)}, u32[]{:S(2)}, u32[]{:S(2)}) %all-to-all-start.2) | async-done | bytes 147488 | tf_op jit(solution)/shard_map/all_to_all | solution.py:222
  136.3 6.0 %collective-permute-start.6 = (bf16[128,1024]{1,0:T(8,128)(2,1)}, bf16[128,1024]{1,0:T(8,128)(2,1)S(1)}, u32[]{:S(2)}, u32[]{:S(2)}) collective-permute-start(bf16[128,1024]{1,0:T(8,128)(2,1)} %copy-done.9), channel_id=1, source_target_pairs={{0,2},{2,0},{4,6},{6,4},{1,3},{3,1},{5,7},{7,5},{8,10},{10,8},{12,... | collective-permute-start | bytes 786440 | tf_op jit(solution)/shard_map/ppermute | solution.py:241
  149.7 12.4 %collective-permute-done.7 = bf16[128,1024]{1,0:T(8,128)(2,1)S(1)} collective-permute-done((bf16[128,1024]{1,0:T(8,128)(2,1)}, bf16[128,1024]{1,0:T(8,128)(2,1)S(1)}, u32[]{:S(2)}, u32[]{:S(2)}) %collective-permute-start.7) | collective-permute-done | bytes 262176 | tf_op jit(solution)/shard_map/ppermute | solution.py:241
  162.1 5.6 %collective-permute-done.8 = bf16[128,1024]{1,0:T(8,128)(2,1)S(1)} collective-permute-done((bf16[128,1024]{1,0:T(8,128)(2,1)}, bf16[128,1024]{1,0:T(8,128)(2,1)S(1)}, u32[]{:S(2)}, u32[]{:S(2)}) %collective-permute-start.8) | collective-permute-done | bytes 262176 | tf_op jit(solution)/shard_map/ppermute | solution.py:241
  174.5 17.4 %collective-permute-done.9 = bf16[8,8,384]{2,1,0:T(8,128)(2,1)} collective-permute-done((bf16[8,8,384]{2,1,0:T(8,128)(2,1)S(1)}, bf16[8,8,384]{2,1,0:T(8,128)(2,1)}, u32[]{:S(2)}, u32[]{:S(2)}) %collective-permute-start.9) | collective-permute-done | bytes 49184 | tf_op jit(solution)/shard_map/ppermute | solution.py:28
  235.9 9.9 %collective-permute-done.19 = bf16[128,1024]{1,0:T(8,128)(2,1)S(1)} collective-permute-done((bf16[128,1024]{1,0:T(8,128)(2,1)S(1)}, bf16[128,1024]{1,0:T(8,128)(2,1)S(1)}, u32[]{:S(2)}, u32[]{:S(2)}) %collective-permute-start.19) | collective-permute-done | bytes 262176 | tf_op jit(solution)/shard_map/ppermute | solution.py:241
  245.8 6.1 %collective-permute-done.20 = bf16[128,1024]{1,0:T(8,128)(2,1)S(1)} collective-permute-done((bf16[128,1024]{1,0:T(8,128)(2,1)S(1)}, bf16[128,1024]{1,0:T(8,128)(2,1)S(1)}, u32[]{:S(2)}, u32[]{:S(2)}) %collective-permute-start.20) | collective-permute-done | bytes 262176 | tf_op jit(solution)/shard_map/ppermute | solution.py:241
  261.3 4.7 %gate_up_terms.5 = (bf16[128,1024]{1,0:T(8,128)(2,1)S(1)}, bf16[128,1024]{1,0:T(8,128)(2,1)}, bf16[128,1024]{1,0:T(8,128)(2,1)}, bf16[128,1024]{1,0:T(8,128)(2,1)}) custom-call(s32[2]{0:T(128)S(1)} %pad_add_fusion.order_ref, bf16[8,72,768]{2,1,0:T(8,128)(2,1)S(1)} %all-to-all-done.3.xn_ref, bf16[8,72,768]{2,1,0:T(8,128)(2,1)S(1)} %collective-permute-done.15.xf_ref, ...), custom_call_target="tpu_custom_call" | custom-call | flops 1610612736 | bytes 4194304 | tf_op jit(solution)/shard_map/gate_up_terms/pallas_call | solution.py:113
  279.0 12.3 %all-to-all-start.4 = ((bf16[32,8,768]{2,1,0:T(8,128)(2,1)}), bf16[32,8,768]{2,1,0:T(8,128)(2,1)S(1)}, u32[]{:S(2)}, u32[]{:S(2)}) async-start(bf16[32,8,768]{2,1,0:T(8,128)(2,1)} %fusion.13), calls=%async_computation.4 | async-start | bytes 786432 | tf_op jit(solution)/shard_map/all_to_all | solution.py:222
  291.3 9.8 %collective-permute-done.23 = bf16[128,1024]{1,0:T(8,128)(2,1)} collective-permute-done((bf16[128,1024]{1,0:T(8,128)(2,1)}, bf16[128,1024]{1,0:T(8,128)(2,1)}, u32[]{:S(2)}, u32[]{:S(2)}) %collective-permute-start.23) | collective-permute-done | bytes 262176 | tf_op jit(solution)/shard_map/ppermute | solution.py:241
  304.3 4.5 %collective-permute-start.30 = (bf16[128,512]{1,0:T(8,128)(2,1)S(1)}, bf16[128,512]{1,0:T(8,128)(2,1)S(1)}, u32[]{:S(2)}, u32[]{:S(2)}) collective-permute-start(bf16[128,512]{1,0:T(8,128)(2,1)S(1)} %fusion.15), channel_id=1, source_target_pairs={{0,4},{2,6},{4,0},{6,2},{1,5},{3,7},{5,1},{7,3},{8,12},{10,14},{12... | collective-permute-start | bytes 393224 | tf_op jit(solution)/shard_map/ppermute | solution.py:241
  319.1 5.3 %collective-permute-done.28 = bf16[256,768]{1,0:T(8,128)(2,1)S(1)} collective-permute-done((bf16[256,768]{1,0:T(8,128)(2,1)S(1)}, bf16[256,768]{1,0:T(8,128)(2,1)S(1)}, u32[]{:S(2)}, u32[]{:S(2)}) %collective-permute-start.28) | collective-permute-done | bytes 393248 | tf_op jit(solution)/shard_map/ppermute | solution.py:28
  325.3 13.7 %all-to-all-start.5 = ((bf16[32,8,768]{2,1,0:T(8,128)(2,1)}), bf16[32,8,768]{2,1,0:T(8,128)(2,1)S(1)}, u32[]{:S(2)}, u32[]{:S(2)}) async-start(bf16[32,8,768]{2,1,0:T(8,128)(2,1)} %bitcast.106), calls=%async_computation.5 | async-start | bytes 786432 | tf_op jit(solution)/shard_map/all_to_all | solution.py:222
  343.0 9.0 %collective-permute-done.33 = bf16[256,768]{1,0:T(8,128)(2,1)S(1)} collective-permute-done((bf16[256,768]{1,0:T(8,128)(2,1)S(1)}, bf16[256,768]{1,0:T(8,128)(2,1)S(1)}, u32[]{:S(2)}, u32[]{:S(2)}) %collective-permute-start.33) | collective-permute-done | bytes 393248 | tf_op jit(solution)/shard_map/ppermute | solution.py:28
  356.6 9.8 %all-to-all-start.6 = ((bf16[32,8,768]{2,1,0:T(8,128)(2,1)}), bf16[32,8,768]{2,1,0:T(8,128)(2,1)S(1)}, u32[]{:S(2)}, u32[]{:S(2)}) async-start(bf16[32,8,768]{2,1,0:T(8,128)(2,1)} %bitcast.35), calls=%async_computation.6 | async-start | bytes 786432 | tf_op jit(solution)/shard_map/all_to_all | solution.py:222
  366.5 17.7 %all-to-all-done.6 = bf16[32,8,768]{2,1,0:T(8,128)(2,1)S(1)} async-done(((bf16[32,8,768]{2,1,0:T(8,128)(2,1)}), bf16[32,8,768]{2,1,0:T(8,128)(2,1)S(1)}, u32[]{:S(2)}, u32[]{:S(2)}) %all-to-all-start.6) | async-done | bytes 393248 | tf_op jit(solution)/shard_map/all_to_all | solution.py:222
  (205 shorter events, 157.3 us)
Async XLA Ops:
  1.8 42.0 %all-to-all-start = ((bf16[32,64,256]{2,1,0:T(8,128)(2,1)}), bf16[32,64,256]{2,1,0:T(8,128)(2,1)}, u32[]{:S(2)}, u32[]{:S(2)}) async-start(bf16[32,64,256]{2,1,0:T(8,128)(2,1)} %broadcast_in_dim.32), calls=%async_computation | async-start | bytes 2097152 | tf_op jit(solution)/shard_map/all_to_all | solution.py:47
  67.3 30.3 %all-to-all-start.1 = ((bf16[32,8,768]{2,1,0:T(8,128)(2,1)}), bf16[32,8,768]{2,1,0:T(8,128)(2,1)S(1)}, u32[]{:S(2)}, u32[]{:S(2)}) async-start(bf16[32,8,768]{2,1,0:T(8,128)(2,1)} %bitcast.107), calls=%async_computation.1 | async-start | bytes 786432 | tf_op jit(solution)/shard_map/all_to_all | solution.py:222
  100.8 16.1 %collective-permute-start.4 = (bf16[4,64,768]{2,1,0:T(8,128)(2,1)S(1)}, bf16[4,64,768]{2,1,0:T(8,128)(2,1)}, u32[]{:S(2)}, u32[]{:S(2)}) collective-permute-start(bf16[4,64,768]{2,1,0:T(8,128)(2,1)S(1)} %bitcast.104), channel_id=1, source_target_pairs={{0,1},{1,0},{2,3},{3,2},{4,5},{5,4},{6,7},{7,6},{8,9},{9,8},{10,11... | collective-permute-start | bytes 1179656 | tf_op jit(solution)/shard_map/ppermute | solution.py:28
  112.9 16.4 %all-to-all-start.2 = ((bf16[4,24,768]{2,1,0:T(8,128)(2,1)}), bf16[4,24,768]{2,1,0:T(8,128)(2,1)}, u32[]{:S(2)}, u32[]{:S(2)}) async-start(bf16[4,24,768]{2,1,0:T(8,128)(2,1)} %fusion.26), calls=%async_computation.2 | async-start | bytes 294912 | tf_op jit(solution)/shard_map/all_to_all | solution.py:222
  132.3 35.4 %all-to-all-start.3 = ((bf16[8,72,768]{2,1,0:T(8,128)(2,1)}), bf16[8,72,768]{2,1,0:T(8,128)(2,1)S(1)}, u32[]{:S(2)}, u32[]{:S(2)}) async-start(bf16[8,72,768]{2,1,0:T(8,128)(2,1)} %broadcast_in_dim.41), calls=%async_computation.3 | async-start | bytes 1769472 | tf_op jit(solution)/shard_map/all_to_all | solution.py:222
  142.3 19.8 %collective-permute-start.7 = (bf16[128,1024]{1,0:T(8,128)(2,1)}, bf16[128,1024]{1,0:T(8,128)(2,1)S(1)}, u32[]{:S(2)}, u32[]{:S(2)}) collective-permute-start(bf16[128,1024]{1,0:T(8,128)(2,1)} %copy-done.8), channel_id=1, source_target_pairs={{0,4},{2,6},{4,0},{6,2},{1,5},{3,7},{5,1},{7,3},{8,12},{10,14},{12... | collective-permute-start | bytes 786440 | tf_op jit(solution)/shard_map/ppermute | solution.py:241
  144.2 23.5 %collective-permute-start.8 = (bf16[128,1024]{1,0:T(8,128)(2,1)}, bf16[128,1024]{1,0:T(8,128)(2,1)S(1)}, u32[]{:S(2)}, u32[]{:S(2)}) collective-permute-start(bf16[128,1024]{1,0:T(8,128)(2,1)} %copy-done.7), channel_id=1, source_target_pairs={{0,6},{2,4},{4,2},{6,0},{1,7},{3,5},{5,3},{7,1},{8,14},{10,12},{12... | collective-permute-start | bytes 786440 | tf_op jit(solution)/shard_map/ppermute | solution.py:241
  168.4 42.5 %collective-permute-start.15 = (bf16[8,72,768]{2,1,0:T(8,128)(2,1)S(1)}, bf16[8,72,768]{2,1,0:T(8,128)(2,1)S(1)}, u32[]{:S(2)}, u32[]{:S(2)}) collective-permute-start(bf16[8,72,768]{2,1,0:T(8,128)(2,1)S(1)} %all-to-all-done.3.xn_ref), channel_id=1, source_target_pairs={{0,64},{64,0},{1,65},{65,1},{2,66},{66,2},{3,67},{67,3},{4,68},{68... | collective-permute-start | bytes 2654216 | tf_op jit(solution)/shard_map/ppermute | solution.py:28
  170.8 21.1 %collective-permute-start.9 = (bf16[8,8,384]{2,1,0:T(8,128)(2,1)S(1)}, bf16[8,8,384]{2,1,0:T(8,128)(2,1)}, u32[]{:S(2)}, u32[]{:S(2)}) collective-permute-start(bf16[8,8,384]{2,1,0:T(8,128)(2,1)S(1)} %slice.151), channel_id=1, source_target_pairs={{0,64},{64,0},{1,65},{65,1},{2,66},{66,2},{3,67},{67,3},{4,68},{68... | collective-permute-start | bytes 147464 | tf_op jit(solution)/shard_map/ppermute | solution.py:28
  213.7 17.5 %collective-permute-start.13 = (bf16[512,512]{1,0:T(8,128)(2,1)}, bf16[512,512]{1,0:T(8,128)(2,1)}, u32[]{:S(2)}, u32[]{:S(2)}) collective-permute-start(bf16[512,512]{1,0:T(8,128)(2,1)} %pad_maximum_fusion.2.h_ref), channel_id=1, source_target_pairs={{0,1},{1,0},{2,3},{3,2},{4,5},{5,4},{6,7},{7,6},{8,9},{9,8},{10,11... | collective-permute-start | bytes 1572872 | tf_op jit(solution)/shard_map/ppermute | solution.py:28
  223.7 22.0 %collective-permute-start.19 = (bf16[128,1024]{1,0:T(8,128)(2,1)S(1)}, bf16[128,1024]{1,0:T(8,128)(2,1)S(1)}, u32[]{:S(2)}, u32[]{:S(2)}) collective-permute-start(bf16[128,1024]{1,0:T(8,128)(2,1)S(1)} %get-tuple-element.53), channel_id=1, source_target_pairs={{0,4},{2,6},{4,0},{6,2},{1,5},{3,7},{5,1},{7,3},{8,12},{10,14},{12... | collective-permute-start | bytes 786440 | tf_op jit(solution)/shard_map/ppermute | solution.py:241
  227.8 24.0 %collective-permute-start.20 = (bf16[128,1024]{1,0:T(8,128)(2,1)S(1)}, bf16[128,1024]{1,0:T(8,128)(2,1)S(1)}, u32[]{:S(2)}, u32[]{:S(2)}) collective-permute-start(bf16[128,1024]{1,0:T(8,128)(2,1)S(1)} %get-tuple-element.54), channel_id=1, source_target_pairs={{0,6},{2,4},{4,2},{6,0},{1,7},{3,5},{5,3},{7,1},{8,14},{10,12},{12... | collective-permute-start | bytes 786440 | tf_op jit(solution)/shard_map/ppermute | solution.py:241
  233.5 36.2 %collective-permute-start.14 = (bf16[256,768]{1,0:T(8,128)(2,1)S(1)}, bf16[256,768]{1,0:T(8,128)(2,1)S(1)}, u32[]{:S(2)}, u32[]{:S(2)}) collective-permute-start(bf16[256,768]{1,0:T(8,128)(2,1)S(1)} %get-tuple-element.49), channel_id=1, source_target_pairs={{0,64},{64,0},{1,65},{65,1},{2,66},{66,2},{3,67},{67,3},{4,68},{68... | collective-permute-start | bytes 1179656 | tf_op jit(solution)/shard_map/ppermute | solution.py:28
  252.1 20.9 %collective-permute-start.24 = (bf16[128,512]{1,0:T(8,128)(2,1)S(1)}, bf16[128,512]{1,0:T(8,128)(2,1)S(1)}, u32[]{:S(2)}, u32[]{:S(2)}) collective-permute-start(bf16[128,512]{1,0:T(8,128)(2,1)S(1)} %fusion.16), channel_id=1, source_target_pairs={{0,2},{2,0},{4,6},{6,4},{1,3},{3,1},{5,7},{7,5},{8,10},{10,8},{12,... | collective-permute-start | bytes 393224 | tf_op jit(solution)/shard_map/ppermute | solution.py:241
  254.0 22.1 %collective-permute-start.25 = (bf16[128,512]{1,0:T(8,128)(2,1)S(1)}, bf16[128,512]{1,0:T(8,128)(2,1)S(1)}, u32[]{:S(2)}, u32[]{:S(2)}) collective-permute-start(bf16[128,512]{1,0:T(8,128)(2,1)S(1)} %fusion.16), channel_id=1, source_target_pairs={{0,4},{2,6},{4,0},{6,2},{1,5},{3,7},{5,1},{7,3},{8,12},{10,14},{12... | collective-permute-start | bytes 393224 | tf_op jit(solution)/shard_map/ppermute | solution.py:241
  258.2 18.0 %collective-permute-start.26 = (bf16[128,512]{1,0:T(8,128)(2,1)S(1)}, bf16[128,512]{1,0:T(8,128)(2,1)S(1)}, u32[]{:S(2)}, u32[]{:S(2)}) collective-permute-start(bf16[128,512]{1,0:T(8,128)(2,1)S(1)} %fusion.16), channel_id=1, source_target_pairs={{0,6},{2,4},{4,2},{6,0},{1,7},{3,5},{5,3},{7,1},{8,14},{10,12},{12... | collective-permute-start | bytes 393224 | tf_op jit(solution)/shard_map/ppermute | solution.py:241
  266.8 24.6 %collective-permute-start.21 = (bf16[128,1024]{1,0:T(8,128)(2,1)}, bf16[128,1024]{1,0:T(8,128)(2,1)S(1)}, u32[]{:S(2)}, u32[]{:S(2)}) collective-permute-start(bf16[128,1024]{1,0:T(8,128)(2,1)} %get-tuple-element.58), channel_id=1, source_target_pairs={{0,2},{2,0},{4,6},{6,4},{1,3},{3,1},{5,7},{7,5},{8,10},{10,8},{12,... | collective-permute-start | bytes 786440 | tf_op jit(solution)/shard_map/ppermute | solution.py:241
  269.7 21.6 %collective-permute-start.22 = (bf16[128,1024]{1,0:T(8,128)(2,1)}, bf16[128,1024]{1,0:T(8,128)(2,1)S(1)}, u32[]{:S(2)}, u32[]{:S(2)}) collective-permute-start(bf16[128,1024]{1,0:T(8,128)(2,1)} %get-tuple-element.59), channel_id=1, source_target_pairs={{0,4},{2,6},{4,0},{6,2},{1,5},{3,7},{5,1},{7,3},{8,12},{10,14},{12... | collective-permute-start | bytes 786440 | tf_op jit(solution)/shard_map/ppermute | solution.py:241
  273.0 28.1 %collective-permute-start.23 = (bf16[128,1024]{1,0:T(8,128)(2,1)}, bf16[128,1024]{1,0:T(8,128)(2,1)}, u32[]{:S(2)}, u32[]{:S(2)}) collective-permute-start(bf16[128,1024]{1,0:T(8,128)(2,1)} %get-tuple-element.60), channel_id=1, source_target_pairs={{0,6},{2,4},{4,2},{6,0},{1,7},{3,5},{5,3},{7,1},{8,14},{10,12},{12... | collective-permute-start | bytes 786440 | tf_op jit(solution)/shard_map/ppermute | solution.py:241
  276.2 35.4 %collective-permute-start.27 = (bf16[512,512]{1,0:T(8,128)(2,1)S(1)}, bf16[512,512]{1,0:T(8,128)(2,1)S(1)}, u32[]{:S(2)}, u32[]{:S(2)}) collective-permute-start(bf16[512,512]{1,0:T(8,128)(2,1)S(1)} %pad_maximum_fusion.3.h_ref), channel_id=1, source_target_pairs={{0,1},{1,0},{2,3},{3,2},{4,5},{5,4},{6,7},{7,6},{8,9},{9,8},{10,11... | collective-permute-start | bytes 1572872 | tf_op jit(solution)/shard_map/ppermute | solution.py:28
  279.0 46.3 %all-to-all-start.4 = ((bf16[32,8,768]{2,1,0:T(8,128)(2,1)}), bf16[32,8,768]{2,1,0:T(8,128)(2,1)S(1)}, u32[]{:S(2)}, u32[]{:S(2)}) async-start(bf16[32,8,768]{2,1,0:T(8,128)(2,1)} %fusion.13), calls=%async_computation.4 | async-start | bytes 786432 | tf_op jit(solution)/shard_map/all_to_all | solution.py:222
  317.2 21.8 %collective-permute-start.32 = (bf16[512,512]{1,0:T(8,128)(2,1)S(1)}, bf16[512,512]{1,0:T(8,128)(2,1)S(1)}, u32[]{:S(2)}, u32[]{:S(2)}) collective-permute-start(bf16[512,512]{1,0:T(8,128)(2,1)S(1)} %pad_maximum_fusion.4.h_ref), channel_id=1, source_target_pairs={{0,1},{1,0},{2,3},{3,2},{4,5},{5,4},{6,7},{7,6},{8,9},{9,8},{10,11... | collective-permute-start | bytes 1572872 | tf_op jit(solution)/shard_map/ppermute | solution.py:28
  325.3 31.3 %all-to-all-start.5 = ((bf16[32,8,768]{2,1,0:T(8,128)(2,1)}), bf16[32,8,768]{2,1,0:T(8,128)(2,1)S(1)}, u32[]{:S(2)}, u32[]{:S(2)}) async-start(bf16[32,8,768]{2,1,0:T(8,128)(2,1)} %bitcast.106), calls=%async_computation.5 | async-start | bytes 786432 | tf_op jit(solution)/shard_map/all_to_all | solution.py:222
  356.6 27.6 %all-to-all-start.6 = ((bf16[32,8,768]{2,1,0:T(8,128)(2,1)}), bf16[32,8,768]{2,1,0:T(8,128)(2,1)S(1)}, u32[]{:S(2)}, u32[]{:S(2)}) async-start(bf16[32,8,768]{2,1,0:T(8,128)(2,1)} %bitcast.35), calls=%async_computation.6 | async-start | bytes 786432 | tf_op jit(solution)/shard_map/all_to_all | solution.py:222
  (37 other events, 549.6 us)

commit v5 on v4

--- a/solution.py
+++ b/solution.py
@@ -18,8 +18,7 @@
 CTX = ("yh", "xh", "xl", "z")
 EXP = ("yl", "c")
 HALF = ("xh", "xl", "z")
-GROUP = ("yh", "xh")
-ROUTE = ("yh", "xh", "z")
+GROUP = ("yh", "xh", "xl")
 SWAP = [(0, 1), (1, 0)]
 Y_XOR = [[(i, i ^ k) for i in range(4)] for k in range(4)]
 
@@ -86,36 +85,34 @@
     return (out_own * (1.0 - share) + got_out * share).astype(BF16), early
 
 
-def expand(order_ref, xn_ref, xf_ref, on_ref, of_ref, w_ref, wo_ref, *rest):
+def expand(order_ref, x_ref, o_ref, w_ref, wo_ref, *rest):
     out_refs, acc_ref = rest[:4], rest[4]
     contract = (((1,), (1,)), ((), ()))
-    rows = acc_ref.shape[0] // 2
-    for p, (a, b) in enumerate(((xn_ref, on_ref), (xf_ref, of_ref))):
-        a, b = (r[...].reshape(rows, r.shape[-1]) for r in (a, b))
-        acc_ref[p * rows : (p + 1) * rows, :] = lax.dot_general(
-            a, w_ref[...], contract, preferred_element_type=F32
-        ) + lax.dot_general(b, wo_ref[...], contract, preferred_element_type=F32)
+    x, o = (r[...].reshape(acc_ref.shape[0], r.shape[-1]) for r in (x_ref, o_ref))
+    acc_ref[...] = lax.dot_general(x, w_ref[...], contract, preferred_element_type=F32) + lax.dot_general(
+        o, wo_ref[...], contract, preferred_element_type=F32
+    )
     share = out_refs[0].shape[0]
     for i, ref in enumerate(out_refs):
         at = pl.multiple_of((order_ref[0] ^ i) * share, share)
         ref[...] = acc_ref[pl.ds(at, share), :].astype(BF16)
 
 
-def gate_up_terms(order, near, far, near_other, far_other, w, wo, block, chunk):
+def gate_up_terms(order, x, other, w, wo, block):
     hidden, feat = w.shape
     cols = hidden // 2
-    rows = 2 * near.shape[0] * block
+    rows = x.shape[0] * block
     share = rows // 4
-    x = pl.BlockSpec((near.shape[0], block, feat), lambda n, o: (0, chunk, 0))
+    spec = pl.BlockSpec((x.shape[0], block, feat), lambda n, o: (0, 0, 0))
     weight = pl.BlockSpec((cols, feat), lambda n, o: (n, 0))
     out = pl.BlockSpec((share, cols), lambda n, o: (0, n))
-    shape = jax.ShapeDtypeStruct((share, hidden), BF16)
+    shape = pltpu.HBM((share, hidden), BF16)
     return pl.pallas_call(
         expand,
         grid_spec=pltpu.PrefetchScalarGridSpec(
             num_scalar_prefetch=1,
             grid=(2,),
-            in_specs=[x, x, x, x, weight, weight],
+            in_specs=[spec, spec, weight, weight],
             out_specs=[out] * 4,
             scratch_shapes=[pltpu.VMEM((rows, cols), F32)],
         ),
@@ -125,10 +122,10 @@
         ),
         compiler_params=pltpu.CompilerParams(vmem_limit_bytes=40 << 20),
         name="gate_up_terms",
-    )(order, near, far, near_other, far_other, w, wo)
-
-
-def contract_hidden(order_ref, h_ref, ho_ref, w_ref, near_ref, far_ref):
+    )(order, x, other, w, wo)
+
+
+def contract_hidden(order_ref, h_ref, ho_ref, w_ref, out_ref):
     core = order_ref[1]
     half = w_ref.shape[0] // 2
     own = pl.multiple_of(core * half, half)
@@ -137,29 +134,19 @@
     acc += jnp.dot(ho_ref[...], w_ref[pl.ds(other, half), :], preferred_element_type=F32)
     share = h_ref.shape[0] // 4
     for i in range(4):
-        block = order_ref[0] ^ i
-        at = pl.multiple_of((block & 1) * share, share)
-        part = acc[i * share : (i + 1) * share].astype(BF16)
-
-        @pl.when(block < 2)
-        def _():
-            near_ref[pl.ds(at, share), :] = part
-
-        @pl.when(block >= 2)
-        def _():
-            far_ref[pl.ds(at, share), :] = part
+        at = pl.multiple_of((order_ref[0] ^ i) * share, share)
+        out_ref[pl.ds(at, share), :] = acc[i * share : (i + 1) * share].astype(BF16)
 
 
 def down_terms(order, h, ho, w):
     rows = h.shape[0]
     hidden, feat = w.shape
     whole = pl.BlockSpec(memory_space=pltpu.VMEM)
-    shape = jax.ShapeDtypeStruct((rows // 2, feat), BF16)
     return pl.pallas_call(
         contract_hidden,
         in_specs=[pl.BlockSpec(memory_space=pltpu.SMEM), whole, whole, whole],
-        out_specs=[whole, whole],
-        out_shape=[shape, shape],
+        out_specs=whole,
+        out_shape=jax.ShapeDtypeStruct((rows, feat), BF16),
         cost_estimate=pl.CostEstimate(
             flops=2 * rows * hidden * feat, transcendentals=0, bytes_accessed=2 * hidden * feat + 4 * rows * hidden
         ),
@@ -214,91 +201,66 @@
     ).astype(BF16)
 
     nz = lax.axis_size("z")
-    n = CAP // 3
-    group = EXPERTS * n
-    rows = nz * group
+    sources = EXPERTS * lax.axis_size("xl")
+    n = CAP // 2
+    block = sources * n
 
     def all_to_all(x, axes):
         return lax.all_to_all(x, axes, split_axis=0, concat_axis=0, tiled=True)
 
-    x_a = jnp.broadcast_to(packed[:, None, :n], (EXPERTS, nz, n, feat)).reshape(-1, n, feat)
-    x_a = all_to_all(x_a, ROUTE)
+    def along_z(x):
+        return all_to_all(jnp.broadcast_to(x[None], (nz,) + x.shape), "z").reshape((nz,) + x.shape)
+
+    squares = jnp.sum(jnp.where(taken, squares[None, None, :], 0.0), axis=2)
+    rows = jnp.concatenate([packed, as_rows(squares, feat)], axis=1)
+    rows = jnp.broadcast_to(rows[:, None], (EXPERTS, 2) + rows.shape[1:]).reshape(sources, CAP + 8, feat)
+    rows = all_to_all(rows, GROUP)
+    part_a, part_b = (rows[:, k * n : (k + 1) * n].reshape(block, feat) for k in range(2))
+    x_a = along_z(part_a)
+    squares = from_row(rows[:, CAP], CAP).reshape(sources, 2, n).transpose(1, 0, 2).reshape(2 * block)
     inverse = lax.rsqrt(lax.psum(squares, EXP) / D + 1e-05)
-    inverse = jnp.sum(jnp.where(taken, inverse[None, None, :], 0.0), axis=2)
     x_a, inverse = lax.optimization_barrier((x_a, inverse))
-    x_a = x_a.reshape(EXPERTS, nz * n, feat)
-    far_a = swap(x_a, "xl")
-    rest = all_to_all(jnp.concatenate([packed[:, n:], as_rows(inverse, feat)], axis=1), GROUP)
-    terms_a = gate_up_terms(order, x_a, far_a, swap(x_a, "c"), swap(far_a, "c"), w_in, w_in_other, nz * n, 0)
-    rest = after(rest, *terms_a)
-    inverse = from_row(rest[:, 2 * n], CAP).reshape(EXPERTS, 3, n).transpose(1, 0, 2).reshape(3 * group)
-    near = jnp.concatenate(
-        [rest[:, :n].reshape(group, feat), rest[:, n : 2 * n].reshape(group, feat), as_rows(inverse, feat)], axis=0
-    )
-    near = all_to_all(jnp.broadcast_to(near[None], (nz,) + near.shape), "z").reshape((nz,) + near.shape)
+    x_b = along_z(jnp.concatenate([part_b, as_rows(inverse, feat)], axis=0))
 
     def over_yl(parts):
         return [parts[0]] + [lax.ppermute(parts[i], "yl", Y_XOR[i]) for i in range(1, 4)]
 
     def hidden_of(parts, inverse):
+        inverse = lax.dynamic_index_in_dim(inverse.reshape(4, -1), me, 0, keepdims=False)
         full = sum(p.astype(F32) for p in parts) * inverse[:, None]
         return (jax.nn.silu(full[:, :half]) * full[:, half:]).astype(BF16)
 
-    def to_xl(down):
-        return down[0], swap(down[1], "xl")
-
-    def total(stay, came):
-        return (stay.astype(F32) + came.astype(F32)).astype(BF16)
-
+    def down_of(parts):
+        hid = jnp.concatenate(parts, axis=0)
+        return down_terms(order, hid, swap(hid, "c"), w_down)
+
+    def give_back(down):
+        return all_to_all(down.reshape(nz, block, feat), "z")
+
+    def over_z(back):
+        return jnp.sum(back.astype(F32), axis=0).astype(BF16).reshape(sources, n, feat)
+
+    terms_a = gate_up_terms(order, x_a, swap(x_a, "c"), w_in, w_in_other, block)
     sums_a = over_yl(terms_a)
-    near = after(near, *sums_a[1:])
-    tail = near[:, 2 * group :, : 9 * group + 96]
-    tails = (tail, swap(tail, "xl"))
-    inverse = jnp.stack([from_row(t[:, 0], 3 * group).reshape(nz, 3, EXPERTS, n) for t in tails])
-    inverse_a = inverse[:, :, 0].transpose(0, 2, 1, 3).reshape(4, rows // 2)
-    inverse_bc = inverse[:, :, 1:].transpose(2, 0, 1, 3, 4).reshape(2, 4, rows // 2)
-
-    def own(v):
-        return lax.dynamic_index_in_dim(v, me, 0, keepdims=False)
-
-    far = swap(near, "xl")
-    near_other = swap(near, "c")
-    hidden_a = over_yl([hidden_of(sums_a, own(inverse_a))] * 4)
-    far = after(far, *hidden_a)
-    far_other = swap(far, "c")
-    terms_b = gate_up_terms(order, near, far, near_other, far_other, w_in, w_in_other, group, 0)
-    hid = jnp.concatenate(hidden_a, axis=0)
-    down_a = down_terms(order, hid, swap(hid, "c"), w_down)
-    stay_a, came_a = to_xl(down_a)
+    x_b = after(x_b, *sums_a[1:])
+    inverse = from_row(x_b[:, block], 2 * block)
+    hidden_a = hidden_of(sums_a, inverse[:, :block])
+    x_b = after(x_b, hidden_a)
+    hids_a = over_yl([hidden_a] * 4)
+    terms_b = gate_up_terms(order, x_b, swap(x_b, "c"), w_in, w_in_other, block)
+    hids_a[1] = after(hids_a[1], *terms_b)
     sums_b = over_yl(terms_b)
-    terms_c = gate_up_terms(
-        order, near, far, near_other, after(far_other, *terms_b), w_in, w_in_other, group, 1
+    down_a = down_of(hids_a)
+    back_a = give_back(down_a)
+    sums_b[1] = after(sums_b[1], down_a)
+    hids_b = over_yl([hidden_of(sums_b, inverse[:, block:])] * 4)
+    back_a = after(back_a, *hids_b[1:])
+    back_b = give_back(down_of(hids_b))
+    returned = all_to_all(jnp.concatenate([over_z(back_a), over_z(back_b)], axis=1), GROUP)
+    returned = jnp.sum(returned.reshape(EXPERTS, 2, CAP, feat).astype(F32), axis=1)
+    moe_rows = jnp.einsum(
+        "ect,ecd->td", taken.astype(F32), returned, precision=lax.Precision.HIGHEST, preferred_element_type=F32
     )
-    sums_b[1] = after(sums_b[1], *down_a)
-    came_a = after(came_a, *sums_b[1:])
-    back_a = all_to_all(total(stay_a, came_a).reshape(-1, n, feat), ROUTE)
-    hidden_b = over_yl([hidden_of(sums_b, own(inverse_bc[0]))] * 4)
-    sums_c = over_yl(terms_c)
-    hid = jnp.concatenate(hidden_b, axis=0)
-    down_b = down_terms(order, hid, swap(hid, "c"), w_down)
-    stay_b, came_b = to_xl(down_b)
-    back_a = after(back_a, *sums_c[1:])
-    hidden_c = over_yl([hidden_of(sums_c, own(inverse_bc[1]))] * 4)
-    hid = jnp.concatenate(hidden_c, axis=0)
-    came_b = after(came_b, hid)
-    down_c = down_terms(order, hid, swap(hid, "c"), w_down)
-
-    def give_back(stay, came):
-        both = total(stay, came).reshape(nz, EXPERTS, n, feat).transpose(1, 0, 2, 3).reshape(-1, n, feat)
-        return all_to_all(both, ROUTE)
-
-    def over_z(back):
-        return jnp.sum(back.reshape(EXPERTS, nz, n, feat).astype(F32), axis=1).astype(BF16)
-
-    back_b = give_back(stay_b, came_b)
-    back_c = give_back(*to_xl(down_c))
-    returned = jnp.concatenate([over_z(back_a), over_z(after(back_b, down_c[0])), over_z(back_c)], axis=1)
-    moe_rows = jnp.einsum("ect,ecd->td", select, returned, preferred_element_type=F32)
     return (route_weight[:, None] * moe_rows).astype(BF16)
 
 

time: 387 us -> 344 us (0.89)
  starting transfers between devices: 166 us -> 95.2 us
  blocking collectives: 13.9 us -> 46.4 us
  waiting for transfers between devices: 142 us -> 157 us
  local copies, waits for them, and re-layouts: 22.1 us -> 11 us
  other arithmetic: 14.8 us -> 10.6 us
    all_to_all x0 -> x2, blocking collectives: none -> 35.8 us  [all_to_all(): return lax.all_to_all(x, axes, split_axis=0, concat_axis=0, tiled=True)]
    ppermute x14 -> x5, waiting for transfers between devices: 39.1 us -> 5.33 us  [swap(): return lax.ppermute(x, axis, SWAP)]
    all_to_all x6 -> x4, starting transfers between devices: 55.6 us -> 24.7 us  [all_to_all(): return lax.all_to_all(x, axes, split_axis=0, concat_axis=0, tiled=True)]
    ppermute x18 -> x12, waiting for transfers between devices: 51.3 us -> 76.9 us  [over_yl(): lax.ppermute(parts[i], 'yl', Y_XOR[i])]
    ppermute x14 -> x5, starting transfers between devices: 30.9 us -> 9.6 us  [swap(): return lax.ppermute(x, axis, SWAP)]
    all_to_all x6 -> x4, waiting for transfers between devices: 31.5 us -> 52.3 us  [all_to_all(): return lax.all_to_all(x, axes, split_axis=0, concat_axis=0, tiled=True)]
    ppermute x18 -> x12, starting transfers between devices: 57.6 us -> 39.6 us  [over_yl(): lax.ppermute(parts[i], 'yl', Y_XOR[i])]
    unnamed x45 -> x33, local copies, waits for them, and re-layouts: 8.35 us -> 2.81 us
  transfers between devices with their start and end apart: 41 -> 24, of which waited for: 20 -> 17; matrix products, arithmetic and copies ran while one was open for 5% -> 3% of each run, Pallas kernels for 5% -> 5%
where the time goes in v5:
time: 344 us; the launch traced here: 343 us
  waiting for transfers between devices  157 us (46%)
  starting transfers between devices  95.2 us (28%)
  blocking collectives  46.4 us (13%)
  Pallas kernels  16.3 us (5%)
  local copies, waits for them, and re-layouts  11 us (3%)
  other arithmetic  10.6 us (3%)
  matrix products  6.29 us (2%)
    ppermute x12, waiting for transfers between devices, over_yl(): lax.ppermute(parts[i], 'yl', Y_XOR[i])  76.9 us
    all_to_all x4, waiting for transfers between devices, all_to_all(): return lax.all_to_all(x, axes, split_axis=0, concat_axis=0, tiled=True)  52.3 us
    ppermute x12, starting transfers between devices, over_yl(): lax.ppermute(parts[i], 'yl', Y_XOR[i])  39.6 us
    all_to_all x2, blocking collectives, all_to_all(): return lax.all_to_all(x, axes, split_axis=0, concat_axis=0, tiled=True)  35.8 us
    all_to_all x4, starting transfers between devices, all_to_all(): return lax.all_to_all(x, axes, split_axis=0, concat_axis=0, tiled=True)  24.7 us
    all_to_all x1, starting transfers between devices, attend(): lax.all_to_all(jnp.broadcast_to(kv[None], (members,) + kv.shape), HALF, s...  13.3 us
    all_to_all x1, waiting for transfers between devices, attend(): lax.all_to_all(jnp.broadcast_to(kv[None], (members,) + kv.shape), HALF, s...  11.4 us
    psum x1, blocking collectives, body(): inverse = lax.rsqrt(lax.psum(squares, EXP) / D + 1e-05)  10.6 us
  transfers between devices with their start and end apart: 24, of which 17 were waited for; matrix products, arithmetic and copies ran while one was open for 3% of the time, Pallas kernels for 5%

profile of v5, /device:TPU:8, one launch (start us, length us, event | category | flops | bytes accessed | tf_op | source)
XLA Modules:
  0.0 343.0 jit_solution(14470437324741629374)
XLA Ops:
  1.8 13.3 %all-to-all-start = ((bf16[32,64,256]{2,1,0:T(8,128)(2,1)}), bf16[32,64,256]{2,1,0:T(8,128)(2,1)}, u32[]{:S(2)}, u32[]{:S(2)}) async-start(bf16[32,64,256]{2,1,0:T(8,128)(2,1)} %broadcast_in_dim.36), calls=%async_computation | async-start | bytes 2097152 | tf_op jit(solution)/shard_map/all_to_all | solution.py:46
  24.6 7.6 %collective-permute-done = bf16[64,768]{1,0:T(8,128)(2,1)S(1)} collective-permute-done((bf16[64,768]{1,0:T(8,128)(2,1)S(1)}, bf16[64,768]{1,0:T(8,128)(2,1)S(1)}, u32[]{:S(2)}, u32[]{:S(2)}) %collective-permute-start) | collective-permute-done | bytes 98336 | tf_op jit(solution)/shard_map/ppermute | solution.py:43
  32.4 11.4 %all-to-all-done = bf16[32,64,256]{2,1,0:T(8,128)(2,1)} async-done(((bf16[32,64,256]{2,1,0:T(8,128)(2,1)}), bf16[32,64,256]{2,1,0:T(8,128)(2,1)}, u32[]{:S(2)}, u32[]{:S(2)}) %all-to-all-start) | async-done | bytes 1048608 | tf_op jit(solution)/shard_map/all_to_all | solution.py:46
  51.5 6.8 %collective-permute-start.2 = (bf16[64,896]{1,0:T(8,128)(2,1)S(1)}, bf16[64,896]{1,0:T(8,128)(2,1)S(1)}, u32[]{:S(2)}, u32[]{:S(2)}) collective-permute-start(bf16[64,896]{1,0:T(8,128)(2,1)S(1)} %fusion.26), channel_id=1, source_target_pairs={{0,256},{1,257},{2,258},{3,259},{4,260},{5,261},{6,262},{7,263},{8... | collective-permute-start | bytes 344072 | tf_op jit(solution)/shard_map/ppermute | solution.py:79
  62.8 20.1 %all_to_all.35 = bf16[8,32,768]{2,1,0:T(8,128)(2,1)S(1)} all-to-all(bf16[8,32,768]{2,1,0:T(8,128)(2,1)S(1)} %bitcast.71), channel_id=1, replica_groups=mesh['yh'=2,'xh'=2,'xl'=2,'z'=8,'yl'=4,'c'=2] {'yh','xh','xl'}, dimensions={0} | all-to-all | bytes 786432 | tf_op jit(solution)/shard_map/all_to_all | solution.py:209
  84.0 6.7 %all-to-all-start.2 = ((bf16[8,96,768]{2,1,0:T(8,128)(2,1)}), bf16[8,96,768]{2,1,0:T(8,128)(2,1)S(1)}, u32[]{:S(2)}, u32[]{:S(2)}) async-start(bf16[8,96,768]{2,1,0:T(8,128)(2,1)} %broadcast_in_dim.77), calls=%async_computation.2 | async-start | bytes 2359296 | tf_op jit(solution)/shard_map/all_to_all | solution.py:209
  91.1 10.6 %psum.7 = f32[192]{0:T(256)S(1)} all-reduce(f32[192]{0:T(256)S(1)} %reshape.148), channel_id=1, replica_groups=mesh['yh'=2,'xh'=2,'xl'=2,'z'=8,'yl'=4,'c'=2] {'yl','c'}, use_global_device_ids=true, to_apply=%region_6.7 | all-reduce | flops 192 | bytes 1536 | tf_op jit(solution)/shard_map/psum | solution.py:221
  101.7 20.6 %all-to-all-done.2.x_ref = bf16[8,96,768]{2,1,0:T(8,128)(2,1)S(1)} async-done(((bf16[8,96,768]{2,1,0:T(8,128)(2,1)}), bf16[8,96,768]{2,1,0:T(8,128)(2,1)S(1)}, u32[]{:S(2)}, u32[]{:S(2)}) %all-to-all-start.2) | async-done | bytes 1179680 | tf_op jit(solution)/shard_map/all_to_all | solution.py:209
  135.1 5.7 %gate_up_terms.2 = (bf16[192,1024]{1,0:T(8,128)(2,1)}, bf16[192,1024]{1,0:T(8,128)(2,1)}, bf16[192,1024]{1,0:T(8,128)(2,1)}, bf16[192,1024]{1,0:T(8,128)(2,1)}) custom-call(s32[2]{0:T(128)S(1)} %pad_add_fusion.order_ref, bf16[8,96,768]{2,1,0:T(8,128)(2,1)S(1)} %copy-done.1, bf16[8,96,768]{2,1,0:T(8,128)(2,1)} %collective-permute-done.3.o_ref, ...), custom_call_target="tpu_custom_call" | custom-call | flops 2415919104 | bytes 4718592 | tf_op jit(solution)/shard_map/gate_up_terms/pallas_call | solution.py:110
  144.7 5.4 %collective-permute-start.6 = (bf16[192,1024]{1,0:T(8,128)(2,1)}, bf16[192,1024]{1,0:T(8,128)(2,1)}, u32[]{:S(2)}, u32[]{:S(2)}) collective-permute-start(bf16[192,1024]{1,0:T(8,128)(2,1)} %get-tuple-element.30), channel_id=1, source_target_pairs={{0,6},{2,4},{4,2},{6,0},{1,7},{3,5},{5,3},{7,1},{8,14},{10,12},{12... | collective-permute-start | bytes 1179656 | tf_op jit(solution)/shard_map/ppermute | solution.py:226
  150.1 4.8 %collective-permute-done.4 = bf16[192,1024]{1,0:T(8,128)(2,1)S(1)} collective-permute-done((bf16[192,1024]{1,0:T(8,128)(2,1)}, bf16[192,1024]{1,0:T(8,128)(2,1)S(1)}, u32[]{:S(2)}, u32[]{:S(2)}) %collective-permute-start.4) | collective-permute-done | bytes 393248 | tf_op jit(solution)/shard_map/ppermute | solution.py:226
  154.9 16.4 %collective-permute-done.5 = bf16[192,1024]{1,0:T(8,128)(2,1)} collective-permute-done((bf16[192,1024]{1,0:T(8,128)(2,1)}, bf16[192,1024]{1,0:T(8,128)(2,1)}, u32[]{:S(2)}, u32[]{:S(2)}) %collective-permute-start.5) | collective-permute-done | bytes 393248 | tf_op jit(solution)/shard_map/ppermute | solution.py:226
  171.4 11.3 %collective-permute-done.6 = bf16[192,1024]{1,0:T(8,128)(2,1)} collective-permute-done((bf16[192,1024]{1,0:T(8,128)(2,1)}, bf16[192,1024]{1,0:T(8,128)(2,1)}, u32[]{:S(2)}, u32[]{:S(2)}) %collective-permute-start.6) | collective-permute-done | bytes 393248 | tf_op jit(solution)/shard_map/ppermute | solution.py:226
  190.4 6.3 %collective-permute-start.9 = (bf16[192,512]{1,0:T(8,128)(2,1)S(1)}, bf16[192,512]{1,0:T(8,128)(2,1)S(1)}, u32[]{:S(2)}, u32[]{:S(2)}) collective-permute-start(bf16[192,512]{1,0:T(8,128)(2,1)S(1)} %fusion.14), channel_id=1, source_target_pairs={{0,4},{2,6},{4,0},{6,2},{1,5},{3,7},{5,1},{7,3},{8,12},{10,14},{12... | collective-permute-start | bytes 589832 | tf_op jit(solution)/shard_map/ppermute | solution.py:226
  201.4 5.2 %collective-permute-done.10 = bf16[192,512]{1,0:T(8,128)(2,1)S(1)} collective-permute-done((bf16[192,512]{1,0:T(8,128)(2,1)S(1)}, bf16[192,512]{1,0:T(8,128)(2,1)S(1)}, u32[]{:S(2)}, u32[]{:S(2)}) %collective-permute-start.10) | collective-permute-done | bytes 196640 | tf_op jit(solution)/shard_map/ppermute | solution.py:226
  210.1 5.6 %collective-permute-start.12 = (bf16[192,1024]{1,0:T(8,128)(2,1)}, bf16[192,1024]{1,0:T(8,128)(2,1)S(1)}, u32[]{:S(2)}, u32[]{:S(2)}) collective-permute-start(bf16[192,1024]{1,0:T(8,128)(2,1)} %get-tuple-element.35), channel_id=1, source_target_pairs={{0,2},{2,0},{4,6},{6,4},{1,3},{3,1},{5,7},{7,5},{8,10},{10,8},{12,... | collective-permute-start | bytes 1179656 | tf_op jit(solution)/shard_map/ppermute | solution.py:226
  224.2 7.2 %all-to-all-start.4 = ((bf16[8,96,768]{2,1,0:T(8,128)(2,1)}), bf16[8,96,768]{2,1,0:T(8,128)(2,1)S(1)}, u32[]{:S(2)}, u32[]{:S(2)}) async-start(bf16[8,96,768]{2,1,0:T(8,128)(2,1)} %bitcast.20), calls=%async_computation.4 | async-start | bytes 2359296 | tf_op jit(solution)/shard_map/all_to_all | solution.py:209
  231.5 12.7 %collective-permute-done.13 = bf16[192,1024]{1,0:T(8,128)(2,1)} collective-permute-done((bf16[192,1024]{1,0:T(8,128)(2,1)}, bf16[192,1024]{1,0:T(8,128)(2,1)}, u32[]{:S(2)}, u32[]{:S(2)}) %collective-permute-start.13) | collective-permute-done | bytes 393248 | tf_op jit(solution)/shard_map/ppermute | solution.py:226
  244.3 10.0 %collective-permute-done.14 = bf16[192,1024]{1,0:T(8,128)(2,1)} collective-permute-done((bf16[192,1024]{1,0:T(8,128)(2,1)}, bf16[192,1024]{1,0:T(8,128)(2,1)}, u32[]{:S(2)}, u32[]{:S(2)}) %collective-permute-start.14) | collective-permute-done | bytes 393248 | tf_op jit(solution)/shard_map/ppermute | solution.py:226
  265.4 9.5 %collective-permute-done.16 = bf16[192,512]{1,0:T(8,128)(2,1)S(1)} collective-permute-done((bf16[192,512]{1,0:T(8,128)(2,1)S(1)}, bf16[192,512]{1,0:T(8,128)(2,1)S(1)}, u32[]{:S(2)}, u32[]{:S(2)}) %collective-permute-start.16) | collective-permute-done | bytes 196640 | tf_op jit(solution)/shard_map/ppermute | solution.py:226
  274.9 4.9 %collective-permute-done.17 = bf16[192,512]{1,0:T(8,128)(2,1)S(1)} collective-permute-done((bf16[192,512]{1,0:T(8,128)(2,1)S(1)}, bf16[192,512]{1,0:T(8,128)(2,1)S(1)}, u32[]{:S(2)}, u32[]{:S(2)}) %collective-permute-start.17) | collective-permute-done | bytes 196640 | tf_op jit(solution)/shard_map/ppermute | solution.py:226
  287.0 7.1 %all-to-all-start.5 = ((bf16[8,96,768]{2,1,0:T(8,128)(2,1)}), bf16[8,96,768]{2,1,0:T(8,128)(2,1)S(1)}, u32[]{:S(2)}, u32[]{:S(2)}) async-start(bf16[8,96,768]{2,1,0:T(8,128)(2,1)} %bitcast.22), calls=%async_computation.5 | async-start | bytes 2359296 | tf_op jit(solution)/shard_map/all_to_all | solution.py:209
  294.3 31.7 %all-to-all-done.5 = bf16[8,96,768]{2,1,0:T(8,128)(2,1)S(1)} async-done(((bf16[8,96,768]{2,1,0:T(8,128)(2,1)}), bf16[8,96,768]{2,1,0:T(8,128)(2,1)S(1)}, u32[]{:S(2)}, u32[]{:S(2)}) %all-to-all-start.5) | async-done | bytes 1179680 | tf_op jit(solution)/shard_map/all_to_all | solution.py:209
  326.3 15.7 %all_to_all.36 = bf16[8,24,768]{2,1,0:T(8,128)(2,1)S(1)} all-to-all(bf16[8,24,768]{2,1,0:T(8,128)(2,1)S(1)} %pad_maximum_fusion.4), channel_id=1, replica_groups=mesh['yh'=2,'xh'=2,'xl'=2,'z'=8,'yl'=4,'c'=2] {'yh','xh','xl'}, dimensions={0} | all-to-all | bytes 589824 | tf_op jit(solution)/shard_map/all_to_all | solution.py:209
  (144 shorter events, 85.8 us)
Async XLA Ops:
  1.8 41.9 %all-to-all-start = ((bf16[32,64,256]{2,1,0:T(8,128)(2,1)}), bf16[32,64,256]{2,1,0:T(8,128)(2,1)}, u32[]{:S(2)}, u32[]{:S(2)}) async-start(bf16[32,64,256]{2,1,0:T(8,128)(2,1)} %broadcast_in_dim.36), calls=%async_computation | async-start | bytes 2097152 | tf_op jit(solution)/shard_map/all_to_all | solution.py:46
  19.3 13.1 %collective-permute-start.1 = (bf16[1024,768]{1,0:T(8,128)(2,1)}, bf16[1024,768]{1,0:T(8,128)(2,1)S(1)}, u32[]{:S(2)}, u32[]{:S(2)}) collective-permute-start(bf16[1024,768]{1,0:T(8,128)(2,1)} %pad_maximum_fusion.1), channel_id=1, source_target_pairs={{0,1},{1,0},{2,3},{3,2},{4,5},{5,4},{6,7},{7,6},{8,9},{9,8},{10,11... | collective-permute-start | bytes 4718600 | tf_op jit(solution)/shard_map/ppermute | solution.py:27
  21.2 11.0 %collective-permute-start = (bf16[64,768]{1,0:T(8,128)(2,1)S(1)}, bf16[64,768]{1,0:T(8,128)(2,1)S(1)}, u32[]{:S(2)}, u32[]{:S(2)}) collective-permute-start(bf16[64,768]{1,0:T(8,128)(2,1)S(1)} %copy-done.9), channel_id=1, source_target_pairs={{256,0},{257,1},{258,2},{259,3},{260,4},{261,5},{262,6},{263,7},{2... | collective-permute-start | bytes 294920 | tf_op jit(solution)/shard_map/ppermute | solution.py:43
  51.5 10.4 %collective-permute-start.2 = (bf16[64,896]{1,0:T(8,128)(2,1)S(1)}, bf16[64,896]{1,0:T(8,128)(2,1)S(1)}, u32[]{:S(2)}, u32[]{:S(2)}) collective-permute-start(bf16[64,896]{1,0:T(8,128)(2,1)S(1)} %fusion.26), channel_id=1, source_target_pairs={{0,256},{1,257},{2,258},{3,259},{4,260},{5,261},{6,262},{7,263},{8... | collective-permute-start | bytes 344072 | tf_op jit(solution)/shard_map/ppermute | solution.py:79
  84.0 38.3 %all-to-all-start.2 = ((bf16[8,96,768]{2,1,0:T(8,128)(2,1)}), bf16[8,96,768]{2,1,0:T(8,128)(2,1)S(1)}, u32[]{:S(2)}, u32[]{:S(2)}) async-start(bf16[8,96,768]{2,1,0:T(8,128)(2,1)} %broadcast_in_dim.77), calls=%async_computation.2 | async-start | bytes 2359296 | tf_op jit(solution)/shard_map/all_to_all | solution.py:209
  123.8 58.9 %all-to-all-start.3 = ((bf16[8,104,768]{2,1,0:T(8,128)(2,1)}), bf16[8,104,768]{2,1,0:T(8,128)(2,1)S(1)}, u32[]{:S(2)}, u32[]{:S(2)}) async-start(bf16[8,104,768]{2,1,0:T(8,128)(2,1)} %broadcast_in_dim.79), calls=%async_computation.3 | async-start | bytes 2555904 | tf_op jit(solution)/shard_map/all_to_all | solution.py:209
  127.4 5.1 %collective-permute-start.3 = (bf16[8,96,768]{2,1,0:T(8,128)(2,1)}, bf16[8,96,768]{2,1,0:T(8,128)(2,1)}, u32[]{:S(2)}, u32[]{:S(2)}) collective-permute-start(bf16[8,96,768]{2,1,0:T(8,128)(2,1)} %copy-done), channel_id=1, source_target_pairs={{0,1},{1,0},{2,3},{3,2},{4,5},{5,4},{6,7},{7,6},{8,9},{9,8},{10,11... | collective-permute-start | bytes 3538952 | tf_op jit(solution)/shard_map/ppermute | solution.py:27
  140.9 14.1 %collective-permute-start.4 = (bf16[192,1024]{1,0:T(8,128)(2,1)}, bf16[192,1024]{1,0:T(8,128)(2,1)S(1)}, u32[]{:S(2)}, u32[]{:S(2)}) collective-permute-start(bf16[192,1024]{1,0:T(8,128)(2,1)} %get-tuple-element.28), channel_id=1, source_target_pairs={{0,2},{2,0},{4,6},{6,4},{1,3},{3,1},{5,7},{7,5},{8,10},{10,8},{12,... | collective-permute-start | bytes 1179656 | tf_op jit(solution)/shard_map/ppermute | solution.py:226
  142.8 28.6 %collective-permute-start.5 = (bf16[192,1024]{1,0:T(8,128)(2,1)}, bf16[192,1024]{1,0:T(8,128)(2,1)}, u32[]{:S(2)}, u32[]{:S(2)}) collective-permute-start(bf16[192,1024]{1,0:T(8,128)(2,1)} %get-tuple-element.29), channel_id=1, source_target_pairs={{0,4},{2,6},{4,0},{6,2},{1,5},{3,7},{5,1},{7,3},{8,12},{10,14},{12... | collective-permute-start | bytes 1179656 | tf_op jit(solution)/shard_map/ppermute | solution.py:226
  144.7 37.9 %collective-permute-start.6 = (bf16[192,1024]{1,0:T(8,128)(2,1)}, bf16[192,1024]{1,0:T(8,128)(2,1)}, u32[]{:S(2)}, u32[]{:S(2)}) collective-permute-start(bf16[192,1024]{1,0:T(8,128)(2,1)} %get-tuple-element.30), channel_id=1, source_target_pairs={{0,6},{2,4},{4,2},{6,0},{1,7},{3,5},{5,3},{7,1},{8,14},{10,12},{12... | collective-permute-start | bytes 1179656 | tf_op jit(solution)/shard_map/ppermute | solution.py:226
  184.7 12.1 %collective-permute-start.8 = (bf16[8,104,768]{2,1,0:T(8,128)(2,1)S(1)}, bf16[8,104,768]{2,1,0:T(8,128)(2,1)S(1)}, u32[]{:S(2)}, u32[]{:S(2)}) collective-permute-start(bf16[8,104,768]{2,1,0:T(8,128)(2,1)S(1)} %all-to-all-done.3.x_ref), channel_id=1, source_target_pairs={{0,1},{1,0},{2,3},{3,2},{4,5},{5,4},{6,7},{7,6},{8,9},{9,8},{10,11... | collective-permute-start | bytes 3833864 | tf_op jit(solution)/shard_map/ppermute | solution.py:27
  186.6 14.8 %collective-permute-start.7 = (bf16[192,512]{1,0:T(8,128)(2,1)S(1)}, bf16[192,512]{1,0:T(8,128)(2,1)S(1)}, u32[]{:S(2)}, u32[]{:S(2)}) collective-permute-start(bf16[192,512]{1,0:T(8,128)(2,1)S(1)} %fusion.14), channel_id=1, source_target_pairs={{0,2},{2,0},{4,6},{6,4},{1,3},{3,1},{5,7},{7,5},{8,10},{10,8},{12,... | collective-permute-start | bytes 589832 | tf_op jit(solution)/shard_map/ppermute | solution.py:226
  188.5 18.0 %collective-permute-start.10 = (bf16[192,512]{1,0:T(8,128)(2,1)S(1)}, bf16[192,512]{1,0:T(8,128)(2,1)S(1)}, u32[]{:S(2)}, u32[]{:S(2)}) collective-permute-start(bf16[192,512]{1,0:T(8,128)(2,1)S(1)} %fusion.14), channel_id=1, source_target_pairs={{0,6},{2,4},{4,2},{6,0},{1,7},{3,5},{5,3},{7,1},{8,14},{10,12},{12... | collective-permute-start | bytes 589832 | tf_op jit(solution)/shard_map/ppermute | solution.py:226
  190.4 17.7 %collective-permute-start.9 = (bf16[192,512]{1,0:T(8,128)(2,1)S(1)}, bf16[192,512]{1,0:T(8,128)(2,1)S(1)}, u32[]{:S(2)}, u32[]{:S(2)}) collective-permute-start(bf16[192,512]{1,0:T(8,128)(2,1)S(1)} %fusion.14), channel_id=1, source_target_pairs={{0,4},{2,6},{4,0},{6,2},{1,5},{3,7},{5,1},{7,3},{8,12},{10,14},{12... | collective-permute-start | bytes 589832 | tf_op jit(solution)/shard_map/ppermute | solution.py:226
  208.2 13.0 %collective-permute-start.11 = (bf16[768,512]{1,0:T(8,128)(2,1)S(1)}, bf16[768,512]{1,0:T(8,128)(2,1)S(1)}, u32[]{:S(2)}, u32[]{:S(2)}) collective-permute-start(bf16[768,512]{1,0:T(8,128)(2,1)S(1)} %pad_maximum_fusion.2.h_ref), channel_id=1, source_target_pairs={{0,1},{1,0},{2,3},{3,2},{4,5},{5,4},{6,7},{7,6},{8,9},{9,8},{10,11... | collective-permute-start | bytes 2359304 | tf_op jit(solution)/shard_map/ppermute | solution.py:27
  210.1 21.4 %collective-permute-start.12 = (bf16[192,1024]{1,0:T(8,128)(2,1)}, bf16[192,1024]{1,0:T(8,128)(2,1)S(1)}, u32[]{:S(2)}, u32[]{:S(2)}) collective-permute-start(bf16[192,1024]{1,0:T(8,128)(2,1)} %get-tuple-element.35), channel_id=1, source_target_pairs={{0,2},{2,0},{4,6},{6,4},{1,3},{3,1},{5,7},{7,5},{8,10},{10,8},{12,... | collective-permute-start | bytes 1179656 | tf_op jit(solution)/shard_map/ppermute | solution.py:226
  215.7 28.6 %collective-permute-start.13 = (bf16[192,1024]{1,0:T(8,128)(2,1)}, bf16[192,1024]{1,0:T(8,128)(2,1)}, u32[]{:S(2)}, u32[]{:S(2)}) collective-permute-start(bf16[192,1024]{1,0:T(8,128)(2,1)} %get-tuple-element.36), channel_id=1, source_target_pairs={{0,4},{2,6},{4,0},{6,2},{1,5},{3,7},{5,1},{7,3},{8,12},{10,14},{12... | collective-permute-start | bytes 1179656 | tf_op jit(solution)/shard_map/ppermute | solution.py:226
  217.6 36.6 %collective-permute-start.14 = (bf16[192,1024]{1,0:T(8,128)(2,1)}, bf16[192,1024]{1,0:T(8,128)(2,1)}, u32[]{:S(2)}, u32[]{:S(2)}) collective-permute-start(bf16[192,1024]{1,0:T(8,128)(2,1)} %get-tuple-element.37), channel_id=1, source_target_pairs={{0,6},{2,4},{4,2},{6,0},{1,7},{3,5},{5,3},{7,1},{8,14},{10,12},{12... | collective-permute-start | bytes 1179656 | tf_op jit(solution)/shard_map/ppermute | solution.py:226
  224.2 62.8 %all-to-all-start.4 = ((bf16[8,96,768]{2,1,0:T(8,128)(2,1)}), bf16[8,96,768]{2,1,0:T(8,128)(2,1)S(1)}, u32[]{:S(2)}, u32[]{:S(2)}) async-start(bf16[8,96,768]{2,1,0:T(8,128)(2,1)} %bitcast.20), calls=%async_computation.4 | async-start | bytes 2359296 | tf_op jit(solution)/shard_map/all_to_all | solution.py:209
  255.7 9.7 %collective-permute-start.15 = (bf16[192,512]{1,0:T(8,128)(2,1)S(1)}, bf16[192,512]{1,0:T(8,128)(2,1)S(1)}, u32[]{:S(2)}, u32[]{:S(2)}) collective-permute-start(bf16[192,512]{1,0:T(8,128)(2,1)S(1)} %fusion.13), channel_id=1, source_target_pairs={{0,2},{2,0},{4,6},{6,4},{1,3},{3,1},{5,7},{7,5},{8,10},{10,8},{12,... | collective-permute-start | bytes 589832 | tf_op jit(solution)/shard_map/ppermute | solution.py:226
  257.6 17.3 %collective-permute-start.16 = (bf16[192,512]{1,0:T(8,128)(2,1)S(1)}, bf16[192,512]{1,0:T(8,128)(2,1)S(1)}, u32[]{:S(2)}, u32[]{:S(2)}) collective-permute-start(bf16[192,512]{1,0:T(8,128)(2,1)S(1)} %fusion.13), channel_id=1, source_target_pairs={{0,4},{2,6},{4,0},{6,2},{1,5},{3,7},{5,1},{7,3},{8,12},{10,14},{12... | collective-permute-start | bytes 589832 | tf_op jit(solution)/shard_map/ppermute | solution.py:226
  261.6 18.2 %collective-permute-start.17 = (bf16[192,512]{1,0:T(8,128)(2,1)S(1)}, bf16[192,512]{1,0:T(8,128)(2,1)S(1)}, u32[]{:S(2)}, u32[]{:S(2)}) collective-permute-start(bf16[192,512]{1,0:T(8,128)(2,1)S(1)} %fusion.13), channel_id=1, source_target_pairs={{0,6},{2,4},{4,2},{6,0},{1,7},{3,5},{5,3},{7,1},{8,14},{10,12},{12... | collective-permute-start | bytes 589832 | tf_op jit(solution)/shard_map/ppermute | solution.py:226
  279.8 4.2 %collective-permute-start.18 = (bf16[768,512]{1,0:T(8,128)(2,1)S(1)}, bf16[768,512]{1,0:T(8,128)(2,1)S(1)}, u32[]{:S(2)}, u32[]{:S(2)}) collective-permute-start(bf16[768,512]{1,0:T(8,128)(2,1)S(1)} %pad_maximum_fusion.3.h_ref), channel_id=1, source_target_pairs={{0,1},{1,0},{2,3},{3,2},{4,5},{5,4},{6,7},{7,6},{8,9},{9,8},{10,11... | collective-permute-start | bytes 2359304 | tf_op jit(solution)/shard_map/ppermute | solution.py:27
  287.0 39.0 %all-to-all-start.5 = ((bf16[8,96,768]{2,1,0:T(8,128)(2,1)}), bf16[8,96,768]{2,1,0:T(8,128)(2,1)S(1)}, u32[]{:S(2)}, u32[]{:S(2)}) async-start(bf16[8,96,768]{2,1,0:T(8,128)(2,1)} %bitcast.22), calls=%async_computation.5 | async-start | bytes 2359296 | tf_op jit(solution)/shard_map/all_to_all | solution.py:209
  (15 other events, 226.2 us)

commit v6 on v5

--- a/solution.py
+++ b/solution.py
@@ -34,12 +34,44 @@
     return [p.astype(BF16) for p in (hi, mid, lo)]
 
 
+def softmax_block(base_ref, own_ref, far_ref, kv_ref, out_ref, lse_ref, message_ref):
+    rows = own_ref.shape[0]
+    count = kv_ref.shape[0]
+    heads = own_ref.shape[1] // HD
+    scale = 1.0 / math.sqrt(HD)
+    keys, values = kv_ref[:, :HD], kv_ref[:, HD:]
+    limit = base_ref[0] + lax.broadcasted_iota(jnp.int32, (rows, count), 0)
+    allowed = lax.broadcasted_iota(jnp.int32, (rows, count), 1) <= limit
+    lane = lax.broadcasted_iota(jnp.int32, (rows, HD), 1)
+    tail = jnp.zeros((rows, HD), F32)
+    for h in range(heads):
+        cols = slice(h * HD, (h + 1) * HD)
+        for far, ref in ((False, own_ref), (True, far_ref)):
+            dots = lax.dot_general(ref[:, cols], keys, (((1,), (1,)), ((), ())), preferred_element_type=F32)
+            if not far:
+                dots = jnp.where(allowed, dots, -1e30)
+            top = jnp.max(dots, axis=1, keepdims=True)
+            weights = jnp.exp2((dots - top) * (scale * math.log2(math.e)))
+            total = jnp.sum(weights, axis=1, keepdims=True)
+            acc = jnp.dot(weights.astype(BF16), values, preferred_element_type=F32)
+            out = acc / total
+            lse = top * scale + jnp.log(total)
+            if far:
+                message_ref[:, cols] = out.astype(BF16)
+                hi = lse.astype(BF16).astype(F32)
+                mid = (lse - hi).astype(BF16).astype(F32)
+                for k, part in enumerate((hi, mid, lse - hi - mid)):
+                    tail = jnp.where(lane == k * heads + h, part, tail)
+            else:
+                out_ref[:, cols] = out
+                lse_ref[:, cols] = jnp.broadcast_to(lse, (rows, HD))
+    message_ref[:, heads * HD :] = tail.astype(BF16)
+
+
 def attend(queries, keys, values, early):
-    rows = queries.shape[0]
-    heads = queries.shape[1] // HD
+    rows, width = queries.shape
+    heads = width // HD
     yh = lax.axis_index("yh")
-    scale = 1.0 / math.sqrt(HD)
-
     foreign = lax.ppermute(queries, "yh", [(1, 0)])
     kv = jnp.concatenate([keys, values], axis=1)
     members = lax.axis_size(HALF)
@@ -47,42 +79,29 @@
         jnp.broadcast_to(kv[None], (members,) + kv.shape), HALF, split_axis=0, concat_axis=0, tiled=True
     ).reshape(members * rows, 2 * HD)
     kv, *early = lax.optimization_barrier((kv,) + early)
-    k_all, v_all = kv[:, :HD], kv[:, HD:]
-    count = members * rows
-
-    def stacked(q):
-        return q.reshape(rows, heads, HD).transpose(1, 0, 2).reshape(heads * rows, HD)
-
-    q_all = jnp.concatenate([stacked(queries), stacked(foreign)], axis=0)
-    own_pos = lax.axis_index(HALF) * rows + jnp.tile(jnp.arange(rows, dtype=jnp.int32), heads)
-    limit = jnp.concatenate([own_pos, jnp.full_like(own_pos, count)])
-    scores = jnp.einsum("qd,kd->qk", q_all, k_all, preferred_element_type=F32) * scale
-    allowed = jnp.arange(count, dtype=jnp.int32)[None, :] <= limit[:, None]
-    scores = jnp.where(allowed, scores, -1e30)
-    top = jnp.max(scores, axis=1)
-    weights = jnp.exp(scores - top[:, None])
-    total = jnp.sum(weights, axis=1)
-    acc = jnp.einsum("qk,kd->qd", weights.astype(BF16), v_all, preferred_element_type=F32)
-    out = acc / total[:, None]
-    lse = top + jnp.log(total)
-
-    n = heads * rows
-
-    def unstacked(o):
-        return o.reshape(heads, rows, HD).transpose(1, 0, 2).reshape(rows, heads * HD)
-
-    out_own, out_far = unstacked(out[:n]), unstacked(out[n:])
-    lse_own, lse_far = lse[:n].reshape(heads, rows).T, lse[n:].reshape(heads, rows).T
-    tail = jnp.concatenate(split3(lse_far), axis=1)
-    tail = jnp.pad(tail, ((0, 0), (0, HD - tail.shape[1])))
-    message = jnp.concatenate([out_far.astype(BF16), tail], axis=1)
+    whole = pl.BlockSpec(memory_space=pltpu.VMEM)
+    out, lse, message = pl.pallas_call(
+        softmax_block,
+        in_specs=[pl.BlockSpec(memory_space=pltpu.SMEM), whole, whole, whole],
+        out_specs=[whole, whole, whole],
+        out_shape=[
+            jax.ShapeDtypeStruct((rows, width), F32),
+            jax.ShapeDtypeStruct((rows, width), F32),
+            jax.ShapeDtypeStruct((rows, width + HD), BF16),
+        ],
+        cost_estimate=pl.CostEstimate(
+            flops=8 * rows * width * members * rows,
+            transcendentals=2 * rows * heads * members * rows,
+            bytes_accessed=4 * members * rows * HD + 16 * rows * width,
+        ),
+        compiler_params=pltpu.CompilerParams(vmem_limit_bytes=48 << 20),
+        name="softmax_block",
+    )((lax.axis_index(HALF) * rows).astype(jnp.int32).reshape(1), queries, foreign, kv)
     got = lax.ppermute(message, "yh", [(0, 1)])
-    got_out = got[:, : heads * HD].astype(F32)
-    parts = got[:, heads * HD : heads * HD + 3 * heads].astype(F32)
+    parts = got[:, width : width + 3 * heads].astype(F32)
     got_lse = parts[:, :heads] + parts[:, heads : 2 * heads] + parts[:, 2 * heads :]
-    share = jnp.where(yh == 1, jax.nn.sigmoid(got_lse - lse_own), 0.0)
-    share = jnp.repeat(share, HD, axis=1)
-    return (out_own * (1.0 - share) + got_out * share).astype(BF16), early
+    share = jnp.where(yh == 1, jax.nn.sigmoid(jnp.repeat(got_lse, HD, axis=1) - lse), 0.0)
+    return (out * (1.0 - share) + got[:, :width].astype(F32) * share).astype(BF16), early
 
 
 def expand(order_ref, x_ref, o_ref, w_ref, wo_ref, *rest):
@@ -122,7 +141,7 @@
         ),
         compiler_params=pltpu.CompilerParams(vmem_limit_bytes=40 << 20),
         name="gate_up_terms",
-    )(order, x, other, w, wo)
+    )(order, x, other, *(pltpu.with_memory_space_constraint(v, pltpu.HBM) for v in (w, wo)))
 
 
 def contract_hidden(order_ref, h_ref, ho_ref, w_ref, out_ref):
@@ -242,14 +261,13 @@
 
     terms_a = gate_up_terms(order, x_a, swap(x_a, "c"), w_in, w_in_other, block)
     sums_a = over_yl(terms_a)
-    x_b = after(x_b, *sums_a[1:])
+    x_b = after(x_b, sums_a[3])
     inverse = from_row(x_b[:, block], 2 * block)
-    hidden_a = hidden_of(sums_a, inverse[:, :block])
-    x_b = after(x_b, hidden_a)
-    hids_a = over_yl([hidden_a] * 4)
     terms_b = gate_up_terms(order, x_b, swap(x_b, "c"), w_in, w_in_other, block)
-    hids_a[1] = after(hids_a[1], *terms_b)
+    sums_a[1] = after(sums_a[1], *terms_b)
+    hids_a = over_yl([hidden_of(sums_a, inverse[:, :block])] * 4)
     sums_b = over_yl(terms_b)
+    hids_a[1] = after(hids_a[1], sums_b[3])
     down_a = down_of(hids_a)
     back_a = give_back(down_a)
     sums_b[1] = after(sums_b[1], down_a)

time: 344 us -> 333 us (0.968)
  Pallas kernels: 16.3 us -> 23.8 us
  starting transfers between devices: 95.2 us -> 88.5 us
  matrix products: 6.29 us -> 1.12 us
    all_to_all x1, waiting for transfers between devices: 11.4 us -> 19.6 us  [attend(): lax.all_to_all(jnp.broadcast_to(kv[None], (members,) + kv.shape), HALF, s...]
    ppermute x1, waiting for transfers between devices: 7.59 us -> 0.01 us  [attend(): foreign = lax.ppermute(queries, 'yh', [(1, 0)])]
    all_to_all x4, starting transfers between devices: 24.7 us -> 18.4 us  [all_to_all(): return lax.all_to_all(x, axes, split_axis=0, concat_axis=0, tiled=True)]
    ppermute x12, waiting for transfers between devices: 76.9 us -> 70.7 us  [over_yl(): lax.ppermute(parts[i], 'yl', Y_XOR[i])]
    pallas_call x0 -> x1, Pallas kernels: none -> 5.88 us  [attend(): pl.pallas_call(softmax_block, in_specs=[pl.BlockSpec(memory_space=pltpu.S...]
    dot_general x2 -> x0, matrix products: 5.18 us -> none  [the longest x1 2.78 us: attend(): jnp.einsum('qk,kd->qd', weights.astype(BF16), v_all, preferred_element_ty...]
    all_to_all x4, waiting for transfers between devices: 52.3 us -> 56.4 us  [all_to_all(): return lax.all_to_all(x, axes, split_axis=0, concat_axis=0, tiled=True)]
where the time goes in v6:
time: 333 us; the launch traced here: 332 us
  waiting for transfers between devices  156 us (47%)
  starting transfers between devices  88.5 us (27%)
  blocking collectives  44.6 us (13%)
  Pallas kernels  23.8 us (7%)
  other arithmetic  9.18 us (3%)
  local copies, waits for them, and re-layouts  7.8 us (2%)
    ppermute x12, waiting for transfers between devices, over_yl(): lax.ppermute(parts[i], 'yl', Y_XOR[i])  70.7 us
    all_to_all x4, waiting for transfers between devices, all_to_all(): return lax.all_to_all(x, axes, split_axis=0, concat_axis=0, tiled=True)  56.4 us
    ppermute x12, starting transfers between devices, over_yl(): lax.ppermute(parts[i], 'yl', Y_XOR[i])  39.2 us
    all_to_all x2, blocking collectives, all_to_all(): return lax.all_to_all(x, axes, split_axis=0, concat_axis=0, tiled=True)  34 us
    all_to_all x1, waiting for transfers between devices, attend(): lax.all_to_all(jnp.broadcast_to(kv[None], (members,) + kv.shape), HALF, s...  19.6 us
    all_to_all x4, starting transfers between devices, all_to_all(): return lax.all_to_all(x, axes, split_axis=0, concat_axis=0, tiled=True)  18.4 us
    all_to_all x1, starting transfers between devices, attend(): lax.all_to_all(jnp.broadcast_to(kv[None], (members,) + kv.shape), HALF, s...  13.2 us
    pallas_call x2, Pallas kernels, gate_up_terms(): pl.pallas_call(expand, grid_spec=pltpu.PrefetchScalarGridSpec(num_scalar_...  12 us
  transfers between devices with their start and end apart: 24, of which 17 were waited for; matrix products, arithmetic and copies ran while one was open for 3% of the time, Pallas kernels for 5%

profile of v6, /device:TPU:8, one launch (start us, length us, event | category | flops | bytes accessed | tf_op | source)
XLA Modules:
  0.0 331.6 jit_solution(12804635196266177137)
XLA Ops:
  1.9 13.2 %all-to-all-start = ((bf16[32,64,256]{2,1,0:T(8,128)(2,1)}), bf16[32,64,256]{2,1,0:T(8,128)(2,1)S(1)}, u32[]{:S(2)}, u32[]{:S(2)}) async-start(bf16[32,64,256]{2,1,0:T(8,128)(2,1)} %broadcast_in_dim.32), calls=%async_computation | async-start | bytes 2097152 | tf_op jit(solution)/shard_map/all_to_all | solution.py:78
  24.0 19.6 %all-to-all-done = bf16[32,64,256]{2,1,0:T(8,128)(2,1)S(1)} async-done(((bf16[32,64,256]{2,1,0:T(8,128)(2,1)}), bf16[32,64,256]{2,1,0:T(8,128)(2,1)S(1)}, u32[]{:S(2)}, u32[]{:S(2)}) %all-to-all-start) | async-done | bytes 1048608 | tf_op jit(solution)/shard_map/all_to_all | solution.py:78
  43.7 5.9 %softmax_block.1 = (f32[64,768]{1,0:T(8,128)S(1)}, f32[64,768]{1,0:T(8,128)S(1)}, bf16[64,896]{1,0:T(8,128)(2,1)S(1)}) custom-call(s32[1]{0:T(128)} %bitcast.3.base_ref, bf16[64,768]{1,0:T(8,128)(2,1)S(1)} %copy-done.1, bf16[64,768]{1,0:T(8,128)(2,1)S(1)} %collective-permute-done.far_ref, bf16[2048,256]{1,0:T(8,128)(2,1)S(1)} %bitcast.50), custom_call_target="tpu_custom_call" | custom-call | flops 805306368 | bytes 1835008 | tf_op jit(solution)/shard_map/softmax_block/pallas_call | solution.py:83
  49.6 6.8 %collective-permute-start.2 = (bf16[64,896]{1,0:T(8,128)(2,1)S(1)}, bf16[64,896]{1,0:T(8,128)(2,1)S(1)}, u32[]{:S(2)}, u32[]{:S(2)}) collective-permute-start(bf16[64,896]{1,0:T(8,128)(2,1)S(1)} %get-tuple-element.28), channel_id=1, source_target_pairs={{0,256},{1,257},{2,258},{3,259},{4,260},{5,261},{6,262},{7,263},{8... | collective-permute-start | bytes 344072 | tf_op jit(solution)/shard_map/ppermute | solution.py:100
  60.8 20.1 %all_to_all.35 = bf16[8,32,768]{2,1,0:T(8,128)(2,1)S(1)} all-to-all(bf16[8,32,768]{2,1,0:T(8,128)(2,1)S(1)} %bitcast.51), channel_id=1, replica_groups=mesh['yh'=2,'xh'=2,'xl'=2,'z'=8,'yl'=4,'c'=2] {'yh','xh','xl'}, dimensions={0} | all-to-all | bytes 786432 | tf_op jit(solution)/shard_map/all_to_all | solution.py:228
  82.1 6.7 %all-to-all-start.2 = ((bf16[8,96,768]{2,1,0:T(8,128)(2,1)}), bf16[8,96,768]{2,1,0:T(8,128)(2,1)S(1)}, u32[]{:S(2)}, u32[]{:S(2)}) async-start(bf16[8,96,768]{2,1,0:T(8,128)(2,1)} %broadcast_in_dim.67), calls=%async_computation.2 | async-start | bytes 2359296 | tf_op jit(solution)/shard_map/all_to_all | solution.py:228
  89.2 10.6 %psum.7 = f32[192]{0:T(256)S(1)} all-reduce(f32[192]{0:T(256)S(1)} %reshape.107), channel_id=1, replica_groups=mesh['yh'=2,'xh'=2,'xl'=2,'z'=8,'yl'=4,'c'=2] {'yl','c'}, use_global_device_ids=true, to_apply=%region_4.5 | all-reduce | flops 192 | bytes 1536 | tf_op jit(solution)/shard_map/psum | solution.py:240
  99.8 20.6 %all-to-all-done.2.x_ref = bf16[8,96,768]{2,1,0:T(8,128)(2,1)S(1)} async-done(((bf16[8,96,768]{2,1,0:T(8,128)(2,1)}), bf16[8,96,768]{2,1,0:T(8,128)(2,1)S(1)}, u32[]{:S(2)}, u32[]{:S(2)}) %all-to-all-start.2) | async-done | bytes 1179680 | tf_op jit(solution)/shard_map/all_to_all | solution.py:228
  130.1 6.2 %gate_up_terms.2 = (bf16[192,1024]{1,0:T(8,128)(2,1)}, bf16[192,1024]{1,0:T(8,128)(2,1)}, bf16[192,1024]{1,0:T(8,128)(2,1)}, bf16[192,1024]{1,0:T(8,128)(2,1)}) custom-call(s32[2]{0:T(128)S(1)} %pad_add_fusion.order_ref, bf16[8,96,768]{2,1,0:T(8,128)(2,1)S(1)} %all-to-all-done.2.x_ref, bf16[8,96,768]{2,1,0:T(8,128)(2,1)} %collective-permute-done.3.o_ref, ...), custom_call_target="tpu_custom_call" | custom-call | flops 2415919104 | bytes 4718592 | tf_op jit(solution)/shard_map/gate_up_terms/pallas_call | solution.py:129
  138.2 15.1 %collective-permute-done.5 = bf16[192,1024]{1,0:T(8,128)(2,1)S(1)} collective-permute-done((bf16[192,1024]{1,0:T(8,128)(2,1)}, bf16[192,1024]{1,0:T(8,128)(2,1)S(1)}, u32[]{:S(2)}, u32[]{:S(2)}) %collective-permute-start.5) | collective-permute-done | bytes 393248 | tf_op jit(solution)/shard_map/ppermute | solution.py:245
  154.1 5.2 %all-to-all-done.3.x_ref = bf16[8,104,768]{2,1,0:T(8,128)(2,1)S(1)} async-done(((bf16[8,104,768]{2,1,0:T(8,128)(2,1)}), bf16[8,104,768]{2,1,0:T(8,128)(2,1)S(1)}, u32[]{:S(2)}, u32[]{:S(2)}) %all-to-all-start.3) | async-done | bytes 1277984 | tf_op jit(solution)/shard_map/all_to_all | solution.py:228
  165.3 5.8 %gate_up_terms.3 = (bf16[192,1024]{1,0:T(8,128)(2,1)}, bf16[192,1024]{1,0:T(8,128)(2,1)}, bf16[192,1024]{1,0:T(8,128)(2,1)}, bf16[192,1024]{1,0:T(8,128)(2,1)}) custom-call(s32[2]{0:T(128)S(1)} %pad_add_fusion.order_ref, bf16[8,104,768]{2,1,0:T(8,128)(2,1)S(1)} %all-to-all-done.3.x_ref, bf16[8,104,768]{2,1,0:T(8,128)(2,1)S(1)} %collective-permute-done.6.o_ref, ...), custom_call_target="tpu_custom_call" | custom-call | flops 2415919104 | bytes 4718592 | tf_op jit(solution)/shard_map/gate_up_terms/pallas_call | solution.py:129
  171.2 5.4 %collective-permute-start.9 = (bf16[192,1024]{1,0:T(8,128)(2,1)}, bf16[192,1024]{1,0:T(8,128)(2,1)S(1)}, u32[]{:S(2)}, u32[]{:S(2)}) collective-permute-start(bf16[192,1024]{1,0:T(8,128)(2,1)} %get-tuple-element.41), channel_id=1, source_target_pairs={{0,6},{2,4},{4,2},{6,0},{1,7},{3,5},{5,3},{7,1},{8,14},{10,12},{12... | collective-permute-start | bytes 1179656 | tf_op jit(solution)/shard_map/ppermute | solution.py:245
  176.5 15.2 %collective-permute-done.7 = bf16[192,1024]{1,0:T(8,128)(2,1)} collective-permute-done((bf16[192,1024]{1,0:T(8,128)(2,1)}, bf16[192,1024]{1,0:T(8,128)(2,1)}, u32[]{:S(2)}, u32[]{:S(2)}) %collective-permute-start.7) | collective-permute-done | bytes 393248 | tf_op jit(solution)/shard_map/ppermute | solution.py:245
  193.2 6.5 %collective-permute-start.8 = (bf16[192,512]{1,0:T(8,128)(2,1)S(1)}, bf16[192,512]{1,0:T(8,128)(2,1)S(1)}, u32[]{:S(2)}, u32[]{:S(2)}) collective-permute-start(bf16[192,512]{1,0:T(8,128)(2,1)S(1)} %fusion.3), channel_id=1, source_target_pairs={{0,2},{2,0},{4,6},{6,4},{1,3},{3,1},{5,7},{7,5},{8,10},{10,8},{12,... | collective-permute-start | bytes 589832 | tf_op jit(solution)/shard_map/ppermute | solution.py:245
  205.3 9.9 %collective-permute-done.10 = bf16[192,512]{1,0:T(8,128)(2,1)S(1)} collective-permute-done((bf16[192,512]{1,0:T(8,128)(2,1)S(1)}, bf16[192,512]{1,0:T(8,128)(2,1)S(1)}, u32[]{:S(2)}, u32[]{:S(2)}) %collective-permute-start.10) | collective-permute-done | bytes 196640 | tf_op jit(solution)/shard_map/ppermute | solution.py:245
  215.3 5.2 %collective-permute-done.11 = bf16[192,512]{1,0:T(8,128)(2,1)S(1)} collective-permute-done((bf16[192,512]{1,0:T(8,128)(2,1)S(1)}, bf16[192,512]{1,0:T(8,128)(2,1)S(1)}, u32[]{:S(2)}, u32[]{:S(2)}) %collective-permute-start.11) | collective-permute-done | bytes 196640 | tf_op jit(solution)/shard_map/ppermute | solution.py:245
  231.2 4.6 %all-to-all-start.4 = ((bf16[8,96,768]{2,1,0:T(8,128)(2,1)}), bf16[8,96,768]{2,1,0:T(8,128)(2,1)}, u32[]{:S(2)}, u32[]{:S(2)}) async-start(bf16[8,96,768]{2,1,0:T(8,128)(2,1)} %bitcast.11), calls=%async_computation.4 | async-start | bytes 2359296 | tf_op jit(solution)/shard_map/all_to_all | solution.py:228
  239.3 6.5 %collective-permute-done.14 = bf16[192,1024]{1,0:T(8,128)(2,1)S(1)} collective-permute-done((bf16[192,1024]{1,0:T(8,128)(2,1)}, bf16[192,1024]{1,0:T(8,128)(2,1)S(1)}, u32[]{:S(2)}, u32[]{:S(2)}) %collective-permute-start.14) | collective-permute-done | bytes 393248 | tf_op jit(solution)/shard_map/ppermute | solution.py:245
  248.0 5.2 %collective-permute-start.15 = (bf16[192,512]{1,0:T(8,128)(2,1)S(1)}, bf16[192,512]{1,0:T(8,128)(2,1)S(1)}, u32[]{:S(2)}, u32[]{:S(2)}) collective-permute-start(bf16[192,512]{1,0:T(8,128)(2,1)S(1)} %fusion.2), channel_id=1, source_target_pairs={{0,2},{2,0},{4,6},{6,4},{1,3},{3,1},{5,7},{7,5},{8,10},{10,8},{12,... | collective-permute-start | bytes 589832 | tf_op jit(solution)/shard_map/ppermute | solution.py:245
  258.6 10.2 %collective-permute-done.16 = bf16[192,512]{1,0:T(8,128)(2,1)S(1)} collective-permute-done((bf16[192,512]{1,0:T(8,128)(2,1)S(1)}, bf16[192,512]{1,0:T(8,128)(2,1)S(1)}, u32[]{:S(2)}, u32[]{:S(2)}) %collective-permute-start.16) | collective-permute-done | bytes 196640 | tf_op jit(solution)/shard_map/ppermute | solution.py:245
  268.8 4.8 %collective-permute-done.17 = bf16[192,512]{1,0:T(8,128)(2,1)S(1)} collective-permute-done((bf16[192,512]{1,0:T(8,128)(2,1)S(1)}, bf16[192,512]{1,0:T(8,128)(2,1)S(1)}, u32[]{:S(2)}, u32[]{:S(2)}) %collective-permute-start.17) | collective-permute-done | bytes 196640 | tf_op jit(solution)/shard_map/ppermute | solution.py:245
  285.8 30.6 %all-to-all-done.5 = bf16[8,96,768]{2,1,0:T(8,128)(2,1)S(1)} async-done(((bf16[8,96,768]{2,1,0:T(8,128)(2,1)}), bf16[8,96,768]{2,1,0:T(8,128)(2,1)S(1)}, u32[]{:S(2)}, u32[]{:S(2)}) %all-to-all-start.5) | async-done | bytes 1179680 | tf_op jit(solution)/shard_map/all_to_all | solution.py:228
  316.7 13.9 %all_to_all.36 = bf16[8,24,768]{2,1,0:T(8,128)(2,1)S(1)} all-to-all(bf16[8,24,768]{2,1,0:T(8,128)(2,1)S(1)} %pad_maximum_fusion.4), channel_id=1, replica_groups=mesh['yh'=2,'xh'=2,'xl'=2,'z'=8,'yl'=4,'c'=2] {'yh','xh','xl'}, dimensions={0} | all-to-all | bytes 589824 | tf_op jit(solution)/shard_map/all_to_all | solution.py:228
  (113 shorter events, 77.4 us)
Async XLA Ops:
  1.9 41.8 %all-to-all-start = ((bf16[32,64,256]{2,1,0:T(8,128)(2,1)}), bf16[32,64,256]{2,1,0:T(8,128)(2,1)S(1)}, u32[]{:S(2)}, u32[]{:S(2)}) async-start(bf16[32,64,256]{2,1,0:T(8,128)(2,1)} %broadcast_in_dim.32), calls=%async_computation | async-start | bytes 2097152 | tf_op jit(solution)/shard_map/all_to_all | solution.py:78
  18.4 5.6 %collective-permute-start.1 = (bf16[1024,768]{1,0:T(8,128)(2,1)}, bf16[1024,768]{1,0:T(8,128)(2,1)}, u32[]{:S(2)}, u32[]{:S(2)}) collective-permute-start(bf16[1024,768]{1,0:T(8,128)(2,1)} %pad_maximum_fusion.1), channel_id=1, source_target_pairs={{0,1},{1,0},{2,3},{3,2},{4,5},{5,4},{6,7},{7,6},{8,9},{9,8},{10,11... | collective-permute-start | bytes 4718600 | tf_op jit(solution)/shard_map/ppermute | solution.py:27
  20.3 23.4 %collective-permute-start = (bf16[64,768]{1,0:T(8,128)(2,1)S(1)}, bf16[64,768]{1,0:T(8,128)(2,1)S(1)}, u32[]{:S(2)}, u32[]{:S(2)}) collective-permute-start(bf16[64,768]{1,0:T(8,128)(2,1)S(1)} %copy-done.1), channel_id=1, source_target_pairs={{256,0},{257,1},{258,2},{259,3},{260,4},{261,5},{262,6},{263,7},{2... | collective-permute-start | bytes 294920 | tf_op jit(solution)/shard_map/ppermute | solution.py:75
  49.6 10.4 %collective-permute-start.2 = (bf16[64,896]{1,0:T(8,128)(2,1)S(1)}, bf16[64,896]{1,0:T(8,128)(2,1)S(1)}, u32[]{:S(2)}, u32[]{:S(2)}) collective-permute-start(bf16[64,896]{1,0:T(8,128)(2,1)S(1)} %get-tuple-element.28), channel_id=1, source_target_pairs={{0,256},{1,257},{2,258},{3,259},{4,260},{5,261},{6,262},{7,263},{8... | collective-permute-start | bytes 344072 | tf_op jit(solution)/shard_map/ppermute | solution.py:100
  82.1 38.3 %all-to-all-start.2 = ((bf16[8,96,768]{2,1,0:T(8,128)(2,1)}), bf16[8,96,768]{2,1,0:T(8,128)(2,1)S(1)}, u32[]{:S(2)}, u32[]{:S(2)}) async-start(bf16[8,96,768]{2,1,0:T(8,128)(2,1)} %broadcast_in_dim.67), calls=%async_computation.2 | async-start | bytes 2359296 | tf_op jit(solution)/shard_map/all_to_all | solution.py:228
  121.6 37.6 %all-to-all-start.3 = ((bf16[8,104,768]{2,1,0:T(8,128)(2,1)}), bf16[8,104,768]{2,1,0:T(8,128)(2,1)S(1)}, u32[]{:S(2)}, u32[]{:S(2)}) async-start(bf16[8,104,768]{2,1,0:T(8,128)(2,1)} %broadcast_in_dim.69), calls=%async_computation.3 | async-start | bytes 2555904 | tf_op jit(solution)/shard_map/all_to_all | solution.py:228
  125.2 4.9 %collective-permute-start.3 = (bf16[8,96,768]{2,1,0:T(8,128)(2,1)S(1)}, bf16[8,96,768]{2,1,0:T(8,128)(2,1)}, u32[]{:S(2)}, u32[]{:S(2)}) collective-permute-start(bf16[8,96,768]{2,1,0:T(8,128)(2,1)S(1)} %all-to-all-done.2.x_ref), channel_id=1, source_target_pairs={{0,1},{1,0},{2,3},{3,2},{4,5},{5,4},{6,7},{7,6},{8,9},{9,8},{10,11... | collective-permute-start | bytes 3538952 | tf_op jit(solution)/shard_map/ppermute | solution.py:27
  136.3 17.0 %collective-permute-start.5 = (bf16[192,1024]{1,0:T(8,128)(2,1)}, bf16[192,1024]{1,0:T(8,128)(2,1)S(1)}, u32[]{:S(2)}, u32[]{:S(2)}) collective-permute-start(bf16[192,1024]{1,0:T(8,128)(2,1)} %get-tuple-element.36), channel_id=1, source_target_pairs={{0,6},{2,4},{4,2},{6,0},{1,7},{3,5},{5,3},{7,1},{8,14},{10,12},{12... | collective-permute-start | bytes 1179656 | tf_op jit(solution)/shard_map/ppermute | solution.py:245
  159.3 6.1 %collective-permute-start.6 = (bf16[8,104,768]{2,1,0:T(8,128)(2,1)S(1)}, bf16[8,104,768]{2,1,0:T(8,128)(2,1)S(1)}, u32[]{:S(2)}, u32[]{:S(2)}) collective-permute-start(bf16[8,104,768]{2,1,0:T(8,128)(2,1)S(1)} %all-to-all-done.3.x_ref), channel_id=1, source_target_pairs={{0,1},{1,0},{2,3},{3,2},{4,5},{5,4},{6,7},{7,6},{8,9},{9,8},{10,11... | collective-permute-start | bytes 3833864 | tf_op jit(solution)/shard_map/ppermute | solution.py:27
  161.2 15.3 %collective-permute-start.4 = (bf16[192,1024]{1,0:T(8,128)(2,1)}, bf16[192,1024]{1,0:T(8,128)(2,1)}, u32[]{:S(2)}, u32[]{:S(2)}) collective-permute-start(bf16[192,1024]{1,0:T(8,128)(2,1)} %get-tuple-element.34), channel_id=1, source_target_pairs={{0,2},{2,0},{4,6},{6,4},{1,3},{3,1},{5,7},{7,5},{8,10},{10,8},{12,... | collective-permute-start | bytes 1179656 | tf_op jit(solution)/shard_map/ppermute | solution.py:245
  163.1 28.6 %collective-permute-start.7 = (bf16[192,1024]{1,0:T(8,128)(2,1)}, bf16[192,1024]{1,0:T(8,128)(2,1)}, u32[]{:S(2)}, u32[]{:S(2)}) collective-permute-start(bf16[192,1024]{1,0:T(8,128)(2,1)} %get-tuple-element.43), channel_id=1, source_target_pairs={{0,4},{2,6},{4,0},{6,2},{1,5},{3,7},{5,1},{7,3},{8,12},{10,14},{12... | collective-permute-start | bytes 1179656 | tf_op jit(solution)/shard_map/ppermute | solution.py:245
  171.2 34.2 %collective-permute-start.9 = (bf16[192,1024]{1,0:T(8,128)(2,1)}, bf16[192,1024]{1,0:T(8,128)(2,1)S(1)}, u32[]{:S(2)}, u32[]{:S(2)}) collective-permute-start(bf16[192,1024]{1,0:T(8,128)(2,1)} %get-tuple-element.41), channel_id=1, source_target_pairs={{0,6},{2,4},{4,2},{6,0},{1,7},{3,5},{5,3},{7,1},{8,14},{10,12},{12... | collective-permute-start | bytes 1179656 | tf_op jit(solution)/shard_map/ppermute | solution.py:245
  193.2 12.2 %collective-permute-start.8 = (bf16[192,512]{1,0:T(8,128)(2,1)S(1)}, bf16[192,512]{1,0:T(8,128)(2,1)S(1)}, u32[]{:S(2)}, u32[]{:S(2)}) collective-permute-start(bf16[192,512]{1,0:T(8,128)(2,1)S(1)} %fusion.3), channel_id=1, source_target_pairs={{0,2},{2,0},{4,6},{6,4},{1,3},{3,1},{5,7},{7,5},{8,10},{10,8},{12,... | collective-permute-start | bytes 589832 | tf_op jit(solution)/shard_map/ppermute | solution.py:245
  199.6 15.6 %collective-permute-start.10 = (bf16[192,512]{1,0:T(8,128)(2,1)S(1)}, bf16[192,512]{1,0:T(8,128)(2,1)S(1)}, u32[]{:S(2)}, u32[]{:S(2)}) collective-permute-start(bf16[192,512]{1,0:T(8,128)(2,1)S(1)} %fusion.3), channel_id=1, source_target_pairs={{0,4},{2,6},{4,0},{6,2},{1,5},{3,7},{5,1},{7,3},{8,12},{10,14},{12... | collective-permute-start | bytes 589832 | tf_op jit(solution)/shard_map/ppermute | solution.py:245
  201.6 18.9 %collective-permute-start.11 = (bf16[192,512]{1,0:T(8,128)(2,1)S(1)}, bf16[192,512]{1,0:T(8,128)(2,1)S(1)}, u32[]{:S(2)}, u32[]{:S(2)}) collective-permute-start(bf16[192,512]{1,0:T(8,128)(2,1)S(1)} %fusion.3), channel_id=1, source_target_pairs={{0,6},{2,4},{4,2},{6,0},{1,7},{3,5},{5,3},{7,1},{8,14},{10,12},{12... | collective-permute-start | bytes 589832 | tf_op jit(solution)/shard_map/ppermute | solution.py:245
  220.5 7.8 %collective-permute-start.12 = (bf16[768,512]{1,0:T(8,128)(2,1)S(1)}, bf16[768,512]{1,0:T(8,128)(2,1)S(1)}, u32[]{:S(2)}, u32[]{:S(2)}) collective-permute-start(bf16[768,512]{1,0:T(8,128)(2,1)S(1)} %pad_maximum_fusion.2.h_ref), channel_id=1, source_target_pairs={{0,1},{1,0},{2,3},{3,2},{4,5},{5,4},{6,7},{7,6},{8,9},{9,8},{10,11... | collective-permute-start | bytes 2359304 | tf_op jit(solution)/shard_map/ppermute | solution.py:27
  222.4 16.9 %collective-permute-start.13 = (bf16[192,1024]{1,0:T(8,128)(2,1)}, bf16[192,1024]{1,0:T(8,128)(2,1)}, u32[]{:S(2)}, u32[]{:S(2)}) collective-permute-start(bf16[192,1024]{1,0:T(8,128)(2,1)} %get-tuple-element.39), channel_id=1, source_target_pairs={{0,2},{2,0},{4,6},{6,4},{1,3},{3,1},{5,7},{7,5},{8,10},{10,8},{12,... | collective-permute-start | bytes 1179656 | tf_op jit(solution)/shard_map/ppermute | solution.py:245
  224.4 21.4 %collective-permute-start.14 = (bf16[192,1024]{1,0:T(8,128)(2,1)}, bf16[192,1024]{1,0:T(8,128)(2,1)S(1)}, u32[]{:S(2)}, u32[]{:S(2)}) collective-permute-start(bf16[192,1024]{1,0:T(8,128)(2,1)} %get-tuple-element.40), channel_id=1, source_target_pairs={{0,4},{2,6},{4,0},{6,2},{1,5},{3,7},{5,1},{7,3},{8,12},{10,14},{12... | collective-permute-start | bytes 1179656 | tf_op jit(solution)/shard_map/ppermute | solution.py:245
  231.2 49.5 %all-to-all-start.4 = ((bf16[8,96,768]{2,1,0:T(8,128)(2,1)}), bf16[8,96,768]{2,1,0:T(8,128)(2,1)}, u32[]{:S(2)}, u32[]{:S(2)}) async-start(bf16[8,96,768]{2,1,0:T(8,128)(2,1)} %bitcast.11), calls=%async_computation.4 | async-start | bytes 2359296 | tf_op jit(solution)/shard_map/all_to_all | solution.py:228
  248.0 10.6 %collective-permute-start.15 = (bf16[192,512]{1,0:T(8,128)(2,1)S(1)}, bf16[192,512]{1,0:T(8,128)(2,1)S(1)}, u32[]{:S(2)}, u32[]{:S(2)}) collective-permute-start(bf16[192,512]{1,0:T(8,128)(2,1)S(1)} %fusion.2), channel_id=1, source_target_pairs={{0,2},{2,0},{4,6},{6,4},{1,3},{3,1},{5,7},{7,5},{8,10},{10,8},{12,... | collective-permute-start | bytes 589832 | tf_op jit(solution)/shard_map/ppermute | solution.py:245
  253.2 15.6 %collective-permute-start.16 = (bf16[192,512]{1,0:T(8,128)(2,1)S(1)}, bf16[192,512]{1,0:T(8,128)(2,1)S(1)}, u32[]{:S(2)}, u32[]{:S(2)}) collective-permute-start(bf16[192,512]{1,0:T(8,128)(2,1)S(1)} %fusion.2), channel_id=1, source_target_pairs={{0,4},{2,6},{4,0},{6,2},{1,5},{3,7},{5,1},{7,3},{8,12},{10,14},{12... | collective-permute-start | bytes 589832 | tf_op jit(solution)/shard_map/ppermute | solution.py:245
  255.2 18.4 %collective-permute-start.17 = (bf16[192,512]{1,0:T(8,128)(2,1)S(1)}, bf16[192,512]{1,0:T(8,128)(2,1)S(1)}, u32[]{:S(2)}, u32[]{:S(2)}) collective-permute-start(bf16[192,512]{1,0:T(8,128)(2,1)S(1)} %fusion.2), channel_id=1, source_target_pairs={{0,6},{2,4},{4,2},{6,0},{1,7},{3,5},{5,3},{7,1},{8,14},{10,12},{12... | collective-permute-start | bytes 589832 | tf_op jit(solution)/shard_map/ppermute | solution.py:245
  273.6 4.2 %collective-permute-start.18 = (bf16[768,512]{1,0:T(8,128)(2,1)S(1)}, bf16[768,512]{1,0:T(8,128)(2,1)S(1)}, u32[]{:S(2)}, u32[]{:S(2)}) collective-permute-start(bf16[768,512]{1,0:T(8,128)(2,1)S(1)} %pad_maximum_fusion.3.h_ref), channel_id=1, source_target_pairs={{0,1},{1,0},{2,3},{3,2},{4,5},{5,4},{6,7},{7,6},{8,9},{9,8},{10,11... | collective-permute-start | bytes 2359304 | tf_op jit(solution)/shard_map/ppermute | solution.py:27
  280.8 35.6 %all-to-all-start.5 = ((bf16[8,96,768]{2,1,0:T(8,128)(2,1)}), bf16[8,96,768]{2,1,0:T(8,128)(2,1)S(1)}, u32[]{:S(2)}, u32[]{:S(2)}) async-start(bf16[8,96,768]{2,1,0:T(8,128)(2,1)} %bitcast.13), calls=%async_computation.5 | async-start | bytes 2359296 | tf_op jit(solution)/shard_map/all_to_all | solution.py:228
  (11 other events, 190.9 us)

commit v7 on v6

--- a/solution.py
+++ b/solution.py
@@ -105,14 +105,14 @@
 
 
 def expand(order_ref, x_ref, o_ref, w_ref, wo_ref, *rest):
-    out_refs, acc_ref = rest[:4], rest[4]
+    keep_ref, pair_ref, send_ref, acc_ref = rest
     contract = (((1,), (1,)), ((), ()))
     x, o = (r[...].reshape(acc_ref.shape[0], r.shape[-1]) for r in (x_ref, o_ref))
     acc_ref[...] = lax.dot_general(x, w_ref[...], contract, preferred_element_type=F32) + lax.dot_general(
         o, wo_ref[...], contract, preferred_element_type=F32
     )
-    share = out_refs[0].shape[0]
-    for i, ref in enumerate(out_refs):
+    share = keep_ref.shape[0]
+    for i, ref in enumerate((keep_ref, send_ref.at[:share], pair_ref, send_ref.at[share:])):
         at = pl.multiple_of((order_ref[0] ^ i) * share, share)
         ref[...] = acc_ref[pl.ds(at, share), :].astype(BF16)
 
@@ -124,18 +124,17 @@
     share = rows // 4
     spec = pl.BlockSpec((x.shape[0], block, feat), lambda n, o: (0, 0, 0))
     weight = pl.BlockSpec((cols, feat), lambda n, o: (n, 0))
-    out = pl.BlockSpec((share, cols), lambda n, o: (0, n))
-    shape = pltpu.HBM((share, hidden), BF16)
+    blocks = (share, share, 2 * share)
     return pl.pallas_call(
         expand,
         grid_spec=pltpu.PrefetchScalarGridSpec(
             num_scalar_prefetch=1,
             grid=(2,),
             in_specs=[spec, spec, weight, weight],
-            out_specs=[out] * 4,
+            out_specs=[pl.BlockSpec((b, cols), lambda n, o: (0, n)) for b in blocks],
             scratch_shapes=[pltpu.VMEM((rows, cols), F32)],
         ),
-        out_shape=[shape] * 4,
+        out_shape=[pltpu.HBM((b, hidden), BF16) for b in blocks],
         cost_estimate=pl.CostEstimate(
             flops=4 * rows * hidden * feat, transcendentals=0, bytes_accessed=4 * hidden * feat + 2 * rows * hidden
         ),
@@ -152,9 +151,9 @@
     acc = jnp.dot(h_ref[...], w_ref[pl.ds(own, half), :], preferred_element_type=F32)
     acc += jnp.dot(ho_ref[...], w_ref[pl.ds(other, half), :], preferred_element_type=F32)
     share = h_ref.shape[0] // 4
-    for i in range(4):
+    for k, i in enumerate((0, 2, 1, 3)):
         at = pl.multiple_of((order_ref[0] ^ i) * share, share)
-        out_ref[pl.ds(at, share), :] = acc[i * share : (i + 1) * share].astype(BF16)
+        out_ref[pl.ds(at, share), :] = acc[k * share : (k + 1) * share].astype(BF16)
 
 
 def down_terms(order, h, ho, w):
@@ -241,16 +240,23 @@
     x_a, inverse = lax.optimization_barrier((x_a, inverse))
     x_b = along_z(jnp.concatenate([part_b, as_rows(inverse, feat)], axis=0))
 
-    def over_yl(parts):
-        return [parts[0]] + [lax.ppermute(parts[i], "yl", Y_XOR[i]) for i in range(1, 4)]
-
-    def hidden_of(parts, inverse):
+    def neighbour(x):
+        return lax.ppermute(x, "yl", Y_XOR[1])
+
+    def across(x):
+        return lax.ppermute(x, "yl", Y_XOR[2])
+
+    def pair_of(terms, got):
+        return (terms[1].astype(F32) + got[got.shape[0] // 2 :].astype(F32)).astype(BF16)
+
+    def hidden_of(terms, got, last, inverse):
         inverse = lax.dynamic_index_in_dim(inverse.reshape(4, -1), me, 0, keepdims=False)
-        full = sum(p.astype(F32) for p in parts) * inverse[:, None]
+        full = terms[0].astype(F32) + got[: got.shape[0] // 2].astype(F32) + last.astype(F32)
+        full = full * inverse[:, None]
         return (jax.nn.silu(full[:, :half]) * full[:, half:]).astype(BF16)
 
-    def down_of(parts):
-        hid = jnp.concatenate(parts, axis=0)
+    def down_of(two, other_two):
+        hid = jnp.concatenate([two, other_two], axis=0)
         return down_terms(order, hid, swap(hid, "c"), w_down)
 
     def give_back(down):
@@ -260,20 +266,23 @@
         return jnp.sum(back.astype(F32), axis=0).astype(BF16).reshape(sources, n, feat)
 
     terms_a = gate_up_terms(order, x_a, swap(x_a, "c"), w_in, w_in_other, block)
-    sums_a = over_yl(terms_a)
-    x_b = after(x_b, sums_a[3])
+    got_a = neighbour(terms_a[2])
+    x_b = after(x_b, got_a)
     inverse = from_row(x_b[:, block], 2 * block)
+    last_a = across(pair_of(terms_a, got_a))
     terms_b = gate_up_terms(order, x_b, swap(x_b, "c"), w_in, w_in_other, block)
-    sums_a[1] = after(sums_a[1], *terms_b)
-    hids_a = over_yl([hidden_of(sums_a, inverse[:, :block])] * 4)
-    sums_b = over_yl(terms_b)
-    hids_a[1] = after(hids_a[1], sums_b[3])
-    down_a = down_of(hids_a)
+    last_a = after(last_a, *terms_b)
+    hidden_a = hidden_of(terms_a, got_a, last_a, inverse[:, :block])
+    got_b = neighbour(terms_b[2])
+    two_a = jnp.concatenate([hidden_a, after(across(hidden_a), got_b)], axis=0)
+    last_b = across(pair_of(terms_b, got_b))
+    down_a = down_of(two_a, after(neighbour(two_a), last_b))
     back_a = give_back(down_a)
-    sums_b[1] = after(sums_b[1], down_a)
-    hids_b = over_yl([hidden_of(sums_b, inverse[:, block:])] * 4)
-    back_a = after(back_a, *hids_b[1:])
-    back_b = give_back(down_of(hids_b))
+    hidden_b = hidden_of(terms_b, got_b, last_b, inverse[:, block:])
+    two_b = jnp.concatenate([hidden_b, after(across(hidden_b), down_a)], axis=0)
+    other_two_b = neighbour(two_b)
+    back_a = after(back_a, other_two_b)
+    back_b = give_back(down_of(two_b, other_two_b))
     returned = all_to_all(jnp.concatenate([over_z(back_a), over_z(back_b)], axis=1), GROUP)
     returned = jnp.sum(returned.reshape(EXPERTS, 2, CAP, feat).astype(F32), axis=1)
     moe_rows = jnp.einsum(

time: 333 us -> 337 us (1.012)
  blocking collectives: 44.6 us -> 48.4 us
    ppermute x12 -> x8, starting transfers between devices: 39.2 us -> 30.2 us  [the longest x4 16.7 us: across(): return lax.ppermute(x, 'yl', Y_XOR[2])]
    all_to_all x4, starting transfers between devices: 18.4 us -> 24.5 us  [all_to_all(): return lax.all_to_all(x, axes, split_axis=0, concat_axis=0, tiled=True)]
    ppermute x12 -> x8, waiting for transfers between devices: 70.7 us -> 75.1 us  [the longest x4 41.9 us: neighbour(): return lax.ppermute(x, 'yl', Y_XOR[1])]
    all_to_all x4, waiting for transfers between devices: 56.4 us -> 52.2 us  [all_to_all(): return lax.all_to_all(x, axes, split_axis=0, concat_axis=0, tiled=True)]
    all_to_all x2, blocking collectives: 34 us -> 37.8 us  [all_to_all(): return lax.all_to_all(x, axes, split_axis=0, concat_axis=0, tiled=True)]
  transfers between devices with their start and end apart: 24 -> 20, of which waited for: 17 -> 17; matrix products, arithmetic and copies ran while one was open for 3% -> 4% of each run, Pallas kernels for 5% -> 4%
where the time goes in v7:
time: 337 us; the launch traced here: 336 us
  waiting for transfers between devices  158 us (47%)
  starting transfers between devices  85.6 us (25%)
  blocking collectives  48.4 us (14%)
  Pallas kernels  23.8 us (7%)
  other arithmetic  11.1 us (3%)
  local copies, waits for them, and re-layouts  7.02 us (2%)
    all_to_all x4, waiting for transfers between devices, all_to_all(): return lax.all_to_all(x, axes, split_axis=0, concat_axis=0, tiled=True)  52.2 us
    ppermute x4, waiting for transfers between devices, neighbour(): return lax.ppermute(x, 'yl', Y_XOR[1])  41.9 us
    all_to_all x2, blocking collectives, all_to_all(): return lax.all_to_all(x, axes, split_axis=0, concat_axis=0, tiled=True)  37.8 us
    ppermute x4, waiting for transfers between devices, across(): return lax.ppermute(x, 'yl', Y_XOR[2])  33.2 us
    all_to_all x4, starting transfers between devices, all_to_all(): return lax.all_to_all(x, axes, split_axis=0, concat_axis=0, tiled=True)  24.5 us
    all_to_all x1, waiting for transfers between devices, attend(): lax.all_to_all(jnp.broadcast_to(kv[None], (members,) + kv.shape), HALF, s...  19.6 us
    ppermute x4, starting transfers between devices, across(): return lax.ppermute(x, 'yl', Y_XOR[2])  16.7 us
    ppermute x4, starting transfers between devices, neighbour(): return lax.ppermute(x, 'yl', Y_XOR[1])  13.5 us
  transfers between devices with their start and end apart: 20, of which 17 were waited for; matrix products, arithmetic and copies ran while one was open for 4% of the time, Pallas kernels for 4%

profile of v7, /device:TPU:8, one launch (start us, length us, event | category | flops | bytes accessed | tf_op | source)
XLA Modules:
  0.0 336.0 jit_solution(11519383969771243014)
XLA Ops:
  1.9 13.2 %all-to-all-start = ((bf16[32,64,256]{2,1,0:T(8,128)(2,1)}), bf16[32,64,256]{2,1,0:T(8,128)(2,1)S(1)}, u32[]{:S(2)}, u32[]{:S(2)}) async-start(bf16[32,64,256]{2,1,0:T(8,128)(2,1)} %broadcast_in_dim.32), calls=%async_computation | async-start | bytes 2097152 | tf_op jit(solution)/shard_map/all_to_all | solution.py:78
  24.0 19.6 %all-to-all-done = bf16[32,64,256]{2,1,0:T(8,128)(2,1)S(1)} async-done(((bf16[32,64,256]{2,1,0:T(8,128)(2,1)}), bf16[32,64,256]{2,1,0:T(8,128)(2,1)S(1)}, u32[]{:S(2)}, u32[]{:S(2)}) %all-to-all-start) | async-done | bytes 1048608 | tf_op jit(solution)/shard_map/all_to_all | solution.py:78
  43.7 5.9 %softmax_block.1 = (f32[64,768]{1,0:T(8,128)S(1)}, f32[64,768]{1,0:T(8,128)S(1)}, bf16[64,896]{1,0:T(8,128)(2,1)S(1)}) custom-call(s32[1]{0:T(128)} %bitcast.3.base_ref, bf16[64,768]{1,0:T(8,128)(2,1)S(1)} %copy-done.1, bf16[64,768]{1,0:T(8,128)(2,1)S(1)} %collective-permute-done.far_ref, bf16[2048,256]{1,0:T(8,128)(2,1)S(1)} %bitcast.50), custom_call_target="tpu_custom_call" | custom-call | flops 805306368 | bytes 1835008 | tf_op jit(solution)/shard_map/softmax_block/pallas_call | solution.py:83
  49.6 6.8 %collective-permute-start.2 = (bf16[64,896]{1,0:T(8,128)(2,1)S(1)}, bf16[64,896]{1,0:T(8,128)(2,1)S(1)}, u32[]{:S(2)}, u32[]{:S(2)}) collective-permute-start(bf16[64,896]{1,0:T(8,128)(2,1)S(1)} %get-tuple-element.27), channel_id=1, source_target_pairs={{0,256},{1,257},{2,258},{3,259},{4,260},{5,261},{6,262},{7,263},{8... | collective-permute-start | bytes 344072 | tf_op jit(solution)/shard_map/ppermute | solution.py:100
  60.8 20.1 %all_to_all.35 = bf16[8,32,768]{2,1,0:T(8,128)(2,1)S(1)} all-to-all(bf16[8,32,768]{2,1,0:T(8,128)(2,1)S(1)} %bitcast.51), channel_id=1, replica_groups=mesh['yh'=2,'xh'=2,'xl'=2,'z'=8,'yl'=4,'c'=2] {'yh','xh','xl'}, dimensions={0} | all-to-all | bytes 786432 | tf_op jit(solution)/shard_map/all_to_all | solution.py:227
  82.1 6.7 %all-to-all-start.2 = ((bf16[8,96,768]{2,1,0:T(8,128)(2,1)}), bf16[8,96,768]{2,1,0:T(8,128)(2,1)S(1)}, u32[]{:S(2)}, u32[]{:S(2)}) async-start(bf16[8,96,768]{2,1,0:T(8,128)(2,1)} %broadcast_in_dim.67), calls=%async_computation.2 | async-start | bytes 2359296 | tf_op jit(solution)/shard_map/all_to_all | solution.py:227
  89.2 10.6 %psum.7 = f32[192]{0:T(256)S(1)} all-reduce(f32[192]{0:T(256)S(1)} %reshape.107), channel_id=1, replica_groups=mesh['yh'=2,'xh'=2,'xl'=2,'z'=8,'yl'=4,'c'=2] {'yl','c'}, use_global_device_ids=true, to_apply=%region_4.5 | all-reduce | flops 192 | bytes 1536 | tf_op jit(solution)/shard_map/psum | solution.py:239
  99.8 20.6 %all-to-all-done.2.x_ref = bf16[8,96,768]{2,1,0:T(8,128)(2,1)S(1)} async-done(((bf16[8,96,768]{2,1,0:T(8,128)(2,1)}), bf16[8,96,768]{2,1,0:T(8,128)(2,1)S(1)}, u32[]{:S(2)}, u32[]{:S(2)}) %all-to-all-start.2) | async-done | bytes 1179680 | tf_op jit(solution)/shard_map/all_to_all | solution.py:227
  130.1 6.2 %gate_up_terms.2 = (bf16[192,1024]{1,0:T(8,128)(2,1)}, bf16[192,1024]{1,0:T(8,128)(2,1)}, bf16[384,1024]{1,0:T(8,128)(2,1)}) custom-call(s32[2]{0:T(128)S(1)} %pad_add_fusion.order_ref, bf16[8,96,768]{2,1,0:T(8,128)(2,1)S(1)} %all-to-all-done.2.x_ref, bf16[8,96,768]{2,1,0:T(8,128)(2,1)} %collective-permute-done.3.o_ref, ...), custom_call_target="tpu_custom_call" | custom-call | flops 2415919104 | bytes 4718592 | tf_op jit(solution)/shard_map/gate_up_terms/pallas_call | solution.py:128
  138.2 19.9 %collective-permute-done.4 = bf16[384,1024]{1,0:T(8,128)(2,1)} collective-permute-done((bf16[384,1024]{1,0:T(8,128)(2,1)}, bf16[384,1024]{1,0:T(8,128)(2,1)}, u32[]{:S(2)}, u32[]{:S(2)}) %collective-permute-start.4) | collective-permute-done | bytes 786464 | tf_op jit(solution)/shard_map/ppermute | solution.py:244
  165.4 5.8 %gate_up_terms.3 = (bf16[192,1024]{1,0:T(8,128)(2,1)}, bf16[192,1024]{1,0:T(8,128)(2,1)}, bf16[384,1024]{1,0:T(8,128)(2,1)}) custom-call(s32[2]{0:T(128)S(1)} %pad_add_fusion.order_ref, bf16[8,104,768]{2,1,0:T(8,128)(2,1)S(1)} %all-to-all-done.3.x_ref, bf16[8,104,768]{2,1,0:T(8,128)(2,1)S(1)} %collective-permute-done.6.o_ref, ...), custom_call_target="tpu_custom_call" | custom-call | flops 2415919104 | bytes 4718592 | tf_op jit(solution)/shard_map/gate_up_terms/pallas_call | solution.py:128
  173.1 8.6 %collective-permute-done.5 = bf16[192,1024]{1,0:T(8,128)(2,1)S(1)} collective-permute-done((bf16[192,1024]{1,0:T(8,128)(2,1)}, bf16[192,1024]{1,0:T(8,128)(2,1)S(1)}, u32[]{:S(2)}, u32[]{:S(2)}) %collective-permute-start.5) | collective-permute-done | bytes 393248 | tf_op jit(solution)/shard_map/ppermute | solution.py:247
  183.0 5.2 %collective-permute-start.7 = (bf16[192,512]{1,0:T(8,128)(2,1)S(1)}, bf16[192,512]{1,0:T(8,128)(2,1)S(1)}, u32[]{:S(2)}, u32[]{:S(2)}) collective-permute-start(bf16[192,512]{1,0:T(8,128)(2,1)S(1)} %fusion.3), channel_id=1, source_target_pairs={{0,4},{2,6},{4,0},{6,2},{1,5},{3,7},{5,1},{7,3},{8,12},{10,14},{12... | collective-permute-start | bytes 589832 | tf_op jit(solution)/shard_map/ppermute | solution.py:247
  188.3 10.5 %collective-permute-done.7 = bf16[192,512]{1,0:T(8,128)(2,1)S(1)} collective-permute-done((bf16[192,512]{1,0:T(8,128)(2,1)S(1)}, bf16[192,512]{1,0:T(8,128)(2,1)S(1)}, u32[]{:S(2)}, u32[]{:S(2)}) %collective-permute-start.7) | collective-permute-done | bytes 196640 | tf_op jit(solution)/shard_map/ppermute | solution.py:247
  210.2 10.1 %collective-permute-done.9 = bf16[384,512]{1,0:T(8,128)(2,1)S(1)} collective-permute-done((bf16[384,512]{1,0:T(8,128)(2,1)S(1)}, bf16[384,512]{1,0:T(8,128)(2,1)S(1)}, u32[]{:S(2)}, u32[]{:S(2)}) %collective-permute-start.9) | collective-permute-done | bytes 393248 | tf_op jit(solution)/shard_map/ppermute | solution.py:244
  220.3 6.9 %collective-permute-done.10 = bf16[192,1024]{1,0:T(8,128)(2,1)S(1)} collective-permute-done((bf16[192,1024]{1,0:T(8,128)(2,1)S(1)}, bf16[192,1024]{1,0:T(8,128)(2,1)S(1)}, u32[]{:S(2)}, u32[]{:S(2)}) %collective-permute-start.10) | collective-permute-done | bytes 393248 | tf_op jit(solution)/shard_map/ppermute | solution.py:247
  235.1 7.2 %all-to-all-start.4 = ((bf16[8,96,768]{2,1,0:T(8,128)(2,1)}), bf16[8,96,768]{2,1,0:T(8,128)(2,1)}, u32[]{:S(2)}, u32[]{:S(2)}) async-start(bf16[8,96,768]{2,1,0:T(8,128)(2,1)} %bitcast.11), calls=%async_computation.4 | async-start | bytes 2359296 | tf_op jit(solution)/shard_map/all_to_all | solution.py:227
  243.7 5.3 %collective-permute-start.12 = (bf16[192,512]{1,0:T(8,128)(2,1)S(1)}, bf16[192,512]{1,0:T(8,128)(2,1)S(1)}, u32[]{:S(2)}, u32[]{:S(2)}) collective-permute-start(bf16[192,512]{1,0:T(8,128)(2,1)S(1)} %fusion.2), channel_id=1, source_target_pairs={{0,4},{2,6},{4,0},{6,2},{1,5},{3,7},{5,1},{7,3},{8,12},{10,14},{12... | collective-permute-start | bytes 589832 | tf_op jit(solution)/shard_map/ppermute | solution.py:247
  249.0 7.2 %collective-permute-done.12 = bf16[192,512]{1,0:T(8,128)(2,1)S(1)} collective-permute-done((bf16[192,512]{1,0:T(8,128)(2,1)S(1)}, bf16[192,512]{1,0:T(8,128)(2,1)S(1)}, u32[]{:S(2)}, u32[]{:S(2)}) %collective-permute-start.12) | collective-permute-done | bytes 196640 | tf_op jit(solution)/shard_map/ppermute | solution.py:247
  256.2 5.3 %collective-permute-start.13 = (bf16[384,512]{1,0:T(8,128)(2,1)S(1)}, bf16[384,512]{1,0:T(8,128)(2,1)S(1)}, u32[]{:S(2)}, u32[]{:S(2)}) collective-permute-start(bf16[384,512]{1,0:T(8,128)(2,1)S(1)} %pad_maximum_fusion.5), channel_id=1, source_target_pairs={{0,2},{2,0},{4,6},{6,4},{1,3},{3,1},{5,7},{7,5},{8,10},{10,8},{12,... | collective-permute-start | bytes 1179656 | tf_op jit(solution)/shard_map/ppermute | solution.py:244
  261.5 9.4 %collective-permute-done.13 = bf16[384,512]{1,0:T(8,128)(2,1)S(1)} collective-permute-done((bf16[384,512]{1,0:T(8,128)(2,1)S(1)}, bf16[384,512]{1,0:T(8,128)(2,1)S(1)}, u32[]{:S(2)}, u32[]{:S(2)}) %collective-permute-start.13) | collective-permute-done | bytes 393248 | tf_op jit(solution)/shard_map/ppermute | solution.py:244
  278.1 6.9 %all-to-all-start.5 = ((bf16[8,96,768]{2,1,0:T(8,128)(2,1)}), bf16[8,96,768]{2,1,0:T(8,128)(2,1)S(1)}, u32[]{:S(2)}, u32[]{:S(2)}) async-start(bf16[8,96,768]{2,1,0:T(8,128)(2,1)} %bitcast.13), calls=%async_computation.5 | async-start | bytes 2359296 | tf_op jit(solution)/shard_map/all_to_all | solution.py:227
  286.5 30.4 %all-to-all-done.5 = bf16[8,96,768]{2,1,0:T(8,128)(2,1)S(1)} async-done(((bf16[8,96,768]{2,1,0:T(8,128)(2,1)}), bf16[8,96,768]{2,1,0:T(8,128)(2,1)S(1)}, u32[]{:S(2)}, u32[]{:S(2)}) %all-to-all-start.5) | async-done | bytes 1179680 | tf_op jit(solution)/shard_map/all_to_all | solution.py:227
  317.3 17.7 %all_to_all.36 = bf16[8,24,768]{2,1,0:T(8,128)(2,1)S(1)} all-to-all(bf16[8,24,768]{2,1,0:T(8,128)(2,1)S(1)} %pad_maximum_fusion.6), channel_id=1, replica_groups=mesh['yh'=2,'xh'=2,'xl'=2,'z'=8,'yl'=4,'c'=2] {'yh','xh','xl'}, dimensions={0} | all-to-all | bytes 589824 | tf_op jit(solution)/shard_map/all_to_all | solution.py:227
  (111 shorter events, 69.3 us)
Async XLA Ops:
  1.9 41.8 %all-to-all-start = ((bf16[32,64,256]{2,1,0:T(8,128)(2,1)}), bf16[32,64,256]{2,1,0:T(8,128)(2,1)S(1)}, u32[]{:S(2)}, u32[]{:S(2)}) async-start(bf16[32,64,256]{2,1,0:T(8,128)(2,1)} %broadcast_in_dim.32), calls=%async_computation | async-start | bytes 2097152 | tf_op jit(solution)/shard_map/all_to_all | solution.py:78
  18.4 5.6 %collective-permute-start.1 = (bf16[1024,768]{1,0:T(8,128)(2,1)}, bf16[1024,768]{1,0:T(8,128)(2,1)}, u32[]{:S(2)}, u32[]{:S(2)}) collective-permute-start(bf16[1024,768]{1,0:T(8,128)(2,1)} %pad_maximum_fusion.1), channel_id=1, source_target_pairs={{0,1},{1,0},{2,3},{3,2},{4,5},{5,4},{6,7},{7,6},{8,9},{9,8},{10,11... | collective-permute-start | bytes 4718600 | tf_op jit(solution)/shard_map/ppermute | solution.py:27
  20.3 23.4 %collective-permute-start = (bf16[64,768]{1,0:T(8,128)(2,1)S(1)}, bf16[64,768]{1,0:T(8,128)(2,1)S(1)}, u32[]{:S(2)}, u32[]{:S(2)}) collective-permute-start(bf16[64,768]{1,0:T(8,128)(2,1)S(1)} %copy-done.1), channel_id=1, source_target_pairs={{256,0},{257,1},{258,2},{259,3},{260,4},{261,5},{262,6},{263,7},{2... | collective-permute-start | bytes 294920 | tf_op jit(solution)/shard_map/ppermute | solution.py:75
  49.6 10.4 %collective-permute-start.2 = (bf16[64,896]{1,0:T(8,128)(2,1)S(1)}, bf16[64,896]{1,0:T(8,128)(2,1)S(1)}, u32[]{:S(2)}, u32[]{:S(2)}) collective-permute-start(bf16[64,896]{1,0:T(8,128)(2,1)S(1)} %get-tuple-element.27), channel_id=1, source_target_pairs={{0,256},{1,257},{2,258},{3,259},{4,260},{5,261},{6,262},{7,263},{8... | collective-permute-start | bytes 344072 | tf_op jit(solution)/shard_map/ppermute | solution.py:100
  82.1 38.3 %all-to-all-start.2 = ((bf16[8,96,768]{2,1,0:T(8,128)(2,1)}), bf16[8,96,768]{2,1,0:T(8,128)(2,1)S(1)}, u32[]{:S(2)}, u32[]{:S(2)}) async-start(bf16[8,96,768]{2,1,0:T(8,128)(2,1)} %broadcast_in_dim.67), calls=%async_computation.2 | async-start | bytes 2359296 | tf_op jit(solution)/shard_map/all_to_all | solution.py:227
  121.6 37.6 %all-to-all-start.3 = ((bf16[8,104,768]{2,1,0:T(8,128)(2,1)}), bf16[8,104,768]{2,1,0:T(8,128)(2,1)S(1)}, u32[]{:S(2)}, u32[]{:S(2)}) async-start(bf16[8,104,768]{2,1,0:T(8,128)(2,1)} %broadcast_in_dim.69), calls=%async_computation.3 | async-start | bytes 2555904 | tf_op jit(solution)/shard_map/all_to_all | solution.py:227
  125.2 4.9 %collective-permute-start.3 = (bf16[8,96,768]{2,1,0:T(8,128)(2,1)S(1)}, bf16[8,96,768]{2,1,0:T(8,128)(2,1)}, u32[]{:S(2)}, u32[]{:S(2)}) collective-permute-start(bf16[8,96,768]{2,1,0:T(8,128)(2,1)S(1)} %all-to-all-done.2.x_ref), channel_id=1, source_target_pairs={{0,1},{1,0},{2,3},{3,2},{4,5},{5,4},{6,7},{7,6},{8,9},{9,8},{10,11... | collective-permute-start | bytes 3538952 | tf_op jit(solution)/shard_map/ppermute | solution.py:27
  136.3 21.8 %collective-permute-start.4 = (bf16[384,1024]{1,0:T(8,128)(2,1)}, bf16[384,1024]{1,0:T(8,128)(2,1)}, u32[]{:S(2)}, u32[]{:S(2)}) collective-permute-start(bf16[384,1024]{1,0:T(8,128)(2,1)} %get-tuple-element.33), channel_id=1, source_target_pairs={{0,2},{2,0},{4,6},{6,4},{1,3},{3,1},{5,7},{7,5},{8,10},{10,8},{12,... | collective-permute-start | bytes 2359304 | tf_op jit(solution)/shard_map/ppermute | solution.py:244
  159.2 6.1 %collective-permute-start.6 = (bf16[8,104,768]{2,1,0:T(8,128)(2,1)S(1)}, bf16[8,104,768]{2,1,0:T(8,128)(2,1)S(1)}, u32[]{:S(2)}, u32[]{:S(2)}) collective-permute-start(bf16[8,104,768]{2,1,0:T(8,128)(2,1)S(1)} %all-to-all-done.3.x_ref), channel_id=1, source_target_pairs={{0,1},{1,0},{2,3},{3,2},{4,5},{5,4},{6,7},{7,6},{8,9},{9,8},{10,11... | collective-permute-start | bytes 3833864 | tf_op jit(solution)/shard_map/ppermute | solution.py:27
  163.2 18.5 %collective-permute-start.5 = (bf16[192,1024]{1,0:T(8,128)(2,1)}, bf16[192,1024]{1,0:T(8,128)(2,1)S(1)}, u32[]{:S(2)}, u32[]{:S(2)}) collective-permute-start(bf16[192,1024]{1,0:T(8,128)(2,1)} %add_convert_fusion.1), channel_id=1, source_target_pairs={{0,4},{2,6},{4,0},{6,2},{1,5},{3,7},{5,1},{7,3},{8,12},{10,14},{12... | collective-permute-start | bytes 1179656 | tf_op jit(solution)/shard_map/ppermute | solution.py:247
  171.2 30.1 %collective-permute-start.8 = (bf16[384,1024]{1,0:T(8,128)(2,1)}, bf16[384,1024]{1,0:T(8,128)(2,1)S(1)}, u32[]{:S(2)}, u32[]{:S(2)}) collective-permute-start(bf16[384,1024]{1,0:T(8,128)(2,1)} %get-tuple-element.39), channel_id=1, source_target_pairs={{0,2},{2,0},{4,6},{6,4},{1,3},{3,1},{5,7},{7,5},{8,10},{10,8},{12,... | collective-permute-start | bytes 2359304 | tf_op jit(solution)/shard_map/ppermute | solution.py:244
  181.7 24.1 %copy-start.8 = (bf16[192,1024]{1,0:T(8,128)(2,1)S(1)}, bf16[192,1024]{1,0:T(8,128)(2,1)}, u32[]{:S(2)}) copy-start(bf16[192,1024]{1,0:T(8,128)(2,1)} %get-tuple-element.38) | copy-start | bytes 1179652
  183.0 15.7 %collective-permute-start.7 = (bf16[192,512]{1,0:T(8,128)(2,1)S(1)}, bf16[192,512]{1,0:T(8,128)(2,1)S(1)}, u32[]{:S(2)}, u32[]{:S(2)}) collective-permute-start(bf16[192,512]{1,0:T(8,128)(2,1)S(1)} %fusion.3), channel_id=1, source_target_pairs={{0,4},{2,6},{4,0},{6,2},{1,5},{3,7},{5,1},{7,3},{8,12},{10,14},{12... | collective-permute-start | bytes 589832 | tf_op jit(solution)/shard_map/ppermute | solution.py:247
  201.3 19.0 %copy-start.2 = (bf16[384,1024]{1,0:T(8,128)(2,1)}, bf16[384,1024]{1,0:T(8,128)(2,1)S(1)}, u32[]{:S(2)}) copy-start(bf16[384,1024]{1,0:T(8,128)(2,1)S(1)} %collective-permute-done.8) | copy-start | bytes 2359300
  201.3 30.9 %copy-start = (bf16[1024,768]{1,0:T(8,128)(2,1)S(1)}, bf16[1024,768]{1,0:T(8,128)(2,1)}, u32[]{:S(2)}) copy-start(bf16[1024,768]{1,0:T(8,128)(2,1)} %w_ref.3) | copy-start | bytes 4718596
  201.3 19.0 %collective-permute-start.9 = (bf16[384,512]{1,0:T(8,128)(2,1)S(1)}, bf16[384,512]{1,0:T(8,128)(2,1)S(1)}, u32[]{:S(2)}, u32[]{:S(2)}) collective-permute-start(bf16[384,512]{1,0:T(8,128)(2,1)S(1)} %pad_maximum_fusion.4), channel_id=1, source_target_pairs={{0,2},{2,0},{4,6},{6,4},{1,3},{3,1},{5,7},{7,5},{8,10},{10,8},{12,... | collective-permute-start | bytes 1179656 | tf_op jit(solution)/shard_map/ppermute | solution.py:244
  205.9 21.3 %collective-permute-start.10 = (bf16[192,1024]{1,0:T(8,128)(2,1)S(1)}, bf16[192,1024]{1,0:T(8,128)(2,1)S(1)}, u32[]{:S(2)}, u32[]{:S(2)}) collective-permute-start(bf16[192,1024]{1,0:T(8,128)(2,1)S(1)} %add_convert_fusion), channel_id=1, source_target_pairs={{0,4},{2,6},{4,0},{6,2},{1,5},{3,7},{5,1},{7,3},{8,12},{10,14},{12... | collective-permute-start | bytes 1179656 | tf_op jit(solution)/shard_map/ppermute | solution.py:247
  228.0 4.2 %collective-permute-start.11 = (bf16[768,512]{1,0:T(8,128)(2,1)S(1)}, bf16[768,512]{1,0:T(8,128)(2,1)S(1)}, u32[]{:S(2)}, u32[]{:S(2)}) collective-permute-start(bf16[768,512]{1,0:T(8,128)(2,1)S(1)} %pad_maximum_fusion.2.h_ref), channel_id=1, source_target_pairs={{0,1},{1,0},{2,3},{3,2},{4,5},{5,4},{6,7},{7,6},{8,9},{9,8},{10,11... | collective-permute-start | bytes 2359304 | tf_op jit(solution)/shard_map/ppermute | solution.py:27
  235.1 43.0 %all-to-all-start.4 = ((bf16[8,96,768]{2,1,0:T(8,128)(2,1)}), bf16[8,96,768]{2,1,0:T(8,128)(2,1)}, u32[]{:S(2)}, u32[]{:S(2)}) async-start(bf16[8,96,768]{2,1,0:T(8,128)(2,1)} %bitcast.11), calls=%async_computation.4 | async-start | bytes 2359296 | tf_op jit(solution)/shard_map/all_to_all | solution.py:227
  243.7 12.5 %collective-permute-start.12 = (bf16[192,512]{1,0:T(8,128)(2,1)S(1)}, bf16[192,512]{1,0:T(8,128)(2,1)S(1)}, u32[]{:S(2)}, u32[]{:S(2)}) collective-permute-start(bf16[192,512]{1,0:T(8,128)(2,1)S(1)} %fusion.2), channel_id=1, source_target_pairs={{0,4},{2,6},{4,0},{6,2},{1,5},{3,7},{5,1},{7,3},{8,12},{10,14},{12... | collective-permute-start | bytes 589832 | tf_op jit(solution)/shard_map/ppermute | solution.py:247
  256.2 14.7 %collective-permute-start.13 = (bf16[384,512]{1,0:T(8,128)(2,1)S(1)}, bf16[384,512]{1,0:T(8,128)(2,1)S(1)}, u32[]{:S(2)}, u32[]{:S(2)}) collective-permute-start(bf16[384,512]{1,0:T(8,128)(2,1)S(1)} %pad_maximum_fusion.5), channel_id=1, source_target_pairs={{0,2},{2,0},{4,6},{6,4},{1,3},{3,1},{5,7},{7,5},{8,10},{10,8},{12,... | collective-permute-start | bytes 1179656 | tf_op jit(solution)/shard_map/ppermute | solution.py:244
  271.0 4.2 %collective-permute-start.14 = (bf16[768,512]{1,0:T(8,128)(2,1)S(1)}, bf16[768,512]{1,0:T(8,128)(2,1)S(1)}, u32[]{:S(2)}, u32[]{:S(2)}) collective-permute-start(bf16[768,512]{1,0:T(8,128)(2,1)S(1)} %pad_maximum_fusion.3.h_ref), channel_id=1, source_target_pairs={{0,1},{1,0},{2,3},{3,2},{4,5},{5,4},{6,7},{7,6},{8,9},{9,8},{10,11... | collective-permute-start | bytes 2359304 | tf_op jit(solution)/shard_map/ppermute | solution.py:27
  278.1 38.9 %all-to-all-start.5 = ((bf16[8,96,768]{2,1,0:T(8,128)(2,1)}), bf16[8,96,768]{2,1,0:T(8,128)(2,1)S(1)}, u32[]{:S(2)}, u32[]{:S(2)}) async-start(bf16[8,96,768]{2,1,0:T(8,128)(2,1)} %bitcast.13), calls=%async_computation.5 | async-start | bytes 2359296 | tf_op jit(solution)/shard_map/all_to_all | solution.py:227
  286.5 48.5 %copy-start.11 = (f32[64]{0:T(128)S(1)}, f32[64]{0:T(128)}, u32[]{:S(2)}) copy-start(f32[64]{0:T(128)} %param.16) | copy-start | bytes 772
  (8 other events, 72.7 us)

commit v8 on v6

--- a/solution.py
+++ b/solution.py
@@ -261,7 +261,7 @@
 
     terms_a = gate_up_terms(order, x_a, swap(x_a, "c"), w_in, w_in_other, block)
     sums_a = over_yl(terms_a)
-    x_b = after(x_b, sums_a[3])
+    x_b = after(x_b, *sums_a[2:])
     inverse = from_row(x_b[:, block], 2 * block)
     terms_b = gate_up_terms(order, x_b, swap(x_b, "c"), w_in, w_in_other, block)
     sums_a[1] = after(sums_a[1], *terms_b)

time: 333 us -> 340 us (1.021)
  starting transfers between devices: 88.5 us -> 92 us
    all_to_all x4, starting transfers between devices: 18.4 us -> 24.7 us  [all_to_all(): return lax.all_to_all(x, axes, split_axis=0, concat_axis=0, tiled=True)]
    ppermute x12, waiting for transfers between devices: 70.7 us -> 76.8 us  [over_yl(): lax.ppermute(parts[i], 'yl', Y_XOR[i])]
    all_to_all x4, waiting for transfers between devices: 56.4 us -> 51 us  [all_to_all(): return lax.all_to_all(x, axes, split_axis=0, concat_axis=0, tiled=True)]
  transfers between devices with their start and end apart: 24 -> 24, of which waited for: 17 -> 20; matrix products, arithmetic and copies ran while one was open for 3% -> 3% of each run, Pallas kernels for 5% -> 5%
where the time goes in v8:
time: 340 us; the launch traced here: 339 us
  waiting for transfers between devices  157 us (46%)
  starting transfers between devices  92 us (27%)
  blocking collectives  47.3 us (14%)
  Pallas kernels  23.8 us (7%)
  other arithmetic  9.08 us (3%)
  local copies, waits for them, and re-layouts  7.82 us (2%)
    ppermute x12, waiting for transfers between devices, over_yl(): lax.ppermute(parts[i], 'yl', Y_XOR[i])  76.8 us
    all_to_all x4, waiting for transfers between devices, all_to_all(): return lax.all_to_all(x, axes, split_axis=0, concat_axis=0, tiled=True)  51 us
    all_to_all x2, blocking collectives, all_to_all(): return lax.all_to_all(x, axes, split_axis=0, concat_axis=0, tiled=True)  36.7 us
    ppermute x12, starting transfers between devices, over_yl(): lax.ppermute(parts[i], 'yl', Y_XOR[i])  36.4 us
    all_to_all x4, starting transfers between devices, all_to_all(): return lax.all_to_all(x, axes, split_axis=0, concat_axis=0, tiled=True)  24.7 us
    all_to_all x1, waiting for transfers between devices, attend(): lax.all_to_all(jnp.broadcast_to(kv[None], (members,) + kv.shape), HALF, s...  19.6 us
    all_to_all x1, starting transfers between devices, attend(): lax.all_to_all(jnp.broadcast_to(kv[None], (members,) + kv.shape), HALF, s...  13.2 us
    pallas_call x2, Pallas kernels, gate_up_terms(): pl.pallas_call(expand, grid_spec=pltpu.PrefetchScalarGridSpec(num_scalar_...  12 us
  transfers between devices with their start and end apart: 24, of which 20 were waited for; matrix products, arithmetic and copies ran while one was open for 3% of the time, Pallas kernels for 5%

profile of v8, /device:TPU:8, one launch (start us, length us, event | category | flops | bytes accessed | tf_op | source)
XLA Modules:
  0.0 339.1 jit_solution(9972407630145426175)
XLA Ops:
  1.9 13.2 %all-to-all-start = ((bf16[32,64,256]{2,1,0:T(8,128)(2,1)}), bf16[32,64,256]{2,1,0:T(8,128)(2,1)S(1)}, u32[]{:S(2)}, u32[]{:S(2)}) async-start(bf16[32,64,256]{2,1,0:T(8,128)(2,1)} %broadcast_in_dim.32), calls=%async_computation | async-start | bytes 2097152 | tf_op jit(solution)/shard_map/all_to_all | solution.py:78
  24.0 19.6 %all-to-all-done = bf16[32,64,256]{2,1,0:T(8,128)(2,1)S(1)} async-done(((bf16[32,64,256]{2,1,0:T(8,128)(2,1)}), bf16[32,64,256]{2,1,0:T(8,128)(2,1)S(1)}, u32[]{:S(2)}, u32[]{:S(2)}) %all-to-all-start) | async-done | bytes 1048608 | tf_op jit(solution)/shard_map/all_to_all | solution.py:78
  43.7 5.9 %softmax_block.1 = (f32[64,768]{1,0:T(8,128)S(1)}, f32[64,768]{1,0:T(8,128)S(1)}, bf16[64,896]{1,0:T(8,128)(2,1)S(1)}) custom-call(s32[1]{0:T(128)} %bitcast.3.base_ref, bf16[64,768]{1,0:T(8,128)(2,1)S(1)} %copy-done.1, bf16[64,768]{1,0:T(8,128)(2,1)S(1)} %collective-permute-done.far_ref, bf16[2048,256]{1,0:T(8,128)(2,1)S(1)} %bitcast.50), custom_call_target="tpu_custom_call" | custom-call | flops 805306368 | bytes 1835008 | tf_op jit(solution)/shard_map/softmax_block/pallas_call | solution.py:83
  49.6 6.8 %collective-permute-start.2 = (bf16[64,896]{1,0:T(8,128)(2,1)S(1)}, bf16[64,896]{1,0:T(8,128)(2,1)S(1)}, u32[]{:S(2)}, u32[]{:S(2)}) collective-permute-start(bf16[64,896]{1,0:T(8,128)(2,1)S(1)} %get-tuple-element.28), channel_id=1, source_target_pairs={{0,256},{1,257},{2,258},{3,259},{4,260},{5,261},{6,262},{7,263},{8... | collective-permute-start | bytes 344072 | tf_op jit(solution)/shard_map/ppermute | solution.py:100
  60.8 20.1 %all_to_all.35 = bf16[8,32,768]{2,1,0:T(8,128)(2,1)S(1)} all-to-all(bf16[8,32,768]{2,1,0:T(8,128)(2,1)S(1)} %bitcast.51), channel_id=1, replica_groups=mesh['yh'=2,'xh'=2,'xl'=2,'z'=8,'yl'=4,'c'=2] {'yh','xh','xl'}, dimensions={0} | all-to-all | bytes 786432 | tf_op jit(solution)/shard_map/all_to_all | solution.py:228
  82.1 6.7 %all-to-all-start.2 = ((bf16[8,96,768]{2,1,0:T(8,128)(2,1)}), bf16[8,96,768]{2,1,0:T(8,128)(2,1)S(1)}, u32[]{:S(2)}, u32[]{:S(2)}) async-start(bf16[8,96,768]{2,1,0:T(8,128)(2,1)} %broadcast_in_dim.67), calls=%async_computation.2 | async-start | bytes 2359296 | tf_op jit(solution)/shard_map/all_to_all | solution.py:228
  89.2 10.6 %psum.7 = f32[192]{0:T(256)S(1)} all-reduce(f32[192]{0:T(256)S(1)} %reshape.107), channel_id=1, replica_groups=mesh['yh'=2,'xh'=2,'xl'=2,'z'=8,'yl'=4,'c'=2] {'yl','c'}, use_global_device_ids=true, to_apply=%region_4.5 | all-reduce | flops 192 | bytes 1536 | tf_op jit(solution)/shard_map/psum | solution.py:240
  99.8 20.6 %all-to-all-done.2.x_ref = bf16[8,96,768]{2,1,0:T(8,128)(2,1)S(1)} async-done(((bf16[8,96,768]{2,1,0:T(8,128)(2,1)}), bf16[8,96,768]{2,1,0:T(8,128)(2,1)S(1)}, u32[]{:S(2)}, u32[]{:S(2)}) %all-to-all-start.2) | async-done | bytes 1179680 | tf_op jit(solution)/shard_map/all_to_all | solution.py:228
  130.1 6.2 %gate_up_terms.2 = (bf16[192,1024]{1,0:T(8,128)(2,1)}, bf16[192,1024]{1,0:T(8,128)(2,1)}, bf16[192,1024]{1,0:T(8,128)(2,1)}, bf16[192,1024]{1,0:T(8,128)(2,1)}) custom-call(s32[2]{0:T(128)S(1)} %pad_add_fusion.order_ref, bf16[8,96,768]{2,1,0:T(8,128)(2,1)S(1)} %all-to-all-done.2.x_ref, bf16[8,96,768]{2,1,0:T(8,128)(2,1)} %collective-permute-done.3.o_ref, ...), custom_call_target="tpu_custom_call" | custom-call | flops 2415919104 | bytes 4718592 | tf_op jit(solution)/shard_map/gate_up_terms/pallas_call | solution.py:129
  140.2 22.4 %collective-permute-done.5 = bf16[192,1024]{1,0:T(8,128)(2,1)S(1)} collective-permute-done((bf16[192,1024]{1,0:T(8,128)(2,1)}, bf16[192,1024]{1,0:T(8,128)(2,1)S(1)}, u32[]{:S(2)}, u32[]{:S(2)}) %collective-permute-start.5) | collective-permute-done | bytes 393248 | tf_op jit(solution)/shard_map/ppermute | solution.py:245
  162.6 8.4 %collective-permute-done.6 = bf16[192,1024]{1,0:T(8,128)(2,1)S(1)} collective-permute-done((bf16[192,1024]{1,0:T(8,128)(2,1)}, bf16[192,1024]{1,0:T(8,128)(2,1)S(1)}, u32[]{:S(2)}, u32[]{:S(2)}) %collective-permute-start.6) | collective-permute-done | bytes 393248 | tf_op jit(solution)/shard_map/ppermute | solution.py:245
  176.6 5.8 %gate_up_terms.3 = (bf16[192,1024]{1,0:T(8,128)(2,1)}, bf16[192,1024]{1,0:T(8,128)(2,1)}, bf16[192,1024]{1,0:T(8,128)(2,1)}, bf16[192,1024]{1,0:T(8,128)(2,1)}) custom-call(s32[2]{0:T(128)S(1)} %pad_add_fusion.order_ref, bf16[8,104,768]{2,1,0:T(8,128)(2,1)S(1)} %all-to-all-done.3.x_ref, bf16[8,104,768]{2,1,0:T(8,128)(2,1)S(1)} %collective-permute-done.7.o_ref, ...), custom_call_target="tpu_custom_call" | custom-call | flops 2415919104 | bytes 4718592 | tf_op jit(solution)/shard_map/gate_up_terms/pallas_call | solution.py:129
  182.4 4.3 %collective-permute-start.9 = (bf16[192,1024]{1,0:T(8,128)(2,1)}, bf16[192,1024]{1,0:T(8,128)(2,1)S(1)}, u32[]{:S(2)}, u32[]{:S(2)}) collective-permute-start(bf16[192,1024]{1,0:T(8,128)(2,1)} %get-tuple-element.42), channel_id=1, source_target_pairs={{0,6},{2,4},{4,2},{6,0},{1,7},{3,5},{5,3},{7,1},{8,14},{10,12},{12... | collective-permute-start | bytes 1179656 | tf_op jit(solution)/shard_map/ppermute | solution.py:245
  192.4 4.2 %collective-permute-start.10 = (bf16[192,512]{1,0:T(8,128)(2,1)S(1)}, bf16[192,512]{1,0:T(8,128)(2,1)S(1)}, u32[]{:S(2)}, u32[]{:S(2)}) collective-permute-start(bf16[192,512]{1,0:T(8,128)(2,1)S(1)} %fusion.3), channel_id=1, source_target_pairs={{0,4},{2,6},{4,0},{6,2},{1,5},{3,7},{5,1},{7,3},{8,12},{10,14},{12... | collective-permute-start | bytes 589832 | tf_op jit(solution)/shard_map/ppermute | solution.py:245
  198.6 4.8 %collective-permute-done.8 = bf16[192,512]{1,0:T(8,128)(2,1)S(1)} collective-permute-done((bf16[192,512]{1,0:T(8,128)(2,1)S(1)}, bf16[192,512]{1,0:T(8,128)(2,1)S(1)}, u32[]{:S(2)}, u32[]{:S(2)}) %collective-permute-start.8) | collective-permute-done | bytes 196640 | tf_op jit(solution)/shard_map/ppermute | solution.py:245
  203.4 10.3 %collective-permute-done.9 = bf16[192,1024]{1,0:T(8,128)(2,1)S(1)} collective-permute-done((bf16[192,1024]{1,0:T(8,128)(2,1)}, bf16[192,1024]{1,0:T(8,128)(2,1)S(1)}, u32[]{:S(2)}, u32[]{:S(2)}) %collective-permute-start.9) | collective-permute-done | bytes 393248 | tf_op jit(solution)/shard_map/ppermute | solution.py:245
  217.4 4.2 %collective-permute-done.11 = bf16[192,512]{1,0:T(8,128)(2,1)S(1)} collective-permute-done((bf16[192,512]{1,0:T(8,128)(2,1)S(1)}, bf16[192,512]{1,0:T(8,128)(2,1)S(1)}, u32[]{:S(2)}, u32[]{:S(2)}) %collective-permute-start.11) | collective-permute-done | bytes 196640 | tf_op jit(solution)/shard_map/ppermute | solution.py:245
  225.5 5.1 %collective-permute-start.14 = (bf16[192,1024]{1,0:T(8,128)(2,1)}, bf16[192,1024]{1,0:T(8,128)(2,1)S(1)}, u32[]{:S(2)}, u32[]{:S(2)}) collective-permute-start(bf16[192,1024]{1,0:T(8,128)(2,1)} %get-tuple-element.41), channel_id=1, source_target_pairs={{0,4},{2,6},{4,0},{6,2},{1,5},{3,7},{5,1},{7,3},{8,12},{10,14},{12... | collective-permute-start | bytes 1179656 | tf_op jit(solution)/shard_map/ppermute | solution.py:245
  233.6 7.2 %all-to-all-start.4 = ((bf16[8,96,768]{2,1,0:T(8,128)(2,1)}), bf16[8,96,768]{2,1,0:T(8,128)(2,1)}, u32[]{:S(2)}, u32[]{:S(2)}) async-start(bf16[8,96,768]{2,1,0:T(8,128)(2,1)} %bitcast.11), calls=%async_computation.4 | async-start | bytes 2359296 | tf_op jit(solution)/shard_map/all_to_all | solution.py:228
  241.7 6.5 %collective-permute-done.14 = bf16[192,1024]{1,0:T(8,128)(2,1)S(1)} collective-permute-done((bf16[192,1024]{1,0:T(8,128)(2,1)}, bf16[192,1024]{1,0:T(8,128)(2,1)S(1)}, u32[]{:S(2)}, u32[]{:S(2)}) %collective-permute-start.14) | collective-permute-done | bytes 393248 | tf_op jit(solution)/shard_map/ppermute | solution.py:245
  260.1 11.0 %collective-permute-done.16 = bf16[192,512]{1,0:T(8,128)(2,1)S(1)} collective-permute-done((bf16[192,512]{1,0:T(8,128)(2,1)S(1)}, bf16[192,512]{1,0:T(8,128)(2,1)S(1)}, u32[]{:S(2)}, u32[]{:S(2)}) %collective-permute-start.16) | collective-permute-done | bytes 196640 | tf_op jit(solution)/shard_map/ppermute | solution.py:245
  282.1 7.1 %all-to-all-start.5 = ((bf16[8,96,768]{2,1,0:T(8,128)(2,1)}), bf16[8,96,768]{2,1,0:T(8,128)(2,1)S(1)}, u32[]{:S(2)}, u32[]{:S(2)}) async-start(bf16[8,96,768]{2,1,0:T(8,128)(2,1)} %bitcast.13), calls=%async_computation.5 | async-start | bytes 2359296 | tf_op jit(solution)/shard_map/all_to_all | solution.py:228
  290.8 30.4 %all-to-all-done.5 = bf16[8,96,768]{2,1,0:T(8,128)(2,1)S(1)} async-done(((bf16[8,96,768]{2,1,0:T(8,128)(2,1)}), bf16[8,96,768]{2,1,0:T(8,128)(2,1)S(1)}, u32[]{:S(2)}, u32[]{:S(2)}) %all-to-all-start.5) | async-done | bytes 1179680 | tf_op jit(solution)/shard_map/all_to_all | solution.py:228
  321.5 16.6 %all_to_all.36 = bf16[8,24,768]{2,1,0:T(8,128)(2,1)S(1)} all-to-all(bf16[8,24,768]{2,1,0:T(8,128)(2,1)S(1)} %pad_maximum_fusion.4), channel_id=1, replica_groups=mesh['yh'=2,'xh'=2,'xl'=2,'z'=8,'yl'=4,'c'=2] {'yh','xh','xl'}, dimensions={0} | all-to-all | bytes 589824 | tf_op jit(solution)/shard_map/all_to_all | solution.py:228
  (117 shorter events, 80.5 us)
Async XLA Ops:
  1.9 41.8 %all-to-all-start = ((bf16[32,64,256]{2,1,0:T(8,128)(2,1)}), bf16[32,64,256]{2,1,0:T(8,128)(2,1)S(1)}, u32[]{:S(2)}, u32[]{:S(2)}) async-start(bf16[32,64,256]{2,1,0:T(8,128)(2,1)} %broadcast_in_dim.32), calls=%async_computation | async-start | bytes 2097152 | tf_op jit(solution)/shard_map/all_to_all | solution.py:78
  18.4 5.6 %collective-permute-start.1 = (bf16[1024,768]{1,0:T(8,128)(2,1)}, bf16[1024,768]{1,0:T(8,128)(2,1)}, u32[]{:S(2)}, u32[]{:S(2)}) collective-permute-start(bf16[1024,768]{1,0:T(8,128)(2,1)} %pad_maximum_fusion.1), channel_id=1, source_target_pairs={{0,1},{1,0},{2,3},{3,2},{4,5},{5,4},{6,7},{7,6},{8,9},{9,8},{10,11... | collective-permute-start | bytes 4718600 | tf_op jit(solution)/shard_map/ppermute | solution.py:27
  20.3 23.3 %collective-permute-start = (bf16[64,768]{1,0:T(8,128)(2,1)S(1)}, bf16[64,768]{1,0:T(8,128)(2,1)S(1)}, u32[]{:S(2)}, u32[]{:S(2)}) collective-permute-start(bf16[64,768]{1,0:T(8,128)(2,1)S(1)} %copy-done.1), channel_id=1, source_target_pairs={{256,0},{257,1},{258,2},{259,3},{260,4},{261,5},{262,6},{263,7},{2... | collective-permute-start | bytes 294920 | tf_op jit(solution)/shard_map/ppermute | solution.py:75
  49.6 10.4 %collective-permute-start.2 = (bf16[64,896]{1,0:T(8,128)(2,1)S(1)}, bf16[64,896]{1,0:T(8,128)(2,1)S(1)}, u32[]{:S(2)}, u32[]{:S(2)}) collective-permute-start(bf16[64,896]{1,0:T(8,128)(2,1)S(1)} %get-tuple-element.28), channel_id=1, source_target_pairs={{0,256},{1,257},{2,258},{3,259},{4,260},{5,261},{6,262},{7,263},{8... | collective-permute-start | bytes 344072 | tf_op jit(solution)/shard_map/ppermute | solution.py:100
  82.1 38.3 %all-to-all-start.2 = ((bf16[8,96,768]{2,1,0:T(8,128)(2,1)}), bf16[8,96,768]{2,1,0:T(8,128)(2,1)S(1)}, u32[]{:S(2)}, u32[]{:S(2)}) async-start(bf16[8,96,768]{2,1,0:T(8,128)(2,1)} %broadcast_in_dim.67), calls=%async_computation.2 | async-start | bytes 2359296 | tf_op jit(solution)/shard_map/all_to_all | solution.py:228
  121.6 50.1 %all-to-all-start.3 = ((bf16[8,104,768]{2,1,0:T(8,128)(2,1)}), bf16[8,104,768]{2,1,0:T(8,128)(2,1)S(1)}, u32[]{:S(2)}, u32[]{:S(2)}) async-start(bf16[8,104,768]{2,1,0:T(8,128)(2,1)} %broadcast_in_dim.69), calls=%async_computation.3 | async-start | bytes 2555904 | tf_op jit(solution)/shard_map/all_to_all | solution.py:228
  125.2 4.9 %collective-permute-start.3 = (bf16[8,96,768]{2,1,0:T(8,128)(2,1)S(1)}, bf16[8,96,768]{2,1,0:T(8,128)(2,1)}, u32[]{:S(2)}, u32[]{:S(2)}) collective-permute-start(bf16[8,96,768]{2,1,0:T(8,128)(2,1)S(1)} %all-to-all-done.2.x_ref), channel_id=1, source_target_pairs={{0,1},{1,0},{2,3},{3,2},{4,5},{5,4},{6,7},{7,6},{8,9},{9,8},{10,11... | collective-permute-start | bytes 3538952 | tf_op jit(solution)/shard_map/ppermute | solution.py:27
  136.3 26.3 %collective-permute-start.5 = (bf16[192,1024]{1,0:T(8,128)(2,1)}, bf16[192,1024]{1,0:T(8,128)(2,1)S(1)}, u32[]{:S(2)}, u32[]{:S(2)}) collective-permute-start(bf16[192,1024]{1,0:T(8,128)(2,1)} %get-tuple-element.36), channel_id=1, source_target_pairs={{0,4},{2,6},{4,0},{6,2},{1,5},{3,7},{5,1},{7,3},{8,12},{10,14},{12... | collective-permute-start | bytes 1179656 | tf_op jit(solution)/shard_map/ppermute | solution.py:245
  138.2 32.7 %collective-permute-start.6 = (bf16[192,1024]{1,0:T(8,128)(2,1)}, bf16[192,1024]{1,0:T(8,128)(2,1)S(1)}, u32[]{:S(2)}, u32[]{:S(2)}) collective-permute-start(bf16[192,1024]{1,0:T(8,128)(2,1)} %get-tuple-element.37), channel_id=1, source_target_pairs={{0,6},{2,4},{4,2},{6,0},{1,7},{3,5},{5,3},{7,1},{8,14},{10,12},{12... | collective-permute-start | bytes 1179656 | tf_op jit(solution)/shard_map/ppermute | solution.py:245
  171.8 4.9 %collective-permute-start.7 = (bf16[8,104,768]{2,1,0:T(8,128)(2,1)S(1)}, bf16[8,104,768]{2,1,0:T(8,128)(2,1)S(1)}, u32[]{:S(2)}, u32[]{:S(2)}) collective-permute-start(bf16[8,104,768]{2,1,0:T(8,128)(2,1)S(1)} %all-to-all-done.3.x_ref), channel_id=1, source_target_pairs={{0,1},{1,0},{2,3},{3,2},{4,5},{5,4},{6,7},{7,6},{8,9},{9,8},{10,11... | collective-permute-start | bytes 3833864 | tf_op jit(solution)/shard_map/ppermute | solution.py:27
  173.7 13.7 %collective-permute-start.4 = (bf16[192,1024]{1,0:T(8,128)(2,1)}, bf16[192,1024]{1,0:T(8,128)(2,1)}, u32[]{:S(2)}, u32[]{:S(2)}) collective-permute-start(bf16[192,1024]{1,0:T(8,128)(2,1)} %get-tuple-element.34), channel_id=1, source_target_pairs={{0,2},{2,0},{4,6},{6,4},{1,3},{3,1},{5,7},{7,5},{8,10},{10,8},{12,... | collective-permute-start | bytes 1179656 | tf_op jit(solution)/shard_map/ppermute | solution.py:245
  182.4 31.2 %collective-permute-start.9 = (bf16[192,1024]{1,0:T(8,128)(2,1)}, bf16[192,1024]{1,0:T(8,128)(2,1)S(1)}, u32[]{:S(2)}, u32[]{:S(2)}) collective-permute-start(bf16[192,1024]{1,0:T(8,128)(2,1)} %get-tuple-element.42), channel_id=1, source_target_pairs={{0,6},{2,4},{4,2},{6,0},{1,7},{3,5},{5,3},{7,1},{8,14},{10,12},{12... | collective-permute-start | bytes 1179656 | tf_op jit(solution)/shard_map/ppermute | solution.py:245
  188.8 14.6 %collective-permute-start.8 = (bf16[192,512]{1,0:T(8,128)(2,1)S(1)}, bf16[192,512]{1,0:T(8,128)(2,1)S(1)}, u32[]{:S(2)}, u32[]{:S(2)}) collective-permute-start(bf16[192,512]{1,0:T(8,128)(2,1)S(1)} %fusion.3), channel_id=1, source_target_pairs={{0,2},{2,0},{4,6},{6,4},{1,3},{3,1},{5,7},{7,5},{8,10},{10,8},{12,... | collective-permute-start | bytes 589832 | tf_op jit(solution)/shard_map/ppermute | solution.py:245
  192.4 25.1 %collective-permute-start.10 = (bf16[192,512]{1,0:T(8,128)(2,1)S(1)}, bf16[192,512]{1,0:T(8,128)(2,1)S(1)}, u32[]{:S(2)}, u32[]{:S(2)}) collective-permute-start(bf16[192,512]{1,0:T(8,128)(2,1)S(1)} %fusion.3), channel_id=1, source_target_pairs={{0,4},{2,6},{4,0},{6,2},{1,5},{3,7},{5,1},{7,3},{8,12},{10,14},{12... | collective-permute-start | bytes 589832 | tf_op jit(solution)/shard_map/ppermute | solution.py:245
  196.6 25.0 %collective-permute-start.11 = (bf16[192,512]{1,0:T(8,128)(2,1)S(1)}, bf16[192,512]{1,0:T(8,128)(2,1)S(1)}, u32[]{:S(2)}, u32[]{:S(2)}) collective-permute-start(bf16[192,512]{1,0:T(8,128)(2,1)S(1)} %fusion.3), channel_id=1, source_target_pairs={{0,6},{2,4},{4,2},{6,0},{1,7},{3,5},{5,3},{7,1},{8,14},{10,12},{12... | collective-permute-start | bytes 589832 | tf_op jit(solution)/shard_map/ppermute | solution.py:245
  221.7 9.0 %collective-permute-start.12 = (bf16[768,512]{1,0:T(8,128)(2,1)S(1)}, bf16[768,512]{1,0:T(8,128)(2,1)S(1)}, u32[]{:S(2)}, u32[]{:S(2)}) collective-permute-start(bf16[768,512]{1,0:T(8,128)(2,1)S(1)} %pad_maximum_fusion.2.h_ref), channel_id=1, source_target_pairs={{0,1},{1,0},{2,3},{3,2},{4,5},{5,4},{6,7},{7,6},{8,9},{9,8},{10,11... | collective-permute-start | bytes 2359304 | tf_op jit(solution)/shard_map/ppermute | solution.py:27
  223.6 18.1 %collective-permute-start.13 = (bf16[192,1024]{1,0:T(8,128)(2,1)}, bf16[192,1024]{1,0:T(8,128)(2,1)}, u32[]{:S(2)}, u32[]{:S(2)}) collective-permute-start(bf16[192,1024]{1,0:T(8,128)(2,1)} %get-tuple-element.40), channel_id=1, source_target_pairs={{0,2},{2,0},{4,6},{6,4},{1,3},{3,1},{5,7},{7,5},{8,10},{10,8},{12,... | collective-permute-start | bytes 1179656 | tf_op jit(solution)/shard_map/ppermute | solution.py:245
  225.5 22.6 %collective-permute-start.14 = (bf16[192,1024]{1,0:T(8,128)(2,1)}, bf16[192,1024]{1,0:T(8,128)(2,1)S(1)}, u32[]{:S(2)}, u32[]{:S(2)}) collective-permute-start(bf16[192,1024]{1,0:T(8,128)(2,1)} %get-tuple-element.41), channel_id=1, source_target_pairs={{0,4},{2,6},{4,0},{6,2},{1,5},{3,7},{5,1},{7,3},{8,12},{10,14},{12... | collective-permute-start | bytes 1179656 | tf_op jit(solution)/shard_map/ppermute | solution.py:245
  233.6 48.6 %all-to-all-start.4 = ((bf16[8,96,768]{2,1,0:T(8,128)(2,1)}), bf16[8,96,768]{2,1,0:T(8,128)(2,1)}, u32[]{:S(2)}, u32[]{:S(2)}) async-start(bf16[8,96,768]{2,1,0:T(8,128)(2,1)} %bitcast.11), calls=%async_computation.4 | async-start | bytes 2359296 | tf_op jit(solution)/shard_map/all_to_all | solution.py:228
  250.4 9.7 %collective-permute-start.15 = (bf16[192,512]{1,0:T(8,128)(2,1)S(1)}, bf16[192,512]{1,0:T(8,128)(2,1)S(1)}, u32[]{:S(2)}, u32[]{:S(2)}) collective-permute-start(bf16[192,512]{1,0:T(8,128)(2,1)S(1)} %fusion.2), channel_id=1, source_target_pairs={{0,2},{2,0},{4,6},{6,4},{1,3},{3,1},{5,7},{7,5},{8,10},{10,8},{12,... | collective-permute-start | bytes 589832 | tf_op jit(solution)/shard_map/ppermute | solution.py:245
  254.4 16.7 %collective-permute-start.16 = (bf16[192,512]{1,0:T(8,128)(2,1)S(1)}, bf16[192,512]{1,0:T(8,128)(2,1)S(1)}, u32[]{:S(2)}, u32[]{:S(2)}) collective-permute-start(bf16[192,512]{1,0:T(8,128)(2,1)S(1)} %fusion.2), channel_id=1, source_target_pairs={{0,4},{2,6},{4,0},{6,2},{1,5},{3,7},{5,1},{7,3},{8,12},{10,14},{12... | collective-permute-start | bytes 589832 | tf_op jit(solution)/shard_map/ppermute | solution.py:245
  257.5 17.5 %collective-permute-start.17 = (bf16[192,512]{1,0:T(8,128)(2,1)S(1)}, bf16[192,512]{1,0:T(8,128)(2,1)S(1)}, u32[]{:S(2)}, u32[]{:S(2)}) collective-permute-start(bf16[192,512]{1,0:T(8,128)(2,1)S(1)} %fusion.2), channel_id=1, source_target_pairs={{0,6},{2,4},{4,2},{6,0},{1,7},{3,5},{5,3},{7,1},{8,14},{10,12},{12... | collective-permute-start | bytes 589832 | tf_op jit(solution)/shard_map/ppermute | solution.py:245
  275.0 4.2 %collective-permute-start.18 = (bf16[768,512]{1,0:T(8,128)(2,1)S(1)}, bf16[768,512]{1,0:T(8,128)(2,1)S(1)}, u32[]{:S(2)}, u32[]{:S(2)}) collective-permute-start(bf16[768,512]{1,0:T(8,128)(2,1)S(1)} %pad_maximum_fusion.3.h_ref), channel_id=1, source_target_pairs={{0,1},{1,0},{2,3},{3,2},{4,5},{5,4},{6,7},{7,6},{8,9},{9,8},{10,11... | collective-permute-start | bytes 2359304 | tf_op jit(solution)/shard_map/ppermute | solution.py:27
  282.1 39.0 %all-to-all-start.5 = ((bf16[8,96,768]{2,1,0:T(8,128)(2,1)}), bf16[8,96,768]{2,1,0:T(8,128)(2,1)S(1)}, u32[]{:S(2)}, u32[]{:S(2)}) async-start(bf16[8,96,768]{2,1,0:T(8,128)(2,1)} %bitcast.13), calls=%async_computation.5 | async-start | bytes 2359296 | tf_op jit(solution)/shard_map/all_to_all | solution.py:228
  (13 other events, 190.2 us)

commit v9 on v6

--- a/solution.py
+++ b/solution.py
@@ -12,6 +12,7 @@
 HD = 128
 EXPERTS = 4
 CAP = 24
+FIRST = 16
 F32 = jnp.float32
 BF16 = jnp.bfloat16
 
@@ -221,8 +222,7 @@
 
     nz = lax.axis_size("z")
     sources = EXPERTS * lax.axis_size("xl")
-    n = CAP // 2
-    block = sources * n
+    block_a, block_b = sources * FIRST, sources * (CAP - FIRST)
 
     def all_to_all(x, axes):
         return lax.all_to_all(x, axes, split_axis=0, concat_axis=0, tiled=True)
@@ -234,9 +234,10 @@
     rows = jnp.concatenate([packed, as_rows(squares, feat)], axis=1)
     rows = jnp.broadcast_to(rows[:, None], (EXPERTS, 2) + rows.shape[1:]).reshape(sources, CAP + 8, feat)
     rows = all_to_all(rows, GROUP)
-    part_a, part_b = (rows[:, k * n : (k + 1) * n].reshape(block, feat) for k in range(2))
+    part_a, part_b = rows[:, :FIRST].reshape(block_a, feat), rows[:, FIRST:CAP].reshape(block_b, feat)
     x_a = along_z(part_a)
-    squares = from_row(rows[:, CAP], CAP).reshape(sources, 2, n).transpose(1, 0, 2).reshape(2 * block)
+    squares = from_row(rows[:, CAP], CAP)
+    squares = jnp.concatenate([squares[:, :FIRST].reshape(block_a), squares[:, FIRST:].reshape(block_b)])
     inverse = lax.rsqrt(lax.psum(squares, EXP) / D + 1e-05)
     x_a, inverse = lax.optimization_barrier((x_a, inverse))
     x_b = along_z(jnp.concatenate([part_b, as_rows(inverse, feat)], axis=0))
@@ -254,26 +255,26 @@
         return down_terms(order, hid, swap(hid, "c"), w_down)
 
     def give_back(down):
-        return all_to_all(down.reshape(nz, block, feat), "z")
+        return all_to_all(down.reshape(nz, -1, feat), "z")
 
     def over_z(back):
-        return jnp.sum(back.astype(F32), axis=0).astype(BF16).reshape(sources, n, feat)
-
-    terms_a = gate_up_terms(order, x_a, swap(x_a, "c"), w_in, w_in_other, block)
+        return jnp.sum(back.astype(F32), axis=0).astype(BF16).reshape(sources, -1, feat)
+
+    terms_a = gate_up_terms(order, x_a, swap(x_a, "c"), w_in, w_in_other, block_a)
     sums_a = over_yl(terms_a)
     x_b = after(x_b, sums_a[3])
-    inverse = from_row(x_b[:, block], 2 * block)
-    terms_b = gate_up_terms(order, x_b, swap(x_b, "c"), w_in, w_in_other, block)
+    inverse = from_row(x_b[:, block_b], block_a + block_b)
+    terms_b = gate_up_terms(order, x_b, swap(x_b, "c"), w_in, w_in_other, block_b)
     sums_a[1] = after(sums_a[1], *terms_b)
-    hids_a = over_yl([hidden_of(sums_a, inverse[:, :block])] * 4)
+    hids_a = over_yl([hidden_of(sums_a, inverse[:, :block_a])] * 4)
     sums_b = over_yl(terms_b)
     hids_a[1] = after(hids_a[1], sums_b[3])
     down_a = down_of(hids_a)
     back_a = give_back(down_a)
     sums_b[1] = after(sums_b[1], down_a)
-    hids_b = over_yl([hidden_of(sums_b, inverse[:, block:])] * 4)
+    hids_b = over_yl([hidden_of(sums_b, inverse[:, block_a:])] * 4)
     back_a = after(back_a, *hids_b[1:])
-    back_b = give_back(down_of(hids_b))
+    back_b = give_back(after(down_of(hids_b), back_a))
     returned = all_to_all(jnp.concatenate([over_z(back_a), over_z(back_b)], axis=1), GROUP)
     returned = jnp.sum(returned.reshape(EXPERTS, 2, CAP, feat).astype(F32), axis=1)
     moe_rows = jnp.einsum(

time: 333 us -> 348 us (1.045)
  waiting for transfers between devices: 156 us -> 167 us
  starting transfers between devices: 88.5 us -> 92.9 us
    all_to_all x4, waiting for transfers between devices: 56.4 us -> 67.5 us  [all_to_all(): return lax.all_to_all(x, axes, split_axis=0, concat_axis=0, tiled=True)]
    all_to_all x4, starting transfers between devices: 18.4 us -> 24.1 us  [all_to_all(): return lax.all_to_all(x, axes, split_axis=0, concat_axis=0, tiled=True)]
  transfers between devices with their start and end apart: 24 -> 24, of which waited for: 17 -> 19; matrix products, arithmetic and copies ran while one was open for 3% -> 2% of each run, Pallas kernels for 5% -> 4%
where the time goes in v9:
time: 348 us; the launch traced here: 347 us
  waiting for transfers between devices  167 us (48%)
  starting transfers between devices  92.9 us (27%)
  blocking collectives  47.5 us (14%)
  Pallas kernels  24.1 us (7%)
  other arithmetic  8.13 us (2%)
  local copies, waits for them, and re-layouts  6.07 us (2%)
    ppermute x12, waiting for transfers between devices, over_yl(): lax.ppermute(parts[i], 'yl', Y_XOR[i])  71 us
    all_to_all x4, waiting for transfers between devices, all_to_all(): return lax.all_to_all(x, axes, split_axis=0, concat_axis=0, tiled=True)  67.5 us
    ppermute x12, starting transfers between devices, over_yl(): lax.ppermute(parts[i], 'yl', Y_XOR[i])  37.8 us
    all_to_all x2, blocking collectives, all_to_all(): return lax.all_to_all(x, axes, split_axis=0, concat_axis=0, tiled=True)  36.9 us
    all_to_all x4, starting transfers between devices, all_to_all(): return lax.all_to_all(x, axes, split_axis=0, concat_axis=0, tiled=True)  24.1 us
    all_to_all x1, waiting for transfers between devices, attend(): lax.all_to_all(jnp.broadcast_to(kv[None], (members,) + kv.shape), HALF, s...  19.6 us
    all_to_all x1, starting transfers between devices, attend(): lax.all_to_all(jnp.broadcast_to(kv[None], (members,) + kv.shape), HALF, s...  13.2 us
    pallas_call x2, Pallas kernels, gate_up_terms(): pl.pallas_call(expand, grid_spec=pltpu.PrefetchScalarGridSpec(num_scalar_...  12.2 us
  transfers between devices with their start and end apart: 24, of which 19 were waited for; matrix products, arithmetic and copies ran while one was open for 2% of the time, Pallas kernels for 4%

profile of v9, /device:TPU:8, one launch (start us, length us, event | category | flops | bytes accessed | tf_op | source)
XLA Modules:
  0.0 347.2 jit_solution(3511259376006521779)
XLA Ops:
  1.8 13.2 %all-to-all-start = ((bf16[32,64,256]{2,1,0:T(8,128)(2,1)}), bf16[32,64,256]{2,1,0:T(8,128)(2,1)S(1)}, u32[]{:S(2)}, u32[]{:S(2)}) async-start(bf16[32,64,256]{2,1,0:T(8,128)(2,1)} %broadcast_in_dim.32), calls=%async_computation | async-start | bytes 2097152 | tf_op jit(solution)/shard_map/all_to_all | solution.py:79
  24.0 19.6 %all-to-all-done = bf16[32,64,256]{2,1,0:T(8,128)(2,1)S(1)} async-done(((bf16[32,64,256]{2,1,0:T(8,128)(2,1)}), bf16[32,64,256]{2,1,0:T(8,128)(2,1)S(1)}, u32[]{:S(2)}, u32[]{:S(2)}) %all-to-all-start) | async-done | bytes 1048608 | tf_op jit(solution)/shard_map/all_to_all | solution.py:79
  43.7 6.0 %softmax_block.1 = (f32[64,768]{1,0:T(8,128)S(1)}, f32[64,768]{1,0:T(8,128)S(1)}, bf16[64,896]{1,0:T(8,128)(2,1)S(1)}) custom-call(s32[1]{0:T(128)} %bitcast.3.base_ref, bf16[64,768]{1,0:T(8,128)(2,1)S(1)} %copy-done.1, bf16[64,768]{1,0:T(8,128)(2,1)S(1)} %collective-permute-done.far_ref, bf16[2048,256]{1,0:T(8,128)(2,1)S(1)} %bitcast.54), custom_call_target="tpu_custom_call" | custom-call | flops 805306368 | bytes 1835008 | tf_op jit(solution)/shard_map/softmax_block/pallas_call | solution.py:84
  49.7 6.8 %collective-permute-start.2 = (bf16[64,896]{1,0:T(8,128)(2,1)S(1)}, bf16[64,896]{1,0:T(8,128)(2,1)S(1)}, u32[]{:S(2)}, u32[]{:S(2)}) collective-permute-start(bf16[64,896]{1,0:T(8,128)(2,1)S(1)} %get-tuple-element.29), channel_id=1, source_target_pairs={{0,256},{1,257},{2,258},{3,259},{4,260},{5,261},{6,262},{7,263},{8... | collective-permute-start | bytes 344072 | tf_op jit(solution)/shard_map/ppermute | solution.py:101
  60.9 20.1 %all_to_all.35 = bf16[8,32,768]{2,1,0:T(8,128)(2,1)S(1)} all-to-all(bf16[8,32,768]{2,1,0:T(8,128)(2,1)S(1)} %bitcast.55), channel_id=1, replica_groups=mesh['yh'=2,'xh'=2,'xl'=2,'z'=8,'yl'=4,'c'=2] {'yh','xh','xl'}, dimensions={0} | all-to-all | bytes 786432 | tf_op jit(solution)/shard_map/all_to_all | solution.py:228
  82.3 6.8 %all-to-all-start.2 = ((bf16[8,128,768]{2,1,0:T(8,128)(2,1)}), bf16[8,128,768]{2,1,0:T(8,128)(2,1)S(1)}, u32[]{:S(2)}, u32[]{:S(2)}) async-start(bf16[8,128,768]{2,1,0:T(8,128)(2,1)} %broadcast_in_dim.67), calls=%async_computation.2 | async-start | bytes 3145728 | tf_op jit(solution)/shard_map/all_to_all | solution.py:228
  89.4 10.6 %psum.7 = f32[192]{0:T(256)S(1)} all-reduce(f32[192]{0:T(256)S(1)} %pad_maximum_fusion.7), channel_id=1, replica_groups=mesh['yh'=2,'xh'=2,'xl'=2,'z'=8,'yl'=4,'c'=2] {'yl','c'}, use_global_device_ids=true, to_apply=%region_4.5 | all-reduce | flops 192 | bytes 1536 | tf_op jit(solution)/shard_map/psum | solution.py:241
  100.0 29.0 %all-to-all-done.2.x_ref = bf16[8,128,768]{2,1,0:T(8,128)(2,1)S(1)} async-done(((bf16[8,128,768]{2,1,0:T(8,128)(2,1)}), bf16[8,128,768]{2,1,0:T(8,128)(2,1)S(1)}, u32[]{:S(2)}, u32[]{:S(2)}) %all-to-all-start.2) | async-done | bytes 1572896 | tf_op jit(solution)/shard_map/all_to_all | solution.py:228
  135.7 7.3 %gate_up_terms.2 = (bf16[256,1024]{1,0:T(8,128)(2,1)}, bf16[256,1024]{1,0:T(8,128)(2,1)}, bf16[256,1024]{1,0:T(8,128)(2,1)}, bf16[256,1024]{1,0:T(8,128)(2,1)}) custom-call(s32[2]{0:T(128)S(1)} %pad_add_fusion.order_ref, bf16[8,128,768]{2,1,0:T(8,128)(2,1)S(1)} %all-to-all-done.2.x_ref, bf16[8,128,768]{2,1,0:T(8,128)(2,1)} %collective-permute-done.3.o_ref, ...), custom_call_target="tpu_custom_call" | custom-call | flops 3221225472 | bytes 5242880 | tf_op jit(solution)/shard_map/gate_up_terms/pallas_call | solution.py:130
  144.8 16.8 %all-to-all-done.3.x_ref = bf16[8,72,768]{2,1,0:T(8,128)(2,1)S(1)} async-done(((bf16[8,72,768]{2,1,0:T(8,128)(2,1)}), bf16[8,72,768]{2,1,0:T(8,128)(2,1)S(1)}, u32[]{:S(2)}, u32[]{:S(2)}) %all-to-all-start.3) | async-done | bytes 884768 | tf_op jit(solution)/shard_map/all_to_all | solution.py:228
  173.3 4.9 %gate_up_terms.3 = (bf16[128,1024]{1,0:T(8,128)(2,1)}, bf16[128,1024]{1,0:T(8,128)(2,1)}, bf16[128,1024]{1,0:T(8,128)(2,1)}, bf16[128,1024]{1,0:T(8,128)(2,1)}) custom-call(s32[2]{0:T(128)S(1)} %pad_add_fusion.order_ref, bf16[8,72,768]{2,1,0:T(8,128)(2,1)S(1)} %all-to-all-done.3.x_ref, bf16[8,72,768]{2,1,0:T(8,128)(2,1)S(1)} %collective-permute-done.6.o_ref, ...), custom_call_target="tpu_custom_call" | custom-call | flops 1610612736 | bytes 4194304 | tf_op jit(solution)/shard_map/gate_up_terms/pallas_call | solution.py:130
  178.2 11.5 %collective-permute-done.4 = bf16[256,1024]{1,0:T(8,128)(2,1)S(1)} collective-permute-done((bf16[256,1024]{1,0:T(8,128)(2,1)}, bf16[256,1024]{1,0:T(8,128)(2,1)S(1)}, u32[]{:S(2)}, u32[]{:S(2)}) %collective-permute-start.4) | collective-permute-done | bytes 524320 | tf_op jit(solution)/shard_map/ppermute | solution.py:246
  189.8 6.5 %collective-permute-done.7 = bf16[256,1024]{1,0:T(8,128)(2,1)} collective-permute-done((bf16[256,1024]{1,0:T(8,128)(2,1)}, bf16[256,1024]{1,0:T(8,128)(2,1)}, u32[]{:S(2)}, u32[]{:S(2)}) %collective-permute-start.7) | collective-permute-done | bytes 524320 | tf_op jit(solution)/shard_map/ppermute | solution.py:246
  197.8 6.1 %collective-permute-start.8 = (bf16[256,512]{1,0:T(8,128)(2,1)S(1)}, bf16[256,512]{1,0:T(8,128)(2,1)S(1)}, u32[]{:S(2)}, u32[]{:S(2)}) collective-permute-start(bf16[256,512]{1,0:T(8,128)(2,1)S(1)} %fusion.2), channel_id=1, source_target_pairs={{0,2},{2,0},{4,6},{6,4},{1,3},{3,1},{5,7},{7,5},{8,10},{10,8},{12,... | collective-permute-start | bytes 786440 | tf_op jit(solution)/shard_map/ppermute | solution.py:246
  214.3 17.0 %collective-permute-done.9 = bf16[128,1024]{1,0:T(8,128)(2,1)S(1)} collective-permute-done((bf16[128,1024]{1,0:T(8,128)(2,1)S(1)}, bf16[128,1024]{1,0:T(8,128)(2,1)S(1)}, u32[]{:S(2)}, u32[]{:S(2)}) %collective-permute-start.9) | collective-permute-done | bytes 262176 | tf_op jit(solution)/shard_map/ppermute | solution.py:246
  235.0 6.1 %collective-permute-done.11 = bf16[256,512]{1,0:T(8,128)(2,1)S(1)} collective-permute-done((bf16[256,512]{1,0:T(8,128)(2,1)S(1)}, bf16[256,512]{1,0:T(8,128)(2,1)S(1)}, u32[]{:S(2)}, u32[]{:S(2)}) %collective-permute-start.11) | collective-permute-done | bytes 262176 | tf_op jit(solution)/shard_map/ppermute | solution.py:246
  249.2 7.0 %all-to-all-start.4 = ((bf16[8,128,768]{2,1,0:T(8,128)(2,1)}), bf16[8,128,768]{2,1,0:T(8,128)(2,1)}, u32[]{:S(2)}, u32[]{:S(2)}) async-start(bf16[8,128,768]{2,1,0:T(8,128)(2,1)} %bitcast.11), calls=%async_computation.4 | async-start | bytes 3145728 | tf_op jit(solution)/shard_map/all_to_all | solution.py:228
  261.9 5.4 %collective-permute-done.13 = bf16[128,1024]{1,0:T(8,128)(2,1)S(1)} collective-permute-done((bf16[128,1024]{1,0:T(8,128)(2,1)S(1)}, bf16[128,1024]{1,0:T(8,128)(2,1)S(1)}, u32[]{:S(2)}, u32[]{:S(2)}) %collective-permute-start.13) | collective-permute-done | bytes 262176 | tf_op jit(solution)/shard_map/ppermute | solution.py:246
  267.3 5.5 %collective-permute-done.14 = bf16[128,1024]{1,0:T(8,128)(2,1)S(1)} collective-permute-done((bf16[128,1024]{1,0:T(8,128)(2,1)S(1)}, bf16[128,1024]{1,0:T(8,128)(2,1)S(1)}, u32[]{:S(2)}, u32[]{:S(2)}) %collective-permute-start.14) | collective-permute-done | bytes 262176 | tf_op jit(solution)/shard_map/ppermute | solution.py:246
  273.0 5.6 %collective-permute-start.15 = (bf16[128,512]{1,0:T(8,128)(2,1)S(1)}, bf16[128,512]{1,0:T(8,128)(2,1)S(1)}, u32[]{:S(2)}, u32[]{:S(2)}) collective-permute-start(bf16[128,512]{1,0:T(8,128)(2,1)S(1)} %fusion.4), channel_id=1, source_target_pairs={{0,2},{2,0},{4,6},{6,4},{1,3},{3,1},{5,7},{7,5},{8,10},{10,8},{12,... | collective-permute-start | bytes 393224 | tf_op jit(solution)/shard_map/ppermute | solution.py:246
  287.5 5.2 %collective-permute-done.17 = bf16[128,512]{1,0:T(8,128)(2,1)S(1)} collective-permute-done((bf16[128,512]{1,0:T(8,128)(2,1)S(1)}, bf16[128,512]{1,0:T(8,128)(2,1)S(1)}, u32[]{:S(2)}, u32[]{:S(2)}) %collective-permute-start.17) | collective-permute-done | bytes 131104 | tf_op jit(solution)/shard_map/ppermute | solution.py:246
  299.0 6.8 %all-to-all-start.5 = ((bf16[8,64,768]{2,1,0:T(8,128)(2,1)}), bf16[8,64,768]{2,1,0:T(8,128)(2,1)S(1)}, u32[]{:S(2)}, u32[]{:S(2)}) async-start(bf16[8,64,768]{2,1,0:T(8,128)(2,1)} %bitcast.14), calls=%async_computation.5 | async-start | bytes 1572864 | tf_op jit(solution)/shard_map/all_to_all | solution.py:228
  307.5 21.8 %all-to-all-done.5 = bf16[8,64,768]{2,1,0:T(8,128)(2,1)S(1)} async-done(((bf16[8,64,768]{2,1,0:T(8,128)(2,1)}), bf16[8,64,768]{2,1,0:T(8,128)(2,1)S(1)}, u32[]{:S(2)}, u32[]{:S(2)}) %all-to-all-start.5) | async-done | bytes 786464 | tf_op jit(solution)/shard_map/all_to_all | solution.py:228
  329.4 16.8 %all_to_all.36 = bf16[8,24,768]{2,1,0:T(8,128)(2,1)S(1)} all-to-all(bf16[8,24,768]{2,1,0:T(8,128)(2,1)S(1)} %pad_maximum_fusion.4), channel_id=1, replica_groups=mesh['yh'=2,'xh'=2,'xl'=2,'z'=8,'yl'=4,'c'=2] {'yh','xh','xl'}, dimensions={0} | all-to-all | bytes 589824 | tf_op jit(solution)/shard_map/all_to_all | solution.py:228
  (112 shorter events, 84.6 us)
Async XLA Ops:
  1.8 41.8 %all-to-all-start = ((bf16[32,64,256]{2,1,0:T(8,128)(2,1)}), bf16[32,64,256]{2,1,0:T(8,128)(2,1)S(1)}, u32[]{:S(2)}, u32[]{:S(2)}) async-start(bf16[32,64,256]{2,1,0:T(8,128)(2,1)} %broadcast_in_dim.32), calls=%async_computation | async-start | bytes 2097152 | tf_op jit(solution)/shard_map/all_to_all | solution.py:79
  18.4 5.6 %collective-permute-start.1 = (bf16[1024,768]{1,0:T(8,128)(2,1)}, bf16[1024,768]{1,0:T(8,128)(2,1)}, u32[]{:S(2)}, u32[]{:S(2)}) collective-permute-start(bf16[1024,768]{1,0:T(8,128)(2,1)} %pad_maximum_fusion.1), channel_id=1, source_target_pairs={{0,1},{1,0},{2,3},{3,2},{4,5},{5,4},{6,7},{7,6},{8,9},{9,8},{10,11... | collective-permute-start | bytes 4718600 | tf_op jit(solution)/shard_map/ppermute | solution.py:28
  20.3 23.4 %collective-permute-start = (bf16[64,768]{1,0:T(8,128)(2,1)S(1)}, bf16[64,768]{1,0:T(8,128)(2,1)S(1)}, u32[]{:S(2)}, u32[]{:S(2)}) collective-permute-start(bf16[64,768]{1,0:T(8,128)(2,1)S(1)} %copy-done.1), channel_id=1, source_target_pairs={{256,0},{257,1},{258,2},{259,3},{260,4},{261,5},{262,6},{263,7},{2... | collective-permute-start | bytes 294920 | tf_op jit(solution)/shard_map/ppermute | solution.py:76
  49.7 10.4 %collective-permute-start.2 = (bf16[64,896]{1,0:T(8,128)(2,1)S(1)}, bf16[64,896]{1,0:T(8,128)(2,1)S(1)}, u32[]{:S(2)}, u32[]{:S(2)}) collective-permute-start(bf16[64,896]{1,0:T(8,128)(2,1)S(1)} %get-tuple-element.29), channel_id=1, source_target_pairs={{0,256},{1,257},{2,258},{3,259},{4,260},{5,261},{6,262},{7,263},{8... | collective-permute-start | bytes 344072 | tf_op jit(solution)/shard_map/ppermute | solution.py:101
  82.3 46.7 %all-to-all-start.2 = ((bf16[8,128,768]{2,1,0:T(8,128)(2,1)}), bf16[8,128,768]{2,1,0:T(8,128)(2,1)S(1)}, u32[]{:S(2)}, u32[]{:S(2)}) async-start(bf16[8,128,768]{2,1,0:T(8,128)(2,1)} %broadcast_in_dim.67), calls=%async_computation.2 | async-start | bytes 3145728 | tf_op jit(solution)/shard_map/all_to_all | solution.py:228
  129.0 6.7 %collective-permute-start.3 = (bf16[8,128,768]{2,1,0:T(8,128)(2,1)S(1)}, bf16[8,128,768]{2,1,0:T(8,128)(2,1)}, u32[]{:S(2)}, u32[]{:S(2)}) collective-permute-start(bf16[8,128,768]{2,1,0:T(8,128)(2,1)S(1)} %all-to-all-done.2.x_ref), channel_id=1, source_target_pairs={{0,1},{1,0},{2,3},{3,2},{4,5},{5,4},{6,7},{7,6},{8,9},{9,8},{10,11... | collective-permute-start | bytes 4718600 | tf_op jit(solution)/shard_map/ppermute | solution.py:28
  132.0 29.6 %all-to-all-start.3 = ((bf16[8,72,768]{2,1,0:T(8,128)(2,1)}), bf16[8,72,768]{2,1,0:T(8,128)(2,1)S(1)}, u32[]{:S(2)}, u32[]{:S(2)}) async-start(bf16[8,72,768]{2,1,0:T(8,128)(2,1)} %broadcast_in_dim.69), calls=%async_computation.3 | async-start | bytes 1769472 | tf_op jit(solution)/shard_map/all_to_all | solution.py:228
  142.9 23.0 %collective-permute-start.5 = (bf16[256,1024]{1,0:T(8,128)(2,1)}, bf16[256,1024]{1,0:T(8,128)(2,1)S(1)}, u32[]{:S(2)}, u32[]{:S(2)}) collective-permute-start(bf16[256,1024]{1,0:T(8,128)(2,1)} %get-tuple-element.37), channel_id=1, source_target_pairs={{0,6},{2,4},{4,2},{6,0},{1,7},{3,5},{5,3},{7,1},{8,14},{10,12},{12... | collective-permute-start | bytes 1572872 | tf_op jit(solution)/shard_map/ppermute | solution.py:246
  165.9 7.4 %collective-permute-start.6 = (bf16[8,72,768]{2,1,0:T(8,128)(2,1)S(1)}, bf16[8,72,768]{2,1,0:T(8,128)(2,1)S(1)}, u32[]{:S(2)}, u32[]{:S(2)}) collective-permute-start(bf16[8,72,768]{2,1,0:T(8,128)(2,1)S(1)} %all-to-all-done.3.x_ref), channel_id=1, source_target_pairs={{0,1},{1,0},{2,3},{3,2},{4,5},{5,4},{6,7},{7,6},{8,9},{9,8},{10,11... | collective-permute-start | bytes 2654216 | tf_op jit(solution)/shard_map/ppermute | solution.py:28
  167.9 21.8 %collective-permute-start.4 = (bf16[256,1024]{1,0:T(8,128)(2,1)}, bf16[256,1024]{1,0:T(8,128)(2,1)S(1)}, u32[]{:S(2)}, u32[]{:S(2)}) collective-permute-start(bf16[256,1024]{1,0:T(8,128)(2,1)} %get-tuple-element.35), channel_id=1, source_target_pairs={{0,2},{2,0},{4,6},{6,4},{1,3},{3,1},{5,7},{7,5},{8,10},{10,8},{12,... | collective-permute-start | bytes 1572872 | tf_op jit(solution)/shard_map/ppermute | solution.py:246
  169.8 26.4 %collective-permute-start.7 = (bf16[256,1024]{1,0:T(8,128)(2,1)}, bf16[256,1024]{1,0:T(8,128)(2,1)}, u32[]{:S(2)}, u32[]{:S(2)}) collective-permute-start(bf16[256,1024]{1,0:T(8,128)(2,1)} %get-tuple-element.44), channel_id=1, source_target_pairs={{0,4},{2,6},{4,0},{6,2},{1,5},{3,7},{5,1},{7,3},{8,12},{10,14},{12... | collective-permute-start | bytes 1572872 | tf_op jit(solution)/shard_map/ppermute | solution.py:246
  197.8 16.5 %collective-permute-start.8 = (bf16[256,512]{1,0:T(8,128)(2,1)S(1)}, bf16[256,512]{1,0:T(8,128)(2,1)S(1)}, u32[]{:S(2)}, u32[]{:S(2)}) collective-permute-start(bf16[256,512]{1,0:T(8,128)(2,1)S(1)} %fusion.2), channel_id=1, source_target_pairs={{0,2},{2,0},{4,6},{6,4},{1,3},{3,1},{5,7},{7,5},{8,10},{10,8},{12,... | collective-permute-start | bytes 786440 | tf_op jit(solution)/shard_map/ppermute | solution.py:246
  203.9 27.4 %collective-permute-start.9 = (bf16[128,1024]{1,0:T(8,128)(2,1)S(1)}, bf16[128,1024]{1,0:T(8,128)(2,1)S(1)}, u32[]{:S(2)}, u32[]{:S(2)}) collective-permute-start(bf16[128,1024]{1,0:T(8,128)(2,1)S(1)} %copy-done.10), channel_id=1, source_target_pairs={{0,6},{2,4},{4,2},{6,0},{1,7},{3,5},{5,3},{7,1},{8,14},{10,12},{12... | collective-permute-start | bytes 786440 | tf_op jit(solution)/shard_map/ppermute | solution.py:246
  205.8 29.2 %collective-permute-start.10 = (bf16[256,512]{1,0:T(8,128)(2,1)S(1)}, bf16[256,512]{1,0:T(8,128)(2,1)S(1)}, u32[]{:S(2)}, u32[]{:S(2)}) collective-permute-start(bf16[256,512]{1,0:T(8,128)(2,1)S(1)} %fusion.2), channel_id=1, source_target_pairs={{0,4},{2,6},{4,0},{6,2},{1,5},{3,7},{5,1},{7,3},{8,12},{10,14},{12... | collective-permute-start | bytes 786440 | tf_op jit(solution)/shard_map/ppermute | solution.py:246
  210.1 31.0 %collective-permute-start.11 = (bf16[256,512]{1,0:T(8,128)(2,1)S(1)}, bf16[256,512]{1,0:T(8,128)(2,1)S(1)}, u32[]{:S(2)}, u32[]{:S(2)}) collective-permute-start(bf16[256,512]{1,0:T(8,128)(2,1)S(1)} %fusion.2), channel_id=1, source_target_pairs={{0,6},{2,4},{4,2},{6,0},{1,7},{3,5},{5,3},{7,1},{8,14},{10,12},{12... | collective-permute-start | bytes 786440 | tf_op jit(solution)/shard_map/ppermute | solution.py:246
  241.2 4.6 %collective-permute-start.12 = (bf16[1024,512]{1,0:T(8,128)(2,1)S(1)}, bf16[1024,512]{1,0:T(8,128)(2,1)S(1)}, u32[]{:S(2)}, u32[]{:S(2)}) collective-permute-start(bf16[1024,512]{1,0:T(8,128)(2,1)S(1)} %pad_maximum_fusion.2.h_ref), channel_id=1, source_target_pairs={{0,1},{1,0},{2,3},{3,2},{4,5},{5,4},{6,7},{7,6},{8,9},{9,8},{10,11... | collective-permute-start | bytes 3145736 | tf_op jit(solution)/shard_map/ppermute | solution.py:28
  249.2 49.8 %all-to-all-start.4 = ((bf16[8,128,768]{2,1,0:T(8,128)(2,1)}), bf16[8,128,768]{2,1,0:T(8,128)(2,1)}, u32[]{:S(2)}, u32[]{:S(2)}) async-start(bf16[8,128,768]{2,1,0:T(8,128)(2,1)} %bitcast.11), calls=%async_computation.4 | async-start | bytes 3145728 | tf_op jit(solution)/shard_map/all_to_all | solution.py:228
  256.2 11.1 %collective-permute-start.13 = (bf16[128,1024]{1,0:T(8,128)(2,1)S(1)}, bf16[128,1024]{1,0:T(8,128)(2,1)S(1)}, u32[]{:S(2)}, u32[]{:S(2)}) collective-permute-start(bf16[128,1024]{1,0:T(8,128)(2,1)S(1)} %copy-done.9), channel_id=1, source_target_pairs={{0,2},{2,0},{4,6},{6,4},{1,3},{3,1},{5,7},{7,5},{8,10},{10,8},{12,... | collective-permute-start | bytes 786440 | tf_op jit(solution)/shard_map/ppermute | solution.py:246
  258.2 14.6 %collective-permute-start.14 = (bf16[128,1024]{1,0:T(8,128)(2,1)S(1)}, bf16[128,1024]{1,0:T(8,128)(2,1)S(1)}, u32[]{:S(2)}, u32[]{:S(2)}) collective-permute-start(bf16[128,1024]{1,0:T(8,128)(2,1)S(1)} %copy-done.8), channel_id=1, source_target_pairs={{0,4},{2,6},{4,0},{6,2},{1,5},{3,7},{5,1},{7,3},{8,12},{10,14},{12... | collective-permute-start | bytes 786440 | tf_op jit(solution)/shard_map/ppermute | solution.py:246
  273.0 10.9 %collective-permute-start.15 = (bf16[128,512]{1,0:T(8,128)(2,1)S(1)}, bf16[128,512]{1,0:T(8,128)(2,1)S(1)}, u32[]{:S(2)}, u32[]{:S(2)}) collective-permute-start(bf16[128,512]{1,0:T(8,128)(2,1)S(1)} %fusion.4), channel_id=1, source_target_pairs={{0,2},{2,0},{4,6},{6,4},{1,3},{3,1},{5,7},{7,5},{8,10},{10,8},{12,... | collective-permute-start | bytes 393224 | tf_op jit(solution)/shard_map/ppermute | solution.py:246
  278.6 9.0 %collective-permute-start.16 = (bf16[128,512]{1,0:T(8,128)(2,1)S(1)}, bf16[128,512]{1,0:T(8,128)(2,1)S(1)}, u32[]{:S(2)}, u32[]{:S(2)}) collective-permute-start(bf16[128,512]{1,0:T(8,128)(2,1)S(1)} %fusion.4), channel_id=1, source_target_pairs={{0,4},{2,6},{4,0},{6,2},{1,5},{3,7},{5,1},{7,3},{8,12},{10,14},{12... | collective-permute-start | bytes 393224 | tf_op jit(solution)/shard_map/ppermute | solution.py:246
  280.5 12.3 %collective-permute-start.17 = (bf16[128,512]{1,0:T(8,128)(2,1)S(1)}, bf16[128,512]{1,0:T(8,128)(2,1)S(1)}, u32[]{:S(2)}, u32[]{:S(2)}) collective-permute-start(bf16[128,512]{1,0:T(8,128)(2,1)S(1)} %fusion.4), channel_id=1, source_target_pairs={{0,6},{2,4},{4,2},{6,0},{1,7},{3,5},{5,3},{7,1},{8,14},{10,12},{12... | collective-permute-start | bytes 393224 | tf_op jit(solution)/shard_map/ppermute | solution.py:246
  292.8 3.8 %collective-permute-start.18 = (bf16[512,512]{1,0:T(8,128)(2,1)S(1)}, bf16[512,512]{1,0:T(8,128)(2,1)S(1)}, u32[]{:S(2)}, u32[]{:S(2)}) collective-permute-start(bf16[512,512]{1,0:T(8,128)(2,1)S(1)} %pad_maximum_fusion.3.h_ref), channel_id=1, source_target_pairs={{0,1},{1,0},{2,3},{3,2},{4,5},{5,4},{6,7},{7,6},{8,9},{9,8},{10,11... | collective-permute-start | bytes 1572872 | tf_op jit(solution)/shard_map/ppermute | solution.py:28
  299.0 30.2 %all-to-all-start.5 = ((bf16[8,64,768]{2,1,0:T(8,128)(2,1)}), bf16[8,64,768]{2,1,0:T(8,128)(2,1)S(1)}, u32[]{:S(2)}, u32[]{:S(2)}) async-start(bf16[8,64,768]{2,1,0:T(8,128)(2,1)} %bitcast.14), calls=%async_computation.5 | async-start | bytes 1572864 | tf_op jit(solution)/shard_map/all_to_all | solution.py:228
  (11 other events, 198.3 us)

commit v10 on v6

--- a/solution.py
+++ b/solution.py
@@ -40,45 +40,42 @@
     heads = own_ref.shape[1] // HD
     scale = 1.0 / math.sqrt(HD)
     keys, values = kv_ref[:, :HD], kv_ref[:, HD:]
-    limit = base_ref[0] + lax.broadcasted_iota(jnp.int32, (rows, count), 0)
-    allowed = lax.broadcasted_iota(jnp.int32, (rows, count), 1) <= limit
+    row = lax.broadcasted_iota(jnp.int32, (2 * rows, count), 0)
+    limit = jnp.where(row < rows, base_ref[0] + row, count)
+    allowed = lax.broadcasted_iota(jnp.int32, (2 * rows, count), 1) <= limit
     lane = lax.broadcasted_iota(jnp.int32, (rows, HD), 1)
     tail = jnp.zeros((rows, HD), F32)
     for h in range(heads):
         cols = slice(h * HD, (h + 1) * HD)
-        for far, ref in ((False, own_ref), (True, far_ref)):
-            dots = lax.dot_general(ref[:, cols], keys, (((1,), (1,)), ((), ())), preferred_element_type=F32)
-            if not far:
-                dots = jnp.where(allowed, dots, -1e30)
-            top = jnp.max(dots, axis=1, keepdims=True)
-            weights = jnp.exp2((dots - top) * (scale * math.log2(math.e)))
-            total = jnp.sum(weights, axis=1, keepdims=True)
-            acc = jnp.dot(weights.astype(BF16), values, preferred_element_type=F32)
-            out = acc / total
-            lse = top * scale + jnp.log(total)
-            if far:
-                message_ref[:, cols] = out.astype(BF16)
-                hi = lse.astype(BF16).astype(F32)
-                mid = (lse - hi).astype(BF16).astype(F32)
-                for k, part in enumerate((hi, mid, lse - hi - mid)):
-                    tail = jnp.where(lane == k * heads + h, part, tail)
-            else:
-                out_ref[:, cols] = out
-                lse_ref[:, cols] = jnp.broadcast_to(lse, (rows, HD))
+        both = jnp.concatenate([own_ref[:, cols], far_ref[:, cols]], axis=0)
+        dots = lax.dot_general(both, keys, (((1,), (1,)), ((), ())), preferred_element_type=F32)
+        dots = jnp.where(allowed, dots, -1e30)
+        top = jnp.max(dots, axis=1, keepdims=True)
+        weights = jnp.exp2((dots - top) * (scale * math.log2(math.e)))
+        total = jnp.sum(weights, axis=1, keepdims=True)
+        out = jnp.dot(weights.astype(BF16), values, preferred_element_type=F32) / total
+        lse = top * scale + jnp.log(total)
+        out_ref[:, cols] = out[:rows]
+        lse_ref[:, cols] = jnp.broadcast_to(lse[:rows], (rows, HD))
+        message_ref[:, cols] = out[rows:].astype(BF16)
+        lse = lse[rows:]
+        hi = lse.astype(BF16).astype(F32)
+        mid = (lse - hi).astype(BF16).astype(F32)
+        for k, part in enumerate((hi, mid, lse - hi - mid)):
+            tail = jnp.where(lane == k * heads + h, part, tail)
     message_ref[:, heads * HD :] = tail.astype(BF16)
 
 
-def attend(queries, keys, values, early):
+def attend(queries, keys, values):
     rows, width = queries.shape
     heads = width // HD
     yh = lax.axis_index("yh")
     foreign = lax.ppermute(queries, "yh", [(1, 0)])
     kv = jnp.concatenate([keys, values], axis=1)
     members = lax.axis_size(HALF)
-    kv = lax.all_to_all(
-        jnp.broadcast_to(kv[None], (members,) + kv.shape), HALF, split_axis=0, concat_axis=0, tiled=True
-    ).reshape(members * rows, 2 * HD)
-    kv, *early = lax.optimization_barrier((kv,) + early)
+    for axes in ("z", ("xh", "xl")):
+        copies = jnp.broadcast_to(kv[None], (lax.axis_size(axes),) + kv.shape)
+        kv = lax.all_to_all(copies, axes, split_axis=0, concat_axis=0, tiled=True).reshape(-1, 2 * HD)
     whole = pl.BlockSpec(memory_space=pltpu.VMEM)
     out, lse, message = pl.pallas_call(
         softmax_block,
@@ -101,7 +98,7 @@
     parts = got[:, width : width + 3 * heads].astype(F32)
     got_lse = parts[:, :heads] + parts[:, heads : 2 * heads] + parts[:, 2 * heads :]
     share = jnp.where(yh == 1, jax.nn.sigmoid(jnp.repeat(got_lse, HD, axis=1) - lse), 0.0)
-    return (out * (1.0 - share) + got[:, :width].astype(F32) * share).astype(BF16), early
+    return (out * (1.0 - share) + got[:, :width].astype(F32) * share).astype(BF16)
 
 
 def expand(order_ref, x_ref, o_ref, w_ref, wo_ref, *rest):
@@ -195,12 +192,12 @@
     me = lax.axis_index("yl")
     order = jnp.stack([me, core]).astype(jnp.int32)
 
-    def halves(which):
-        cut = partial(lax.dynamic_slice_in_dim, start_index=which * half, slice_size=half, axis=0)
-        return jnp.concatenate([cut(w_gate), cut(w_up)], axis=0)
-
-    w_in = halves(core)
-    w_in_other = swap(halves(1 - core), "c")
+    def prepare(*weights):
+        def halves(which):
+            cut = partial(lax.dynamic_slice_in_dim, start_index=which * half, slice_size=half, axis=0)
+            return jnp.concatenate([cut(w) for w in weights], axis=0)
+
+        return halves(core), swap(halves(1 - core), "c")
 
     chosen = routes[:, 0]
     expert_ids = jnp.arange(EXPERTS, dtype=jnp.int32)
@@ -212,7 +209,7 @@
     )
     select = taken.astype(BF16)
 
-    attn, (w_in, w_in_other) = attend(queries, keys, values, (w_in, w_in_other))
+    attn = attend(queries, keys, values)
     mixed = residual.astype(F32) + attn.astype(F32)
     squares = jnp.sum(mixed * mixed, axis=1)
     packed = jnp.einsum(
@@ -238,7 +235,8 @@
     x_a = along_z(part_a)
     squares = from_row(rows[:, CAP], CAP).reshape(sources, 2, n).transpose(1, 0, 2).reshape(2 * block)
     inverse = lax.rsqrt(lax.psum(squares, EXP) / D + 1e-05)
-    x_a, inverse = lax.optimization_barrier((x_a, inverse))
+    inverse, w_gate, w_up = lax.optimization_barrier((inverse, w_gate, w_up))
+    x_a, w_in, w_in_other = lax.optimization_barrier((x_a,) + prepare(w_gate, w_up))
     x_b = along_z(jnp.concatenate([part_b, as_rows(inverse, feat)], axis=0))
 
     def over_yl(parts):

time: 333 us -> 327 us (0.982)
  blocking collectives: 44.6 us -> 68.5 us
  waiting for transfers between devices: 156 us -> 133 us
  starting transfers between devices: 88.5 us -> 83.1 us
    all_to_all x0 -> x1, blocking collectives: none -> 22 us  [attend(): lax.all_to_all(copies, axes, split_axis=0, concat_axis=0, tiled=True)]
    all_to_all x1, waiting for transfers between devices: 19.6 us -> 2.9 us  [attend(): lax.all_to_all(copies, axes, split_axis=0, concat_axis=0, tiled=True)]
    ppermute x12, waiting for transfers between devices: 70.7 us -> 58.3 us  [over_yl(): lax.ppermute(parts[i], 'yl', Y_XOR[i])]
    all_to_all x1, starting transfers between devices: 13.2 us -> 4.29 us  [attend(): lax.all_to_all(copies, axes, split_axis=0, concat_axis=0, tiled=True)]
    ppermute x1, waiting for transfers between devices: 0.01 us -> 8.73 us  [attend(): foreign = lax.ppermute(queries, 'yh', [(1, 0)])]
  transfers between devices with their start and end apart: 24 -> 24, of which waited for: 17 -> 19; matrix products, arithmetic and copies ran while one was open for 3% -> 4% of each run, Pallas kernels for 5% -> 6%
where the time goes in v10:
time: 327 us; the launch traced here: 326 us
  waiting for transfers between devices  133 us (41%)
  starting transfers between devices  83.1 us (25%)
  blocking collectives  68.5 us (21%)
  Pallas kernels  21.3 us (7%)
  other arithmetic  10.4 us (3%)
  local copies, waits for them, and re-layouts  7.91 us (2%)
    ppermute x12, waiting for transfers between devices, over_yl(): lax.ppermute(parts[i], 'yl', Y_XOR[i])  58.3 us
    all_to_all x4, waiting for transfers between devices, all_to_all(): return lax.all_to_all(x, axes, split_axis=0, concat_axis=0, tiled=True)  54.6 us
    ppermute x12, starting transfers between devices, over_yl(): lax.ppermute(parts[i], 'yl', Y_XOR[i])  39.4 us
    all_to_all x2, blocking collectives, all_to_all(): return lax.all_to_all(x, axes, split_axis=0, concat_axis=0, tiled=True)  36.2 us
    all_to_all x1, blocking collectives, attend(): lax.all_to_all(copies, axes, split_axis=0, concat_axis=0, tiled=True)  22 us
    all_to_all x4, starting transfers between devices, all_to_all(): return lax.all_to_all(x, axes, split_axis=0, concat_axis=0, tiled=True)  21.7 us
    pallas_call x2, Pallas kernels, gate_up_terms(): pl.pallas_call(expand, grid_spec=pltpu.PrefetchScalarGridSpec(num_scalar_...  12.1 us
    psum x1, blocking collectives, body(): inverse = lax.rsqrt(lax.psum(squares, EXP) / D + 1e-05)  10.3 us
  transfers between devices with their start and end apart: 24, of which 19 were waited for; matrix products, arithmetic and copies ran while one was open for 4% of the time, Pallas kernels for 6%

profile of v10, /device:TPU:8, one launch (start us, length us, event | category | flops | bytes accessed | tf_op | source)
XLA Modules:
  0.0 325.9 jit_solution(493683575653851164)
XLA Ops:
  0.8 22.0 %all_to_all.40 = bf16[8,64,256]{2,1,0:T(8,128)(2,1)S(1)} all-to-all(bf16[8,64,256]{2,1,0:T(8,128)(2,1)S(1)} %broadcast_in_dim.36), channel_id=1, replica_groups=mesh['yh'=2,'xh'=2,'xl'=2,'z'=8,'yl'=4,'c'=2] {'z'}, dimensions={0} | all-to-all | bytes 524288 | tf_op jit(solution)/shard_map/all_to_all | solution.py:78
  23.8 4.3 %all-to-all-start.1 = ((bf16[4,512,256]{2,1,0:T(8,128)(2,1)}), bf16[4,512,256]{2,1,0:T(8,128)(2,1)S(1)}, u32[]{:S(2)}, u32[]{:S(2)}) async-start(bf16[4,512,256]{2,1,0:T(8,128)(2,1)} %broadcast_in_dim.38), calls=%async_computation.1 | async-start | bytes 2097152 | tf_op jit(solution)/shard_map/all_to_all | solution.py:78
  29.8 8.7 %collective-permute-done.far_ref = bf16[64,768]{1,0:T(8,128)(2,1)S(1)} collective-permute-done((bf16[64,768]{1,0:T(8,128)(2,1)S(1)}, bf16[64,768]{1,0:T(8,128)(2,1)S(1)}, u32[]{:S(2)}, u32[]{:S(2)}) %collective-permute-start) | collective-permute-done | bytes 98336 | tf_op jit(solution)/shard_map/ppermute | solution.py:73
  44.7 6.8 %collective-permute-start.1 = (bf16[64,896]{1,0:T(8,128)(2,1)S(1)}, bf16[64,896]{1,0:T(8,128)(2,1)S(1)}, u32[]{:S(2)}, u32[]{:S(2)}) collective-permute-start(bf16[64,896]{1,0:T(8,128)(2,1)S(1)} %get-tuple-element.28), channel_id=1, source_target_pairs={{0,256},{1,257},{2,258},{3,259},{4,260},{5,261},{6,262},{7,263},{8... | collective-permute-start | bytes 344072 | tf_op jit(solution)/shard_map/ppermute | solution.py:97
  56.0 20.4 %all_to_all.41 = bf16[8,32,768]{2,1,0:T(8,128)(2,1)S(1)} all-to-all(bf16[8,32,768]{2,1,0:T(8,128)(2,1)S(1)} %bitcast.52), channel_id=1, replica_groups=mesh['yh'=2,'xh'=2,'xl'=2,'z'=8,'yl'=4,'c'=2] {'yh','xh','xl'}, dimensions={0} | all-to-all | bytes 786432 | tf_op jit(solution)/shard_map/all_to_all | solution.py:225
  81.7 10.3 %psum.7 = f32[192]{0:T(256)S(1)} all-reduce(f32[192]{0:T(256)S(1)} %reshape.108), channel_id=1, replica_groups=mesh['yh'=2,'xh'=2,'xl'=2,'z'=8,'yl'=4,'c'=2] {'yl','c'}, use_global_device_ids=true, to_apply=%region_4.5 | all-reduce | flops 192 | bytes 1536 | tf_op jit(solution)/shard_map/psum | solution.py:237
  98.3 10.3 %all-to-all-done.3.x_ref = bf16[8,96,768]{2,1,0:T(8,128)(2,1)S(1)} async-done(((bf16[8,96,768]{2,1,0:T(8,128)(2,1)}), bf16[8,96,768]{2,1,0:T(8,128)(2,1)S(1)}, u32[]{:S(2)}, u32[]{:S(2)}) %all-to-all-start.3) | async-done | bytes 1179680 | tf_op jit(solution)/shard_map/all_to_all | solution.py:225
  120.6 6.2 %gate_up_terms.2 = (bf16[192,1024]{1,0:T(8,128)(2,1)}, bf16[192,1024]{1,0:T(8,128)(2,1)}, bf16[192,1024]{1,0:T(8,128)(2,1)}, bf16[192,1024]{1,0:T(8,128)(2,1)}) custom-call(s32[2]{0:T(128)S(1)} %pad_add_fusion.order_ref, bf16[8,96,768]{2,1,0:T(8,128)(2,1)S(1)} %all-to-all-done.3.x_ref, bf16[8,96,768]{2,1,0:T(8,128)(2,1)} %collective-permute-done.3.o_ref, ...), custom_call_target="tpu_custom_call" | custom-call | flops 2415919104 | bytes 4718592 | tf_op jit(solution)/shard_map/gate_up_terms/pallas_call | solution.py:126
  129.1 13.8 %all-to-all-done.4.x_ref = bf16[8,104,768]{2,1,0:T(8,128)(2,1)S(1)} async-done(((bf16[8,104,768]{2,1,0:T(8,128)(2,1)}), bf16[8,104,768]{2,1,0:T(8,128)(2,1)S(1)}, u32[]{:S(2)}, u32[]{:S(2)}) %all-to-all-start.4) | async-done | bytes 1277984 | tf_op jit(solution)/shard_map/all_to_all | solution.py:225
  142.9 5.6 %collective-permute-done.5 = bf16[192,1024]{1,0:T(8,128)(2,1)} collective-permute-done((bf16[192,1024]{1,0:T(8,128)(2,1)}, bf16[192,1024]{1,0:T(8,128)(2,1)}, u32[]{:S(2)}, u32[]{:S(2)}) %collective-permute-start.5) | collective-permute-done | bytes 393248 | tf_op jit(solution)/shard_map/ppermute | solution.py:243
  155.6 5.8 %gate_up_terms.3 = (bf16[192,1024]{1,0:T(8,128)(2,1)}, bf16[192,1024]{1,0:T(8,128)(2,1)}, bf16[192,1024]{1,0:T(8,128)(2,1)}, bf16[192,1024]{1,0:T(8,128)(2,1)}) custom-call(s32[2]{0:T(128)S(1)} %pad_add_fusion.order_ref, bf16[8,104,768]{2,1,0:T(8,128)(2,1)S(1)} %all-to-all-done.4.x_ref, bf16[8,104,768]{2,1,0:T(8,128)(2,1)S(1)} %collective-permute-done.6.o_ref, ...), custom_call_target="tpu_custom_call" | custom-call | flops 2415919104 | bytes 4718592 | tf_op jit(solution)/shard_map/gate_up_terms/pallas_call | solution.py:126
  161.5 4.3 %collective-permute-start.9 = (bf16[192,1024]{1,0:T(8,128)(2,1)}, bf16[192,1024]{1,0:T(8,128)(2,1)S(1)}, u32[]{:S(2)}, u32[]{:S(2)}) collective-permute-start(bf16[192,1024]{1,0:T(8,128)(2,1)} %get-tuple-element.43), channel_id=1, source_target_pairs={{0,6},{2,4},{4,2},{6,0},{1,7},{3,5},{5,3},{7,1},{8,14},{10,12},{12... | collective-permute-start | bytes 1179656 | tf_op jit(solution)/shard_map/ppermute | solution.py:243
  166.4 15.6 %collective-permute-done.7 = bf16[192,1024]{1,0:T(8,128)(2,1)} collective-permute-done((bf16[192,1024]{1,0:T(8,128)(2,1)}, bf16[192,1024]{1,0:T(8,128)(2,1)}, u32[]{:S(2)}, u32[]{:S(2)}) %collective-permute-start.7) | collective-permute-done | bytes 393248 | tf_op jit(solution)/shard_map/ppermute | solution.py:243
  183.6 6.4 %collective-permute-start.8 = (bf16[192,512]{1,0:T(8,128)(2,1)S(1)}, bf16[192,512]{1,0:T(8,128)(2,1)S(1)}, u32[]{:S(2)}, u32[]{:S(2)}) collective-permute-start(bf16[192,512]{1,0:T(8,128)(2,1)S(1)} %fusion.3), channel_id=1, source_target_pairs={{0,2},{2,0},{4,6},{6,4},{1,3},{3,1},{5,7},{7,5},{8,10},{10,8},{12,... | collective-permute-start | bytes 589832 | tf_op jit(solution)/shard_map/ppermute | solution.py:243
  195.4 9.2 %collective-permute-done.10 = bf16[192,512]{1,0:T(8,128)(2,1)S(1)} collective-permute-done((bf16[192,512]{1,0:T(8,128)(2,1)S(1)}, bf16[192,512]{1,0:T(8,128)(2,1)S(1)}, u32[]{:S(2)}, u32[]{:S(2)}) %collective-permute-start.10) | collective-permute-done | bytes 196640 | tf_op jit(solution)/shard_map/ppermute | solution.py:243
  204.6 4.8 %collective-permute-done.11 = bf16[192,512]{1,0:T(8,128)(2,1)S(1)} collective-permute-done((bf16[192,512]{1,0:T(8,128)(2,1)S(1)}, bf16[192,512]{1,0:T(8,128)(2,1)S(1)}, u32[]{:S(2)}, u32[]{:S(2)}) %collective-permute-start.11) | collective-permute-done | bytes 196640 | tf_op jit(solution)/shard_map/ppermute | solution.py:243
  220.2 7.3 %all-to-all-start.5 = ((bf16[8,96,768]{2,1,0:T(8,128)(2,1)}), bf16[8,96,768]{2,1,0:T(8,128)(2,1)}, u32[]{:S(2)}, u32[]{:S(2)}) async-start(bf16[8,96,768]{2,1,0:T(8,128)(2,1)} %bitcast.12), calls=%async_computation.5 | async-start | bytes 2359296 | tf_op jit(solution)/shard_map/all_to_all | solution.py:225
  228.3 6.5 %collective-permute-done.14 = bf16[192,1024]{1,0:T(8,128)(2,1)S(1)} collective-permute-done((bf16[192,1024]{1,0:T(8,128)(2,1)}, bf16[192,1024]{1,0:T(8,128)(2,1)S(1)}, u32[]{:S(2)}, u32[]{:S(2)}) %collective-permute-start.14) | collective-permute-done | bytes 393248 | tf_op jit(solution)/shard_map/ppermute | solution.py:243
  237.0 5.2 %collective-permute-start.15 = (bf16[192,512]{1,0:T(8,128)(2,1)S(1)}, bf16[192,512]{1,0:T(8,128)(2,1)S(1)}, u32[]{:S(2)}, u32[]{:S(2)}) collective-permute-start(bf16[192,512]{1,0:T(8,128)(2,1)S(1)} %fusion.2), channel_id=1, source_target_pairs={{0,2},{2,0},{4,6},{6,4},{1,3},{3,1},{5,7},{7,5},{8,10},{10,8},{12,... | collective-permute-start | bytes 589832 | tf_op jit(solution)/shard_map/ppermute | solution.py:243
  247.6 10.2 %collective-permute-done.16 = bf16[192,512]{1,0:T(8,128)(2,1)S(1)} collective-permute-done((bf16[192,512]{1,0:T(8,128)(2,1)S(1)}, bf16[192,512]{1,0:T(8,128)(2,1)S(1)}, u32[]{:S(2)}, u32[]{:S(2)}) %collective-permute-start.16) | collective-permute-done | bytes 196640 | tf_op jit(solution)/shard_map/ppermute | solution.py:243
  257.8 4.8 %collective-permute-done.17 = bf16[192,512]{1,0:T(8,128)(2,1)S(1)} collective-permute-done((bf16[192,512]{1,0:T(8,128)(2,1)S(1)}, bf16[192,512]{1,0:T(8,128)(2,1)S(1)}, u32[]{:S(2)}, u32[]{:S(2)}) %collective-permute-start.17) | collective-permute-done | bytes 196640 | tf_op jit(solution)/shard_map/ppermute | solution.py:243
  269.7 7.1 %all-to-all-start.6 = ((bf16[8,96,768]{2,1,0:T(8,128)(2,1)}), bf16[8,96,768]{2,1,0:T(8,128)(2,1)S(1)}, u32[]{:S(2)}, u32[]{:S(2)}) async-start(bf16[8,96,768]{2,1,0:T(8,128)(2,1)} %bitcast.14), calls=%async_computation.6 | async-start | bytes 2359296 | tf_op jit(solution)/shard_map/all_to_all | solution.py:225
  278.4 30.4 %all-to-all-done.6 = bf16[8,96,768]{2,1,0:T(8,128)(2,1)S(1)} async-done(((bf16[8,96,768]{2,1,0:T(8,128)(2,1)}), bf16[8,96,768]{2,1,0:T(8,128)(2,1)S(1)}, u32[]{:S(2)}, u32[]{:S(2)}) %all-to-all-start.6) | async-done | bytes 1179680 | tf_op jit(solution)/shard_map/all_to_all | solution.py:225
  309.1 15.8 %all_to_all.42 = bf16[8,24,768]{2,1,0:T(8,128)(2,1)S(1)} all-to-all(bf16[8,24,768]{2,1,0:T(8,128)(2,1)S(1)} %pad_maximum_fusion.4), channel_id=1, replica_groups=mesh['yh'=2,'xh'=2,'xl'=2,'z'=8,'yl'=4,'c'=2] {'yh','xh','xl'}, dimensions={0} | all-to-all | bytes 589824 | tf_op jit(solution)/shard_map/all_to_all | solution.py:225
  (113 shorter events, 83.5 us)
Async XLA Ops:
  23.8 17.6 %all-to-all-start.1 = ((bf16[4,512,256]{2,1,0:T(8,128)(2,1)}), bf16[4,512,256]{2,1,0:T(8,128)(2,1)S(1)}, u32[]{:S(2)}, u32[]{:S(2)}) async-start(bf16[4,512,256]{2,1,0:T(8,128)(2,1)} %broadcast_in_dim.38), calls=%async_computation.1 | async-start | bytes 2097152 | tf_op jit(solution)/shard_map/all_to_all | solution.py:78
  28.1 10.4 %collective-permute-start = (bf16[64,768]{1,0:T(8,128)(2,1)S(1)}, bf16[64,768]{1,0:T(8,128)(2,1)S(1)}, u32[]{:S(2)}, u32[]{:S(2)}) collective-permute-start(bf16[64,768]{1,0:T(8,128)(2,1)S(1)} %copy-done.1), channel_id=1, source_target_pairs={{256,0},{257,1},{258,2},{259,3},{260,4},{261,5},{262,6},{263,7},{2... | collective-permute-start | bytes 294920 | tf_op jit(solution)/shard_map/ppermute | solution.py:73
  44.7 10.4 %collective-permute-start.1 = (bf16[64,896]{1,0:T(8,128)(2,1)S(1)}, bf16[64,896]{1,0:T(8,128)(2,1)S(1)}, u32[]{:S(2)}, u32[]{:S(2)}) collective-permute-start(bf16[64,896]{1,0:T(8,128)(2,1)S(1)} %get-tuple-element.28), channel_id=1, source_target_pairs={{0,256},{1,257},{2,258},{3,259},{4,260},{5,261},{6,262},{7,263},{8... | collective-permute-start | bytes 344072 | tf_op jit(solution)/shard_map/ppermute | solution.py:97
  77.6 31.0 %all-to-all-start.3 = ((bf16[8,96,768]{2,1,0:T(8,128)(2,1)}), bf16[8,96,768]{2,1,0:T(8,128)(2,1)S(1)}, u32[]{:S(2)}, u32[]{:S(2)}) async-start(bf16[8,96,768]{2,1,0:T(8,128)(2,1)} %broadcast_in_dim.76), calls=%async_computation.3 | async-start | bytes 2359296 | tf_op jit(solution)/shard_map/all_to_all | solution.py:225
  96.2 19.5 %collective-permute-start.2 = (bf16[1024,768]{1,0:T(8,128)(2,1)}, bf16[1024,768]{1,0:T(8,128)(2,1)}, u32[]{:S(2)}, u32[]{:S(2)}) collective-permute-start(bf16[1024,768]{1,0:T(8,128)(2,1)} %pad_maximum_fusion.1), channel_id=1, source_target_pairs={{0,1},{1,0},{2,3},{3,2},{4,5},{5,4},{6,7},{7,6},{8,9},{9,8},{10,11... | collective-permute-start | bytes 4718600 | tf_op jit(solution)/shard_map/ppermute | solution.py:27
  109.8 33.1 %all-to-all-start.4 = ((bf16[8,104,768]{2,1,0:T(8,128)(2,1)}), bf16[8,104,768]{2,1,0:T(8,128)(2,1)S(1)}, u32[]{:S(2)}, u32[]{:S(2)}) async-start(bf16[8,104,768]{2,1,0:T(8,128)(2,1)} %broadcast_in_dim.78), calls=%async_computation.4 | async-start | bytes 2555904 | tf_op jit(solution)/shard_map/all_to_all | solution.py:225
  115.8 4.9 %collective-permute-start.3 = (bf16[8,96,768]{2,1,0:T(8,128)(2,1)S(1)}, bf16[8,96,768]{2,1,0:T(8,128)(2,1)}, u32[]{:S(2)}, u32[]{:S(2)}) collective-permute-start(bf16[8,96,768]{2,1,0:T(8,128)(2,1)S(1)} %all-to-all-done.3.x_ref), channel_id=1, source_target_pairs={{0,1},{1,0},{2,3},{3,2},{4,5},{5,4},{6,7},{7,6},{8,9},{9,8},{10,11... | collective-permute-start | bytes 3538952 | tf_op jit(solution)/shard_map/ppermute | solution.py:27
  126.9 21.6 %collective-permute-start.5 = (bf16[192,1024]{1,0:T(8,128)(2,1)}, bf16[192,1024]{1,0:T(8,128)(2,1)}, u32[]{:S(2)}, u32[]{:S(2)}) collective-permute-start(bf16[192,1024]{1,0:T(8,128)(2,1)} %get-tuple-element.38), channel_id=1, source_target_pairs={{0,6},{2,4},{4,2},{6,0},{1,7},{3,5},{5,3},{7,1},{8,14},{10,12},{12... | collective-permute-start | bytes 1179656 | tf_op jit(solution)/shard_map/ppermute | solution.py:243
  148.5 7.1 %collective-permute-start.6 = (bf16[8,104,768]{2,1,0:T(8,128)(2,1)S(1)}, bf16[8,104,768]{2,1,0:T(8,128)(2,1)S(1)}, u32[]{:S(2)}, u32[]{:S(2)}) collective-permute-start(bf16[8,104,768]{2,1,0:T(8,128)(2,1)S(1)} %all-to-all-done.4.x_ref), channel_id=1, source_target_pairs={{0,1},{1,0},{2,3},{3,2},{4,5},{5,4},{6,7},{7,6},{8,9},{9,8},{10,11... | collective-permute-start | bytes 3833864 | tf_op jit(solution)/shard_map/ppermute | solution.py:27
  150.4 16.0 %collective-permute-start.4 = (bf16[192,1024]{1,0:T(8,128)(2,1)}, bf16[192,1024]{1,0:T(8,128)(2,1)}, u32[]{:S(2)}, u32[]{:S(2)}) collective-permute-start(bf16[192,1024]{1,0:T(8,128)(2,1)} %get-tuple-element.36), channel_id=1, source_target_pairs={{0,2},{2,0},{4,6},{6,4},{1,3},{3,1},{5,7},{7,5},{8,10},{10,8},{12,... | collective-permute-start | bytes 1179656 | tf_op jit(solution)/shard_map/ppermute | solution.py:243
  152.3 29.7 %collective-permute-start.7 = (bf16[192,1024]{1,0:T(8,128)(2,1)}, bf16[192,1024]{1,0:T(8,128)(2,1)}, u32[]{:S(2)}, u32[]{:S(2)}) collective-permute-start(bf16[192,1024]{1,0:T(8,128)(2,1)} %get-tuple-element.45), channel_id=1, source_target_pairs={{0,4},{2,6},{4,0},{6,2},{1,5},{3,7},{5,1},{7,3},{8,12},{10,14},{12... | collective-permute-start | bytes 1179656 | tf_op jit(solution)/shard_map/ppermute | solution.py:243
  161.5 34.0 %collective-permute-start.9 = (bf16[192,1024]{1,0:T(8,128)(2,1)}, bf16[192,1024]{1,0:T(8,128)(2,1)S(1)}, u32[]{:S(2)}, u32[]{:S(2)}) collective-permute-start(bf16[192,1024]{1,0:T(8,128)(2,1)} %get-tuple-element.43), channel_id=1, source_target_pairs={{0,6},{2,4},{4,2},{6,0},{1,7},{3,5},{5,3},{7,1},{8,14},{10,12},{12... | collective-permute-start | bytes 1179656 | tf_op jit(solution)/shard_map/ppermute | solution.py:243
  183.6 11.8 %collective-permute-start.8 = (bf16[192,512]{1,0:T(8,128)(2,1)S(1)}, bf16[192,512]{1,0:T(8,128)(2,1)S(1)}, u32[]{:S(2)}, u32[]{:S(2)}) collective-permute-start(bf16[192,512]{1,0:T(8,128)(2,1)S(1)} %fusion.3), channel_id=1, source_target_pairs={{0,2},{2,0},{4,6},{6,4},{1,3},{3,1},{5,7},{7,5},{8,10},{10,8},{12,... | collective-permute-start | bytes 589832 | tf_op jit(solution)/shard_map/ppermute | solution.py:243
  190.0 14.6 %collective-permute-start.10 = (bf16[192,512]{1,0:T(8,128)(2,1)S(1)}, bf16[192,512]{1,0:T(8,128)(2,1)S(1)}, u32[]{:S(2)}, u32[]{:S(2)}) collective-permute-start(bf16[192,512]{1,0:T(8,128)(2,1)S(1)} %fusion.3), channel_id=1, source_target_pairs={{0,4},{2,6},{4,0},{6,2},{1,5},{3,7},{5,1},{7,3},{8,12},{10,14},{12... | collective-permute-start | bytes 589832 | tf_op jit(solution)/shard_map/ppermute | solution.py:243
  191.9 17.5 %collective-permute-start.11 = (bf16[192,512]{1,0:T(8,128)(2,1)S(1)}, bf16[192,512]{1,0:T(8,128)(2,1)S(1)}, u32[]{:S(2)}, u32[]{:S(2)}) collective-permute-start(bf16[192,512]{1,0:T(8,128)(2,1)S(1)} %fusion.3), channel_id=1, source_target_pairs={{0,6},{2,4},{4,2},{6,0},{1,7},{3,5},{5,3},{7,1},{8,14},{10,12},{12... | collective-permute-start | bytes 589832 | tf_op jit(solution)/shard_map/ppermute | solution.py:243
  209.5 7.7 %collective-permute-start.12 = (bf16[768,512]{1,0:T(8,128)(2,1)S(1)}, bf16[768,512]{1,0:T(8,128)(2,1)S(1)}, u32[]{:S(2)}, u32[]{:S(2)}) collective-permute-start(bf16[768,512]{1,0:T(8,128)(2,1)S(1)} %pad_maximum_fusion.2.h_ref), channel_id=1, source_target_pairs={{0,1},{1,0},{2,3},{3,2},{4,5},{5,4},{6,7},{7,6},{8,9},{9,8},{10,11... | collective-permute-start | bytes 2359304 | tf_op jit(solution)/shard_map/ppermute | solution.py:27
  211.4 16.9 %collective-permute-start.13 = (bf16[192,1024]{1,0:T(8,128)(2,1)}, bf16[192,1024]{1,0:T(8,128)(2,1)S(1)}, u32[]{:S(2)}, u32[]{:S(2)}) collective-permute-start(bf16[192,1024]{1,0:T(8,128)(2,1)} %get-tuple-element.41), channel_id=1, source_target_pairs={{0,2},{2,0},{4,6},{6,4},{1,3},{3,1},{5,7},{7,5},{8,10},{10,8},{12,... | collective-permute-start | bytes 1179656 | tf_op jit(solution)/shard_map/ppermute | solution.py:243
  213.3 21.4 %collective-permute-start.14 = (bf16[192,1024]{1,0:T(8,128)(2,1)}, bf16[192,1024]{1,0:T(8,128)(2,1)S(1)}, u32[]{:S(2)}, u32[]{:S(2)}) collective-permute-start(bf16[192,1024]{1,0:T(8,128)(2,1)} %get-tuple-element.42), channel_id=1, source_target_pairs={{0,4},{2,6},{4,0},{6,2},{1,5},{3,7},{5,1},{7,3},{8,12},{10,14},{12... | collective-permute-start | bytes 1179656 | tf_op jit(solution)/shard_map/ppermute | solution.py:243
  220.2 49.5 %all-to-all-start.5 = ((bf16[8,96,768]{2,1,0:T(8,128)(2,1)}), bf16[8,96,768]{2,1,0:T(8,128)(2,1)}, u32[]{:S(2)}, u32[]{:S(2)}) async-start(bf16[8,96,768]{2,1,0:T(8,128)(2,1)} %bitcast.12), calls=%async_computation.5 | async-start | bytes 2359296 | tf_op jit(solution)/shard_map/all_to_all | solution.py:225
  237.0 10.6 %collective-permute-start.15 = (bf16[192,512]{1,0:T(8,128)(2,1)S(1)}, bf16[192,512]{1,0:T(8,128)(2,1)S(1)}, u32[]{:S(2)}, u32[]{:S(2)}) collective-permute-start(bf16[192,512]{1,0:T(8,128)(2,1)S(1)} %fusion.2), channel_id=1, source_target_pairs={{0,2},{2,0},{4,6},{6,4},{1,3},{3,1},{5,7},{7,5},{8,10},{10,8},{12,... | collective-permute-start | bytes 589832 | tf_op jit(solution)/shard_map/ppermute | solution.py:243
  242.2 15.6 %collective-permute-start.16 = (bf16[192,512]{1,0:T(8,128)(2,1)S(1)}, bf16[192,512]{1,0:T(8,128)(2,1)S(1)}, u32[]{:S(2)}, u32[]{:S(2)}) collective-permute-start(bf16[192,512]{1,0:T(8,128)(2,1)S(1)} %fusion.2), channel_id=1, source_target_pairs={{0,4},{2,6},{4,0},{6,2},{1,5},{3,7},{5,1},{7,3},{8,12},{10,14},{12... | collective-permute-start | bytes 589832 | tf_op jit(solution)/shard_map/ppermute | solution.py:243
  244.1 18.4 %collective-permute-start.17 = (bf16[192,512]{1,0:T(8,128)(2,1)S(1)}, bf16[192,512]{1,0:T(8,128)(2,1)S(1)}, u32[]{:S(2)}, u32[]{:S(2)}) collective-permute-start(bf16[192,512]{1,0:T(8,128)(2,1)S(1)} %fusion.2), channel_id=1, source_target_pairs={{0,6},{2,4},{4,2},{6,0},{1,7},{3,5},{5,3},{7,1},{8,14},{10,12},{12... | collective-permute-start | bytes 589832 | tf_op jit(solution)/shard_map/ppermute | solution.py:243
  262.6 4.2 %collective-permute-start.18 = (bf16[768,512]{1,0:T(8,128)(2,1)S(1)}, bf16[768,512]{1,0:T(8,128)(2,1)S(1)}, u32[]{:S(2)}, u32[]{:S(2)}) collective-permute-start(bf16[768,512]{1,0:T(8,128)(2,1)S(1)} %pad_maximum_fusion.3.h_ref), channel_id=1, source_target_pairs={{0,1},{1,0},{2,3},{3,2},{4,5},{5,4},{6,7},{7,6},{8,9},{9,8},{10,11... | collective-permute-start | bytes 2359304 | tf_op jit(solution)/shard_map/ppermute | solution.py:27
  269.7 39.1 %all-to-all-start.6 = ((bf16[8,96,768]{2,1,0:T(8,128)(2,1)}), bf16[8,96,768]{2,1,0:T(8,128)(2,1)S(1)}, u32[]{:S(2)}, u32[]{:S(2)}) async-start(bf16[8,96,768]{2,1,0:T(8,128)(2,1)} %bitcast.14), calls=%async_computation.6 | async-start | bytes 2359296 | tf_op jit(solution)/shard_map/all_to_all | solution.py:225
  (10 other events, 169.5 us)

commit v11 on v10

--- a/solution.py
+++ b/solution.py
@@ -265,7 +265,7 @@
     sums_a[1] = after(sums_a[1], *terms_b)
     hids_a = over_yl([hidden_of(sums_a, inverse[:, :block])] * 4)
     sums_b = over_yl(terms_b)
-    hids_a[1] = after(hids_a[1], sums_b[3])
+    hids_a[1] = after(hids_a[1], *sums_b[2:])
     down_a = down_of(hids_a)
     back_a = give_back(down_a)
     sums_b[1] = after(sums_b[1], down_a)

time: 327 us -> 332 us (1.015)
  waiting for transfers between devices: 133 us -> 141 us
    ppermute x12, waiting for transfers between devices: 58.3 us -> 65.9 us  [over_yl(): lax.ppermute(parts[i], 'yl', Y_XOR[i])]
  transfers between devices with their start and end apart: 24 -> 24, of which waited for: 19 -> 19; matrix products, arithmetic and copies ran while one was open for 4% -> 4% of each run, Pallas kernels for 6% -> 5%
where the time goes in v11:
time: 332 us; the launch traced here: 331 us
  waiting for transfers between devices  141 us (42%)
  starting transfers between devices  80.7 us (24%)
  blocking collectives  67.6 us (20%)
  Pallas kernels  21.3 us (6%)
  other arithmetic  10.4 us (3%)
  local copies, waits for them, and re-layouts  7.91 us (2%)
    ppermute x12, waiting for transfers between devices, over_yl(): lax.ppermute(parts[i], 'yl', Y_XOR[i])  65.9 us
    all_to_all x4, waiting for transfers between devices, all_to_all(): return lax.all_to_all(x, axes, split_axis=0, concat_axis=0, tiled=True)  54.6 us
    ppermute x12, starting transfers between devices, over_yl(): lax.ppermute(parts[i], 'yl', Y_XOR[i])  37 us
    all_to_all x2, blocking collectives, all_to_all(): return lax.all_to_all(x, axes, split_axis=0, concat_axis=0, tiled=True)  35.3 us
    all_to_all x1, blocking collectives, attend(): lax.all_to_all(copies, axes, split_axis=0, concat_axis=0, tiled=True)  22 us
    all_to_all x4, starting transfers between devices, all_to_all(): return lax.all_to_all(x, axes, split_axis=0, concat_axis=0, tiled=True)  21.7 us
    pallas_call x2, Pallas kernels, gate_up_terms(): pl.pallas_call(expand, grid_spec=pltpu.PrefetchScalarGridSpec(num_scalar_...  12.1 us
    psum x1, blocking collectives, body(): inverse = lax.rsqrt(lax.psum(squares, EXP) / D + 1e-05)  10.3 us
  transfers between devices with their start and end apart: 24, of which 19 were waited for; matrix products, arithmetic and copies ran while one was open for 4% of the time, Pallas kernels for 5%

profile of v11, /device:TPU:8, one launch (start us, length us, event | category | flops | bytes accessed | tf_op | source)
XLA Modules:
  0.0 330.5 jit_solution(16192415865293949905)
XLA Ops:
  0.8 22.0 %all_to_all.40 = bf16[8,64,256]{2,1,0:T(8,128)(2,1)S(1)} all-to-all(bf16[8,64,256]{2,1,0:T(8,128)(2,1)S(1)} %broadcast_in_dim.36), channel_id=1, replica_groups=mesh['yh'=2,'xh'=2,'xl'=2,'z'=8,'yl'=4,'c'=2] {'z'}, dimensions={0} | all-to-all | bytes 524288 | tf_op jit(solution)/shard_map/all_to_all | solution.py:78
  23.8 4.3 %all-to-all-start.1 = ((bf16[4,512,256]{2,1,0:T(8,128)(2,1)}), bf16[4,512,256]{2,1,0:T(8,128)(2,1)S(1)}, u32[]{:S(2)}, u32[]{:S(2)}) async-start(bf16[4,512,256]{2,1,0:T(8,128)(2,1)} %broadcast_in_dim.38), calls=%async_computation.1 | async-start | bytes 2097152 | tf_op jit(solution)/shard_map/all_to_all | solution.py:78
  29.8 8.7 %collective-permute-done.far_ref = bf16[64,768]{1,0:T(8,128)(2,1)S(1)} collective-permute-done((bf16[64,768]{1,0:T(8,128)(2,1)S(1)}, bf16[64,768]{1,0:T(8,128)(2,1)S(1)}, u32[]{:S(2)}, u32[]{:S(2)}) %collective-permute-start) | collective-permute-done | bytes 98336 | tf_op jit(solution)/shard_map/ppermute | solution.py:73
  44.7 6.8 %collective-permute-start.1 = (bf16[64,896]{1,0:T(8,128)(2,1)S(1)}, bf16[64,896]{1,0:T(8,128)(2,1)S(1)}, u32[]{:S(2)}, u32[]{:S(2)}) collective-permute-start(bf16[64,896]{1,0:T(8,128)(2,1)S(1)} %get-tuple-element.28), channel_id=1, source_target_pairs={{0,256},{1,257},{2,258},{3,259},{4,260},{5,261},{6,262},{7,263},{8... | collective-permute-start | bytes 344072 | tf_op jit(solution)/shard_map/ppermute | solution.py:97
  56.0 20.4 %all_to_all.41 = bf16[8,32,768]{2,1,0:T(8,128)(2,1)S(1)} all-to-all(bf16[8,32,768]{2,1,0:T(8,128)(2,1)S(1)} %bitcast.52), channel_id=1, replica_groups=mesh['yh'=2,'xh'=2,'xl'=2,'z'=8,'yl'=4,'c'=2] {'yh','xh','xl'}, dimensions={0} | all-to-all | bytes 786432 | tf_op jit(solution)/shard_map/all_to_all | solution.py:225
  81.7 10.3 %psum.7 = f32[192]{0:T(256)S(1)} all-reduce(f32[192]{0:T(256)S(1)} %reshape.108), channel_id=1, replica_groups=mesh['yh'=2,'xh'=2,'xl'=2,'z'=8,'yl'=4,'c'=2] {'yl','c'}, use_global_device_ids=true, to_apply=%region_4.5 | all-reduce | flops 192 | bytes 1536 | tf_op jit(solution)/shard_map/psum | solution.py:237
  98.3 10.3 %all-to-all-done.3.x_ref = bf16[8,96,768]{2,1,0:T(8,128)(2,1)S(1)} async-done(((bf16[8,96,768]{2,1,0:T(8,128)(2,1)}), bf16[8,96,768]{2,1,0:T(8,128)(2,1)S(1)}, u32[]{:S(2)}, u32[]{:S(2)}) %all-to-all-start.3) | async-done | bytes 1179680 | tf_op jit(solution)/shard_map/all_to_all | solution.py:225
  120.6 6.2 %gate_up_terms.2 = (bf16[192,1024]{1,0:T(8,128)(2,1)}, bf16[192,1024]{1,0:T(8,128)(2,1)}, bf16[192,1024]{1,0:T(8,128)(2,1)}, bf16[192,1024]{1,0:T(8,128)(2,1)}) custom-call(s32[2]{0:T(128)S(1)} %pad_add_fusion.order_ref, bf16[8,96,768]{2,1,0:T(8,128)(2,1)S(1)} %all-to-all-done.3.x_ref, bf16[8,96,768]{2,1,0:T(8,128)(2,1)} %collective-permute-done.3.o_ref, ...), custom_call_target="tpu_custom_call" | custom-call | flops 2415919104 | bytes 4718592 | tf_op jit(solution)/shard_map/gate_up_terms/pallas_call | solution.py:126
  129.1 13.8 %all-to-all-done.4.x_ref = bf16[8,104,768]{2,1,0:T(8,128)(2,1)S(1)} async-done(((bf16[8,104,768]{2,1,0:T(8,128)(2,1)}), bf16[8,104,768]{2,1,0:T(8,128)(2,1)S(1)}, u32[]{:S(2)}, u32[]{:S(2)}) %all-to-all-start.4) | async-done | bytes 1277984 | tf_op jit(solution)/shard_map/all_to_all | solution.py:225
  142.9 5.6 %collective-permute-done.5 = bf16[192,1024]{1,0:T(8,128)(2,1)} collective-permute-done((bf16[192,1024]{1,0:T(8,128)(2,1)}, bf16[192,1024]{1,0:T(8,128)(2,1)}, u32[]{:S(2)}, u32[]{:S(2)}) %collective-permute-start.5) | collective-permute-done | bytes 393248 | tf_op jit(solution)/shard_map/ppermute | solution.py:243
  155.6 5.9 %gate_up_terms.3 = (bf16[192,1024]{1,0:T(8,128)(2,1)}, bf16[192,1024]{1,0:T(8,128)(2,1)}, bf16[192,1024]{1,0:T(8,128)(2,1)}, bf16[192,1024]{1,0:T(8,128)(2,1)}) custom-call(s32[2]{0:T(128)S(1)} %pad_add_fusion.order_ref, bf16[8,104,768]{2,1,0:T(8,128)(2,1)S(1)} %all-to-all-done.4.x_ref, bf16[8,104,768]{2,1,0:T(8,128)(2,1)S(1)} %collective-permute-done.6.o_ref, ...), custom_call_target="tpu_custom_call" | custom-call | flops 2415919104 | bytes 4718592 | tf_op jit(solution)/shard_map/gate_up_terms/pallas_call | solution.py:126
  161.5 4.3 %collective-permute-start.10 = (bf16[192,1024]{1,0:T(8,128)(2,1)}, bf16[192,1024]{1,0:T(8,128)(2,1)S(1)}, u32[]{:S(2)}, u32[]{:S(2)}) collective-permute-start(bf16[192,1024]{1,0:T(8,128)(2,1)} %get-tuple-element.43), channel_id=1, source_target_pairs={{0,6},{2,4},{4,2},{6,0},{1,7},{3,5},{5,3},{7,1},{8,14},{10,12},{12... | collective-permute-start | bytes 1179656 | tf_op jit(solution)/shard_map/ppermute | solution.py:243
  168.6 21.8 %collective-permute-done.7 = bf16[192,1024]{1,0:T(8,128)(2,1)} collective-permute-done((bf16[192,1024]{1,0:T(8,128)(2,1)}, bf16[192,1024]{1,0:T(8,128)(2,1)}, u32[]{:S(2)}, u32[]{:S(2)}) %collective-permute-start.7) | collective-permute-done | bytes 393248 | tf_op jit(solution)/shard_map/ppermute | solution.py:243
  192.0 6.4 %collective-permute-start.8 = (bf16[192,512]{1,0:T(8,128)(2,1)S(1)}, bf16[192,512]{1,0:T(8,128)(2,1)S(1)}, u32[]{:S(2)}, u32[]{:S(2)}) collective-permute-start(bf16[192,512]{1,0:T(8,128)(2,1)S(1)} %fusion.3), channel_id=1, source_target_pairs={{0,2},{2,0},{4,6},{6,4},{1,3},{3,1},{5,7},{7,5},{8,10},{10,8},{12,... | collective-permute-start | bytes 589832 | tf_op jit(solution)/shard_map/ppermute | solution.py:243
  203.9 11.9 %collective-permute-done.9 = bf16[192,1024]{1,0:T(8,128)(2,1)S(1)} collective-permute-done((bf16[192,1024]{1,0:T(8,128)(2,1)}, bf16[192,1024]{1,0:T(8,128)(2,1)S(1)}, u32[]{:S(2)}, u32[]{:S(2)}) %collective-permute-start.9) | collective-permute-done | bytes 393248 | tf_op jit(solution)/shard_map/ppermute | solution.py:243
  215.7 4.1 %collective-permute-done.11 = bf16[192,512]{1,0:T(8,128)(2,1)S(1)} collective-permute-done((bf16[192,512]{1,0:T(8,128)(2,1)S(1)}, bf16[192,512]{1,0:T(8,128)(2,1)S(1)}, u32[]{:S(2)}, u32[]{:S(2)}) %collective-permute-start.11) | collective-permute-done | bytes 196640 | tf_op jit(solution)/shard_map/ppermute | solution.py:243
  219.8 6.3 %collective-permute-done.12 = bf16[192,512]{1,0:T(8,128)(2,1)S(1)} collective-permute-done((bf16[192,512]{1,0:T(8,128)(2,1)S(1)}, bf16[192,512]{1,0:T(8,128)(2,1)S(1)}, u32[]{:S(2)}, u32[]{:S(2)}) %collective-permute-start.12) | collective-permute-done | bytes 196640 | tf_op jit(solution)/shard_map/ppermute | solution.py:243
  233.3 7.3 %all-to-all-start.5 = ((bf16[8,96,768]{2,1,0:T(8,128)(2,1)}), bf16[8,96,768]{2,1,0:T(8,128)(2,1)}, u32[]{:S(2)}, u32[]{:S(2)}) async-start(bf16[8,96,768]{2,1,0:T(8,128)(2,1)} %bitcast.12), calls=%async_computation.5 | async-start | bytes 2359296 | tf_op jit(solution)/shard_map/all_to_all | solution.py:225
  248.9 4.3 %collective-permute-start.17 = (bf16[192,512]{1,0:T(8,128)(2,1)S(1)}, bf16[192,512]{1,0:T(8,128)(2,1)S(1)}, u32[]{:S(2)}, u32[]{:S(2)}) collective-permute-start(bf16[192,512]{1,0:T(8,128)(2,1)S(1)} %fusion.2), channel_id=1, source_target_pairs={{0,6},{2,4},{4,2},{6,0},{1,7},{3,5},{5,3},{7,1},{8,14},{10,12},{12... | collective-permute-start | bytes 589832 | tf_op jit(solution)/shard_map/ppermute | solution.py:243
  253.7 9.0 %collective-permute-done.16 = bf16[192,512]{1,0:T(8,128)(2,1)S(1)} collective-permute-done((bf16[192,512]{1,0:T(8,128)(2,1)S(1)}, bf16[192,512]{1,0:T(8,128)(2,1)S(1)}, u32[]{:S(2)}, u32[]{:S(2)}) %collective-permute-start.16) | collective-permute-done | bytes 196640 | tf_op jit(solution)/shard_map/ppermute | solution.py:243
  262.7 5.5 %collective-permute-done.17 = bf16[192,512]{1,0:T(8,128)(2,1)S(1)} collective-permute-done((bf16[192,512]{1,0:T(8,128)(2,1)S(1)}, bf16[192,512]{1,0:T(8,128)(2,1)S(1)}, u32[]{:S(2)}, u32[]{:S(2)}) %collective-permute-start.17) | collective-permute-done | bytes 196640 | tf_op jit(solution)/shard_map/ppermute | solution.py:243
  275.3 7.1 %all-to-all-start.6 = ((bf16[8,96,768]{2,1,0:T(8,128)(2,1)}), bf16[8,96,768]{2,1,0:T(8,128)(2,1)S(1)}, u32[]{:S(2)}, u32[]{:S(2)}) async-start(bf16[8,96,768]{2,1,0:T(8,128)(2,1)} %bitcast.14), calls=%async_computation.6 | async-start | bytes 2359296 | tf_op jit(solution)/shard_map/all_to_all | solution.py:225
  284.0 30.4 %all-to-all-done.6 = bf16[8,96,768]{2,1,0:T(8,128)(2,1)S(1)} async-done(((bf16[8,96,768]{2,1,0:T(8,128)(2,1)}), bf16[8,96,768]{2,1,0:T(8,128)(2,1)S(1)}, u32[]{:S(2)}, u32[]{:S(2)}) %all-to-all-start.6) | async-done | bytes 1179680 | tf_op jit(solution)/shard_map/all_to_all | solution.py:225
  314.7 14.9 %all_to_all.42 = bf16[8,24,768]{2,1,0:T(8,128)(2,1)S(1)} all-to-all(bf16[8,24,768]{2,1,0:T(8,128)(2,1)S(1)} %pad_maximum_fusion.4), channel_id=1, replica_groups=mesh['yh'=2,'xh'=2,'xl'=2,'z'=8,'yl'=4,'c'=2] {'yh','xh','xl'}, dimensions={0} | all-to-all | bytes 589824 | tf_op jit(solution)/shard_map/all_to_all | solution.py:225
  (113 shorter events, 82.5 us)
Async XLA Ops:
  23.8 17.6 %all-to-all-start.1 = ((bf16[4,512,256]{2,1,0:T(8,128)(2,1)}), bf16[4,512,256]{2,1,0:T(8,128)(2,1)S(1)}, u32[]{:S(2)}, u32[]{:S(2)}) async-start(bf16[4,512,256]{2,1,0:T(8,128)(2,1)} %broadcast_in_dim.38), calls=%async_computation.1 | async-start | bytes 2097152 | tf_op jit(solution)/shard_map/all_to_all | solution.py:78
  28.1 10.4 %collective-permute-start = (bf16[64,768]{1,0:T(8,128)(2,1)S(1)}, bf16[64,768]{1,0:T(8,128)(2,1)S(1)}, u32[]{:S(2)}, u32[]{:S(2)}) collective-permute-start(bf16[64,768]{1,0:T(8,128)(2,1)S(1)} %copy-done.1), channel_id=1, source_target_pairs={{256,0},{257,1},{258,2},{259,3},{260,4},{261,5},{262,6},{263,7},{2... | collective-permute-start | bytes 294920 | tf_op jit(solution)/shard_map/ppermute | solution.py:73
  44.7 10.4 %collective-permute-start.1 = (bf16[64,896]{1,0:T(8,128)(2,1)S(1)}, bf16[64,896]{1,0:T(8,128)(2,1)S(1)}, u32[]{:S(2)}, u32[]{:S(2)}) collective-permute-start(bf16[64,896]{1,0:T(8,128)(2,1)S(1)} %get-tuple-element.28), channel_id=1, source_target_pairs={{0,256},{1,257},{2,258},{3,259},{4,260},{5,261},{6,262},{7,263},{8... | collective-permute-start | bytes 344072 | tf_op jit(solution)/shard_map/ppermute | solution.py:97
  77.6 31.0 %all-to-all-start.3 = ((bf16[8,96,768]{2,1,0:T(8,128)(2,1)}), bf16[8,96,768]{2,1,0:T(8,128)(2,1)S(1)}, u32[]{:S(2)}, u32[]{:S(2)}) async-start(bf16[8,96,768]{2,1,0:T(8,128)(2,1)} %broadcast_in_dim.76), calls=%async_computation.3 | async-start | bytes 2359296 | tf_op jit(solution)/shard_map/all_to_all | solution.py:225
  96.2 19.5 %collective-permute-start.2 = (bf16[1024,768]{1,0:T(8,128)(2,1)}, bf16[1024,768]{1,0:T(8,128)(2,1)}, u32[]{:S(2)}, u32[]{:S(2)}) collective-permute-start(bf16[1024,768]{1,0:T(8,128)(2,1)} %pad_maximum_fusion.1), channel_id=1, source_target_pairs={{0,1},{1,0},{2,3},{3,2},{4,5},{5,4},{6,7},{7,6},{8,9},{9,8},{10,11... | collective-permute-start | bytes 4718600 | tf_op jit(solution)/shard_map/ppermute | solution.py:27
  109.8 33.1 %all-to-all-start.4 = ((bf16[8,104,768]{2,1,0:T(8,128)(2,1)}), bf16[8,104,768]{2,1,0:T(8,128)(2,1)S(1)}, u32[]{:S(2)}, u32[]{:S(2)}) async-start(bf16[8,104,768]{2,1,0:T(8,128)(2,1)} %broadcast_in_dim.78), calls=%async_computation.4 | async-start | bytes 2555904 | tf_op jit(solution)/shard_map/all_to_all | solution.py:225
  115.8 4.9 %collective-permute-start.3 = (bf16[8,96,768]{2,1,0:T(8,128)(2,1)S(1)}, bf16[8,96,768]{2,1,0:T(8,128)(2,1)}, u32[]{:S(2)}, u32[]{:S(2)}) collective-permute-start(bf16[8,96,768]{2,1,0:T(8,128)(2,1)S(1)} %all-to-all-done.3.x_ref), channel_id=1, source_target_pairs={{0,1},{1,0},{2,3},{3,2},{4,5},{5,4},{6,7},{7,6},{8,9},{9,8},{10,11... | collective-permute-start | bytes 3538952 | tf_op jit(solution)/shard_map/ppermute | solution.py:27
  126.9 21.6 %collective-permute-start.5 = (bf16[192,1024]{1,0:T(8,128)(2,1)}, bf16[192,1024]{1,0:T(8,128)(2,1)}, u32[]{:S(2)}, u32[]{:S(2)}) collective-permute-start(bf16[192,1024]{1,0:T(8,128)(2,1)} %get-tuple-element.38), channel_id=1, source_target_pairs={{0,6},{2,4},{4,2},{6,0},{1,7},{3,5},{5,3},{7,1},{8,14},{10,12},{12... | collective-permute-start | bytes 1179656 | tf_op jit(solution)/shard_map/ppermute | solution.py:243
  148.5 7.1 %collective-permute-start.6 = (bf16[8,104,768]{2,1,0:T(8,128)(2,1)S(1)}, bf16[8,104,768]{2,1,0:T(8,128)(2,1)S(1)}, u32[]{:S(2)}, u32[]{:S(2)}) collective-permute-start(bf16[8,104,768]{2,1,0:T(8,128)(2,1)S(1)} %all-to-all-done.4.x_ref), channel_id=1, source_target_pairs={{0,1},{1,0},{2,3},{3,2},{4,5},{5,4},{6,7},{7,6},{8,9},{9,8},{10,11... | collective-permute-start | bytes 3833864 | tf_op jit(solution)/shard_map/ppermute | solution.py:27
  150.4 18.2 %collective-permute-start.4 = (bf16[192,1024]{1,0:T(8,128)(2,1)}, bf16[192,1024]{1,0:T(8,128)(2,1)}, u32[]{:S(2)}, u32[]{:S(2)}) collective-permute-start(bf16[192,1024]{1,0:T(8,128)(2,1)} %get-tuple-element.36), channel_id=1, source_target_pairs={{0,2},{2,0},{4,6},{6,4},{1,3},{3,1},{5,7},{7,5},{8,10},{10,8},{12,... | collective-permute-start | bytes 1179656 | tf_op jit(solution)/shard_map/ppermute | solution.py:243
  152.3 38.1 %collective-permute-start.7 = (bf16[192,1024]{1,0:T(8,128)(2,1)}, bf16[192,1024]{1,0:T(8,128)(2,1)}, u32[]{:S(2)}, u32[]{:S(2)}) collective-permute-start(bf16[192,1024]{1,0:T(8,128)(2,1)} %get-tuple-element.45), channel_id=1, source_target_pairs={{0,4},{2,6},{4,0},{6,2},{1,5},{3,7},{5,1},{7,3},{8,12},{10,14},{12... | collective-permute-start | bytes 1179656 | tf_op jit(solution)/shard_map/ppermute | solution.py:243
  161.5 42.4 %collective-permute-start.10 = (bf16[192,1024]{1,0:T(8,128)(2,1)}, bf16[192,1024]{1,0:T(8,128)(2,1)S(1)}, u32[]{:S(2)}, u32[]{:S(2)}) collective-permute-start(bf16[192,1024]{1,0:T(8,128)(2,1)} %get-tuple-element.43), channel_id=1, source_target_pairs={{0,6},{2,4},{4,2},{6,0},{1,7},{3,5},{5,3},{7,1},{8,14},{10,12},{12... | collective-permute-start | bytes 1179656 | tf_op jit(solution)/shard_map/ppermute | solution.py:243
  165.8 49.9 %collective-permute-start.9 = (bf16[192,1024]{1,0:T(8,128)(2,1)}, bf16[192,1024]{1,0:T(8,128)(2,1)S(1)}, u32[]{:S(2)}, u32[]{:S(2)}) collective-permute-start(bf16[192,1024]{1,0:T(8,128)(2,1)} %get-tuple-element.42), channel_id=1, source_target_pairs={{0,4},{2,6},{4,0},{6,2},{1,5},{3,7},{5,1},{7,3},{8,12},{10,14},{12... | collective-permute-start | bytes 1179656 | tf_op jit(solution)/shard_map/ppermute | solution.py:243
  192.0 11.8 %collective-permute-start.8 = (bf16[192,512]{1,0:T(8,128)(2,1)S(1)}, bf16[192,512]{1,0:T(8,128)(2,1)S(1)}, u32[]{:S(2)}, u32[]{:S(2)}) collective-permute-start(bf16[192,512]{1,0:T(8,128)(2,1)S(1)} %fusion.3), channel_id=1, source_target_pairs={{0,2},{2,0},{4,6},{6,4},{1,3},{3,1},{5,7},{7,5},{8,10},{10,8},{12,... | collective-permute-start | bytes 589832 | tf_op jit(solution)/shard_map/ppermute | solution.py:243
  198.4 21.4 %collective-permute-start.11 = (bf16[192,512]{1,0:T(8,128)(2,1)S(1)}, bf16[192,512]{1,0:T(8,128)(2,1)S(1)}, u32[]{:S(2)}, u32[]{:S(2)}) collective-permute-start(bf16[192,512]{1,0:T(8,128)(2,1)S(1)} %fusion.3), channel_id=1, source_target_pairs={{0,4},{2,6},{4,0},{6,2},{1,5},{3,7},{5,1},{7,3},{8,12},{10,14},{12... | collective-permute-start | bytes 589832 | tf_op jit(solution)/shard_map/ppermute | solution.py:243
  200.3 25.8 %collective-permute-start.12 = (bf16[192,512]{1,0:T(8,128)(2,1)S(1)}, bf16[192,512]{1,0:T(8,128)(2,1)S(1)}, u32[]{:S(2)}, u32[]{:S(2)}) collective-permute-start(bf16[192,512]{1,0:T(8,128)(2,1)S(1)} %fusion.3), channel_id=1, source_target_pairs={{0,6},{2,4},{4,2},{6,0},{1,7},{3,5},{5,3},{7,1},{8,14},{10,12},{12... | collective-permute-start | bytes 589832 | tf_op jit(solution)/shard_map/ppermute | solution.py:243
  226.2 4.2 %collective-permute-start.13 = (bf16[768,512]{1,0:T(8,128)(2,1)S(1)}, bf16[768,512]{1,0:T(8,128)(2,1)S(1)}, u32[]{:S(2)}, u32[]{:S(2)}) collective-permute-start(bf16[768,512]{1,0:T(8,128)(2,1)S(1)} %pad_maximum_fusion.2.h_ref), channel_id=1, source_target_pairs={{0,1},{1,0},{2,3},{3,2},{4,5},{5,4},{6,7},{7,6},{8,9},{9,8},{10,11... | collective-permute-start | bytes 2359304 | tf_op jit(solution)/shard_map/ppermute | solution.py:27
  228.1 13.6 %collective-permute-start.14 = (bf16[192,1024]{1,0:T(8,128)(2,1)}, bf16[192,1024]{1,0:T(8,128)(2,1)S(1)}, u32[]{:S(2)}, u32[]{:S(2)}) collective-permute-start(bf16[192,1024]{1,0:T(8,128)(2,1)} %get-tuple-element.41), channel_id=1, source_target_pairs={{0,2},{2,0},{4,6},{6,4},{1,3},{3,1},{5,7},{7,5},{8,10},{10,8},{12,... | collective-permute-start | bytes 1179656 | tf_op jit(solution)/shard_map/ppermute | solution.py:243
  233.3 42.0 %all-to-all-start.5 = ((bf16[8,96,768]{2,1,0:T(8,128)(2,1)}), bf16[8,96,768]{2,1,0:T(8,128)(2,1)}, u32[]{:S(2)}, u32[]{:S(2)}) async-start(bf16[8,96,768]{2,1,0:T(8,128)(2,1)} %bitcast.12), calls=%async_computation.5 | async-start | bytes 2359296 | tf_op jit(solution)/shard_map/all_to_all | solution.py:225
  244.0 9.7 %collective-permute-start.15 = (bf16[192,512]{1,0:T(8,128)(2,1)S(1)}, bf16[192,512]{1,0:T(8,128)(2,1)S(1)}, u32[]{:S(2)}, u32[]{:S(2)}) collective-permute-start(bf16[192,512]{1,0:T(8,128)(2,1)S(1)} %fusion.2), channel_id=1, source_target_pairs={{0,2},{2,0},{4,6},{6,4},{1,3},{3,1},{5,7},{7,5},{8,10},{10,8},{12,... | collective-permute-start | bytes 589832 | tf_op jit(solution)/shard_map/ppermute | solution.py:243
  246.5 16.1 %collective-permute-start.16 = (bf16[192,512]{1,0:T(8,128)(2,1)S(1)}, bf16[192,512]{1,0:T(8,128)(2,1)S(1)}, u32[]{:S(2)}, u32[]{:S(2)}) collective-permute-start(bf16[192,512]{1,0:T(8,128)(2,1)S(1)} %fusion.2), channel_id=1, source_target_pairs={{0,4},{2,6},{4,0},{6,2},{1,5},{3,7},{5,1},{7,3},{8,12},{10,14},{12... | collective-permute-start | bytes 589832 | tf_op jit(solution)/shard_map/ppermute | solution.py:243
  248.9 19.2 %collective-permute-start.17 = (bf16[192,512]{1,0:T(8,128)(2,1)S(1)}, bf16[192,512]{1,0:T(8,128)(2,1)S(1)}, u32[]{:S(2)}, u32[]{:S(2)}) collective-permute-start(bf16[192,512]{1,0:T(8,128)(2,1)S(1)} %fusion.2), channel_id=1, source_target_pairs={{0,6},{2,4},{4,2},{6,0},{1,7},{3,5},{5,3},{7,1},{8,14},{10,12},{12... | collective-permute-start | bytes 589832 | tf_op jit(solution)/shard_map/ppermute | solution.py:243
  268.2 4.2 %collective-permute-start.18 = (bf16[768,512]{1,0:T(8,128)(2,1)S(1)}, bf16[768,512]{1,0:T(8,128)(2,1)S(1)}, u32[]{:S(2)}, u32[]{:S(2)}) collective-permute-start(bf16[768,512]{1,0:T(8,128)(2,1)S(1)} %pad_maximum_fusion.3.h_ref), channel_id=1, source_target_pairs={{0,1},{1,0},{2,3},{3,2},{4,5},{5,4},{6,7},{7,6},{8,9},{9,8},{10,11... | collective-permute-start | bytes 2359304 | tf_op jit(solution)/shard_map/ppermute | solution.py:27
  275.3 39.1 %all-to-all-start.6 = ((bf16[8,96,768]{2,1,0:T(8,128)(2,1)}), bf16[8,96,768]{2,1,0:T(8,128)(2,1)S(1)}, u32[]{:S(2)}, u32[]{:S(2)}) async-start(bf16[8,96,768]{2,1,0:T(8,128)(2,1)} %bitcast.14), calls=%async_computation.6 | async-start | bytes 2359296 | tf_op jit(solution)/shard_map/all_to_all | solution.py:225
  (10 other events, 183.8 us)
